TPU v7x, 32 devices: a whole 2x2x4 slice. The times are simulated.
32 devices in a mesh: fsdp: 16 (over z, y, x), tp: 2 (over core).
Axes of the slice: x: 2, y: 2, z: 4, core: 2. Of those that a mesh axis runs over, the one named last changes fastest.
Arguments:
- tokens: bfloat16 [2, 4096, 2048], P(None, ('fsdp', 'tp')), may hold values from -6 to 6
- seg_ids: int32 [2, 4096], P(None, 'fsdp'), may hold values from 0 to 31, never falling along the last dimension, each value on 1 to 400 neighbouring positions
- norm1_gain: bfloat16 [2048], P('fsdp'), may hold values from 0.5 to 1.5
- in_weight: bfloat16 [2048, 3, 2048], P(None, None, ('fsdp', 'tp')), may hold values from -0.125 to 0.125
- conv_weight: bfloat16 [3, 2048], P(None, ('fsdp', 'tp')), may hold values from -3.5 to 3.5
- out_weight: bfloat16 [2048, 2048], P(('fsdp', 'tp')), may hold values from -0.125 to 0.125
- norm2_gain: bfloat16 [2048], P('fsdp'), may hold values from 0.5 to 1.5
- gate_weight: bfloat16 [2048, 5632], P(None, ('fsdp', 'tp')), may hold values from -0.125 to 0.125
- up_weight: bfloat16 [2048, 5632], P(None, ('fsdp', 'tp')), may hold values from -0.125 to 0.125
- down_weight: bfloat16 [5632, 2048], P(('fsdp', 'tp')), may hold values from -0.109375 to 0.109375
- cotangent: bfloat16 [2, 4096, 2048], P(None, ('fsdp', 'tp')), may hold values from -6 to 6
Outputs:
- block_output: bfloat16 [2, 4096, 2048], P(None, ('fsdp', 'tp'))
- input_grad: bfloat16 [2, 4096, 2048], P(None, ('fsdp', 'tp'))
- norm1_grad: float32 [2048], P('fsdp')
- in_grad: float32 [2048, 3, 2048], P(None, None, ('fsdp', 'tp'))
- conv_grad: float32 [3, 2048], P(None, ('fsdp', 'tp'))
- out_grad: float32 [2048, 2048], P(('fsdp', 'tp'))
- norm2_grad: float32 [2048], P('fsdp')
- gate_grad: float32 [2048, 5632], P(None, ('fsdp', 'tp'))
- up_grad: float32 [2048, 5632], P(None, ('fsdp', 'tp'))
- down_grad: float32 [5632, 2048], P(('fsdp', 'tp'))
Inputs may be any that keep to these rules, and one draw needn't show every extreme that they name: `seg_ids`: along each micro-batch's 4096 rows the ids never fall; a document spans at most 400 rows, and one spans exactly min(400, 2048).
All inputs are finite; a program needn't handle non-finite values.
Results may differ from a plain program's by a relative error of at most 0.02.
Values may be sent and summed in bfloat16 or wider, within the bound.
No kernel may reach another device: no remote copies, remote signals or barrier semaphores. Data moves between devices by JAX's collectives and lax.ppermute only.
A program may use at most 168 MiB of HBM per device.

v0:
```python
import jax
import jax.numpy as jnp
from jax import lax
from jax.sharding import PartitionSpec as P

EPS = 1e-05


def matmul(left, right):
    return jnp.dot(left, right, preferred_element_type=jnp.float32)


def times_trans(left, right):
    return lax.dot_general(
        left, right, (((1,), (1,)), ((), ())), preferred_element_type=jnp.float32
    )


def trans_times(left, right):
    return lax.dot_general(
        left, right, (((0,), (0,)), ((), ())), preferred_element_type=jnp.float32
    )


def shift_down(value, places):
    return jnp.concatenate([jnp.zeros((places, value.shape[1]), value.dtype), value[:-places]], 0)


def shift_up(value, places):
    return jnp.concatenate([value[places:], jnp.zeros((places, value.shape[1]), value.dtype)], 0)


def same_doc(seg_row, places):
    equal = (seg_row[places:] == seg_row[:-places]).astype(jnp.float32)
    return jnp.concatenate([jnp.zeros((places,), jnp.float32), equal], 0)[:, None]


def norm_back(value, scale, gain, grad_norm):
    scaled = grad_norm * gain
    grad_value = scale * scaled - value * scale**3 * jnp.mean(scaled * value, -1, keepdims=True)
    grad_gain = jnp.sum(grad_norm * value * scale, 0)
    return (grad_value, grad_gain)


def gather_mixer(norm1_gain, in_weight, conv_weight, out_weight):
    return (
        lax.all_gather(norm1_gain, "fsdp", axis=0, tiled=True),
        lax.all_gather(in_weight, "fsdp", axis=2, tiled=True),
        lax.all_gather(conv_weight, "fsdp", axis=1, tiled=True),
        lax.all_gather(out_weight, "fsdp", axis=0, tiled=True),
    )


def gather_ffn(norm2_gain, gate_weight, up_weight, down_weight):
    return (
        lax.all_gather(norm2_gain, "fsdp", axis=0, tiled=True),
        lax.all_gather(gate_weight, "fsdp", axis=1, tiled=True),
        lax.all_gather(up_weight, "fsdp", axis=1, tiled=True),
        lax.all_gather(down_weight, "fsdp", axis=0, tiled=True),
    )


def gather_rows(value):
    return lax.all_gather(value, "tp", axis=0, tiled=True)


def sum_rows(value):
    return lax.psum_scatter(value, "tp", scatter_dimension=0, tiled=True)


def gather_grads(value):
    return lax.all_gather(value, "tp", axis=0, tiled=True)


def sum_grads(value):
    return lax.psum_scatter(value, "tp", scatter_dimension=0, tiled=True)


def reduce_weights(gradients):
    return (
        lax.psum_scatter(
            gradients[0].astype(jnp.bfloat16), "fsdp", scatter_dimension=0, tiled=True
        ).astype(jnp.float32),
        lax.psum_scatter(
            gradients[1].astype(jnp.bfloat16), "fsdp", scatter_dimension=2, tiled=True
        ).astype(jnp.float32),
        lax.psum_scatter(
            gradients[2].astype(jnp.bfloat16), "fsdp", scatter_dimension=1, tiled=True
        ).astype(jnp.float32),
        lax.psum_scatter(
            gradients[3].astype(jnp.bfloat16), "fsdp", scatter_dimension=0, tiled=True
        ).astype(jnp.float32),
        lax.psum_scatter(
            gradients[4].astype(jnp.bfloat16), "fsdp", scatter_dimension=0, tiled=True
        ).astype(jnp.float32),
        lax.psum_scatter(
            gradients[5].astype(jnp.bfloat16), "fsdp", scatter_dimension=1, tiled=True
        ).astype(jnp.float32),
        lax.psum_scatter(
            gradients[6].astype(jnp.bfloat16), "fsdp", scatter_dimension=1, tiled=True
        ).astype(jnp.float32),
        lax.psum_scatter(
            gradients[7].astype(jnp.bfloat16), "fsdp", scatter_dimension=0, tiled=True
        ).astype(jnp.float32),
    )


def on_device(
    tokens,
    seg_ids,
    norm1_gain,
    in_weight,
    conv_weight,
    out_weight,
    norm2_gain,
    gate_weight,
    up_weight,
    down_weight,
    cotangent,
):
    micro_count = tokens.shape[0]
    block_rows = []
    grad_rows = []
    summed = None
    for micro_idx in range(micro_count):
        gain_raw, in_mat, kernel_raw, out_mat = gather_mixer(
            norm1_gain, in_weight, conv_weight, out_weight
        )
        gain_raw_two, gate_mat, up_mat, down_mat = gather_ffn(
            norm2_gain, gate_weight, up_weight, down_weight
        )
        model_width = in_mat.shape[0]
        channels = in_mat.shape[2]
        in_flat = in_mat.reshape(model_width, 3 * channels)
        kernel = kernel_raw.astype(jnp.float32)
        gain_one = gain_raw.astype(jnp.float32)
        gain_two = gain_raw_two.astype(jnp.float32)
        inputs_f = tokens[micro_idx].astype(jnp.float32)
        scale_one = lax.rsqrt(jnp.mean(inputs_f * inputs_f, -1, keepdims=True) + EPS)
        normed = gather_rows((inputs_f * scale_one * gain_one).astype(jnp.bfloat16))
        projected = matmul(normed, in_flat).reshape(normed.shape[0], 3, channels)
        b_part = projected[:, 0]
        c_part = projected[:, 1]
        x_part = projected[:, 2]
        seg_row = seg_ids[micro_idx]
        mask_one = same_doc(seg_row, 1)
        mask_two = same_doc(seg_row, 2)
        gated_in = c_part * x_part
        conv_out = (
            kernel[0] * gated_in
            + kernel[1] * mask_one * shift_down(gated_in, 1)
            + kernel[2] * mask_two * shift_down(gated_in, 2)
        )
        mixed = (b_part * conv_out).astype(jnp.bfloat16)
        resid = inputs_f + sum_rows(matmul(mixed, out_mat))
        scale_two = lax.rsqrt(jnp.mean(resid * resid, -1, keepdims=True) + EPS)
        normed_two = gather_rows((resid * scale_two * gain_two).astype(jnp.bfloat16))
        gate_pre = matmul(normed_two, gate_mat)
        up_pre = matmul(normed_two, up_mat)
        sigma = jax.nn.sigmoid(gate_pre)
        activated = gate_pre * sigma
        hidden = (activated * up_pre).astype(jnp.bfloat16)
        block_rows.append((resid + sum_rows(matmul(hidden, down_mat))).astype(jnp.bfloat16))
        gain_raw, in_mat, kernel_raw, out_mat = gather_mixer(
            norm1_gain, in_weight, conv_weight, out_weight
        )
        gain_raw_two, gate_mat, up_mat, down_mat = gather_ffn(
            norm2_gain, gate_weight, up_weight, down_weight
        )
        in_flat = in_mat.reshape(model_width, 3 * channels)
        kernel = kernel_raw.astype(jnp.float32)
        gain_one = gain_raw.astype(jnp.float32)
        gain_two = gain_raw_two.astype(jnp.float32)
        grad_out = cotangent[micro_idx].astype(jnp.float32)
        grad_full = gather_grads(cotangent[micro_idx])
        grad_hidden = times_trans(grad_full, down_mat)
        down_term = trans_times(hidden, grad_full)
        grad_gate = (grad_hidden * up_pre * sigma * (1.0 + gate_pre * (1.0 - sigma))).astype(
            jnp.bfloat16
        )
        grad_up = (grad_hidden * activated).astype(jnp.bfloat16)
        gate_term = trans_times(normed_two, grad_gate)
        up_term = trans_times(normed_two, grad_up)
        grad_normed_two = sum_grads(times_trans(grad_gate, gate_mat) + times_trans(grad_up, up_mat))
        resid_back, norm_two_term = norm_back(resid, scale_two, gain_two, grad_normed_two)
        grad_resid = grad_out + resid_back
        grad_mixer = gather_grads(grad_resid.astype(jnp.bfloat16))
        out_term = trans_times(mixed, grad_mixer)
        grad_mixed = times_trans(grad_mixer, out_mat)
        grad_b = grad_mixed * conv_out
        grad_conv = grad_mixed * b_part
        grad_gated = (
            kernel[0] * grad_conv
            + kernel[1] * shift_up(mask_one * grad_conv, 1)
            + kernel[2] * shift_up(mask_two * grad_conv, 2)
        )
        conv_term = jnp.stack(
            [
                jnp.sum(grad_conv * gated_in, 0),
                jnp.sum(grad_conv * mask_one * shift_down(gated_in, 1), 0),
                jnp.sum(grad_conv * mask_two * shift_down(gated_in, 2), 0),
            ],
            0,
        )
        grad_projected = jnp.stack([grad_b, grad_gated * x_part, grad_gated * c_part], 1).astype(
            jnp.bfloat16
        )
        grad_flat = grad_projected.reshape(grad_projected.shape[0], 3 * channels)
        in_term = trans_times(normed, grad_flat).reshape(model_width, 3, channels)
        grad_normed = sum_grads(times_trans(grad_flat, in_flat))
        input_back, norm_one_term = norm_back(inputs_f, scale_one, gain_one, grad_normed)
        grad_rows.append((grad_resid + input_back).astype(jnp.bfloat16))
        gradients = (
            norm_one_term,
            in_term,
            conv_term,
            out_term,
            norm_two_term,
            gate_term,
            up_term,
            down_term,
        )
        reduced = reduce_weights(gradients)
        summed = (
            reduced
            if summed is None
            else tuple((first + second for first, second in zip(summed, reduced)))
        )
    gain_sum_one, gain_sum_two = lax.psum((summed[0], summed[4]), "tp")
    return (
        jnp.stack(block_rows),
        jnp.stack(grad_rows),
        gain_sum_one,
        summed[1],
        summed[2],
        summed[3],
        gain_sum_two,
        summed[5],
        summed[6],
        summed[7],
    )


def solution(mesh):
    return jax.shard_map(
        on_device,
        mesh=mesh,
        in_specs=(
            P(None, ("fsdp", "tp"), None),
            P(None, "fsdp"),
            P("fsdp"),
            P(None, None, ("fsdp", "tp")),
            P(None, ("fsdp", "tp")),
            P(("fsdp", "tp"), None),
            P("fsdp"),
            P(None, ("fsdp", "tp")),
            P(None, ("fsdp", "tp")),
            P(("fsdp", "tp"), None),
            P(None, ("fsdp", "tp"), None),
        ),
        out_specs=(
            P(None, ("fsdp", "tp"), None),
            P(None, ("fsdp", "tp"), None),
            P("fsdp"),
            P(None, None, ("fsdp", "tp")),
            P(None, ("fsdp", "tp")),
            P(("fsdp", "tp"), None),
            P("fsdp"),
            P(None, ("fsdp", "tp")),
            P(None, ("fsdp", "tp")),
            P(("fsdp", "tp"), None),
        ),
        check_vma=False,
    )
```

profile of v0, /device:TPU:0, one launch (start us, length us, event | category | flops | bytes accessed | tf_op | source)
XLA Modules:
  0.0 3363.0 jit_solution(2361333119843832031)
XLA Ops:
  7.2 42.4 %all-gather.2 = bf16[16,1,128]{2,1,0:T(2,128)(2,1)S(1)} all-gather(bf16[1,1,128]{2,1,0:T(2,128)(2,1)} %bitcast.238), channel_id=1, replica_groups=mesh['fsdp'=16,'tp'=2] {'fsdp'}, dimensions={0}, use_global_device_ids=true | all-gather | bytes 4352 | tf_op jit(solution)/shard_map/all_gather | solution.py:47
  56.3 35.7 %all-gather.3 = bf16[16,64,3]{1,2,0:T(4,128)(2,1)S(1)} all-gather(bf16[1,64,3]{1,2,0:T(4,128)(2,1)S(1)} %bitcast.237), channel_id=1, replica_groups=mesh['fsdp'=16,'tp'=2] {'fsdp'}, dimensions={0}, use_global_device_ids=true | all-gather | bytes 6528 | tf_op jit(solution)/shard_map/all_gather | solution.py:49
  92.5 122.6 %all-gather.21.cloned.1.call-done = bf16[2048,3,1024]{0,2,1:T(8,128)(2,1)} async-done(((bf16[2048,3,64]{0,2,1:T(8,128)(2,1)}), bf16[2048,3,1024]{0,2,1:T(8,128)(2,1)}) %all-gather.21.cloned.1.call-update) | async-done | bytes 12582928 | tf_op jit(solution)/shard_map/all_gather | solution.py:48
  215.1 6.7 fusion.2
  224.5 6.7 fusion
  236.7 67.7 %all-gather.23.cloned.1.call-done = bf16[1024,2048]{1,0:T(8,128)(2,1)} async-done(((bf16[64,2048]{1,0:T(8,128)(2,1)}), bf16[1024,2048]{1,0:T(8,128)(2,1)}) %all-gather.23.cloned.1.call-update) | async-done | bytes 4194320 | tf_op jit(solution)/shard_map/all_gather | solution.py:50
  304.4 4.8 fusion.56
  309.4 4.7 fusion.60
  314.9 38.2 %all-gather.4 = bf16[16,1,128]{2,1,0:T(2,128)(2,1)S(1)} all-gather(bf16[1,1,128]{2,1,0:T(2,128)(2,1)S(1)} %bitcast.239), channel_id=1, replica_groups=mesh['fsdp'=16,'tp'=2] {'fsdp'}, dimensions={0}, use_global_device_ids=true | all-gather | bytes 4352 | tf_op jit(solution)/shard_map/all_gather | solution.py:56
  353.2 2.8 multiply_reduce_fusion.11
  360.8 116.0 %all-gather.27.cloned.1.call-done = bf16[2048,2816]{0,1:T(8,128)(2,1)} async-done(((bf16[2048,176]{0,1:T(8,128)(2,1)}), bf16[2048,2816]{0,1:T(8,128)(2,1)}) %all-gather.27.cloned.1.call-update) | async-done | bytes 11534352 | tf_op jit(solution)/shard_map/all_gather | solution.py:57
  476.8 9.4 all-gather.25.cloned.1.call-done
  486.2 9.5 fusion.57
  495.6 136.6 %all-gather.29.cloned.1.call-done = bf16[2048,2816]{0,1:T(8,128)(2,1)} async-done(((bf16[2048,176]{0,1:T(8,128)(2,1)}), bf16[2048,2816]{0,1:T(8,128)(2,1)}) %all-gather.29.cloned.1.call-update) | async-done | bytes 11534352 | tf_op jit(solution)/shard_map/all_gather | solution.py:58
  632.3 9.2 fusion.58
  641.5 146.1 %all-gather.31.cloned.1.call-done = bf16[2816,2048]{1,0:T(8,128)(2,1)} async-done(((bf16[176,2048]{1,0:T(8,128)(2,1)}), bf16[2816,2048]{1,0:T(8,128)(2,1)}) %all-gather.31.cloned.1.call-update) | async-done | bytes 11534352 | tf_op jit(solution)/shard_map/all_gather | solution.py:59
  787.6 11.4 multiply_convert_fusion.2
  799.1 7.2 fusion.64
  806.3 9.2 convolution_add_fusion.1
  815.6 7.9 reduce-scatter.33.cloned.1.call-done
  823.4 3.3 multiply_reduce_fusion.1
  827.4 9.7 all-gather.35.cloned.1.call-done
  837.1 9.5 fusion.61
  846.6 9.6 fusion.62
  856.2 11.4 multiply_convert_fusion
  867.6 7.2 fusion.65
  874.8 9.0 convolution_add_fusion
  883.9 9.2 fusion.59
  893.2 9.4 fusion.63
  904.8 2.9 reduce-scatter.27.cloned.1.call-done
  907.7 13.0 reduce-scatter.31.cloned.1.call-done
  920.7 5.4 fusion.52
  927.1 9.4 all-gather.37.cloned.1.call-done
  936.5 5.1 multiply_reduce_fusion.7
  944.2 4.1 all-gather.39.cloned.1.call-done
  948.3 5.1 multiply_reduce_fusion.4
  964.7 9.9 convolution_bitcast_fusion.1
  977.5 7.9 convolution_bitcast_fusion
  985.5 3.4 convolution_convert_fusion.8
  990.3 3.3 convolution_convert_fusion.9
  995.3 6.0 convolution_convert_fusion.5
  1003.0 6.0 convolution_convert_fusion.4
  1010.3 6.0 convolution_convert_fusion.3
  1017.7 5.9 convolution_convert_fusion.2
  1025.3 6.0 convolution_convert_fusion.1
  1032.9 6.0 convolution_convert_fusion
  1041.1 7.6 convolution_convert_fusion.6
  1050.9 7.6 convolution_convert_fusion.7
  1063.5 49.9 %reduce-scatter.61.cloned.1.call-done = bf16[64,3]{1,0:T(8,128)(2,1)} async-done(((bf16[1024,3]{1,0:T(8,128)(2,1)}), bf16[64,3]{1,0:T(8,128)(2,1)}) %reduce-scatter.61.cloned.1.call-update) | async-done | bytes 400
  1114.8 6.8 reduce-scatter.35.cloned.1.call-done
  1121.6 13.2 reduce-scatter.39.cloned.1.call-done
  1136.9 78.0 %all-reduce.15 = (bf16[2048]{0:T(1024)(128)(2,1)S(1)}, bf16[2048]{0:T(1024)(128)(2,1)S(1)}, bf16[2048]{0:T(1024)(128)(2,1)S(1)}, bf16[2048]{0:T(1024)(128)(2,1)S(1)}) all-reduce(bf16[2048]{0:T(1024)(128)(2,1)S(1)} %get-tuple-element.16, bf16[2048]{0:T(1024)(128)(2,1)S(1)} %get-tuple-element.19, ...), channel_id=13, replica_groups=mesh['fsdp'=16,'tp'=2] {'fsdp'}, use_global_device_ids=true, to_apply=%region_19.0.clone | all-reduce | flops 8192 | bytes 32768
  1215.1 3.0 all-reduce.14
  1221.3 14.8 reduce-scatter.47.cloned.1.call-done
  1236.1 97.2 %reduce-scatter.45.cloned.1.call-done = bf16[64,2048]{1,0:T(8,128)(2,1)} async-done(((bf16[1024,2048]{1,0:T(8,128)(2,1)}), bf16[64,2048]{1,0:T(8,128)(2,1)}) %reduce-scatter.45.cloned.1.call-update) | async-done | bytes 262160 | tf_op jit(solution)/shard_map/reduce_scatter | solution.py:90
  1335.1 240.8 %reduce-scatter.49.cloned.1.call-done = bf16[2048,176]{0,1:T(8,128)(2,1)} async-done(((bf16[2048,2816]{0,1:T(8,128)(2,1)}), bf16[2048,176]{0,1:T(8,128)(2,1)}) %reduce-scatter.49.cloned.1.call-update) | async-done | bytes 720912 | tf_op jit(solution)/shard_map/reduce_scatter | solution.py:96
  1575.9 247.7 %reduce-scatter.51.cloned.1.call-done = bf16[2048,176]{0,1:T(8,128)(2,1)} async-done(((bf16[2048,2816]{0,1:T(8,128)(2,1)}), bf16[2048,176]{0,1:T(8,128)(2,1)}) %reduce-scatter.51.cloned.1.call-update) | async-done | bytes 720912 | tf_op jit(solution)/shard_map/reduce_scatter | solution.py:96
  1826.3 245.3 %reduce-scatter.53.cloned.1.call-done = bf16[2048,176]{0,1:T(8,128)(2,1)} async-done(((bf16[2048,2816]{0,1:T(8,128)(2,1)}), bf16[2048,176]{0,1:T(8,128)(2,1)}) %reduce-scatter.53.cloned.1.call-update) | async-done | bytes 720912 | tf_op jit(solution)/shard_map/reduce_scatter | solution.py:99
  2071.5 247.9 %reduce-scatter.55.cloned.1.call-done = bf16[2048,176]{0,1:T(8,128)(2,1)} async-done(((bf16[2048,2816]{0,1:T(8,128)(2,1)}), bf16[2048,176]{0,1:T(8,128)(2,1)}) %reduce-scatter.55.cloned.1.call-update) | async-done | bytes 720912 | tf_op jit(solution)/shard_map/reduce_scatter | solution.py:99
  2322.0 245.1 %reduce-scatter.57.cloned.1.call-done = bf16[176,2048]{1,0:T(8,128)(2,1)} async-done(((bf16[2816,2048]{1,0:T(8,128)(2,1)}), bf16[176,2048]{1,0:T(8,128)(2,1)}) %reduce-scatter.57.cloned.1.call-update) | async-done | bytes 720912 | tf_op jit(solution)/shard_map/reduce_scatter | solution.py:102
  2567.1 247.9 %reduce-scatter.59.cloned.1.call-done = bf16[176,2048]{1,0:T(8,128)(2,1)} async-done(((bf16[2816,2048]{1,0:T(8,128)(2,1)}), bf16[176,2048]{1,0:T(8,128)(2,1)}) %reduce-scatter.59.cloned.1.call-update) | async-done | bytes 720912 | tf_op jit(solution)/shard_map/reduce_scatter | solution.py:102
  2817.6 266.4 %reduce-scatter.43.cloned.1.call-done = bf16[2048,3,64]{0,2,1:T(8,128)(2,1)} async-done(((bf16[2048,3,1024]{0,2,1:T(8,128)(2,1)}), bf16[2048,3,64]{0,2,1:T(8,128)(2,1)}) %reduce-scatter.43.cloned.1.call-update) | async-done | bytes 786448 | tf_op jit(solution)/shard_map/reduce_scatter | solution.py:84
  3084.0 269.0 %reduce-scatter.41.cloned.1.call-done = bf16[2048,3,64]{0,2,1:T(8,128)(2,1)} async-done(((bf16[2048,3,1024]{0,2,1:T(8,128)(2,1)}), bf16[2048,3,64]{0,2,1:T(8,128)(2,1)}) %reduce-scatter.41.cloned.1.call-update) | async-done | bytes 786448 | tf_op jit(solution)/shard_map/reduce_scatter | solution.py:84
  3353.0 2.7 convert_add_fusion.2
  (261 shorter events, 77.5 us)
Async XLA Ops:
  7.2 49.1 %copy-start.59 = (bf16[3,64]{1,0:T(4,128)(2,1)S(1)}, bf16[3,64]{1,0:T(4,128)(2,1)}, u32[]{:S(2)}) copy-start(bf16[3,64]{1,0:T(4,128)(2,1)} %param.15) | copy-start | bytes 1156
  7.2 85.0 %copy-start.51 = (s32[2,256]{1,0:T(2,128)S(1)}, s32[2,256]{1,0:T(2,128)}, u32[]{:S(2)}) copy-start(s32[2,256]{1,0:T(2,128)} %param.12) | copy-start | bytes 6148
  7.2 85.3 %all-gather.19.cloned.1.call-start = ((), (), s32[]{:S(2)}) async-start(), calls=%async_computation.20 | async-start | bytes 1572864 | tf_op jit(solution)/shard_map/all_gather | solution.py:64
  51.7 2.5 copy-start.55
  54.2 160.9 %all-gather.21.cloned.1.call-start = ((), (), s32[]{:S(2)}) async-start(), calls=%async_computation.21 | async-start | bytes 13369344 | tf_op jit(solution)/shard_map/all_gather | solution.py:48
  55.0 169.6 %all-gather.33.cloned.1.call-start = ((), (), s32[]{:S(2)}) async-start(), calls=%async_computation.29 | async-start | bytes 1572864 | tf_op jit(solution)/shard_map/all_gather | solution.py:64
  55.7 248.7 %all-gather.23.cloned.1.call-start = ((), (), s32[]{:S(2)}) async-start(), calls=%async_computation.22 | async-start | bytes 4456448 | tf_op jit(solution)/shard_map/all_gather | solution.py:50
  56.3 296.9 %reduce-scatter.25.cloned.1.call-start = ((), (), s32[]{:S(2)}) async-start(), calls=%async_computation.23 | async-start | bytes 3145728 | tf_op jit(solution)/shard_map/reduce_scatter | solution.py:68
  231.3 3.0 copy-start.5
  236.7 72.6 %copy-start.24 = (bf16[256,1024]{1,0:T(8,128)(2,1)}, bf16[256,1024]{1,0:T(8,128)(2,1)S(1)}, u32[]{:S(2)}) copy-start(bf16[256,1024]{1,0:T(8,128)(2,1)S(1)} %get-tuple-element.54) | copy-start | bytes 1572868
  236.7 72.7 %copy-start.26 = (bf16[256,1024]{1,0:T(8,128)(2,1)}, bf16[256,1024]{1,0:T(8,128)(2,1)S(1)}, u32[]{:S(2)}) copy-start(bf16[256,1024]{1,0:T(8,128)(2,1)S(1)} %get-tuple-element.87) | copy-start | bytes 1572868
  309.3 43.9 %reduce-scatter.29.cloned.1.call-start = ((), (), s32[]{:S(2)}) async-start(), calls=%async_computation.30 | async-start | bytes 3145728 | tf_op jit(solution)/shard_map/reduce_scatter | solution.py:68
  309.3 5.6 copy-start.60
  314.1 39.1 %copy-start = (bf16[2,128,2048]{2,1,0:T(8,128)(2,1)S(1)}, bf16[2,128,2048]{2,1,0:T(8,128)(2,1)}, u32[]{:S(2)}) copy-start(bf16[2,128,2048]{2,1,0:T(8,128)(2,1)} %param.11) | copy-start | bytes 3145732
  314.1 162.7 %all-gather.27.cloned.1.call-start = ((), (), s32[]{:S(2)}) async-start(), calls=%async_computation.25 | async-start | bytes 12255232 | tf_op jit(solution)/shard_map/all_gather | solution.py:57
  314.9 171.3 %all-gather.25.cloned.1.call-start = ((), (), s32[]{:S(2)}) async-start(), calls=%async_computation.24 | async-start | bytes 1572864 | tf_op jit(solution)/shard_map/all_gather | solution.py:64
  356.0 2.7 copy-start.17
  357.9 274.3 %all-gather.29.cloned.1.call-start = ((), (), s32[]{:S(2)}) async-start(), calls=%async_computation.26 | async-start | bytes 12255232 | tf_op jit(solution)/shard_map/all_gather | solution.py:58
  358.7 282.8 %all-gather.41.cloned.1.call-start = ((), (), s32[]{:S(2)}) async-start(), calls=%async_computation.49 | async-start | bytes 1572864 | tf_op jit(solution)/shard_map/all_gather | solution.py:72
  359.8 427.8 %all-gather.31.cloned.1.call-start = ((), (), s32[]{:S(2)}) async-start(), calls=%async_computation.27 | async-start | bytes 12255232 | tf_op jit(solution)/shard_map/all_gather | solution.py:59
  360.5 462.9 %reduce-scatter.33.cloned.1.call-start = ((), (), s32[]{:S(2)}) async-start(), calls=%async_computation.33 | async-start | bytes 3145728 | tf_op jit(solution)/shard_map/reduce_scatter | solution.py:76
  486.2 146.1 %copy-start.11 = (bf16[256,2048]{1,0:T(8,128)(2,1)S(1)}, bf16[256,2048]{1,0:T(8,128)(2,1)}, u32[]{:S(2)}) copy-start(bf16[256,2048]{1,0:T(8,128)(2,1)} %all-gather.25.cloned.1.call-done) | copy-start | bytes 3145732
  799.1 7.2 copy-start.41
  799.1 7.2 copy-start.39
  806.3 17.1 copy-start.8
  815.5 21.6 all-gather.35.cloned.1.call-start
  826.8 29.4 all-gather.43.cloned.1.call-start
  827.3 75.4 %reduce-scatter.37.cloned.1.call-start = ((), (), s32[]{:S(2)}) async-start(), calls=%async_computation.36 | async-start | bytes 3145728 | tf_op jit(solution)/shard_map/reduce_scatter | solution.py:76
  837.1 9.5 copy-start.13
  867.6 7.2 copy-start.45
  867.6 7.2 copy-start.43
  883.9 23.9 reduce-scatter.27.cloned.1.call-start
  893.1 27.6 reduce-scatter.31.cloned.1.call-start
  902.6 33.9 %all-gather.37.cloned.1.call-start = ((), (), s32[]{:S(2)}) async-start(), calls=%async_computation.34 | async-start | bytes 1572864 | tf_op jit(solution)/shard_map/all_gather | solution.py:72
  926.1 22.2 all-gather.39.cloned.1.call-start
  926.9 135.8 %reduce-scatter.63.cloned.1.call-start = ((), (), s32[]{:S(2)}) async-start(), calls=%async_computation.52 | async-start | bytes 278528
  953.4 2.5 copy-start.20
  953.8 3.1 copy-start.3
  953.8 3.3 copy-start.10
  961.2 152.2 %reduce-scatter.61.cloned.1.call-start = ((), (), s32[]{:S(2)}) async-start(), calls=%async_computation.51 | async-start | bytes 278528
  964.7 157.0 %reduce-scatter.35.cloned.1.call-start = ((), (), s32[]{:S(2)}) async-start(), calls=%async_computation.35 | async-start | bytes 3145728 | tf_op jit(solution)/shard_map/reduce_scatter | solution.py:76
  974.6 160.2 %reduce-scatter.39.cloned.1.call-start = ((), (), s32[]{:S(2)}) async-start(), calls=%async_computation.38 | async-start | bytes 3145728 | tf_op jit(solution)/shard_map/reduce_scatter | solution.py:76
  974.7 2.8 copy-start.32
  977.5 8.0 copy-start.22
  977.5 8.0 copy-start.27
  985.5 250.6 %reduce-scatter.47.cloned.1.call-start = ((), (), s32[]{:S(2)}) async-start(), calls=%async_computation.42 | async-start | bytes 4456448 | tf_op jit(solution)/shard_map/reduce_scatter | solution.py:90
  989.0 344.3 %reduce-scatter.45.cloned.1.call-start = ((), (), s32[]{:S(2)}) async-start(), calls=%async_computation.41 | async-start | bytes 4456448 | tf_op jit(solution)/shard_map/reduce_scatter | solution.py:90
  993.6 582.3 %reduce-scatter.49.cloned.1.call-start = ((), (), s32[]{:S(2)}) async-start(), calls=%async_computation.43 | async-start | bytes 12255232 | tf_op jit(solution)/shard_map/reduce_scatter | solution.py:96
  1001.3 822.3 %reduce-scatter.51.cloned.1.call-start = ((), (), s32[]{:S(2)}) async-start(), calls=%async_computation.44 | async-start | bytes 12255232 | tf_op jit(solution)/shard_map/reduce_scatter | solution.py:96
  1009.0 1062.5 %reduce-scatter.53.cloned.1.call-start = ((), (), s32[]{:S(2)}) async-start(), calls=%async_computation.45 | async-start | bytes 12255232 | tf_op jit(solution)/shard_map/reduce_scatter | solution.py:99
  1016.3 1303.1 %reduce-scatter.55.cloned.1.call-start = ((), (), s32[]{:S(2)}) async-start(), calls=%async_computation.46 | async-start | bytes 12255232 | tf_op jit(solution)/shard_map/reduce_scatter | solution.py:99
  1023.6 1543.5 %reduce-scatter.57.cloned.1.call-start = ((), (), s32[]{:S(2)}) async-start(), calls=%async_computation.47 | async-start | bytes 12255232 | tf_op jit(solution)/shard_map/reduce_scatter | solution.py:102
  1031.2 1783.7 %reduce-scatter.59.cloned.1.call-start = ((), (), s32[]{:S(2)}) async-start(), calls=%async_computation.48 | async-start | bytes 12255232 | tf_op jit(solution)/shard_map/reduce_scatter | solution.py:102
  1038.9 2045.1 %reduce-scatter.43.cloned.1.call-start = ((), (), s32[]{:S(2)}) async-start(), calls=%async_computation.40 | async-start | bytes 13369344 | tf_op jit(solution)/shard_map/reduce_scatter | solution.py:84
  1048.7 2304.2 %reduce-scatter.41.cloned.1.call-start = ((), (), s32[]{:S(2)}) async-start(), calls=%async_computation.39 | async-start | bytes 13369344 | tf_op jit(solution)/shard_map/reduce_scatter | solution.py:84
  1058.6 76.2 %copy-start.50 = (f32[16,1,128]{2,1,0:T(1,128)S(1)}, f32[16,1,128]{2,1,0:T(1,128)}, u32[]{:S(2)}) copy-start(f32[16,1,128]{2,1,0:T(1,128)} %copy-done.49) | copy-start | bytes 24580
  1058.6 76.2 %copy-start.54 = (f32[128]{0:T(128)S(1)}, f32[128]{0:T(128)}, u32[]{:S(2)}) copy-start(f32[128]{0:T(128)} %copy-done.53) | copy-start | bytes 1540
  1058.6 76.2 %copy-start.56 = (f32[128]{0:T(128)S(1)}, f32[128]{0:T(128)}, u32[]{:S(2)}) copy-start(f32[128]{0:T(128)} %copy-done.55) | copy-start | bytes 1540
  1058.6 76.2 %copy-start.1 = (bf16[2,128,2048]{2,1,0:T(8,128)(2,1)S(1)}, bf16[2,128,2048]{2,1,0:T(8,128)(2,1)}, u32[]{:S(2)}) copy-start(bf16[2,128,2048]{2,1,0:T(8,128)(2,1)} %param.11) | copy-start | bytes 3145732
  1058.6 78.3 %copy-start.52 = (bf16[2048]{0:T(1024)(128)(2,1)S(1)}, bf16[2048]{0:T(1024)(128)(2,1)}, u32[]{:S(2)}) copy-start(bf16[2048]{0:T(1024)(128)(2,1)} %get-tuple-element.10) | copy-start | bytes 12292
  1058.6 159.4 %copy-start.15 = (f32[128,2048]{1,0:T(8,128)S(1)}, f32[128,2048]{1,0:T(8,128)}, u32[]{:S(2)}) copy-start(f32[128,2048]{1,0:T(8,128)} %get-tuple-element.47) | copy-start | bytes 3145732
  1058.6 159.4 %copy-start.16 = (f32[128,2048]{1,0:T(8,128)S(1)}, f32[128,2048]{1,0:T(8,128)}, u32[]{:S(2)}) copy-start(f32[128,2048]{1,0:T(8,128)} %get-tuple-element.69) | copy-start | bytes 3145732
  1058.6 159.4 %copy-start.57 = (f32[128]{0:T(128)S(1)}, f32[128]{0:T(128)}, u32[]{:S(2)}) copy-start(f32[128]{0:T(128)} %get-tuple-element.92) | copy-start | bytes 1540
  1058.7 159.4 %copy-start.58 = (f32[128]{0:T(128)S(1)}, f32[128]{0:T(128)}, u32[]{:S(2)}) copy-start(f32[128]{0:T(128)} %get-tuple-element.101) | copy-start | bytes 1540
  (31 other events, 44.5 us)
Sparse Core Ops, SparseCore 0:
  54.3 4.8 all-gather.18
  62.0 153.0 all-gather.20
  217.3 7.2 all-gather.32
  227.1 77.2 all-gather.22
  309.4 8.2 reduce-scatter.24
  319.8 10.7 reduce-scatter.28
  333.4 143.3 all-gather.26
  478.9 7.2 all-gather.24
  488.9 143.3 all-gather.28
  634.2 7.2 all-gather.40
  644.3 143.3 all-gather.30
  815.6 7.7 reduce-scatter.32
  826.9 10.2 all-gather.34
  839.2 10.1 all-gather.42
  884.0 10.7 reduce-scatter.36
  896.9 10.7 reduce-scatter.26
  909.9 10.7 reduce-scatter.30
  926.3 10.2 all-gather.36
  938.1 10.1 all-gather.38
  961.3 77.2 reduce-scatter.62
  1041.0 72.4 reduce-scatter.60
  1115.6 5.9 reduce-scatter.34
  1124.0 10.7 reduce-scatter.38
  1136.9 99.1 reduce-scatter.46
  1238.4 94.8 reduce-scatter.44
  1335.4 240.4 reduce-scatter.48
  1578.1 245.5 reduce-scatter.50
  1826.0 245.5 reduce-scatter.52
  2073.8 245.5 reduce-scatter.54
  2321.6 245.4 reduce-scatter.56
  2569.4 245.5 reduce-scatter.58
  2817.3 266.6 reduce-scatter.42
  3086.1 266.7 reduce-scatter.40
where the time goes:
time: 3370 us; the launch traced here: 3360 us
  waiting for transfers between devices  2840 us (84%)
  matrix products  220 us (7%)
  blocking collectives  197 us (6%)
  other arithmetic  51.4 us (2%)
    reduce_scatter x2, waiting for transfers between devices, reduce_weights(): lax.psum_scatter(gradients[1].astype(jnp.bfloat16), 'fsdp', scatter_dimen...  535 us
    reduce_scatter x2, waiting for transfers between devices, reduce_weights(): lax.psum_scatter(gradients[6].astype(jnp.bfloat16), 'fsdp', scatter_dimen...  493 us
    reduce_scatter x2, waiting for transfers between devices, reduce_weights(): lax.psum_scatter(gradients[7].astype(jnp.bfloat16), 'fsdp', scatter_dimen...  493 us
    reduce_scatter x2, waiting for transfers between devices, reduce_weights(): lax.psum_scatter(gradients[5].astype(jnp.bfloat16), 'fsdp', scatter_dimen...  489 us
    all_gather x1, waiting for transfers between devices, gather_ffn(): lax.all_gather(down_weight, 'fsdp', axis=0, tiled=True)  146 us
    all_gather x1, waiting for transfers between devices, gather_ffn(): lax.all_gather(up_weight, 'fsdp', axis=1, tiled=True)  137 us
    all_gather x1, waiting for transfers between devices, gather_mixer(): lax.all_gather(in_weight, 'fsdp', axis=2, tiled=True)  123 us
    all_gather x1, waiting for transfers between devices, gather_ffn(): lax.all_gather(gate_weight, 'fsdp', axis=1, tiled=True)  116 us
  transfers between devices with their start and end apart: 33, of which 27 were waited for; matrix products, arithmetic and copies ran while one was open for 6% of the time, Pallas kernels for 0%

commit v1 on v0

v1 whole, which is shorter than its diff:
```python
import jax
import jax.numpy as jnp
from jax import lax
from jax.sharding import PartitionSpec as P

EPS = 1e-05
RING = (0, 1, 3, 2)
PLANE = 4


def matmul(left, right):
    return jnp.dot(left, right, preferred_element_type=jnp.float32)


def times_trans(left, right):
    return lax.dot_general(
        left, right, (((1,), (1,)), ((), ())), preferred_element_type=jnp.float32
    )


def trans_times(left, right):
    return lax.dot_general(
        left, right, (((0,), (0,)), ((), ())), preferred_element_type=jnp.float32
    )


def low(value):
    return value.astype(jnp.bfloat16)


def high(value):
    return value.astype(jnp.float32)


class Groups:
    def __init__(self, fsdp, tp):
        self.fsdp, self.tp = fsdp, tp
        self.deep = fsdp // PLANE
        self.columns = [[b + PLANE * a for a in range(self.deep)] for b in range(PLANE)]

    def around(self, value, places):
        place = {b: i for i, b in enumerate(RING)}
        pairs = [
            (i, i - i % PLANE + RING[(place[i % PLANE] + places) % PLANE])
            for i in range(self.fsdp)
        ]
        return lax.ppermute(value, "fsdp", pairs)

    def along(self, value, places):
        pairs = [(i, (i + PLANE * places) % self.fsdp) for i in range(self.fsdp)]
        return lax.ppermute(value, "fsdp", pairs)

    def across(self, value, places):
        pairs = [(i, (i + places) % self.tp) for i in range(self.tp)]
        return lax.ppermute(value, "tp", pairs)

    def next_core(self, value):
        return lax.ppermute(value, "tp", [(i, i + 1) for i in range(self.tp - 1)])

    def last_core(self, value):
        return lax.ppermute(value, "tp", [(i + 1, i) for i in range(self.tp - 1)])

    def gather_plane(self, rows):
        half = rows.shape[0] // 2
        back = self.around(rows, 1)
        ahead = self.around(rows, -1)
        top = self.around(back[:half], 1)
        bottom = self.around(ahead[half:], -1)
        return jnp.concatenate([rows, back, top, bottom, ahead], 0)

    def reduce_plane(self, rows):
        count = rows.shape[0] // PLANE
        half = count // 2
        own, back, far, ahead = (rows[k * count : (k + 1) * count] for k in range(PLANE))
        top = self.around(low(far[:half]), -1)
        bottom = self.around(low(far[half:]), 1)
        back_sum = jnp.concatenate([low(high(back[:half]) + high(top)), low(back[half:])], 0)
        ahead_sum = jnp.concatenate([low(ahead[:half]), low(high(ahead[half:]) + high(bottom))], 0)
        one = self.around(back_sum, -1)
        two = self.around(ahead_sum, 1)
        return high(own) + high(one) + high(two)

    def gather_column(self, value):
        return lax.all_gather(
            value, "fsdp", axis=0, tiled=True, axis_index_groups=self.columns
        )

    def reduce_column(self, value):
        return lax.psum_scatter(
            value, "fsdp", scatter_dimension=0, tiled=True, axis_index_groups=self.columns
        )

    def cores(self, value):
        return [value] + [self.across(value, j) for j in range(1, self.tp)]

    def sum_cores(self, terms):
        total = terms[0]
        for j in range(1, self.tp):
            total = total + high(self.across(low(terms[j]), -j))
        return total

    def sum_all(self, value):
        total = value
        for j in range(1, self.tp):
            total = total + self.across(value, j)
        for move, size in ((self.around, PLANE), (self.along, self.deep)):
            part = total
            for j in range(1, size):
                total = total + move(part, j)
        return total

    def gather_features(self, value):
        me = lax.axis_index("fsdp")
        place = jnp.zeros((PLANE,), jnp.int32).at[jnp.array(RING)].set(jnp.arange(PLANE))
        mine = place[me % PLANE]
        flat = jnp.stack([value] + [self.around(value, j) for j in range(1, PLANE)])
        flat = flat[(mine - place) % PLANE]
        deep = jnp.stack([flat] + [self.along(flat, j) for j in range(1, self.deep)])
        deep = deep[(me // PLANE - jnp.arange(self.deep)) % self.deep]
        count, width = value.shape
        return deep.transpose(2, 0, 1, 3).reshape(count, self.fsdp * width)


def rms_scale(value):
    return lax.rsqrt(jnp.mean(value * value, -1, keepdims=True) + EPS)


def norm_back(value, scale, gain, grad_norm):
    scaled = grad_norm * gain
    grad_value = scale * scaled - value * scale**3 * jnp.mean(scaled * value, -1, keepdims=True)
    grad_gain = jnp.sum(grad_norm * value * scale, 0)
    return (grad_value, grad_gain)


def shift_down(value, places, before):
    return jnp.concatenate([before[:, 2 - places :], value[:, :-places]], 1)


def shift_up(value, places, after):
    return jnp.concatenate([value[:, places:], after[:, :places]], 1)


def on_device(
    tokens,
    seg_ids,
    norm1_gain,
    in_weight,
    conv_weight,
    out_weight,
    norm2_gain,
    gate_weight,
    up_weight,
    down_weight,
    cotangent,
    fsdp,
    tp,
):
    groups = Groups(fsdp, tp)
    deep = groups.deep
    micro_count, own_rows, width = tokens.shape
    rows = micro_count * own_rows
    share = in_weight.shape[2]
    hidden_share = gate_weight.shape[1]
    segments = PLANE * micro_count
    seq_len = seg_ids.shape[1]

    tokens_own = tokens.reshape(rows, width)
    cot_own = cotangent.reshape(rows, width)
    tokens_all = groups.gather_plane(tokens_own)

    gains = groups.gather_features(jnp.stack([norm1_gain, norm2_gain]))
    gain_one = high(gains[0])
    gain_two = high(gains[1])

    pad_rows = 16
    extra = jnp.zeros((pad_rows, width), jnp.bfloat16).at[0, : 3 * share].set(
        conv_weight.reshape(-1)
    )
    mixer = jnp.concatenate(
        [in_weight.transpose(1, 2, 0).reshape(3 * share, width), out_weight, extra], 0
    )
    mixer = groups.gather_column(mixer).reshape(deep, 4 * share + pad_rows, width)
    gate = groups.gather_column(gate_weight.T)
    up = groups.gather_column(up_weight.T)
    down = groups.gather_column(down_weight)

    taps = groups.cores(
        high(mixer[:, 4 * share, : 3 * share])
        .reshape(deep, 3, share)
        .transpose(1, 0, 2)
        .reshape(3, deep * share)
    )
    mats = groups.cores(
        mixer[:, : 4 * share]
        .reshape(deep, 4, share, width)
        .transpose(1, 0, 2, 3)
        .reshape(4, deep * share, width)
    )
    gate = groups.cores(gate)
    up = groups.cores(up)
    down = groups.cores(down)

    core = lax.axis_index("tp")
    same = []
    for places in (1, 2):
        equal = (seg_ids[:, places:] == seg_ids[:, :-places]).astype(jnp.float32)
        equal = jnp.concatenate([jnp.zeros((micro_count, places), jnp.float32), equal], 1)
        same.append(lax.dynamic_slice_in_dim(equal, core * own_rows, own_rows, 1))
    same = jnp.stack(same)
    same = jnp.stack([same] + [groups.around(same, k) for k in range(1, PLANE)])
    mask_one = same[:, 0].reshape(segments, own_rows, 1)
    mask_two = same[:, 1].reshape(segments, own_rows, 1)

    wide = high(tokens_all)
    scale_all = rms_scale(wide)
    normed = low(wide * scale_all * gain_one)
    parts = [
        [times_trans(normed, mat[k]).reshape(segments, own_rows, -1) for k in range(3)]
        for mat in mats
    ]
    gated_in = [part[1] * part[2] for part in parts]
    ends = [groups.next_core(value[:, -2:]) for value in gated_in]
    before = [ends[(j - 1) % tp] for j in range(tp)]
    one_back = [mask_one * shift_down(v, 1, b) for v, b in zip(gated_in, before)]
    two_back = [mask_two * shift_down(v, 2, b) for v, b in zip(gated_in, before)]
    conv_out = [
        tap[0] * v + tap[1] * one + tap[2] * two
        for tap, v, one, two in zip(taps, gated_in, one_back, two_back)
    ]
    mixed = [low(part[0] * out).reshape(PLANE * rows, -1) for part, out in zip(parts, conv_out)]
    mixer_out = sum(matmul(value, mat[3]) for value, mat in zip(mixed, mats))
    tokens_f = high(tokens_own)
    scale_one = rms_scale(tokens_f)
    resid = tokens_f + groups.reduce_plane(low(mixer_out))

    scale_two = rms_scale(resid)
    normed_two = groups.gather_plane(low(resid * scale_two * gain_two))
    cot_all = groups.gather_plane(cot_own)
    gate_pre = [times_trans(normed_two, mat) for mat in gate]
    up_pre = [times_trans(normed_two, mat) for mat in up]
    sigma = [jax.nn.sigmoid(value) for value in gate_pre]
    activated = [value * sig for value, sig in zip(gate_pre, sigma)]
    hidden = [low(act * value) for act, value in zip(activated, up_pre)]
    down_sum = groups.sum_cores([trans_times(value, cot_all) for value in hidden])
    down_grad = groups.reduce_column(low(down_sum))
    ffn_out = sum(matmul(value, mat) for value, mat in zip(hidden, down))

    grad_hidden = [times_trans(cot_all, mat) for mat in down]
    grad_gate = [
        low(gh * u * s * (1.0 + g * (1.0 - s)))
        for gh, u, s, g in zip(grad_hidden, up_pre, sigma, gate_pre)
    ]
    grad_up = [low(gh * act) for gh, act in zip(grad_hidden, activated)]
    back_two = sum(matmul(value, mat) for value, mat in zip(grad_gate, gate)) + sum(
        matmul(value, mat) for value, mat in zip(grad_up, up)
    )
    grad_normed_two = groups.reduce_plane(low(back_two))
    gate_sum = groups.sum_cores([trans_times(value, normed_two) for value in grad_gate])
    gate_grad = groups.reduce_column(low(gate_sum))
    up_sum = groups.sum_cores([trans_times(value, normed_two) for value in grad_up])
    up_grad = groups.reduce_column(low(up_sum))
    resid_back, norm_two_term = norm_back(resid, scale_two, gain_two, grad_normed_two)
    grad_resid = high(cot_own) + resid_back
    block_output = low(resid + groups.reduce_plane(low(ffn_out)))

    grad_mixer = groups.gather_plane(low(grad_resid))
    grad_mixed = [
        times_trans(grad_mixer, mat[3]).reshape(segments, own_rows, -1) for mat in mats
    ]
    grad_conv = [value * part[0] for value, part in zip(grad_mixed, parts)]
    masked_one = [mask_one * value for value in grad_conv]
    masked_two = [mask_two * value for value in grad_conv]
    starts = [
        groups.last_core(jnp.concatenate([one[:, :2], two[:, :2]], 0))
        for one, two in zip(masked_one, masked_two)
    ]
    after = [starts[(j + 1) % tp] for j in range(tp)]
    grad_gated = [
        tap[0] * value
        + tap[1] * shift_up(one, 1, edge[:segments])
        + tap[2] * shift_up(two, 2, edge[segments:])
        for tap, value, one, two, edge in zip(taps, grad_conv, masked_one, masked_two, after)
    ]
    grads = [
        [
            low(value).reshape(PLANE * rows, -1)
            for value in (gm * out, gg * part[2], gg * part[1])
        ]
        for gm, out, gg, part in zip(grad_mixed, conv_out, grad_gated, parts)
    ]
    back_one = sum(
        sum(matmul(value, mat[k]) for k, value in enumerate(grad)) for grad, mat in zip(grads, mats)
    )
    grad_normed = groups.reduce_plane(low(back_one))

    def column_sum(terms):
        return groups.reduce_column(low(groups.sum_cores(terms)))

    out_grad = column_sum([trans_times(value, grad_mixer) for value in mixed])
    in_grad = [
        column_sum([trans_times(grad[k], normed) for grad in grads]) for k in range(3)
    ]
    conv_term = groups.sum_cores(
        [
            jnp.stack([jnp.sum(gc * value, (0, 1)) for value in (gi, one, two)])
            for gc, gi, one, two in zip(grad_conv, gated_in, one_back, two_back)
        ]
    )
    conv_sum = conv_term
    for k in range(1, deep):
        conv_sum = conv_sum + groups.along(conv_term, k)
    chip = lax.axis_index("fsdp")
    conv_grad = lax.dynamic_slice_in_dim(
        conv_sum.reshape(3, deep * share), chip // PLANE * share, share, 1
    )
    input_back, norm_one_term = norm_back(tokens_f, scale_one, gain_one, grad_normed)
    input_grad = low(grad_resid + input_back)
    gain_sums = groups.sum_all(jnp.stack([norm_one_term, norm_two_term]))
    gain_share = norm1_gain.shape[0]
    gain_grads = lax.dynamic_slice_in_dim(gain_sums, chip * gain_share, gain_share, 1)
    return (
        block_output.reshape(tokens.shape),
        input_grad.reshape(tokens.shape),
        gain_grads[0],
        high(jnp.stack(in_grad)).transpose(2, 0, 1),
        conv_grad,
        high(out_grad),
        gain_grads[1],
        high(gate_grad).T,
        high(up_grad).T,
        high(down_grad),
    )


def solution(mesh):
    fsdp, tp = mesh.shape["fsdp"], mesh.shape["tp"]

    def body(*args):
        return on_device(*args, fsdp, tp)

    return jax.shard_map(
        body,
        mesh=mesh,
        in_specs=(
            P(None, ("fsdp", "tp"), None),
            P(None, "fsdp"),
            P("fsdp"),
            P(None, None, ("fsdp", "tp")),
            P(None, ("fsdp", "tp")),
            P(("fsdp", "tp"), None),
            P("fsdp"),
            P(None, ("fsdp", "tp")),
            P(None, ("fsdp", "tp")),
            P(("fsdp", "tp"), None),
            P(None, ("fsdp", "tp"), None),
        ),
        out_specs=(
            P(None, ("fsdp", "tp"), None),
            P(None, ("fsdp", "tp"), None),
            P("fsdp"),
            P(None, None, ("fsdp", "tp")),
            P(None, ("fsdp", "tp")),
            P(("fsdp", "tp"), None),
            P("fsdp"),
            P(None, ("fsdp", "tp")),
            P(None, ("fsdp", "tp")),
            P(("fsdp", "tp"), None),
        ),
        check_vma=False,
    )
```

time: 3370 us -> 776 us (0.23)
  waiting for transfers between devices: 2840 us -> 388 us
  blocking collectives: 197 us -> 0 us
  starting transfers between devices: 2.15 us -> 69.7 us
    reduce_scatter x18 -> x7, waiting for transfers between devices: 2170 us -> 89.5 us  [reduce_column(): lax.psum_scatter(value, 'fsdp', scatter_dimension=0, tiled=True, axis_ind...]
    all_gather x13 -> x4, waiting for transfers between devices: 623 us -> 96.6 us  [gather_column(): lax.all_gather(value, 'fsdp', axis=0, tiled=True, axis_index_groups=self....]
    ppermute x0 -> x68, waiting for transfers between devices: none -> 201 us  [the longest x41 182 us: around(): return lax.ppermute(value, 'fsdp', pairs)]
    all_gather x3 -> x0, blocking collectives: 116 us -> none  [the longest x1 42.4 us: gather_mixer(): lax.all_gather(norm1_gain, 'fsdp', axis=0, tiled=True)]
    unnamed x1 -> x0, blocking collectives: 78 us -> none
    ppermute x0 -> x68, starting transfers between devices: none -> 68.9 us  [the longest x41 46.7 us: around(): return lax.ppermute(value, 'fsdp', pairs)]
    unnamed x35 -> x11, waiting for transfers between devices: 55.5 us -> 0.86 us
    dot_general x10 -> x14, matrix products: 83.4 us -> 61.7 us  [times_trans(): lax.dot_general(left, right, (((1,), (1,)), ((), ())), preferred_element_...]
  transfers between devices with their start and end apart: 33 -> 79, of which waited for: 27 -> 38; matrix products, arithmetic and copies ran while one was open for 6% -> 30% of each run, Pallas kernels for 0% -> 0%
where the time goes in v1:
time: 776 us; the launch traced here: 767 us
  waiting for transfers between devices  388 us (50%)
  matrix products  205 us (26%)
  starting transfers between devices  69.7 us (9%)
  other arithmetic  46.4 us (6%)
  local copies, waits for them, and re-layouts  42.8 us (6%)
  between operations  15.9 us (2%)
    ppermute x41, waiting for transfers between devices, around(): return lax.ppermute(value, 'fsdp', pairs)  182 us
    all_gather x4, waiting for transfers between devices, gather_column(): lax.all_gather(value, 'fsdp', axis=0, tiled=True, axis_index_groups=self....  96.6 us
    reduce_scatter x7, waiting for transfers between devices, reduce_column(): lax.psum_scatter(value, 'fsdp', scatter_dimension=0, tiled=True, axis_ind...  89.5 us
    dot_general x14, matrix products, matmul(): return jnp.dot(left, right, preferred_element_type=jnp.float32)  86.4 us
    dot_general x14, matrix products, times_trans(): lax.dot_general(left, right, (((1,), (1,)), ((), ())), preferred_element_...  61.7 us
    dot_general x14, matrix products, trans_times(): lax.dot_general(left, right, (((0,), (0,)), ((), ())), preferred_element_...  56.5 us
    ppermute x41, starting transfers between devices, around(): return lax.ppermute(value, 'fsdp', pairs)  46.7 us
    unnamed x166, local copies, waits for them, and re-layouts  18.7 us
  transfers between devices with their start and end apart: 79, of which 38 were waited for; matrix products, arithmetic and copies ran while one was open for 30% of the time, Pallas kernels for 0%

profile of v1, /device:TPU:0, one launch (start us, length us, event | category | flops | bytes accessed | tf_op | source)
XLA Modules:
  0.0 766.9 jit_solution(3560345499415325372)
XLA Ops:
  11.3 3.0 collective-permute-start.4
  24.9 16.6 %collective-permute-done.10 = f32[2,2,128]{2,1,0:T(2,128)S(1)} collective-permute-done((f32[2,2,128]{2,1,0:T(2,128)S(1)}, f32[2,2,128]{2,1,0:T(2,128)S(1)}, u32[]{:S(2)}, u32[]{:S(2)}) %collective-permute-start.10) | collective-permute-done | bytes 2080 | tf_op jit(solution)/shard_map/ppermute | solution.py:47
  41.4 2.6 collective-permute-start.8
  47.9 3.0 collective-permute-done.7
  53.0 45.6 %all-gather.5.cloned.1.call-done = bf16[1088,2048]{1,0:T(8,128)(2,1)} async-done(((bf16[272,2048]{1,0:T(8,128)(2,1)}), bf16[1088,2048]{1,0:T(8,128)(2,1)}) %all-gather.5.cloned.1.call-update) | async-done | bytes 4456464 | tf_op jit(solution)/shard_map/all_gather | solution.py:84
  98.6 2.5 slice.414
  108.5 3.1 fusion.2
  112.5 2.8 fusion.66
  122.4 4.0 fusion.26
  126.4 3.9 fusion.70
  130.4 2.5 collective-permute-start.14
  132.9 4.2 multiply_convert_fusion.13
  137.1 2.9 multiply_convert_fusion.14
  141.4 2.5 add_convert_fusion.3
  151.4 11.0 %collective-permute-done.17 = bf16[128,2048]{1,0:T(8,128)(2,1)} collective-permute-done((bf16[128,2048]{1,0:T(8,128)(2,1)}, bf16[128,2048]{1,0:T(8,128)(2,1)}, u32[]{:S(2)}, u32[]{:S(2)}) %collective-permute-start.17) | collective-permute-done | bytes 524320 | tf_op jit(solution)/shard_map/ppermute | solution.py:47
  168.3 18.0 %collective-permute-done.32 = bf16[256,2048]{1,0:T(8,128)(2,1)} collective-permute-done((bf16[256,2048]{1,0:T(8,128)(2,1)S(1)}, bf16[256,2048]{1,0:T(8,128)(2,1)}, u32[]{:S(2)}, u32[]{:S(2)}) %collective-permute-start.32) | collective-permute-done | bytes 1048608 | tf_op jit(solution)/shard_map/ppermute | solution.py:47
  190.4 16.8 %collective-permute-done.18 = bf16[256,2048]{1,0:T(8,128)(2,1)S(1)} collective-permute-done((bf16[256,2048]{1,0:T(8,128)(2,1)S(1)}, bf16[256,2048]{1,0:T(8,128)(2,1)S(1)}, u32[]{:S(2)}, u32[]{:S(2)}) %collective-permute-start.18) | collective-permute-done | bytes 1048608 | tf_op jit(solution)/shard_map/ppermute | solution.py:47
  225.6 51.0 %all-gather.11.cloned.1.call-done = bf16[704,2048]{1,0:T(8,128)(2,1)} async-done(((bf16[176,2048]{1,0:T(8,128)(2,1)}), bf16[704,2048]{1,0:T(8,128)(2,1)}) %all-gather.11.cloned.1.call-update) | async-done | bytes 2883600 | tf_op jit(solution)/shard_map/all_gather | solution.py:84
  281.4 6.1 fusion.77
  288.9 3.2 collective-permute-done.22
  292.2 2.7 collective-permute-done.24
  296.2 3.2 fusion.73
  299.4 5.0 fusion.75
  304.4 5.0 fusion.76
  309.5 8.6 %multiply_convert_fusion = (bf16[1024,704]{0,1:T(8,128)(2,1)S(1)}, bf16[1024,704]{0,1:T(8,128)(2,1)S(1)}, bf16[1024,704]{0,1:T(8,128)(2,1)}) fusion(f32[1024,704]{0,1:T(8,128)S(1)} %fusion.75, f32[1024,704]{0,1:T(8,128)S(1)} %fusion.76, bf16[1024,2048]{1,0:T(8,128)(2,1)} %constant_dynamic-update-slice_fusion.10, ...), kind=kOutput, calls=%fused_computation.21 | convolution fusion | flops 2963603456 | bytes 17170432 | tf_op jit(solution)/shard_map/dot_general | solution.py:16
  319.2 7.8 %fusion.79 = f32[1024,2048]{1,0:T(8,128)} fusion(bf16[1024,704]{0,1:T(8,128)(2,1)S(1)} %get-tuple-element.52, bf16[704,2048]{1,0:T(8,128)(2,1)} %collective-permute-done.25), kind=kOutput, calls=%fused_computation.234 | convolution fusion | flops 2952790016 | bytes 12713984 | tf_op jit(solution)/shard_map/dot_general | solution.py:12
  327.0 5.6 multiply_convert_fusion.3
  332.6 5.8 fusion.78
  338.4 5.8 fusion.80
  344.2 11.4 %add_convert_fusion.1 = bf16[1024,2048]{1,0:T(8,128)(2,1)S(1)} fusion(f32[1024,2048]{1,0:T(8,128)} %fusion.80, f32[1024,2048]{1,0:T(8,128)} %fusion.78, f32[1024,2048]{1,0:T(8,128)} %fusion.79, bf16[1024,704]{0,1:T(8,128)(2,1)S(1)} %get-tuple-element.51, bf16[704,2048]{1,0:T(8,128)(2,1)} %collective-permute-done.26), kind=kOutput, calls=%fused_computation.8 | convolution fusion | flops 2961178624 | bytes 33685504 | tf_op jit(solution)/shard_map/dot_general | solution.py:12
  358.1 5.0 fusion.74
  363.1 4.0 add_convert_fusion.2
  372.6 9.7 %collective-permute-done.28 = bf16[128,2048]{1,0:T(8,128)(2,1)S(1)} collective-permute-done((bf16[128,2048]{1,0:T(8,128)(2,1)S(1)}, bf16[128,2048]{1,0:T(8,128)(2,1)S(1)}, u32[]{:S(2)}, u32[]{:S(2)}) %collective-permute-start.28) | collective-permute-done | bytes 524320 | tf_op jit(solution)/shard_map/ppermute | solution.py:47
  385.6 19.2 %collective-permute-done.37 = bf16[256,2048]{1,0:T(8,128)(2,1)S(1)} collective-permute-done((bf16[256,2048]{1,0:T(8,128)(2,1)S(1)}, bf16[256,2048]{1,0:T(8,128)(2,1)S(1)}, u32[]{:S(2)}, u32[]{:S(2)}) %collective-permute-start.37) | collective-permute-done | bytes 1048608 | tf_op jit(solution)/shard_map/ppermute | solution.py:47
  406.3 19.0 %collective-permute-done.29 = bf16[256,2048]{1,0:T(8,128)(2,1)S(1)} collective-permute-done((bf16[256,2048]{1,0:T(8,128)(2,1)S(1)}, bf16[256,2048]{1,0:T(8,128)(2,1)S(1)}, u32[]{:S(2)}, u32[]{:S(2)}) %collective-permute-start.29) | collective-permute-done | bytes 1048608 | tf_op jit(solution)/shard_map/ppermute | solution.py:47
  425.7 3.0 subtract_add_fusion
  431.1 21.2 %collective-permute-done.40 = bf16[256,2048]{1,0:T(8,128)(2,1)S(1)} collective-permute-done((bf16[256,2048]{1,0:T(8,128)(2,1)S(1)}, bf16[256,2048]{1,0:T(8,128)(2,1)S(1)}, u32[]{:S(2)}, u32[]{:S(2)}) %collective-permute-start.40) | collective-permute-done | bytes 1048608 | tf_op jit(solution)/shard_map/ppermute | solution.py:47
  455.0 8.4 %collective-permute-done.41 = bf16[128,2048]{1,0:T(8,128)(2,1)S(1)} collective-permute-done((bf16[128,2048]{1,0:T(8,128)(2,1)S(1)}, bf16[128,2048]{1,0:T(8,128)(2,1)S(1)}, u32[]{:S(2)}, u32[]{:S(2)}) %collective-permute-start.41) | collective-permute-done | bytes 524320 | tf_op jit(solution)/shard_map/ppermute | solution.py:47
  466.4 3.6 fusion.19
  472.4 6.0 multiply_reduce_fusion.9
  489.5 3.7 convolution_convert_fusion.5
  501.5 7.5 convolution_convert_fusion
  511.1 4.7 collective-permute-done.59
  518.1 8.3 %add_convert_fusion.4 = bf16[704,2048]{1,0:T(8,128)(2,1)} fusion(bf16[704,2048]{1,0:T(8,128)(2,1)} %collective-permute-done.67, bf16[1024,704]{0,1:T(8,128)(2,1)} %get-tuple-element.56, bf16[1024,2048]{1,0:T(8,128)(2,1)} %constant_dynamic-update-slice_fusion.10), kind=kOutput, calls=%fused_computation.11 | convolution fusion | flops 2957115392 | bytes 11403264 | tf_op jit(solution)/shard_map/dot_general | solution.py:22
  526.5 5.9 convolution_convert_fusion.1
  532.7 5.1 collective-permute-done.66
  537.8 4.5 add_convert_fusion.5
  542.6 7.5 convolution_convert_fusion.2
  550.2 4.6 fusion.81
  554.8 5.9 fusion.24
  560.7 4.6 fusion.82
  565.4 4.5 fusion.83
  569.9 5.9 fusion.34
  575.8 17.2 %add_convert_fusion = bf16[1024,2048]{1,0:T(8,128)(2,1)} fusion(f32[1024,2048]{1,0:T(8,128)} %fusion.24, f32[1024,2048]{1,0:T(8,128)} %fusion.34, f32[1024,2048]{1,0:T(8,128)} %fusion.83, f32[1024,2048]{1,0:T(8,128)} %fusion.81, f32[1024,2048]{1,0:T(8,128)} %fusion.82, bf16[1024,256]{1,0:T(8,128)(2,1)S(1)} %bitcast.257, ...), kind=kOutput, calls=%fused_computation.7 | convolution fusion | flops 1086324736 | bytes 47710208 | tf_op jit(solution)/shard_map/dot_general | solution.py:12
  596.9 6.3 add_convert_fusion.6
  603.2 5.9 collective-permute-done.46
  618.2 2.5 collective-permute-start.63
  620.6 16.5 %collective-permute-done.47 = bf16[256,2048]{1,0:T(8,128)(2,1)} collective-permute-done((bf16[256,2048]{1,0:T(8,128)(2,1)}, bf16[256,2048]{1,0:T(8,128)(2,1)}, u32[]{:S(2)}, u32[]{:S(2)}) %collective-permute-start.47) | collective-permute-done | bytes 1048608 | tf_op jit(solution)/shard_map/ppermute | solution.py:47
  638.9 3.3 fusion.13
  651.5 2.9 collective-permute-start.56
  654.4 3.7 fusion.10
  663.3 2.4 convert_element_type.460
  665.7 33.5 %reduce-scatter.18.cloned.1.call-done = bf16[176,2048]{1,0:T(8,128)(2,1)} async-done(((bf16[704,2048]{1,0:T(8,128)(2,1)}), bf16[176,2048]{1,0:T(8,128)(2,1)}) %reduce-scatter.18.cloned.1.call-update) | async-done | bytes 720912 | tf_op jit(solution)/shard_map/reduce_scatter | solution.py:89
  701.5 56.0 %reduce-scatter.16.cloned.1.call-done = bf16[176,2048]{1,0:T(8,128)(2,1)} async-done(((bf16[704,2048]{1,0:T(8,128)(2,1)}), bf16[176,2048]{1,0:T(8,128)(2,1)}) %reduce-scatter.16.cloned.1.call-update) | async-done | bytes 720912 | tf_op jit(solution)/shard_map/reduce_scatter | solution.py:89
  (428 shorter events, 162.8 us)
Async XLA Ops:
  7.2 91.3 %all-gather.5.cloned.1.call-start = ((), (), s32[]{:S(2)}) async-start(), calls=%async_computation.7 | async-start | bytes 5570560 | tf_op jit(solution)/shard_map/all_gather | solution.py:84
  10.5 210.3 %all-gather.7.cloned.1.call-start = ((), (), s32[]{:S(2)}) async-start(), calls=%async_computation.8 | async-start | bytes 3604480 | tf_op jit(solution)/shard_map/all_gather | solution.py:84
  11.3 213.8 %all-gather.9.cloned.1.call-start = ((), (), s32[]{:S(2)}) async-start(), calls=%async_computation.9 | async-start | bytes 3604480 | tf_op jit(solution)/shard_map/all_gather | solution.py:84
  11.3 10.8 %collective-permute-start.4 = (bf16[2,128]{1,0:T(2,128)(2,1)S(1)}, bf16[2,128]{1,0:T(2,128)(2,1)S(1)}, u32[]{:S(2)}, u32[]{:S(2)}) collective-permute-start(bf16[2,128]{1,0:T(2,128)(2,1)S(1)} %pad_maximum_fusion.16), channel_id=1, source_target_pairs={{0,2},{2,6},{4,0},{6,4},{8,10},{10,14},{12,8},{14,12},{16,18},{18,... | collective-permute-start | bytes 1544 | tf_op jit(solution)/shard_map/ppermute | solution.py:47
  14.3 8.4 %collective-permute-start.5 = (bf16[2,128]{1,0:T(2,128)(2,1)S(1)}, bf16[2,128]{1,0:T(2,128)(2,1)S(1)}, u32[]{:S(2)}, u32[]{:S(2)}) collective-permute-start(bf16[2,128]{1,0:T(2,128)(2,1)S(1)} %pad_maximum_fusion.16), channel_id=1, source_target_pairs={{0,6},{2,4},{4,2},{6,0},{8,14},{10,12},{12,10},{14,8},{16,22},{18,... | collective-permute-start | bytes 1544 | tf_op jit(solution)/shard_map/ppermute | solution.py:47
  15.8 8.3 %collective-permute-start.6 = (bf16[2,128]{1,0:T(2,128)(2,1)S(1)}, bf16[2,128]{1,0:T(2,128)(2,1)S(1)}, u32[]{:S(2)}, u32[]{:S(2)}) collective-permute-start(bf16[2,128]{1,0:T(2,128)(2,1)S(1)} %pad_maximum_fusion.16), channel_id=1, source_target_pairs={{0,4},{2,0},{4,6},{6,2},{8,12},{10,8},{12,14},{14,10},{16,20},{18,... | collective-permute-start | bytes 1544 | tf_op jit(solution)/shard_map/ppermute | solution.py:47
  17.3 28.8 %collective-permute-start = (bf16[256,2048]{1,0:T(8,128)(2,1)S(1)}, bf16[256,2048]{1,0:T(8,128)(2,1)S(1)}, u32[]{:S(2)}, u32[]{:S(2)}) collective-permute-start(bf16[256,2048]{1,0:T(8,128)(2,1)S(1)} %bitcast.222), channel_id=1, source_target_pairs={{0,2},{2,6},{4,0},{6,4},{8,10},{10,14},{12,8},{14,12},{16,18},{18,... | collective-permute-start | bytes 3145736 | tf_op jit(solution)/shard_map/ppermute | solution.py:47
  17.8 33.6 %collective-permute-start.2 = (bf16[256,2048]{1,0:T(8,128)(2,1)S(1)}, bf16[256,2048]{1,0:T(8,128)(2,1)S(1)}, u32[]{:S(2)}, u32[]{:S(2)}) collective-permute-start(bf16[256,2048]{1,0:T(8,128)(2,1)S(1)} %bitcast.223), channel_id=1, source_target_pairs={{0,4},{2,0},{4,6},{6,2},{8,12},{10,8},{12,14},{14,10},{16,20},{18,... | collective-permute-start | bytes 3145736 | tf_op jit(solution)/shard_map/ppermute | solution.py:47
  19.4 257.3 %all-gather.11.cloned.1.call-start = ((), (), s32[]{:S(2)}) async-start(), calls=%async_computation.10 | async-start | bytes 3604480 | tf_op jit(solution)/shard_map/all_gather | solution.py:84
  22.1 19.3 %collective-permute-start.10 = (f32[2,2,128]{2,1,0:T(2,128)S(1)}, f32[2,2,128]{2,1,0:T(2,128)S(1)}, u32[]{:S(2)}, u32[]{:S(2)}) collective-permute-start(f32[2,2,128]{2,1,0:T(2,128)S(1)} %get-tuple-element.108), channel_id=1, source_target_pairs={{0,2},{2,6},{4,0},{6,4},{8,10},{10,14},{12,8},{14,12},{16,18},{18,... | collective-permute-start | bytes 6152 | tf_op jit(solution)/shard_map/ppermute | solution.py:47
  22.7 21.3 %collective-permute-start.11 = (f32[2,2,128]{2,1,0:T(2,128)S(1)}, f32[2,2,128]{2,1,0:T(2,128)S(1)}, u32[]{:S(2)}, u32[]{:S(2)}) collective-permute-start(f32[2,2,128]{2,1,0:T(2,128)S(1)} %get-tuple-element.108), channel_id=1, source_target_pairs={{0,6},{2,4},{4,2},{6,0},{8,14},{10,12},{12,10},{14,8},{16,22},{18,... | collective-permute-start | bytes 6152 | tf_op jit(solution)/shard_map/ppermute | solution.py:47
  24.1 21.2 %collective-permute-start.12 = (f32[2,2,128]{2,1,0:T(2,128)S(1)}, f32[2,2,128]{2,1,0:T(2,128)S(1)}, u32[]{:S(2)}, u32[]{:S(2)}) collective-permute-start(f32[2,2,128]{2,1,0:T(2,128)S(1)} %get-tuple-element.108), channel_id=1, source_target_pairs={{0,4},{2,0},{4,6},{6,2},{8,12},{10,8},{12,14},{14,10},{16,20},{18,... | collective-permute-start | bytes 6152 | tf_op jit(solution)/shard_map/ppermute | solution.py:47
  41.4 6.2 collective-permute-start.8
  46.9 59.4 %collective-permute-start.1 = (bf16[128,2048]{1,0:T(8,128)(2,1)}, bf16[128,2048]{1,0:T(8,128)(2,1)}, u32[]{:S(2)}, u32[]{:S(2)}) collective-permute-start(bf16[128,2048]{1,0:T(8,128)(2,1)} %slice.411), channel_id=1, source_target_pairs={{0,2},{2,6},{4,0},{6,4},{8,10},{10,14},{12,8},{14,12},{16,18},{18,... | collective-permute-start | bytes 1572872 | tf_op jit(solution)/shard_map/ppermute | solution.py:47
  51.5 55.9 %collective-permute-start.3 = (bf16[128,2048]{1,0:T(8,128)(2,1)S(1)}, bf16[128,2048]{1,0:T(8,128)(2,1)S(1)}, u32[]{:S(2)}, u32[]{:S(2)}) collective-permute-start(bf16[128,2048]{1,0:T(8,128)(2,1)S(1)} %slice.412), channel_id=1, source_target_pairs={{0,4},{2,0},{4,6},{6,2},{8,12},{10,8},{12,14},{14,10},{16,20},{18,... | collective-permute-start | bytes 1572872 | tf_op jit(solution)/shard_map/ppermute | solution.py:47
  105.2 17.2 %collective-permute-start.13 = (bf16[4,256,2048]{2,1,0:T(8,128)(2,1)}, bf16[4,256,2048]{2,1,0:T(8,128)(2,1)}, u32[]{:S(2)}, u32[]{:S(2)}) collective-permute-start(bf16[4,256,2048]{2,1,0:T(8,128)(2,1)} %bitcast.38), channel_id=1, source_target_pairs={{0,1},{1,0},{2,3},{3,2},{4,5},{5,4},{6,7},{7,6},{8,9},{9,8},{10,11... | collective-permute-start | bytes 12582920 | tf_op jit(solution)/shard_map/ppermute | solution.py:55
  112.5 9.3 %collective-permute-start.15 = (f32[3,256]{1,0:T(4,128)S(1)}, f32[3,256]{1,0:T(4,128)S(1)}, u32[]{:S(2)}, u32[]{:S(2)}) collective-permute-start(f32[3,256]{1,0:T(4,128)S(1)} %reshape.428), channel_id=1, source_target_pairs={{0,1},{1,0},{2,3},{3,2},{4,5},{5,4},{6,7},{7,6},{8,9},{9,8},{10,11... | collective-permute-start | bytes 9224 | tf_op jit(solution)/shard_map/ppermute | solution.py:55
  130.4 6.7 collective-permute-start.14
  147.2 15.2 %collective-permute-start.17 = (bf16[128,2048]{1,0:T(8,128)(2,1)}, bf16[128,2048]{1,0:T(8,128)(2,1)}, u32[]{:S(2)}, u32[]{:S(2)}) collective-permute-start(bf16[128,2048]{1,0:T(8,128)(2,1)} %get-tuple-element.77), channel_id=1, source_target_pairs={{0,4},{2,0},{4,6},{6,2},{8,12},{10,8},{12,14},{14,10},{16,20},{18,... | collective-permute-start | bytes 1572872 | tf_op jit(solution)/shard_map/ppermute | solution.py:47
  148.7 15.2 %collective-permute-start.19 = (bf16[128,2048]{1,0:T(8,128)(2,1)}, bf16[128,2048]{1,0:T(8,128)(2,1)}, u32[]{:S(2)}, u32[]{:S(2)}) collective-permute-start(bf16[128,2048]{1,0:T(8,128)(2,1)} %get-tuple-element.78), channel_id=1, source_target_pairs={{0,2},{2,6},{4,0},{6,4},{8,10},{10,14},{12,8},{14,12},{16,18},{18,... | collective-permute-start | bytes 1572872 | tf_op jit(solution)/shard_map/ppermute | solution.py:47
  149.2 37.1 %collective-permute-start.32 = (bf16[256,2048]{1,0:T(8,128)(2,1)S(1)}, bf16[256,2048]{1,0:T(8,128)(2,1)}, u32[]{:S(2)}, u32[]{:S(2)}) collective-permute-start(bf16[256,2048]{1,0:T(8,128)(2,1)S(1)} %bitcast.237), channel_id=1, source_target_pairs={{0,2},{2,6},{4,0},{6,4},{8,10},{10,14},{12,8},{14,12},{16,18},{18,... | collective-permute-start | bytes 3145736 | tf_op jit(solution)/shard_map/ppermute | solution.py:47
  150.7 37.3 %collective-permute-start.34 = (bf16[256,2048]{1,0:T(8,128)(2,1)S(1)}, bf16[256,2048]{1,0:T(8,128)(2,1)S(1)}, u32[]{:S(2)}, u32[]{:S(2)}) collective-permute-start(bf16[256,2048]{1,0:T(8,128)(2,1)S(1)} %bitcast.238), channel_id=1, source_target_pairs={{0,4},{2,0},{4,6},{6,2},{8,12},{10,8},{12,14},{14,10},{16,20},{18,... | collective-permute-start | bytes 3145736 | tf_op jit(solution)/shard_map/ppermute | solution.py:47
  151.3 507.9 %reduce-scatter.14.cloned.1.call-start = ((), (), s32[]{:S(2)}) async-start(), calls=%async_computation.14 | async-start | bytes 1310720 | tf_op jit(solution)/shard_map/reduce_scatter | solution.py:89
  166.1 41.1 %collective-permute-start.18 = (bf16[256,2048]{1,0:T(8,128)(2,1)S(1)}, bf16[256,2048]{1,0:T(8,128)(2,1)S(1)}, u32[]{:S(2)}, u32[]{:S(2)}) collective-permute-start(bf16[256,2048]{1,0:T(8,128)(2,1)S(1)} %pad_maximum_fusion), channel_id=1, source_target_pairs={{0,4},{2,0},{4,6},{6,2},{8,12},{10,8},{12,14},{14,10},{16,20},{18,... | collective-permute-start | bytes 3145736 | tf_op jit(solution)/shard_map/ppermute | solution.py:47
  167.7 41.0 %collective-permute-start.20 = (bf16[256,2048]{1,0:T(8,128)(2,1)S(1)}, bf16[256,2048]{1,0:T(8,128)(2,1)S(1)}, u32[]{:S(2)}, u32[]{:S(2)}) collective-permute-start(bf16[256,2048]{1,0:T(8,128)(2,1)S(1)} %pad_maximum_fusion.1), channel_id=1, source_target_pairs={{0,2},{2,6},{4,0},{6,4},{8,10},{10,14},{12,8},{14,12},{16,18},{18,... | collective-permute-start | bytes 3145736 | tf_op jit(solution)/shard_map/ppermute | solution.py:47
  187.4 32.5 %collective-permute-start.33 = (bf16[128,2048]{1,0:T(8,128)(2,1)S(1)}, bf16[128,2048]{1,0:T(8,128)(2,1)S(1)}, u32[]{:S(2)}, u32[]{:S(2)}) collective-permute-start(bf16[128,2048]{1,0:T(8,128)(2,1)S(1)} %slice.457), channel_id=1, source_target_pairs={{0,2},{2,6},{4,0},{6,4},{8,10},{10,14},{12,8},{14,12},{16,18},{18,... | collective-permute-start | bytes 1572872 | tf_op jit(solution)/shard_map/ppermute | solution.py:47
  188.9 31.9 %collective-permute-start.35 = (bf16[128,2048]{1,0:T(8,128)(2,1)}, bf16[128,2048]{1,0:T(8,128)(2,1)}, u32[]{:S(2)}, u32[]{:S(2)}) collective-permute-start(bf16[128,2048]{1,0:T(8,128)(2,1)} %slice.458), channel_id=1, source_target_pairs={{0,4},{2,0},{4,6},{6,2},{8,12},{10,8},{12,14},{14,10},{16,20},{18,... | collective-permute-start | bytes 1572872 | tf_op jit(solution)/shard_map/ppermute | solution.py:47
  212.4 64.3 %collective-permute-start.21 = (bf16[256,2048]{1,0:T(8,128)(2,1)}, bf16[256,2048]{1,0:T(8,128)(2,1)}, u32[]{:S(2)}, u32[]{:S(2)}) collective-permute-start(bf16[256,2048]{1,0:T(8,128)(2,1)} %get-tuple-element.44), channel_id=1, source_target_pairs={{0,2},{2,6},{4,0},{6,4},{8,10},{10,14},{12,8},{14,12},{16,18},{18,... | collective-permute-start | bytes 3145736 | tf_op jit(solution)/shard_map/ppermute | solution.py:47
  212.9 66.4 %collective-permute-start.23 = (bf16[256,2048]{1,0:T(8,128)(2,1)}, bf16[256,2048]{1,0:T(8,128)(2,1)}, u32[]{:S(2)}, u32[]{:S(2)}) collective-permute-start(bf16[256,2048]{1,0:T(8,128)(2,1)} %get-tuple-element.44), channel_id=1, source_target_pairs={{0,4},{2,0},{4,6},{6,2},{8,12},{10,8},{12,14},{14,10},{16,20},{18,... | collective-permute-start | bytes 3145736 | tf_op jit(solution)/shard_map/ppermute | solution.py:47
  220.8 78.6 %collective-permute-start.25 = (bf16[704,2048]{1,0:T(8,128)(2,1)}, bf16[704,2048]{1,0:T(8,128)(2,1)}, u32[]{:S(2)}, u32[]{:S(2)}) collective-permute-start(bf16[704,2048]{1,0:T(8,128)(2,1)} %all-gather.7.cloned.1.call-done), channel_id=1, source_target_pairs={{0,1},{1,0},{2,3},{3,2},{4,5},{5,4},{6,7},{7,6},{8,9},{9,8},{10,11... | collective-permute-start | bytes 8650760 | tf_op jit(solution)/shard_map/ppermute | solution.py:55
  225.1 79.4 %collective-permute-start.26 = (bf16[704,2048]{1,0:T(8,128)(2,1)}, bf16[704,2048]{1,0:T(8,128)(2,1)}, u32[]{:S(2)}, u32[]{:S(2)}) collective-permute-start(bf16[704,2048]{1,0:T(8,128)(2,1)} %all-gather.9.cloned.1.call-done), channel_id=1, source_target_pairs={{0,1},{1,0},{2,3},{3,2},{4,5},{5,4},{6,7},{7,6},{8,9},{9,8},{10,11... | collective-permute-start | bytes 8650760 | tf_op jit(solution)/shard_map/ppermute | solution.py:55
  276.6 32.8 %collective-permute-start.27 = (bf16[704,2048]{1,0:T(8,128)(2,1)}, bf16[704,2048]{1,0:T(8,128)(2,1)S(1)}, u32[]{:S(2)}, u32[]{:S(2)}) collective-permute-start(bf16[704,2048]{1,0:T(8,128)(2,1)} %all-gather.11.cloned.1.call-done), channel_id=1, source_target_pairs={{0,1},{1,0},{2,3},{3,2},{4,5},{5,4},{6,7},{7,6},{8,9},{9,8},{10,11... | collective-permute-start | bytes 8650760 | tf_op jit(solution)/shard_map/ppermute | solution.py:55
  277.7 14.4 %collective-permute-start.22 = (bf16[128,2048]{1,0:T(8,128)(2,1)S(1)}, bf16[128,2048]{1,0:T(8,128)(2,1)S(1)}, u32[]{:S(2)}, u32[]{:S(2)}) collective-permute-start(bf16[128,2048]{1,0:T(8,128)(2,1)S(1)} %slice.448), channel_id=1, source_target_pairs={{0,2},{2,6},{4,0},{6,4},{8,10},{10,14},{12,8},{14,12},{16,18},{18,... | collective-permute-start | bytes 1572872 | tf_op jit(solution)/shard_map/ppermute | solution.py:47
  280.3 14.5 %collective-permute-start.24 = (bf16[128,2048]{1,0:T(8,128)(2,1)S(1)}, bf16[128,2048]{1,0:T(8,128)(2,1)S(1)}, u32[]{:S(2)}, u32[]{:S(2)}) collective-permute-start(bf16[128,2048]{1,0:T(8,128)(2,1)S(1)} %slice.449), channel_id=1, source_target_pairs={{0,4},{2,0},{4,6},{6,2},{8,12},{10,8},{12,14},{14,10},{16,20},{18,... | collective-permute-start | bytes 1572872 | tf_op jit(solution)/shard_map/ppermute | solution.py:47
  355.8 13.7 %collective-permute-start.36 = (bf16[128,2048]{1,0:T(8,128)(2,1)S(1)}, bf16[128,2048]{1,0:T(8,128)(2,1)S(1)}, u32[]{:S(2)}, u32[]{:S(2)}) collective-permute-start(bf16[128,2048]{1,0:T(8,128)(2,1)S(1)} %get-tuple-element.65), channel_id=1, source_target_pairs={{0,4},{2,0},{4,6},{6,2},{8,12},{10,8},{12,14},{14,10},{16,20},{18,... | collective-permute-start | bytes 1572872 | tf_op jit(solution)/shard_map/ppermute | solution.py:47
  356.4 13.5 %collective-permute-start.38 = (bf16[128,2048]{1,0:T(8,128)(2,1)S(1)}, bf16[128,2048]{1,0:T(8,128)(2,1)S(1)}, u32[]{:S(2)}, u32[]{:S(2)}) collective-permute-start(bf16[128,2048]{1,0:T(8,128)(2,1)S(1)} %get-tuple-element.66), channel_id=1, source_target_pairs={{0,2},{2,6},{4,0},{6,4},{8,10},{10,14},{12,8},{14,12},{16,18},{18,... | collective-permute-start | bytes 1572872 | tf_op jit(solution)/shard_map/ppermute | solution.py:47
  367.4 14.9 %collective-permute-start.28 = (bf16[128,2048]{1,0:T(8,128)(2,1)S(1)}, bf16[128,2048]{1,0:T(8,128)(2,1)S(1)}, u32[]{:S(2)}, u32[]{:S(2)}) collective-permute-start(bf16[128,2048]{1,0:T(8,128)(2,1)S(1)} %get-tuple-element.71), channel_id=1, source_target_pairs={{0,4},{2,0},{4,6},{6,2},{8,12},{10,8},{12,14},{14,10},{16,20},{18,... | collective-permute-start | bytes 1572872 | tf_op jit(solution)/shard_map/ppermute | solution.py:47
  368.0 14.9 %collective-permute-start.30 = (bf16[128,2048]{1,0:T(8,128)(2,1)S(1)}, bf16[128,2048]{1,0:T(8,128)(2,1)S(1)}, u32[]{:S(2)}, u32[]{:S(2)}) collective-permute-start(bf16[128,2048]{1,0:T(8,128)(2,1)S(1)} %get-tuple-element.72), channel_id=1, source_target_pairs={{0,2},{2,6},{4,0},{6,4},{8,10},{10,14},{12,8},{14,12},{16,18},{18,... | collective-permute-start | bytes 1572872 | tf_op jit(solution)/shard_map/ppermute | solution.py:47
  370.4 34.4 %collective-permute-start.37 = (bf16[256,2048]{1,0:T(8,128)(2,1)S(1)}, bf16[256,2048]{1,0:T(8,128)(2,1)S(1)}, u32[]{:S(2)}, u32[]{:S(2)}) collective-permute-start(bf16[256,2048]{1,0:T(8,128)(2,1)S(1)} %pad_maximum_fusion.4), channel_id=1, source_target_pairs={{0,4},{2,0},{4,6},{6,2},{8,12},{10,8},{12,14},{14,10},{16,20},{18,... | collective-permute-start | bytes 3145736 | tf_op jit(solution)/shard_map/ppermute | solution.py:47
  372.0 33.3 %collective-permute-start.39 = (bf16[256,2048]{1,0:T(8,128)(2,1)S(1)}, bf16[256,2048]{1,0:T(8,128)(2,1)S(1)}, u32[]{:S(2)}, u32[]{:S(2)}) collective-permute-start(bf16[256,2048]{1,0:T(8,128)(2,1)S(1)} %pad_maximum_fusion.5), channel_id=1, source_target_pairs={{0,2},{2,6},{4,0},{6,4},{8,10},{10,14},{12,8},{14,12},{16,18},{18,... | collective-permute-start | bytes 3145736 | tf_op jit(solution)/shard_map/ppermute | solution.py:47
  383.4 41.9 %collective-permute-start.29 = (bf16[256,2048]{1,0:T(8,128)(2,1)S(1)}, bf16[256,2048]{1,0:T(8,128)(2,1)S(1)}, u32[]{:S(2)}, u32[]{:S(2)}) collective-permute-start(bf16[256,2048]{1,0:T(8,128)(2,1)S(1)} %pad_maximum_fusion.2), channel_id=1, source_target_pairs={{0,4},{2,0},{4,6},{6,2},{8,12},{10,8},{12,14},{14,10},{16,20},{18,... | collective-permute-start | bytes 3145736 | tf_op jit(solution)/shard_map/ppermute | solution.py:47
  385.0 40.7 %collective-permute-start.31 = (bf16[256,2048]{1,0:T(8,128)(2,1)S(1)}, bf16[256,2048]{1,0:T(8,128)(2,1)S(1)}, u32[]{:S(2)}, u32[]{:S(2)}) collective-permute-start(bf16[256,2048]{1,0:T(8,128)(2,1)S(1)} %pad_maximum_fusion.3), channel_id=1, source_target_pairs={{0,2},{2,6},{4,0},{6,4},{8,10},{10,14},{12,8},{14,12},{16,18},{18,... | collective-permute-start | bytes 3145736 | tf_op jit(solution)/shard_map/ppermute | solution.py:47
  429.0 23.3 %collective-permute-start.40 = (bf16[256,2048]{1,0:T(8,128)(2,1)S(1)}, bf16[256,2048]{1,0:T(8,128)(2,1)S(1)}, u32[]{:S(2)}, u32[]{:S(2)}) collective-permute-start(bf16[256,2048]{1,0:T(8,128)(2,1)S(1)} %get-tuple-element.42), channel_id=1, source_target_pairs={{0,2},{2,6},{4,0},{6,4},{8,10},{10,14},{12,8},{14,12},{16,18},{18,... | collective-permute-start | bytes 3145736 | tf_op jit(solution)/shard_map/ppermute | solution.py:47
  430.5 23.3 %collective-permute-start.42 = (bf16[256,2048]{1,0:T(8,128)(2,1)S(1)}, bf16[256,2048]{1,0:T(8,128)(2,1)S(1)}, u32[]{:S(2)}, u32[]{:S(2)}) collective-permute-start(bf16[256,2048]{1,0:T(8,128)(2,1)S(1)} %get-tuple-element.42), channel_id=1, source_target_pairs={{0,4},{2,0},{4,6},{6,2},{8,12},{10,8},{12,14},{14,10},{16,20},{18,... | collective-permute-start | bytes 3145736 | tf_op jit(solution)/shard_map/ppermute | solution.py:47
  452.3 11.1 %collective-permute-start.41 = (bf16[128,2048]{1,0:T(8,128)(2,1)S(1)}, bf16[128,2048]{1,0:T(8,128)(2,1)S(1)}, u32[]{:S(2)}, u32[]{:S(2)}) collective-permute-start(bf16[128,2048]{1,0:T(8,128)(2,1)S(1)} %slice.466), channel_id=1, source_target_pairs={{0,2},{2,6},{4,0},{6,4},{8,10},{10,14},{12,8},{14,12},{16,18},{18,... | collective-permute-start | bytes 1572872 | tf_op jit(solution)/shard_map/ppermute | solution.py:47
  453.9 11.0 %collective-permute-start.43 = (bf16[128,2048]{1,0:T(8,128)(2,1)S(1)}, bf16[128,2048]{1,0:T(8,128)(2,1)S(1)}, u32[]{:S(2)}, u32[]{:S(2)}) collective-permute-start(bf16[128,2048]{1,0:T(8,128)(2,1)S(1)} %slice.467), channel_id=1, source_target_pairs={{0,4},{2,0},{4,6},{6,2},{8,12},{10,8},{12,14},{14,10},{16,20},{18,... | collective-permute-start | bytes 1572872 | tf_op jit(solution)/shard_map/ppermute | solution.py:47
  472.3 188.6 %reduce-scatter.8.cloned.1.call-start = ((), (), s32[]{:S(2)}) async-start(), calls=%async_computation.11 | async-start | bytes 1310720 | tf_op jit(solution)/shard_map/reduce_scatter | solution.py:89
  488.0 172.9 %reduce-scatter.10.cloned.1.call-start = ((), (), s32[]{:S(2)}) async-start(), calls=%async_computation.12 | async-start | bytes 1310720 | tf_op jit(solution)/shard_map/reduce_scatter | solution.py:89
  501.3 159.6 %reduce-scatter.12.cloned.1.call-start = ((), (), s32[]{:S(2)}) async-start(), calls=%async_computation.13 | async-start | bytes 1310720 | tf_op jit(solution)/shard_map/reduce_scatter | solution.py:89
  509.0 9.1 %collective-permute-start.67 = (bf16[704,2048]{1,0:T(8,128)(2,1)}, bf16[704,2048]{1,0:T(8,128)(2,1)}, u32[]{:S(2)}, u32[]{:S(2)}) collective-permute-start(bf16[704,2048]{1,0:T(8,128)(2,1)} %convolution_convert_fusion), channel_id=1, source_target_pairs={{0,1},{1,0},{2,3},{3,2},{4,5},{5,4},{6,7},{7,6},{8,9},{9,8},{10,11... | collective-permute-start | bytes 8650760 | tf_op jit(solution)/shard_map/ppermute | solution.py:55
  518.1 145.2 %reduce-scatter.20.cloned.1.call-start = ((), (), s32[]{:S(2)}) async-start(), calls=%async_computation.17 | async-start | bytes 3604480 | tf_op jit(solution)/shard_map/reduce_scatter | solution.py:89
  526.4 172.7 %reduce-scatter.18.cloned.1.call-start = ((), (), s32[]{:S(2)}) async-start(), calls=%async_computation.16 | async-start | bytes 3604480 | tf_op jit(solution)/shard_map/reduce_scatter | solution.py:89
  542.3 215.2 %reduce-scatter.16.cloned.1.call-start = ((), (), s32[]{:S(2)}) async-start(), calls=%async_computation.15 | async-start | bytes 3604480 | tf_op jit(solution)/shard_map/reduce_scatter | solution.py:89
  550.1 46.8 %collective-permute-start.65 = (bf16[704,2048]{1,0:T(8,128)(2,1)}, bf16[704,2048]{1,0:T(8,128)(2,1)}, u32[]{:S(2)}, u32[]{:S(2)}) collective-permute-start(bf16[704,2048]{1,0:T(8,128)(2,1)} %convolution_convert_fusion.2), channel_id=1, source_target_pairs={{0,1},{1,0},{2,3},{3,2},{4,5},{5,4},{6,7},{7,6},{8,9},{9,8},{10,11... | collective-permute-start | bytes 8650760 | tf_op jit(solution)/shard_map/ppermute | solution.py:55
  594.8 14.3 %collective-permute-start.46 = (bf16[128,2048]{1,0:T(8,128)(2,1)S(1)}, bf16[128,2048]{1,0:T(8,128)(2,1)S(1)}, u32[]{:S(2)}, u32[]{:S(2)}) collective-permute-start(bf16[128,2048]{1,0:T(8,128)(2,1)S(1)} %get-tuple-element.59), channel_id=1, source_target_pairs={{0,4},{2,0},{4,6},{6,2},{8,12},{10,8},{12,14},{14,10},{16,20},{18,... | collective-permute-start | bytes 1572872 | tf_op jit(solution)/shard_map/ppermute | solution.py:47
  595.0 14.1 %collective-permute-start.48 = (bf16[128,2048]{1,0:T(8,128)(2,1)S(1)}, bf16[128,2048]{1,0:T(8,128)(2,1)S(1)}, u32[]{:S(2)}, u32[]{:S(2)}) collective-permute-start(bf16[128,2048]{1,0:T(8,128)(2,1)S(1)} %get-tuple-element.60), channel_id=1, source_target_pairs={{0,2},{2,6},{4,0},{6,4},{8,10},{10,14},{12,8},{14,12},{16,18},{18,... | collective-permute-start | bytes 1572872 | tf_op jit(solution)/shard_map/ppermute | solution.py:47
  611.8 25.3 %collective-permute-start.47 = (bf16[256,2048]{1,0:T(8,128)(2,1)}, bf16[256,2048]{1,0:T(8,128)(2,1)}, u32[]{:S(2)}, u32[]{:S(2)}) collective-permute-start(bf16[256,2048]{1,0:T(8,128)(2,1)} %pad_maximum_fusion.6), channel_id=1, source_target_pairs={{0,4},{2,0},{4,6},{6,2},{8,12},{10,8},{12,14},{14,10},{16,20},{18,... | collective-permute-start | bytes 3145736 | tf_op jit(solution)/shard_map/ppermute | solution.py:47
  614.4 24.5 %collective-permute-start.49 = (bf16[256,2048]{1,0:T(8,128)(2,1)}, bf16[256,2048]{1,0:T(8,128)(2,1)}, u32[]{:S(2)}, u32[]{:S(2)}) collective-permute-start(bf16[256,2048]{1,0:T(8,128)(2,1)} %pad_maximum_fusion.7), channel_id=1, source_target_pairs={{0,2},{2,6},{4,0},{6,4},{8,10},{10,14},{12,8},{14,12},{16,18},{18,... | collective-permute-start | bytes 3145736 | tf_op jit(solution)/shard_map/ppermute | solution.py:47
  616.8 25.6 %collective-permute-start.61 = (f32[3,256]{1,0:T(4,128)S(1)}, f32[3,256]{1,0:T(4,128)S(1)}, u32[]{:S(2)}, u32[]{:S(2)}) collective-permute-start(f32[3,256]{1,0:T(4,128)S(1)} %maximum_add_fusion), channel_id=1, source_target_pairs={{0,8},{2,10},{4,12},{6,14},{8,16},{10,18},{12,20},{14,22},{16,24},... | collective-permute-start | bytes 9224 | tf_op jit(solution)/shard_map/ppermute | solution.py:51
  616.8 25.5 %collective-permute-start.62 = (f32[3,256]{1,0:T(4,128)S(1)}, f32[3,256]{1,0:T(4,128)S(1)}, u32[]{:S(2)}, u32[]{:S(2)}) collective-permute-start(f32[3,256]{1,0:T(4,128)S(1)} %maximum_add_fusion), channel_id=1, source_target_pairs={{0,16},{2,18},{4,20},{6,22},{8,24},{10,26},{12,28},{14,30},{16,0},... | collective-permute-start | bytes 9224 | tf_op jit(solution)/shard_map/ppermute | solution.py:51
  618.2 24.2 %collective-permute-start.63 = (f32[3,256]{1,0:T(4,128)S(1)}, f32[3,256]{1,0:T(4,128)S(1)}, u32[]{:S(2)}, u32[]{:S(2)}) collective-permute-start(f32[3,256]{1,0:T(4,128)S(1)} %maximum_add_fusion), channel_id=1, source_target_pairs={{0,24},{2,26},{4,28},{6,30},{8,0},{10,2},{12,4},{14,6},{16,8},{18,... | collective-permute-start | bytes 9224 | tf_op jit(solution)/shard_map/ppermute | solution.py:51
  650.5 7.6 collective-permute-start.54
  650.6 7.6 collective-permute-start.55
  651.5 7.1 collective-permute-start.56
  (91 other events, 721.6 us)
Sparse Core Ops, SparseCore 0:
  10.6 87.9 all-gather.4
  100.1 57.6 all-gather.6
  159.4 57.8 all-gather.8
  218.7 57.8 all-gather.10
  472.4 25.0 reduce-scatter.13
  499.8 25.7 reduce-scatter.7
  527.9 25.7 reduce-scatter.9
  556.7 25.7 reduce-scatter.11
  584.8 55.0 reduce-scatter.19
  642.1 57.0 reduce-scatter.17
  701.5 56.0 reduce-scatter.15

commit v2 on v1

v2 whole, which is shorter than its diff:
```python
import jax
import jax.numpy as jnp
from jax import lax
from jax.experimental import pallas as pl
from jax.experimental.pallas import tpu as pltpu
from jax.sharding import PartitionSpec as P

EPS = 1e-05


def matmul(left, right):
    return jnp.dot(left, right, preferred_element_type=jnp.float32)


def times_trans(left, right):
    return lax.dot_general(
        left, right, (((1,), (1,)), ((), ())), preferred_element_type=jnp.float32
    )


def trans_times(left, right):
    return lax.dot_general(
        left, right, (((0,), (0,)), ((), ())), preferred_element_type=jnp.float32
    )


def low(value):
    return value.astype(jnp.bfloat16)


def high(value):
    return value.astype(jnp.float32)


def kernel_call(body, grid, in_specs, out_specs, out_shape, flops, moved):
    return pl.pallas_call(
        body,
        grid=grid,
        in_specs=in_specs,
        out_specs=out_specs,
        out_shape=out_shape,
        compiler_params=pltpu.CompilerParams(
            dimension_semantics=("arbitrary",), vmem_limit_bytes=48 * 1024 * 1024
        ),
        cost_estimate=pl.CostEstimate(flops=1, bytes_accessed=1, transcendentals=0),
    )


def size_of(*arrays):
    return sum(array.size * array.dtype.itemsize for array in arrays)


def whole(shape):
    return pl.BlockSpec(shape, lambda i: (0, 0), pipeline_mode=pl.Buffered(1))


def sum_of_products(lefts, rights, tile=512):
    rows, width = lefts[0].shape[0], rights[0].shape[1]
    count = len(lefts)

    def body(*refs):
        total = matmul(refs[0][...], refs[count][...])
        for k in range(1, count):
            total = total + matmul(refs[k][...], refs[count + k][...])
        refs[-1][...] = low(total)

    depth = sum(left.shape[1] for left in lefts)
    return kernel_call(
        body,
        (width // tile,),
        [whole(left.shape) for left in lefts]
        + [pl.BlockSpec((right.shape[0], tile), lambda i: (0, i)) for right in rights],
        pl.BlockSpec((rows, tile), lambda i: (0, i)),
        jax.ShapeDtypeStruct((rows, width), jnp.bfloat16),
        2 * rows * depth * width,
        size_of(*lefts, *rights) + 2 * rows * width,
    )(*lefts, *rights)


def ffn_ahead(normed, gate, up, tile=256):
    rows, width = normed.shape
    units = gate.shape[0]
    tile = min(tile, rows)

    def body(normed_ref, gate_ref, up_ref, hidden_ref, gate_slope_ref, up_slope_ref):
        pre = times_trans(normed_ref[...], gate_ref[...])
        value = times_trans(normed_ref[...], up_ref[...])
        sigma = jax.nn.sigmoid(pre)
        activated = pre * sigma
        hidden_ref[...] = low(activated * value)
        gate_slope_ref[...] = low(value * sigma * (1.0 + pre * (1.0 - sigma)))
        up_slope_ref[...] = low(activated)

    out = jax.ShapeDtypeStruct((rows, units), jnp.bfloat16)
    spec = pl.BlockSpec((tile, units), lambda i: (i, 0))
    return kernel_call(
        body,
        (rows // tile,),
        [pl.BlockSpec((tile, width), lambda i: (i, 0)), whole(gate.shape), whole(up.shape)],
        [spec] * 3,
        [out] * 3,
        4 * rows * width * units,
        size_of(normed, gate, up) + 6 * rows * units,
    )(normed, gate, up)


def ffn_back(grad, down, gate, up, gate_slope, up_slope, tile=256):
    rows, width = grad.shape
    units = down[0].shape[0]
    tile = min(tile, rows)
    count = len(down)
    mats = [mat for group in zip(down, gate, up) for mat in group]
    slopes = [slope for group in zip(gate_slope, up_slope) for slope in group]

    wide = -(-units // 256) * 256

    def body(grad_ref, *refs):
        mat_refs, slope_refs = refs[: 3 * count], refs[3 * count : 5 * count]
        out_refs, total_ref = refs[5 * count : 7 * count], refs[7 * count]
        downs, others, pieces, sems = refs[7 * count + 1 :]
        first = pl.program_id(0) == 0
        copies = []
        for j in range(count):
            targets = [downs.at[j]]
            targets += [others.at[pl.ds((2 * j + k) * wide, units)] for k in range(2)]
            for k, target in enumerate(targets):
                at = 3 * j + k
                copies.append(pltpu.make_async_copy(mat_refs[at], target, sems.at[at]))

        @pl.when(first)
        def _():
            for copy in copies[::3] + copies[1::3] + copies[2::3]:
                copy.start()
            if wide > units:
                pieces[...] = jnp.zeros_like(pieces)
                for at in range(2 * count):
                    others[at * wide + units : (at + 1) * wide, :] = jnp.zeros(
                        (wide - units, width), jnp.bfloat16
                    )
            for copy in copies[::3]:
                copy.wait()

        for j in range(count):
            grad_hidden = times_trans(grad_ref[...], downs[j])
            for k in range(2):
                at = 2 * j + k
                piece = low(grad_hidden * high(slope_refs[at][...]))
                out_refs[at][...] = piece
                pieces[:, at * wide : at * wide + units] = piece

        @pl.when(first)
        def _():
            for copy in copies[1::3] + copies[2::3]:
                copy.wait()

        total_ref[...] = low(matmul(pieces[...], others[...]))

    out = jax.ShapeDtypeStruct((rows, units), jnp.bfloat16)
    spec = pl.BlockSpec((tile, units), lambda i: (i, 0))
    row_spec = pl.BlockSpec((tile, width), lambda i: (i, 0))
    found = pl.pallas_call(
        body,
        grid=(rows // tile,),
        in_specs=[row_spec]
        + [pl.BlockSpec(memory_space=pl.ANY)] * (3 * count)
        + [spec] * (2 * count),
        out_specs=[spec] * (2 * count) + [row_spec],
        out_shape=[out] * (2 * count) + [jax.ShapeDtypeStruct((rows, width), jnp.bfloat16)],
        scratch_shapes=[
            pltpu.VMEM((count, units, width), jnp.bfloat16),
            pltpu.VMEM((2 * count * wide, width), jnp.bfloat16),
            pltpu.VMEM((tile, 2 * count * wide), jnp.bfloat16),
            pltpu.SemaphoreType.DMA((3 * count,)),
        ],
        compiler_params=pltpu.CompilerParams(
            dimension_semantics=("arbitrary",), vmem_limit_bytes=48 * 1024 * 1024
        ),
        cost_estimate=pl.CostEstimate(flops=1, bytes_accessed=1, transcendentals=0),
    )(grad, *mats, *slopes)
    return [found[2 * j] for j in range(count)], [found[2 * j + 1] for j in range(count)], found[-1]


class Order:
    def __init__(self):
        self.last = ()

    def __call__(self, *values):
        values = lax.optimization_barrier((values, self.last))[0]
        return values if len(values) > 1 else values[0]

    def did(self, *results):
        self.last = results

    def wait(self, *results):
        self.last = (*self.last, *results)


class Groups:
    def __init__(self, fsdp, tp, order):
        self.fsdp, self.tp, self.order = fsdp, tp, order
        self.deep = fsdp // 4
        self.columns = [[b + 4 * a for a in range(self.deep)] for b in range(4)]

    def along(self, value):
        pairs = [(i, (i + 4) % self.fsdp) for i in range(self.fsdp)]
        return lax.ppermute(value, "fsdp", pairs)

    def swap(self, value, bit):
        return lax.ppermute(value, "fsdp", [(i, i ^ bit) for i in range(self.fsdp)])

    def across(self, value, places):
        pairs = [(i, (i + places) % self.tp) for i in range(self.tp)]
        return lax.ppermute(value, "tp", pairs)

    def next_core(self, value):
        return lax.ppermute(value, "tp", [(i, i + 1) for i in range(self.tp - 1)])

    def last_core(self, value):
        return lax.ppermute(value, "tp", [(i + 1, i) for i in range(self.tp - 1)])

    def cores(self, value):
        value = self.order(value)
        return [value] + [self.across(value, j) for j in range(1, self.tp)]

    def sum_cores(self, sent):
        return [self.across(self.order(value), -j) for j, value in enumerate(sent, 1)]

    def sum_cores_of(self, value):
        total = value
        for j in range(1, self.tp):
            total = total + self.across(value, j)
        return total

    def sum_bits(self, value, bits):
        for bit in bits:
            value = value + self.swap(value, bit)
        return value

    def gather_ordered(self, value):
        return lax.all_gather(
            value, "fsdp", axis=0, tiled=True, axis_index_groups=self.columns
        )

    def reduce_ordered(self, value):
        return lax.psum_scatter(
            value, "fsdp", scatter_dimension=0, tiled=True, axis_index_groups=self.columns
        )

    def stack(self, value, bits):
        stack = value[None]
        for bit in bits:
            stack = jnp.concatenate([stack, self.swap(self.order(stack), bit)], 0)
        return stack


class Rows:
    def __init__(self, groups, rows):
        self.groups, self.rows = groups, groups.order(rows)
        self.one = groups.swap(self.rows, 1)
        self.two = groups.swap(self.rows, 2)

    def middle(self):
        half = self.rows.shape[0] // 2
        self.groups.order.wait(self.one, self.two)
        top, bottom = self.groups.order(self.two[:half], self.one[half:])
        self.top = self.groups.swap(top, 1)
        self.bottom = self.groups.swap(bottom, 2)

    def end(self):
        order = self.groups.order
        order.wait(self.top, self.bottom)
        return jnp.concatenate(
            order(self.rows, self.one, self.two, self.top, self.bottom), 0
        )


class Sums:
    def __init__(self, groups, blocks, late=False):
        self.groups, self.late, blocks = groups, late, groups.order(blocks)
        own, one, two, far = (
            (block[: block.shape[0] // 2], block[block.shape[0] // 2 :])
            for block in jnp.split(blocks, 4)
        )
        self.own, self.one, self.two = own, one, two
        self.far = groups.swap(far[0], 1), groups.swap(far[1], 2)
        if not late:
            self.direct = groups.swap(one[0], 1), groups.swap(two[1], 2)

    def middle(self):
        order, swap = self.groups.order, self.groups.swap
        order.wait(self.far)
        first, second = order(*self.far)
        second = low(high(self.one[1]) + high(second))
        first = low(high(self.two[0]) + high(first))
        if self.late:
            second = jnp.concatenate([self.one[0], second], 0)
            first = jnp.concatenate([first, self.two[1]], 0)
        order.did(first, second)
        first, second = order(first, second)
        self.summed = swap(second, 1), swap(first, 2)

    def end(self):
        order = self.groups.order
        if self.late:
            order.wait(self.summed)
            one, two = order(*self.summed)
            return high(jnp.concatenate(self.own, 0)) + high(one) + high(two)
        order.wait(self.direct, self.summed)
        (one_first, two_second), (one_second, two_first) = order(self.direct, self.summed)
        return jnp.concatenate(
            [
                high(self.own[0]) + high(one_first) + high(two_first),
                high(self.own[1]) + high(one_second) + high(two_second),
            ],
            0,
        )


def after(value, *before):
    return lax.optimization_barrier((value, *before))[0]


def rms_scale(value):
    return lax.rsqrt(jnp.mean(value * value, -1, keepdims=True) + EPS)


def norm_back(value, scale, gain, grad_norm):
    scaled = grad_norm * gain
    return scale * scaled - value * scale**3 * jnp.mean(scaled * value, -1, keepdims=True)


def shift_down(value, places, before):
    return jnp.concatenate([before[:, 2 - places :], value[:, :-places]], 1)


def shift_up(value, places, after):
    return jnp.concatenate([value[:, places:], after[:, :places]], 1)


def on_device(
    tokens,
    seg_ids,
    norm1_gain,
    in_weight,
    conv_weight,
    out_weight,
    norm2_gain,
    gate_weight,
    up_weight,
    down_weight,
    cotangent,
    fsdp,
    tp,
):
    order = Order()
    groups = Groups(fsdp, tp, order)
    deep = groups.deep
    micro_count, own_rows, width = tokens.shape
    rows = micro_count * own_rows
    share = in_weight.shape[2]
    hidden_share = gate_weight.shape[1]
    wide_share = deep * share
    segments = 4 * micro_count
    chip = lax.axis_index("fsdp")
    core = lax.axis_index("tp")

    plane_bits, column_bits, bit = (1, 2), [], 4
    while bit < fsdp:
        column_bits.append(bit)
        bit *= 2

    mixer_own = jnp.concatenate(
        [in_weight.transpose(1, 2, 0).reshape(3 * share, width), out_weight], 0
    )
    mixer_all = groups.gather_ordered(mixer_own)
    gate_own, up_own = gate_weight.T, up_weight.T
    gate_all = groups.gather_ordered(after(gate_own, mixer_own))
    up_all = groups.gather_ordered(after(up_own, gate_own))
    down_all = groups.gather_ordered(after(down_weight, up_own))

    plane = chip // 4
    same = []
    for places in (1, 2):
        equal = (seg_ids[:, places:] == seg_ids[:, :-places]).astype(jnp.float32)
        equal = jnp.concatenate([jnp.zeros((micro_count, places), jnp.float32), equal], 1)
        same.append(lax.dynamic_slice_in_dim(equal, core * own_rows, own_rows, 1))
    tokens_own = tokens.reshape(rows, width)
    cot_own = cotangent.reshape(rows, width)
    token_rows = Rows(groups, tokens_own)
    gains = groups.stack(jnp.stack([norm1_gain, norm2_gain]), column_bits)
    order.wait(gains, gate_own, up_own)
    taps = groups.stack(conv_weight, column_bits)
    order.wait(taps)
    gains = groups.stack(gains, plane_bits[:1])
    same = groups.stack(jnp.stack(same), plane_bits[:1])
    token_rows.middle()
    order.wait(gains, same)
    gains = groups.stack(gains, plane_bits[1:])
    same = groups.stack(same, plane_bits[1:])
    order.wait(gains, same)
    tokens_all = token_rows.end()
    order.did(tokens_all)
    taps = taps[jnp.arange(deep) ^ plane].transpose(1, 0, 2).reshape(3, wide_share)
    taps = [high(tap) for tap in groups.cores(taps)]
    order.wait(taps)
    cot_rows = Rows(groups, cot_own)
    same = same.reshape(4, 2, micro_count, own_rows)
    mask_one = same[:, 0].reshape(segments, own_rows, 1)
    mask_two = same[:, 1].reshape(segments, own_rows, 1)
    gains = gains.reshape(4, deep, 2, -1).swapaxes(0, 1).reshape(fsdp, 2, -1)
    gains = gains[jnp.arange(fsdp) ^ chip].transpose(1, 0, 2).reshape(2, width)
    gain_one = high(gains[0])
    gain_two = high(gains[1])
    tokens_now, gain_now = order(tokens_all, gain_one)
    wide = high(tokens_now)
    scale_all = rms_scale(wide)
    normed = low(wide * scale_all * gain_now)
    order.did(normed)
    cot_rows.middle()
    order.wait(mixer_all)

    mixers = groups.cores(mixer_all)
    in_mats, out_mats, parts, gated_in = [], [], [], []
    for j in range(tp):
        if j:
            order.wait(mixers[j])
        mat = order(mixers[j]).reshape(deep, 4, share, width).transpose(1, 0, 2, 3)
        in_mats.append(mat[:3].reshape(3 * wide_share, width))
        out_mats.append(mat[3].reshape(wide_share, width))
        order.did(in_mats[-1], out_mats[-1])
        normed_now, mat = order(normed, in_mats[-1])
        projected = times_trans(normed_now, mat).reshape(segments, own_rows, 3 * wide_share)
        parts.append([projected[..., k * wide_share : (k + 1) * wide_share] for k in range(3)])
        gated_in.append(parts[-1][1] * parts[-1][2])
        order.did(parts[-1], gated_in[-1])
    ends = groups.next_core(order(jnp.stack([value[:, -2:] for value in gated_in])))
    order.wait(ends)
    parts, gated_in, ends = order(parts, gated_in, ends)
    before = [ends[(j - 1) % tp] for j in range(tp)]
    one_back = [mask_one * shift_down(v, 1, b) for v, b in zip(gated_in, before)]
    two_back = [mask_two * shift_down(v, 2, b) for v, b in zip(gated_in, before)]
    conv_out = [
        tap[0] * v + tap[1] * one + tap[2] * two
        for tap, v, one, two in zip(taps, gated_in, one_back, two_back)
    ]
    mixed = [low(part[0] * out).reshape(4 * rows, -1) for part, out in zip(parts, conv_out)]
    mixer_out = sum_of_products(mixed, out_mats)
    order.did(mixer_out)
    cot_all = cot_rows.end()
    order.wait(cot_all)
    mixer_sums = Sums(groups, mixer_out)
    mixer_sums.middle()
    mixer_sum = mixer_sums.end()
    order.wait(gate_all)
    mixer_sum, tokens_now = order(mixer_sum, tokens_own)
    tokens_f = high(tokens_own)
    resid = high(tokens_now) + mixer_sum

    scale_two = rms_scale(resid)
    normed_own = low(resid * scale_two * gain_two)
    order.did(normed_own)
    two_rows = Rows(groups, normed_own)
    two_rows.middle()
    gate = groups.cores(gate_all)
    order.wait(gate)
    order.wait(up_all)
    up = groups.cores(up_all)
    normed_two = two_rows.end()
    order.did(normed_two)
    hidden, gate_slope, up_slope = [], [], []
    for j in range(tp):
        if j:
            order.wait(up[j])
        found = ffn_ahead(*order(normed_two, gate[j], up[j]))
        order.did(*found)
        for kept, value in zip((hidden, gate_slope, up_slope), found):
            kept.append(value)
    def core_terms(left, right):
        left, right = order(left, right)
        sent = [low(trans_times(value, right)) for value in left[1:]]
        order.did(sent)
        return groups.sum_cores(sent)

    def own_term(left, right, got):
        order.wait(got)
        left, right, got = order(left, right, got)
        total = trans_times(left, right)
        for value in got:
            total = total + high(value)
        total = low(total)
        order.did(total)
        return total

    got = core_terms(hidden, cot_all)
    down_total = own_term(hidden[0], cot_all, got)
    order.wait(down_all)
    down_grad = groups.reduce_ordered(order(down_total))
    down_mats = groups.cores(down_all)
    order.wait(down_mats)
    grad_gate, grad_up, back_two = ffn_back(
        *order(cot_all, down_mats, gate, up, gate_slope, up_slope)
    )
    order.did(grad_gate, grad_up, back_two)
    two_sums = Sums(groups, back_two)
    gate_got = core_terms(grad_gate, normed_two)
    gate_total = own_term(grad_gate[0], normed_two, gate_got)
    two_sums.middle()
    order.wait(down_grad)
    gate_grad = groups.reduce_ordered(order(gate_total))
    up_got = core_terms(grad_up, normed_two)
    grad_normed_two = two_sums.end()
    resid_back = norm_back(resid, scale_two, gain_two, grad_normed_two)
    grad_resid = high(cot_own) + resid_back
    grad_low = low(grad_resid)
    order.did(grad_low)
    mixer_rows = Rows(groups, grad_low)
    up_total = own_term(grad_up[0], normed_two, up_got)
    mixer_rows.middle()
    norm_two_term = jnp.sum(grad_normed_two * resid * scale_two, 0)
    order.wait(gate_grad)
    up_grad = groups.reduce_ordered(order(up_total))
    hidden_now, down_now = order(hidden, down_mats)
    ffn_out = sum_of_products(hidden_now, down_now)
    order.did(ffn_out, norm_two_term)
    ffn_sums = Sums(groups, ffn_out, True)
    grad_mixer = mixer_rows.end()
    order.did(grad_mixer)

    grad_now, mats_now = order(grad_mixer, out_mats)
    grad_mixed = [
        times_trans(grad_now, mat).reshape(segments, own_rows, -1) for mat in mats_now
    ]
    grad_conv = [value * part[0] for value, part in zip(grad_mixed, parts)]
    grad_b = [
        low(value * out).reshape(4 * rows, -1) for value, out in zip(grad_mixed, conv_out)
    ]
    masked_one = [mask_one * value for value in grad_conv]
    masked_two = [mask_two * value for value in grad_conv]
    edges = jnp.stack(
        [jnp.concatenate([one[:, :2], two[:, :2]], 0) for one, two in zip(masked_one, masked_two)]
    )
    order.did(grad_b, grad_conv, edges)
    starts = groups.last_core(order(edges))
    ffn_sums.middle()
    b_got = core_terms(grad_b, normed)
    out_got = core_terms(mixed, grad_mixer)
    order.wait(starts)
    grad_conv_now, masked_one, masked_two, starts = order(
        grad_conv, masked_one, masked_two, starts
    )
    after_edge = [starts[(j + 1) % tp] for j in range(tp)]
    grad_gated = [
        tap[0] * value
        + tap[1] * shift_up(one, 1, edge[:segments])
        + tap[2] * shift_up(two, 2, edge[segments:])
        for tap, value, one, two, edge in zip(
            taps, grad_conv_now, masked_one, masked_two, after_edge
        )
    ]
    grad_cx = [
        jnp.concatenate([low(gg * part[k]).reshape(4 * rows, -1) for k in (2, 1)], 1)
        for gg, part in zip(grad_gated, parts)
    ]
    order.did(grad_cx)
    cx_got = core_terms(grad_cx, normed)
    b_total = own_term(grad_b[0], normed, b_got)
    out_total = own_term(mixed[0], grad_mixer, out_got)
    cx_total = own_term(grad_cx[0], normed, cx_got)
    mixer_total = (
        jnp.concatenate([b_total, cx_total, out_total], 0)
        .reshape(4, deep, share, width)
        .transpose(1, 0, 2, 3)
        .reshape(4 * wide_share, width)
    )
    order.did(mixer_total)
    order.wait(up_grad)
    block_output = low(resid + ffn_sums.end())
    order.did(block_output)
    mixer_grad = groups.reduce_ordered(order(mixer_total))
    b_mats = [mat[:wide_share] for mat in in_mats]
    cx_mats = [mat[wide_share:] for mat in in_mats]
    back_one = sum_of_products(*order(grad_b + grad_cx, b_mats + cx_mats))
    order.did(back_one)
    one_rows = Sums(groups, back_one)
    back_now = order(back_one)
    norm_one_term = jnp.sum(high(back_now) * wide * scale_all, 0)
    conv_terms = [
        jnp.stack([jnp.sum(gc * value, (0, 1)) for value in (gi, one, two)])
        for gc, gi, one, two in zip(grad_conv, gated_in, one_back, two_back)
    ]
    order.did(norm_one_term, conv_terms)
    one_rows.middle()
    conv_sum = conv_terms[0]
    for j in range(1, tp):
        conv_sum = conv_sum + groups.across(order(conv_terms[j]), -j)
    gain_sums = groups.sum_cores_of(order(jnp.stack([norm_one_term, norm_two_term])))
    conv_sum = groups.sum_bits(conv_sum, column_bits)
    gain_sums = groups.sum_bits(gain_sums, column_bits)
    conv_total = lax.dynamic_slice_in_dim(conv_sum, plane * share, share, 1)
    order.wait(conv_total, gain_sums)
    grad_normed = one_rows.end()
    input_back = norm_back(tokens_f, rms_scale(tokens_f), gain_one, grad_normed)
    input_grad = low(grad_resid + input_back)
    order.did(input_grad)
    gain_sums = groups.sum_bits(order(gain_sums), plane_bits)
    gate_grad, up_grad = order(gate_grad, up_grad)
    gate_grad, up_grad = high(gate_grad).T, high(up_grad).T
    order.did(gate_grad, up_grad)
    order.wait(mixer_grad)
    mixer_grad = high(mixer_grad).reshape(4, share, width)
    gain_share = norm1_gain.shape[0]
    gain_grads = lax.dynamic_slice_in_dim(gain_sums, chip * gain_share, gain_share, 1)
    return (
        block_output.reshape(tokens.shape),
        input_grad.reshape(tokens.shape),
        gain_grads[0],
        mixer_grad[:3].transpose(2, 0, 1),
        conv_total,
        mixer_grad[3],
        gain_grads[1],
        gate_grad,
        up_grad,
        high(down_grad),
    )


def solution(mesh):
    fsdp, tp = mesh.shape["fsdp"], mesh.shape["tp"]

    def body(*args):
        return on_device(*args, fsdp, tp)

    return jax.shard_map(
        body,
        mesh=mesh,
        in_specs=(
            P(None, ("fsdp", "tp"), None),
            P(None, "fsdp"),
            P("fsdp"),
            P(None, None, ("fsdp", "tp")),
            P(None, ("fsdp", "tp")),
            P(("fsdp", "tp"), None),
            P("fsdp"),
            P(None, ("fsdp", "tp")),
            P(None, ("fsdp", "tp")),
            P(("fsdp", "tp"), None),
            P(None, ("fsdp", "tp"), None),
        ),
        out_specs=(
            P(None, ("fsdp", "tp"), None),
            P(None, ("fsdp", "tp"), None),
            P("fsdp"),
            P(None, None, ("fsdp", "tp")),
            P(None, ("fsdp", "tp")),
            P(("fsdp", "tp"), None),
            P("fsdp"),
            P(None, ("fsdp", "tp")),
            P(None, ("fsdp", "tp")),
            P(("fsdp", "tp"), None),
        ),
        check_vma=False,
    )
```

time: 776 us -> 582 us (0.75)
  matrix products: 205 us -> 52.3 us
  waiting for transfers between devices: 388 us -> 236 us
  Pallas kernels: 0 us -> 74.1 us
  local copies, waits for them, and re-layouts: 42.8 us -> 78.6 us
    reduce_scatter x7 -> x4, waiting for transfers between devices: 89.5 us -> 1.33 us  [reduce_ordered(): lax.psum_scatter(value, 'fsdp', scatter_dimension=0, tiled=True, axis_ind...]
    dot_general x14 -> x0, matrix products: 86.4 us -> none  [matmul(): return jnp.dot(left, right, preferred_element_type=jnp.float32)]
    all_gather x4, waiting for transfers between devices: 96.6 us -> 20 us  [gather_ordered(): lax.all_gather(value, 'fsdp', axis=0, tiled=True, axis_index_groups=self....]
    pallas_call x0 -> x6, Pallas kernels: none -> 74.1 us  [the longest x1 28.4 us: ffn_back(): pl.pallas_call(body, grid=(rows // tile,), in_specs=[row_spec] + [pl.Bloc...]
    dot_general x14 -> x4, matrix products: 61.7 us -> 9.46 us  [times_trans(): lax.dot_general(left, right, (((1,), (1,)), ((), ())), preferred_element_...]
    slice x18 -> x25, local copies, waits for them, and re-layouts: 14 us -> 38 us  [the longest x8 9.42 us: middle(): top, bottom = self.groups.order(self.two[:half], self.one[half:])]
    unnamed x166 -> x168, local copies, waits for them, and re-layouts: 18.7 us -> 33 us
    dot_general x14 -> x12, matrix products: 56.5 us -> 42.8 us  [trans_times(): lax.dot_general(left, right, (((0,), (0,)), ((), ())), preferred_element_...]
  transfers between devices with their start and end apart: 79 -> 75, of which waited for: 38 -> 43; matrix products, arithmetic and copies ran while one was open for 30% -> 26% of each run, Pallas kernels for 0% -> 13%
where the time goes in v2:
time: 582 us; the launch traced here: 572 us
  waiting for transfers between devices  236 us (41%)
  local copies, waits for them, and re-layouts  78.6 us (14%)
  Pallas kernels  74.1 us (13%)
  starting transfers between devices  63.7 us (11%)
  matrix products  52.3 us (9%)
  other arithmetic  51.7 us (9%)
  between operations  16 us (3%)
    ppermute x52, waiting for transfers between devices, swap(): return lax.ppermute(value, 'fsdp', [(i, i ^ bit) for i in range(self.fsdp)])  198 us
    ppermute x52, starting transfers between devices, swap(): return lax.ppermute(value, 'fsdp', [(i, i ^ bit) for i in range(self.fsdp)])  55.6 us
    dot_general x12, matrix products, trans_times(): lax.dot_general(left, right, (((0,), (0,)), ((), ())), preferred_element_...  42.8 us
    unnamed x168, local copies, waits for them, and re-layouts  33 us
    pallas_call x1, Pallas kernels, ffn_back(): pl.pallas_call(body, grid=(rows // tile,), in_specs=[row_spec] + [pl.Bloc...  28.4 us
    pallas_call x3, Pallas kernels, sum_of_products(): kernel_call(body, (width // tile,), [whole(left.shape) for left in lefts]...  23.4 us
    convert_element_type x15, other arithmetic, low(): return value.astype(jnp.bfloat16)  23.1 us
    pallas_call x2, Pallas kernels, ffn_ahead(): kernel_call(body, (rows // tile,), [pl.BlockSpec((tile, width), lambda i:...  22.3 us
  transfers between devices with their start and end apart: 75, of which 43 were waited for; matrix products, arithmetic and copies ran while one was open for 26% of the time, Pallas kernels for 13%

profile of v2, /device:TPU:0, one launch (start us, length us, event | category | flops | bytes accessed | tf_op | source)
XLA Modules:
  0.0 572.5 jit_solution(7776769443579711585)
XLA Ops:
  7.3 2.4 pad_maximum_fusion.4
  9.7 3.0 collective-permute-start.1
  17.9 2.6 collective-permute-start.3
  24.0 2.0 collective-permute-done.4
  26.0 2.6 collective-permute-start.5
  28.6 2.0 collective-permute-done.5
  33.4 4.1 collective-permute-done.8
  38.4 1.9 slice.471
  44.4 9.9 %collective-permute-done.10 = bf16[1,2,4,2,128]{4,3,2,1,0:T(2,128)(2,1)S(1)} collective-permute-done((bf16[1,2,4,2,128]{4,3,2,1,0:T(2,128)(2,1)S(1)}, bf16[1,2,4,2,128]{4,3,2,1,0:T(2,128)(2,1)S(1)}, u32[]{:S(2)}, u32[]{:S(2)}) %collective-permute-start.10) | collective-permute-done | bytes 4128 | tf_op jit(solution)/shard_map/ppermute | solution.py:209
  60.8 3.0 fusion.2
  63.8 20.2 %collective-permute-done.14 = bf16[256,2048]{1,0:T(8,128)(2,1)S(1)} collective-permute-done((bf16[256,2048]{1,0:T(8,128)(2,1)S(1)}, bf16[256,2048]{1,0:T(8,128)(2,1)S(1)}, u32[]{:S(2)}, u32[]{:S(2)}) %collective-permute-start.14) | collective-permute-done | bytes 1048608 | tf_op jit(solution)/shard_map/ppermute | solution.py:209
  84.3 9.5 %all-gather.5.cloned.1.call-done = bf16[1024,2048]{1,0:T(8,128)(2,1)} async-done(((bf16[256,2048]{1,0:T(8,128)(2,1)}), bf16[1024,2048]{1,0:T(8,128)(2,1)}) %all-gather.5.cloned.1.call-update) | async-done | bytes 4194320 | tf_op jit(solution)/shard_map/all_gather | solution.py:240
  93.9 2.3 slice.473
  101.6 3.4 fusion.34
  106.9 3.5 fusion.26
  110.4 2.7 slice.478
  113.5 3.4 fusion.35
  118.9 2.6 collective-permute-start.16
  128.7 4.3 shard_map.186
  133.1 2.9 collective-permute-done.17
  138.2 2.5 constant_dynamic-update-slice_fusion.8
  148.7 10.8 %collective-permute-done.22 = bf16[128,2048]{1,0:T(8,128)(2,1)S(1)} collective-permute-done((bf16[128,2048]{1,0:T(8,128)(2,1)S(1)}, bf16[128,2048]{1,0:T(8,128)(2,1)S(1)}, u32[]{:S(2)}, u32[]{:S(2)}) %collective-permute-start.22) | collective-permute-done | bytes 524320 | tf_op jit(solution)/shard_map/ppermute | solution.py:209
  163.4 7.4 %collective-permute-done.20 = bf16[128,2048]{1,0:T(8,128)(2,1)S(1)} collective-permute-done((bf16[128,2048]{1,0:T(8,128)(2,1)}, bf16[128,2048]{1,0:T(8,128)(2,1)S(1)}, u32[]{:S(2)}, u32[]{:S(2)}) %collective-permute-start.20) | collective-permute-done | bytes 524320 | tf_op jit(solution)/shard_map/ppermute | solution.py:209
  172.2 8.2 %collective-permute-done.23 = bf16[128,2048]{1,0:T(8,128)(2,1)S(1)} collective-permute-done((bf16[128,2048]{1,0:T(8,128)(2,1)}, bf16[128,2048]{1,0:T(8,128)(2,1)S(1)}, u32[]{:S(2)}, u32[]{:S(2)}) %collective-permute-start.23) | collective-permute-done | bytes 524320 | tf_op jit(solution)/shard_map/ppermute | solution.py:209
  183.6 2.2 multiply_reduce_fusion.2
  187.9 20.5 %collective-permute-done.26 = bf16[256,2048]{1,0:T(8,128)(2,1)S(1)} collective-permute-done((bf16[256,2048]{1,0:T(8,128)(2,1)S(1)}, bf16[256,2048]{1,0:T(8,128)(2,1)S(1)}, u32[]{:S(2)}, u32[]{:S(2)}) %collective-permute-start.26) | collective-permute-done | bytes 1048608 | tf_op jit(solution)/shard_map/ppermute | solution.py:209
  210.5 10.5 %all-gather.9.cloned.1.call-done.up_ref.refs_2_ = bf16[704,2048]{1,0:T(8,128)(2,1)} async-done(((bf16[176,2048]{1,0:T(8,128)(2,1)}), bf16[704,2048]{1,0:T(8,128)(2,1)}) %all-gather.9.cloned.1.call-update) | async-done | bytes 2883600 | tf_op jit(solution)/shard_map/all_gather | solution.py:240
  222.8 1.9 slice.499
  227.7 11.5 %collective-permute-done.27 = bf16[128,2048]{1,0:T(8,128)(2,1)S(1)} collective-permute-done((bf16[128,2048]{1,0:T(8,128)(2,1)}, bf16[128,2048]{1,0:T(8,128)(2,1)S(1)}, u32[]{:S(2)}, u32[]{:S(2)}) %collective-permute-start.27) | collective-permute-done | bytes 524320 | tf_op jit(solution)/shard_map/ppermute | solution.py:209
  244.5 2.0 copy-done.21
  246.5 10.9 %shard_map.187 = (bf16[1024,704]{1,0:T(8,128)(2,1)S(1)}, bf16[1024,704]{1,0:T(8,128)(2,1)S(1)}, bf16[1024,704]{1,0:T(8,128)(2,1)S(1)}) custom-call(bf16[1024,2048]{1,0:T(8,128)(2,1)} %copy-done.21, bf16[704,2048]{1,0:T(8,128)(2,1)} %all-gather.7.cloned.1.call-done.gate_ref.refs_1_, bf16[704,2048]{1,0:T(8,128)(2,1)} %all-gather.9.cloned.1.call-done.up_ref.refs_2_), custom_call_target="tpu_custom_call" | custom-call | flops 1 | bytes 1 | tf_op jit(solution)/shard_map/pallas_call | solution.py:96
  259.7 11.4 %shard_map.188 = (bf16[1024,704]{1,0:T(8,128)(2,1)S(1)}, bf16[1024,704]{1,0:T(8,128)(2,1)S(1)}, bf16[1024,704]{1,0:T(8,128)(2,1)S(1)}) custom-call(bf16[1024,2048]{1,0:T(8,128)(2,1)} %copy-done.21, bf16[704,2048]{1,0:T(8,128)(2,1)} %collective-permute-done.29.gate_ref.refs_4_, bf16[704,2048]{1,0:T(8,128)(2,1)} %collective-permute-done.30.up_ref.refs_5_), custom_call_target="tpu_custom_call" | custom-call | flops 1 | bytes 1 | tf_op jit(solution)/shard_map/pallas_call | solution.py:96
  271.2 7.1 %convolution_convert_fusion.2 = bf16[704,2048]{1,0:T(8,128)(2,1)S(1)} fusion(bf16[1024,704]{1,0:T(8,128)(2,1)S(1)} %get-tuple-element.325.refs_1_, bf16[1024,2048]{1,0:T(8,128)(2,1)} %constant_dynamic-update-slice_fusion.5.grad_ref), kind=kOutput, calls=%fused_computation.17 | convolution fusion | flops 2954231808 | bytes 8519680 | tf_op jit(solution)/shard_map/dot_general | solution.py:22
  278.4 5.3 collective-permute-done.31
  283.6 6.9 %add_convert_fusion.2 = bf16[704,2048]{1,0:T(8,128)(2,1)} fusion(bf16[704,2048]{1,0:T(8,128)(2,1)S(1)} %collective-permute-done.31, bf16[1024,704]{1,0:T(8,128)(2,1)S(1)} %get-tuple-element.324.refs_0_, bf16[1024,2048]{1,0:T(8,128)(2,1)} %constant_dynamic-update-slice_fusion.5.grad_ref), kind=kOutput, calls=%fused_computation.12 | convolution fusion | flops 2957115392 | bytes 11403264 | tf_op jit(solution)/shard_map/dot_general | solution.py:22
  291.2 5.0 collective-permute-done.32.refs_3_
  296.2 28.4 %shard_map.189 = (bf16[1024,704]{1,0:T(8,128)(2,1)S(1)}, bf16[1024,704]{1,0:T(8,128)(2,1)S(1)}, bf16[1024,704]{1,0:T(8,128)(2,1)S(1)}, bf16[1024,704]{1,0:T(8,128)(2,1)}, bf16[1024,2048]{1,0:T(8,128)(2,1)}) custom-call(bf16[1024,2048]{1,0:T(8,128)(2,1)} %constant_dynamic-update-slice_fusion.5.grad_ref, ...), custom_call_target="tpu_custom_call" | custom-call | flops 1 | bytes 1 | tf_op jit(solution)/shard_map/pallas_call | solution.py:161
  324.7 3.4 convolution_convert_fusion.1
  333.4 4.5 add_convert_fusion.1
  338.0 6.1 %collective-permute-done.34 = bf16[128,2048]{1,0:T(8,128)(2,1)S(1)} collective-permute-done((bf16[128,2048]{1,0:T(8,128)(2,1)}, bf16[128,2048]{1,0:T(8,128)(2,1)S(1)}, u32[]{:S(2)}, u32[]{:S(2)}) %collective-permute-start.34) | collective-permute-done | bytes 524320 | tf_op jit(solution)/shard_map/ppermute | solution.py:209
  345.3 2.7 add_convert_fusion.10
  352.4 6.2 %convolution_convert_fusion = bf16[704,2048]{1,0:T(8,128)(2,1)S(1)} fusion(bf16[1024,704]{1,0:T(8,128)(2,1)} %get-tuple-element.310, bf16[1024,2048]{1,0:T(8,128)(2,1)} %copy-done.21), kind=kOutput, calls=%fused_computation.15 | convolution fusion | flops 2954231808 | bytes 8519680 | tf_op jit(solution)/shard_map/dot_general | solution.py:22
  358.7 4.8 collective-permute-done.38
  364.4 9.6 %collective-permute-done.39 = bf16[128,2048]{1,0:T(8,128)(2,1)S(1)} collective-permute-done((bf16[128,2048]{1,0:T(8,128)(2,1)}, bf16[128,2048]{1,0:T(8,128)(2,1)S(1)}, u32[]{:S(2)}, u32[]{:S(2)}) %collective-permute-start.39) | collective-permute-done | bytes 524320 | tf_op jit(solution)/shard_map/ppermute | solution.py:209
  376.9 2.1 fusion.24
  380.3 22.4 %collective-permute-done.42 = bf16[256,2048]{1,0:T(8,128)(2,1)S(1)} collective-permute-done((bf16[256,2048]{1,0:T(8,128)(2,1)S(1)}, bf16[256,2048]{1,0:T(8,128)(2,1)S(1)}, u32[]{:S(2)}, u32[]{:S(2)}) %collective-permute-start.42) | collective-permute-done | bytes 1048608 | tf_op jit(solution)/shard_map/ppermute | solution.py:209
  404.8 4.6 add_convert_fusion
  413.7 9.5 %shard_map.190 = bf16[1024,2048]{1,0:T(8,128)(2,1)} custom-call(bf16[1024,704]{1,0:T(8,128)(2,1)S(1)} %copy-done.2, bf16[1024,704]{1,0:T(8,128)(2,1)S(1)} %copy-done.14, bf16[704,2048]{1,0:T(8,128)(2,1)S(1)} %copy-done, bf16[704,2048]{1,0:T(8,128)(2,1)} %collective-permute-done.32.refs_3_), custom_call_target="tpu_custom_call" | custom-call | flops 1 | bytes 1 | tf_op jit(solution)/shard_map/pallas_call | solution.py:68
  446.6 2.5 convolution_convert_fusion.3
  452.2 3.3 collective-permute-done.49
  458.3 2.5 add_convert_fusion.3
  461.5 2.3 copy.32
  463.8 12.1 %collective-permute-done.47 = bf16[256,2048]{1,0:T(8,128)(2,1)S(1)} collective-permute-done((bf16[256,2048]{1,0:T(8,128)(2,1)S(1)}, bf16[256,2048]{1,0:T(8,128)(2,1)S(1)}, u32[]{:S(2)}, u32[]{:S(2)}) %collective-permute-start.47) | collective-permute-done | bytes 1048608 | tf_op jit(solution)/shard_map/ppermute | solution.py:209
  478.2 4.1 add_convert_fusion.5
  490.0 9.6 %shard_map.191 = bf16[1024,2048]{1,0:T(8,128)(2,1)} custom-call(bf16[1024,256]{1,0:T(8,128)(2,1)S(1)} %bitcast.177, bf16[1024,256]{1,0:T(8,128)(2,1)S(1)} %bitcast.175, bf16[1024,512]{1,0:T(8,128)(2,1)S(1)} %pad_maximum_fusion.7.refs_2_, bf16[1024,512]{1,0:T(8,128)(2,1)S(1)} %pad_maximum_fusion.8.refs_3_, bf16[256,2048]{1,0:T(8,128)(2,1)S(1)} %bitcast.168, ...), custom_call_target="tpu_custom_call" | custom-call | flops 1 | bytes 1 | tf_op jit(solution)/shard_map/pallas_call | solution.py:68
  499.6 2.9 fusion.25
  506.6 3.6 fusion.4
  510.2 7.1 %collective-permute-done.56 = bf16[128,2048]{1,0:T(8,128)(2,1)S(1)} collective-permute-done((bf16[128,2048]{1,0:T(8,128)(2,1)S(1)}, bf16[128,2048]{1,0:T(8,128)(2,1)S(1)}, u32[]{:S(2)}, u32[]{:S(2)}) %collective-permute-start.56) | collective-permute-done | bytes 524320 | tf_op jit(solution)/shard_map/ppermute | solution.py:209
  518.8 2.4 add_convert_fusion.6
  524.8 4.4 collective-permute-done.60
  529.2 6.5 %collective-permute-done.63 = f32[2,2048]{1,0:T(2,128)S(1)} collective-permute-done((f32[2,2048]{1,0:T(2,128)S(1)}, f32[2,2048]{1,0:T(2,128)S(1)}, u32[]{:S(2)}, u32[]{:S(2)}) %collective-permute-start.63) | collective-permute-done | bytes 16416 | tf_op jit(solution)/shard_map/ppermute | solution.py:209
  537.0 4.4 collective-permute-done.61
  542.0 5.5 collective-permute-done.64
  562.8 2.5 slice.520
  (416 shorter events, 163.9 us)
Async XLA Ops:
  7.2 86.6 %all-gather.5.cloned.1.call-start = ((), (), s32[]{:S(2)}) async-start(), calls=%async_computation.4 | async-start | bytes 5242880 | tf_op jit(solution)/shard_map/all_gather | solution.py:240
  9.7 173.9 %all-gather.7.cloned.1.call-start = ((), (), s32[]{:S(2)}) async-start(), calls=%async_computation.5 | async-start | bytes 3604480 | tf_op jit(solution)/shard_map/all_gather | solution.py:240
  9.7 27.8 %collective-permute-start.1 = (bf16[256,2048]{1,0:T(8,128)(2,1)S(1)}, bf16[256,2048]{1,0:T(8,128)(2,1)S(1)}, u32[]{:S(2)}, u32[]{:S(2)}) collective-permute-start(bf16[256,2048]{1,0:T(8,128)(2,1)S(1)} %bitcast.189), channel_id=1, source_target_pairs={{0,4},{2,6},{4,0},{6,2},{8,12},{10,14},{12,8},{14,10},{16,20},{18,... | collective-permute-start | bytes 3145736 | tf_op jit(solution)/shard_map/ppermute | solution.py:209
  12.8 25.6 %collective-permute-start = (bf16[256,2048]{1,0:T(8,128)(2,1)S(1)}, bf16[256,2048]{1,0:T(8,128)(2,1)}, u32[]{:S(2)}, u32[]{:S(2)}) collective-permute-start(bf16[256,2048]{1,0:T(8,128)(2,1)S(1)} %bitcast.190), channel_id=1, source_target_pairs={{0,2},{2,0},{4,6},{6,4},{8,10},{10,8},{12,14},{14,12},{16,18},{18,... | collective-permute-start | bytes 3145736 | tf_op jit(solution)/shard_map/ppermute | solution.py:209
  30.7 6.9 %collective-permute-start.8 = (bf16[1,4,2,128]{3,2,1,0:T(2,128)(2,1)S(1)}, bf16[1,4,2,128]{3,2,1,0:T(2,128)(2,1)S(1)}, u32[]{:S(2)}, u32[]{:S(2)}) collective-permute-start(bf16[1,4,2,128]{3,2,1,0:T(2,128)(2,1)S(1)} %fusion.72), channel_id=1, source_target_pairs={{0,2},{2,0},{4,6},{6,4},{8,10},{10,8},{12,14},{14,12},{16,18},{18,... | collective-permute-start | bytes 6152 | tf_op jit(solution)/shard_map/ppermute | solution.py:209
  31.9 10.4 %collective-permute-start.9 = (f32[1,2,2,128]{3,2,1,0:T(2,128)S(1)}, f32[1,2,2,128]{3,2,1,0:T(2,128)S(1)}, u32[]{:S(2)}, u32[]{:S(2)}) collective-permute-start(f32[1,2,2,128]{3,2,1,0:T(2,128)S(1)} %maximum_bitcast_fusion.2), channel_id=1, source_target_pairs={{0,2},{2,0},{4,6},{6,4},{8,10},{10,8},{12,14},{14,12},{16,18},{18,... | collective-permute-start | bytes 6152 | tf_op jit(solution)/shard_map/ppermute | solution.py:209
  40.2 14.7 %collective-permute-start.6 = (bf16[128,2048]{1,0:T(8,128)(2,1)}, bf16[128,2048]{1,0:T(8,128)(2,1)S(1)}, u32[]{:S(2)}, u32[]{:S(2)}) collective-permute-start(bf16[128,2048]{1,0:T(8,128)(2,1)} %slice.470), channel_id=1, source_target_pairs={{0,2},{2,0},{4,6},{6,4},{8,10},{10,8},{12,14},{14,12},{16,18},{18,... | collective-permute-start | bytes 1572872 | tf_op jit(solution)/shard_map/ppermute | solution.py:209
  41.7 13.2 %collective-permute-start.7 = (bf16[128,2048]{1,0:T(8,128)(2,1)}, bf16[128,2048]{1,0:T(8,128)(2,1)S(1)}, u32[]{:S(2)}, u32[]{:S(2)}) collective-permute-start(bf16[128,2048]{1,0:T(8,128)(2,1)} %slice.471), channel_id=1, source_target_pairs={{0,4},{2,6},{4,0},{6,2},{8,12},{10,14},{12,8},{14,10},{16,20},{18,... | collective-permute-start | bytes 1572872 | tf_op jit(solution)/shard_map/ppermute | solution.py:209
  42.3 12.0 %collective-permute-start.10 = (bf16[1,2,4,2,128]{4,3,2,1,0:T(2,128)(2,1)S(1)}, bf16[1,2,4,2,128]{4,3,2,1,0:T(2,128)(2,1)S(1)}, u32[]{:S(2)}, u32[]{:S(2)}) collective-permute-start(bf16[1,2,4,2,128]{4,3,2,1,0:T(2,128)(2,1)S(1)} %fusion.71), channel_id=1, source_target_pairs={{0,4},{2,6},{4,0},{6,2},{8,12},{10,14},{12,8},{14,10},{16,20},{18,... | collective-permute-start | bytes 12296 | tf_op jit(solution)/shard_map/ppermute | solution.py:209
  43.9 11.1 %collective-permute-start.11 = (f32[1,2,2,2,128]{4,3,2,1,0:T(2,128)S(1)}, f32[1,2,2,2,128]{4,3,2,1,0:T(2,128)S(1)}, u32[]{:S(2)}, u32[]{:S(2)}) collective-permute-start(f32[1,2,2,2,128]{4,3,2,1,0:T(2,128)S(1)} %fusion.21), channel_id=1, source_target_pairs={{0,4},{2,6},{4,0},{6,2},{8,12},{10,14},{12,8},{14,10},{16,20},{18,... | collective-permute-start | bytes 12296 | tf_op jit(solution)/shard_map/ppermute | solution.py:209
  58.7 25.2 %collective-permute-start.14 = (bf16[256,2048]{1,0:T(8,128)(2,1)S(1)}, bf16[256,2048]{1,0:T(8,128)(2,1)S(1)}, u32[]{:S(2)}, u32[]{:S(2)}) collective-permute-start(bf16[256,2048]{1,0:T(8,128)(2,1)S(1)} %bitcast.198), channel_id=1, source_target_pairs={{0,4},{2,6},{4,0},{6,2},{8,12},{10,14},{12,8},{14,10},{16,20},{18,... | collective-permute-start | bytes 3145736 | tf_op jit(solution)/shard_map/ppermute | solution.py:209
  59.3 25.1 %collective-permute-start.13 = (bf16[256,2048]{1,0:T(8,128)(2,1)S(1)}, bf16[256,2048]{1,0:T(8,128)(2,1)}, u32[]{:S(2)}, u32[]{:S(2)}) collective-permute-start(bf16[256,2048]{1,0:T(8,128)(2,1)S(1)} %bitcast.199), channel_id=1, source_target_pairs={{0,2},{2,0},{4,6},{6,4},{8,10},{10,8},{12,14},{14,12},{16,18},{18,... | collective-permute-start | bytes 3145736 | tf_op jit(solution)/shard_map/ppermute | solution.py:209
  93.8 13.0 %collective-permute-start.15 = (bf16[1024,2048]{1,0:T(8,128)(2,1)}, bf16[1024,2048]{1,0:T(8,128)(2,1)}, u32[]{:S(2)}, u32[]{:S(2)}) collective-permute-start(bf16[1024,2048]{1,0:T(8,128)(2,1)} %all-gather.5.cloned.1.call-done), channel_id=1, source_target_pairs={{0,1},{1,0},{2,3},{3,2},{4,5},{5,4},{6,7},{7,6},{8,9},{9,8},{10,11... | collective-permute-start | bytes 12582920 | tf_op jit(solution)/shard_map/ppermute | solution.py:213
  93.9 127.1 %all-gather.9.cloned.1.call-start = ((), (), s32[]{:S(2)}) async-start(), calls=%async_computation.6 | async-start | bytes 3604480 | tf_op jit(solution)/shard_map/all_gather | solution.py:240
  118.9 6.7 %collective-permute-start.16 = (f32[2,8,2,256]{3,2,1,0:T(2,128)S(1)}, f32[2,8,2,256]{3,2,1,0:T(2,128)S(1)}, u32[]{:S(2)}, u32[]{:S(2)}) collective-permute-start(f32[2,8,2,256]{3,2,1,0:T(2,128)S(1)} %pad_maximum_fusion.10), channel_id=1, source_target_pairs={{0,1},{2,3},{4,5},{6,7},{8,9},{10,11},{12,13},{14,15},{16,17},{18,... | collective-permute-start | bytes 98312 | tf_op jit(solution)/shard_map/ppermute | solution.py:216
  122.7 13.3 %collective-permute-start.17 = (bf16[128,2048]{1,0:T(8,128)(2,1)S(1)}, bf16[128,2048]{1,0:T(8,128)(2,1)S(1)}, u32[]{:S(2)}, u32[]{:S(2)}) collective-permute-start(bf16[128,2048]{1,0:T(8,128)(2,1)S(1)} %slice.495), channel_id=1, source_target_pairs={{0,2},{2,0},{4,6},{6,4},{8,10},{10,8},{12,14},{14,12},{16,18},{18,... | collective-permute-start | bytes 1572872 | tf_op jit(solution)/shard_map/ppermute | solution.py:209
  124.2 12.9 %collective-permute-start.18 = (bf16[128,2048]{1,0:T(8,128)(2,1)S(1)}, bf16[128,2048]{1,0:T(8,128)(2,1)S(1)}, u32[]{:S(2)}, u32[]{:S(2)}) collective-permute-start(bf16[128,2048]{1,0:T(8,128)(2,1)S(1)} %slice.496), channel_id=1, source_target_pairs={{0,4},{2,6},{4,0},{6,2},{8,12},{10,14},{12,8},{14,10},{16,20},{18,... | collective-permute-start | bytes 1572872 | tf_op jit(solution)/shard_map/ppermute | solution.py:209
  144.7 14.9 %collective-permute-start.22 = (bf16[128,2048]{1,0:T(8,128)(2,1)S(1)}, bf16[128,2048]{1,0:T(8,128)(2,1)S(1)}, u32[]{:S(2)}, u32[]{:S(2)}) collective-permute-start(bf16[128,2048]{1,0:T(8,128)(2,1)S(1)} %get-tuple-element.452), channel_id=1, source_target_pairs={{0,4},{2,6},{4,0},{6,2},{8,12},{10,14},{12,8},{14,10},{16,20},{18,... | collective-permute-start | bytes 1572872 | tf_op jit(solution)/shard_map/ppermute | solution.py:209
  146.1 14.9 %collective-permute-start.21 = (bf16[128,2048]{1,0:T(8,128)(2,1)S(1)}, bf16[128,2048]{1,0:T(8,128)(2,1)S(1)}, u32[]{:S(2)}, u32[]{:S(2)}) collective-permute-start(bf16[128,2048]{1,0:T(8,128)(2,1)S(1)} %get-tuple-element.453), channel_id=1, source_target_pairs={{0,2},{2,0},{4,6},{6,4},{8,10},{10,8},{12,14},{14,12},{16,18},{18,... | collective-permute-start | bytes 1572872 | tf_op jit(solution)/shard_map/ppermute | solution.py:209
  146.7 24.1 %collective-permute-start.20 = (bf16[128,2048]{1,0:T(8,128)(2,1)}, bf16[128,2048]{1,0:T(8,128)(2,1)S(1)}, u32[]{:S(2)}, u32[]{:S(2)}) collective-permute-start(bf16[128,2048]{1,0:T(8,128)(2,1)} %get-tuple-element.454), channel_id=1, source_target_pairs={{0,4},{2,6},{4,0},{6,2},{8,12},{10,14},{12,8},{14,10},{16,20},{18,... | collective-permute-start | bytes 1572872 | tf_op jit(solution)/shard_map/ppermute | solution.py:209
  147.2 24.9 %collective-permute-start.19 = (bf16[128,2048]{1,0:T(8,128)(2,1)}, bf16[128,2048]{1,0:T(8,128)(2,1)S(1)}, u32[]{:S(2)}, u32[]{:S(2)}) collective-permute-start(bf16[128,2048]{1,0:T(8,128)(2,1)} %get-tuple-element.455), channel_id=1, source_target_pairs={{0,2},{2,0},{4,6},{6,4},{8,10},{10,8},{12,14},{14,12},{16,18},{18,... | collective-permute-start | bytes 1572872 | tf_op jit(solution)/shard_map/ppermute | solution.py:209
  162.1 18.2 %collective-permute-start.23 = (bf16[128,2048]{1,0:T(8,128)(2,1)}, bf16[128,2048]{1,0:T(8,128)(2,1)S(1)}, u32[]{:S(2)}, u32[]{:S(2)}) collective-permute-start(bf16[128,2048]{1,0:T(8,128)(2,1)} %get-tuple-element.244), channel_id=1, source_target_pairs={{0,2},{2,0},{4,6},{6,4},{8,10},{10,8},{12,14},{14,12},{16,18},{18,... | collective-permute-start | bytes 1572872 | tf_op jit(solution)/shard_map/ppermute | solution.py:209
  162.7 17.7 %collective-permute-start.24 = (bf16[128,2048]{1,0:T(8,128)(2,1)S(1)}, bf16[128,2048]{1,0:T(8,128)(2,1)S(1)}, u32[]{:S(2)}, u32[]{:S(2)}) collective-permute-start(bf16[128,2048]{1,0:T(8,128)(2,1)S(1)} %get-tuple-element.245), channel_id=1, source_target_pairs={{0,4},{2,6},{4,0},{6,2},{8,12},{10,14},{12,8},{14,10},{16,20},{18,... | collective-permute-start | bytes 1572872 | tf_op jit(solution)/shard_map/ppermute | solution.py:209
  163.3 127.2 %all-gather.11.cloned.1.call-start = ((), (), s32[]{:S(2)}) async-start(), calls=%async_computation.7 | async-start | bytes 3604480 | tf_op jit(solution)/shard_map/all_gather | solution.py:240
  186.1 22.3 %collective-permute-start.26 = (bf16[256,2048]{1,0:T(8,128)(2,1)S(1)}, bf16[256,2048]{1,0:T(8,128)(2,1)S(1)}, u32[]{:S(2)}, u32[]{:S(2)}) collective-permute-start(bf16[256,2048]{1,0:T(8,128)(2,1)S(1)} %multiply_convert_fusion), channel_id=1, source_target_pairs={{0,4},{2,6},{4,0},{6,2},{8,12},{10,14},{12,8},{14,10},{16,20},{18,... | collective-permute-start | bytes 3145736 | tf_op jit(solution)/shard_map/ppermute | solution.py:209
  187.3 22.2 %collective-permute-start.25 = (bf16[256,2048]{1,0:T(8,128)(2,1)S(1)}, bf16[256,2048]{1,0:T(8,128)(2,1)S(1)}, u32[]{:S(2)}, u32[]{:S(2)}) collective-permute-start(bf16[256,2048]{1,0:T(8,128)(2,1)S(1)} %multiply_convert_fusion), channel_id=1, source_target_pairs={{0,2},{2,0},{4,6},{6,4},{8,10},{10,8},{12,14},{14,12},{16,18},{18,... | collective-permute-start | bytes 3145736 | tf_op jit(solution)/shard_map/ppermute | solution.py:209
  210.5 10.5 %collective-permute-start.29 = (bf16[704,2048]{1,0:T(8,128)(2,1)}, bf16[704,2048]{1,0:T(8,128)(2,1)}, u32[]{:S(2)}, u32[]{:S(2)}) collective-permute-start(bf16[704,2048]{1,0:T(8,128)(2,1)} %all-gather.7.cloned.1.call-done.gate_ref.refs_1_), channel_id=1, source_target_pairs={{0,1},{1,0},{2,3},{3,2},{4,5},{5,4},{6,7},{7,6},{8,9},{9,8},{10,11... | collective-permute-start | bytes 8650760 | tf_op jit(solution)/shard_map/ppermute | solution.py:213
  220.9 38.7 %collective-permute-start.30 = (bf16[704,2048]{1,0:T(8,128)(2,1)}, bf16[704,2048]{1,0:T(8,128)(2,1)}, u32[]{:S(2)}, u32[]{:S(2)}) collective-permute-start(bf16[704,2048]{1,0:T(8,128)(2,1)} %all-gather.9.cloned.1.call-done.up_ref.refs_2_), channel_id=1, source_target_pairs={{0,1},{1,0},{2,3},{3,2},{4,5},{5,4},{6,7},{7,6},{8,9},{9,8},{10,11... | collective-permute-start | bytes 8650760 | tf_op jit(solution)/shard_map/ppermute | solution.py:213
  224.7 14.5 %collective-permute-start.27 = (bf16[128,2048]{1,0:T(8,128)(2,1)}, bf16[128,2048]{1,0:T(8,128)(2,1)S(1)}, u32[]{:S(2)}, u32[]{:S(2)}) collective-permute-start(bf16[128,2048]{1,0:T(8,128)(2,1)} %slice.498), channel_id=1, source_target_pairs={{0,2},{2,0},{4,6},{6,4},{8,10},{10,8},{12,14},{14,12},{16,18},{18,... | collective-permute-start | bytes 1572872 | tf_op jit(solution)/shard_map/ppermute | solution.py:209
  226.2 14.4 %collective-permute-start.28 = (bf16[128,2048]{1,0:T(8,128)(2,1)}, bf16[128,2048]{1,0:T(8,128)(2,1)}, u32[]{:S(2)}, u32[]{:S(2)}) collective-permute-start(bf16[128,2048]{1,0:T(8,128)(2,1)} %slice.499), channel_id=1, source_target_pairs={{0,4},{2,6},{4,0},{6,2},{8,12},{10,14},{12,8},{14,10},{16,20},{18,... | collective-permute-start | bytes 1572872 | tf_op jit(solution)/shard_map/ppermute | solution.py:209
  227.7 120.4 %reduce-scatter.5.cloned.1.call-start = ((), (), s32[]{:S(2)}) async-start(), calls=%async_computation.8 | async-start | bytes 3604480 | tf_op jit(solution)/shard_map/reduce_scatter | solution.py:245
  278.3 5.3 collective-permute-start.31
  290.6 5.6 collective-permute-start.32
  290.7 120.1 %reduce-scatter.7.cloned.1.call-start = ((), (), s32[]{:S(2)}) async-start(), calls=%async_computation.9 | async-start | bytes 3604480 | tf_op jit(solution)/shard_map/reduce_scatter | solution.py:245
  328.1 5.3 collective-permute-start.35
  329.6 14.4 %collective-permute-start.34 = (bf16[128,2048]{1,0:T(8,128)(2,1)}, bf16[128,2048]{1,0:T(8,128)(2,1)S(1)}, u32[]{:S(2)}, u32[]{:S(2)}) collective-permute-start(bf16[128,2048]{1,0:T(8,128)(2,1)} %get-tuple-element.444), channel_id=1, source_target_pairs={{0,4},{2,6},{4,0},{6,2},{8,12},{10,14},{12,8},{14,10},{16,20},{18,... | collective-permute-start | bytes 1572872 | tf_op jit(solution)/shard_map/ppermute | solution.py:209
  331.1 14.2 %collective-permute-start.33 = (bf16[128,2048]{1,0:T(8,128)(2,1)}, bf16[128,2048]{1,0:T(8,128)(2,1)}, u32[]{:S(2)}, u32[]{:S(2)}) collective-permute-start(bf16[128,2048]{1,0:T(8,128)(2,1)} %get-tuple-element.445), channel_id=1, source_target_pairs={{0,2},{2,0},{4,6},{6,4},{8,10},{10,8},{12,14},{14,12},{16,18},{18,... | collective-permute-start | bytes 1572872 | tf_op jit(solution)/shard_map/ppermute | solution.py:209
  348.1 130.1 %reduce-scatter.9.cloned.1.call-start = ((), (), s32[]{:S(2)}) async-start(), calls=%async_computation.10 | async-start | bytes 3604480 | tf_op jit(solution)/shard_map/reduce_scatter | solution.py:245
  348.3 15.1 %collective-permute-start.38 = (bf16[128,2048]{1,0:T(8,128)(2,1)}, bf16[128,2048]{1,0:T(8,128)(2,1)S(1)}, u32[]{:S(2)}, u32[]{:S(2)}) collective-permute-start(bf16[128,2048]{1,0:T(8,128)(2,1)} %get-tuple-element.442), channel_id=1, source_target_pairs={{0,4},{2,6},{4,0},{6,2},{8,12},{10,14},{12,8},{14,10},{16,20},{18,... | collective-permute-start | bytes 1572872 | tf_op jit(solution)/shard_map/ppermute | solution.py:209
  349.3 15.1 %collective-permute-start.37 = (bf16[128,2048]{1,0:T(8,128)(2,1)}, bf16[128,2048]{1,0:T(8,128)(2,1)S(1)}, u32[]{:S(2)}, u32[]{:S(2)}) collective-permute-start(bf16[128,2048]{1,0:T(8,128)(2,1)} %get-tuple-element.443), channel_id=1, source_target_pairs={{0,2},{2,0},{4,6},{6,4},{8,10},{10,8},{12,14},{14,12},{16,18},{18,... | collective-permute-start | bytes 1572872 | tf_op jit(solution)/shard_map/ppermute | solution.py:209
  350.0 24.0 %collective-permute-start.39 = (bf16[128,2048]{1,0:T(8,128)(2,1)}, bf16[128,2048]{1,0:T(8,128)(2,1)S(1)}, u32[]{:S(2)}, u32[]{:S(2)}) collective-permute-start(bf16[128,2048]{1,0:T(8,128)(2,1)} %get-tuple-element.313), channel_id=1, source_target_pairs={{0,2},{2,0},{4,6},{6,4},{8,10},{10,8},{12,14},{14,12},{16,18},{18,... | collective-permute-start | bytes 1572872 | tf_op jit(solution)/shard_map/ppermute | solution.py:209
  351.4 22.6 %collective-permute-start.40 = (bf16[128,2048]{1,0:T(8,128)(2,1)S(1)}, bf16[128,2048]{1,0:T(8,128)(2,1)S(1)}, u32[]{:S(2)}, u32[]{:S(2)}) collective-permute-start(bf16[128,2048]{1,0:T(8,128)(2,1)S(1)} %get-tuple-element.314), channel_id=1, source_target_pairs={{0,4},{2,6},{4,0},{6,2},{8,12},{10,14},{12,8},{14,10},{16,20},{18,... | collective-permute-start | bytes 1572872 | tf_op jit(solution)/shard_map/ppermute | solution.py:209
  358.6 46.0 %collective-permute-start.36 = (bf16[704,2048]{1,0:T(8,128)(2,1)S(1)}, bf16[704,2048]{1,0:T(8,128)(2,1)S(1)}, u32[]{:S(2)}, u32[]{:S(2)}) collective-permute-start(bf16[704,2048]{1,0:T(8,128)(2,1)S(1)} %convolution_convert_fusion), channel_id=1, source_target_pairs={{0,1},{1,0},{2,3},{3,2},{4,5},{5,4},{6,7},{7,6},{8,9},{9,8},{10,11... | collective-permute-start | bytes 8650760 | tf_op jit(solution)/shard_map/ppermute | solution.py:213
  379.1 23.7 %collective-permute-start.42 = (bf16[256,2048]{1,0:T(8,128)(2,1)S(1)}, bf16[256,2048]{1,0:T(8,128)(2,1)S(1)}, u32[]{:S(2)}, u32[]{:S(2)}) collective-permute-start(bf16[256,2048]{1,0:T(8,128)(2,1)S(1)} %get-tuple-element.331), channel_id=1, source_target_pairs={{0,4},{2,6},{4,0},{6,2},{8,12},{10,14},{12,8},{14,10},{16,20},{18,... | collective-permute-start | bytes 3145736 | tf_op jit(solution)/shard_map/ppermute | solution.py:209
  379.7 23.9 %collective-permute-start.41 = (bf16[256,2048]{1,0:T(8,128)(2,1)S(1)}, bf16[256,2048]{1,0:T(8,128)(2,1)S(1)}, u32[]{:S(2)}, u32[]{:S(2)}) collective-permute-start(bf16[256,2048]{1,0:T(8,128)(2,1)S(1)} %get-tuple-element.331), channel_id=1, source_target_pairs={{0,2},{2,0},{4,6},{6,4},{8,10},{10,8},{12,14},{14,12},{16,18},{18,... | collective-permute-start | bytes 3145736 | tf_op jit(solution)/shard_map/ppermute | solution.py:209
  409.4 13.8 %collective-permute-start.45 = (bf16[128,2048]{1,0:T(8,128)(2,1)}, bf16[128,2048]{1,0:T(8,128)(2,1)}, u32[]{:S(2)}, u32[]{:S(2)}) collective-permute-start(bf16[128,2048]{1,0:T(8,128)(2,1)} %slice.500), channel_id=1, source_target_pairs={{0,2},{2,0},{4,6},{6,4},{8,10},{10,8},{12,14},{14,12},{16,18},{18,... | collective-permute-start | bytes 1572872 | tf_op jit(solution)/shard_map/ppermute | solution.py:209
  410.0 13.2 %collective-permute-start.46 = (bf16[128,2048]{1,0:T(8,128)(2,1)}, bf16[128,2048]{1,0:T(8,128)(2,1)}, u32[]{:S(2)}, u32[]{:S(2)}) collective-permute-start(bf16[128,2048]{1,0:T(8,128)(2,1)} %slice.501), channel_id=1, source_target_pairs={{0,4},{2,6},{4,0},{6,2},{8,12},{10,14},{12,8},{14,10},{16,20},{18,... | collective-permute-start | bytes 1572872 | tf_op jit(solution)/shard_map/ppermute | solution.py:209
  423.2 137.8 %reduce-scatter.11.cloned.1.call-start = ((), (), s32[]{:S(2)}) async-start(), calls=%async_computation.11 | async-start | bytes 5242880 | tf_op jit(solution)/shard_map/reduce_scatter | solution.py:245
  425.0 13.4 %collective-permute-start.44 = (bf16[128,2048]{1,0:T(8,128)(2,1)S(1)}, bf16[128,2048]{1,0:T(8,128)(2,1)S(1)}, u32[]{:S(2)}, u32[]{:S(2)}) collective-permute-start(bf16[128,2048]{1,0:T(8,128)(2,1)S(1)} %get-tuple-element.436), channel_id=1, source_target_pairs={{0,4},{2,6},{4,0},{6,2},{8,12},{10,14},{12,8},{14,10},{16,20},{18,... | collective-permute-start | bytes 1572872 | tf_op jit(solution)/shard_map/ppermute | solution.py:209
  426.3 12.2 %collective-permute-start.43 = (bf16[128,2048]{1,0:T(8,128)(2,1)S(1)}, bf16[128,2048]{1,0:T(8,128)(2,1)S(1)}, u32[]{:S(2)}, u32[]{:S(2)}) collective-permute-start(bf16[128,2048]{1,0:T(8,128)(2,1)S(1)} %get-tuple-element.437), channel_id=1, source_target_pairs={{0,2},{2,0},{4,6},{6,4},{8,10},{10,8},{12,14},{14,12},{16,18},{18,... | collective-permute-start | bytes 1572872 | tf_op jit(solution)/shard_map/ppermute | solution.py:209
  436.7 6.2 %collective-permute-start.50 = (f32[2,16,2,256]{3,2,1,0:T(2,128)S(1)}, f32[2,16,2,256]{3,2,1,0:T(2,128)S(1)}, u32[]{:S(2)}, u32[]{:S(2)}) collective-permute-start(f32[2,16,2,256]{3,2,1,0:T(2,128)S(1)} %pad_maximum_fusion.9), channel_id=1, source_target_pairs={{1,0},{3,2},{5,4},{7,6},{9,8},{11,10},{13,12},{15,14},{17,16},{19,... | collective-permute-start | bytes 196616 | tf_op jit(solution)/shard_map/ppermute | solution.py:219
  449.1 9.2 %collective-permute-start.51 = (bf16[512,2048]{1,0:T(8,128)(2,1)S(1)}, bf16[512,2048]{1,0:T(8,128)(2,1)S(1)}, u32[]{:S(2)}, u32[]{:S(2)}) collective-permute-start(bf16[512,2048]{1,0:T(8,128)(2,1)S(1)} %convolution_convert_fusion.3), channel_id=1, source_target_pairs={{0,1},{1,0},{2,3},{3,2},{4,5},{5,4},{6,7},{7,6},{8,9},{9,8},{10,11... | collective-permute-start | bytes 6291464 | tf_op jit(solution)/shard_map/ppermute | solution.py:213
  450.3 6.7 %collective-permute-start.52 = (bf16[256,2048]{1,0:T(8,128)(2,1)S(1)}, bf16[256,2048]{1,0:T(8,128)(2,1)S(1)}, u32[]{:S(2)}, u32[]{:S(2)}) collective-permute-start(bf16[256,2048]{1,0:T(8,128)(2,1)S(1)} %convolution_convert_fusion.4), channel_id=1, source_target_pairs={{0,1},{1,0},{2,3},{3,2},{4,5},{5,4},{6,7},{7,6},{8,9},{9,8},{10,11... | collective-permute-start | bytes 3145736 | tf_op jit(solution)/shard_map/ppermute | solution.py:213
  450.7 25.1 %collective-permute-start.47 = (bf16[256,2048]{1,0:T(8,128)(2,1)S(1)}, bf16[256,2048]{1,0:T(8,128)(2,1)S(1)}, u32[]{:S(2)}, u32[]{:S(2)}) collective-permute-start(bf16[256,2048]{1,0:T(8,128)(2,1)S(1)} %pad_maximum_fusion.6), channel_id=1, source_target_pairs={{0,2},{2,0},{4,6},{6,4},{8,10},{10,8},{12,14},{14,12},{16,18},{18,... | collective-permute-start | bytes 3145736 | tf_op jit(solution)/shard_map/ppermute | solution.py:209
  451.3 25.5 %collective-permute-start.48 = (bf16[256,2048]{1,0:T(8,128)(2,1)S(1)}, bf16[256,2048]{1,0:T(8,128)(2,1)}, u32[]{:S(2)}, u32[]{:S(2)}) collective-permute-start(bf16[256,2048]{1,0:T(8,128)(2,1)S(1)} %pad_maximum_fusion.5), channel_id=1, source_target_pairs={{0,4},{2,6},{4,0},{6,2},{8,12},{10,14},{12,8},{14,10},{16,20},{18,... | collective-permute-start | bytes 3145736 | tf_op jit(solution)/shard_map/ppermute | solution.py:209
  502.5 14.8 %collective-permute-start.56 = (bf16[128,2048]{1,0:T(8,128)(2,1)S(1)}, bf16[128,2048]{1,0:T(8,128)(2,1)S(1)}, u32[]{:S(2)}, u32[]{:S(2)}) collective-permute-start(bf16[128,2048]{1,0:T(8,128)(2,1)S(1)} %get-tuple-element.426), channel_id=1, source_target_pairs={{0,4},{2,6},{4,0},{6,2},{8,12},{10,14},{12,8},{14,10},{16,20},{18,... | collective-permute-start | bytes 1572872 | tf_op jit(solution)/shard_map/ppermute | solution.py:209
  504.0 14.9 %collective-permute-start.55 = (bf16[128,2048]{1,0:T(8,128)(2,1)S(1)}, bf16[128,2048]{1,0:T(8,128)(2,1)S(1)}, u32[]{:S(2)}, u32[]{:S(2)}) collective-permute-start(bf16[128,2048]{1,0:T(8,128)(2,1)S(1)} %get-tuple-element.427), channel_id=1, source_target_pairs={{0,2},{2,0},{4,6},{6,4},{8,10},{10,8},{12,14},{14,12},{16,18},{18,... | collective-permute-start | bytes 1572872 | tf_op jit(solution)/shard_map/ppermute | solution.py:209
  505.4 42.1 %collective-permute-start.54 = (bf16[128,2048]{1,0:T(8,128)(2,1)}, bf16[128,2048]{1,0:T(8,128)(2,1)S(1)}, u32[]{:S(2)}, u32[]{:S(2)}) collective-permute-start(bf16[128,2048]{1,0:T(8,128)(2,1)} %get-tuple-element.428), channel_id=1, source_target_pairs={{0,4},{2,6},{4,0},{6,2},{8,12},{10,14},{12,8},{14,10},{16,20},{18,... | collective-permute-start | bytes 1572872 | tf_op jit(solution)/shard_map/ppermute | solution.py:209
  506.0 41.6 %collective-permute-start.53 = (bf16[128,2048]{1,0:T(8,128)(2,1)}, bf16[128,2048]{1,0:T(8,128)(2,1)S(1)}, u32[]{:S(2)}, u32[]{:S(2)}) collective-permute-start(bf16[128,2048]{1,0:T(8,128)(2,1)} %get-tuple-element.429), channel_id=1, source_target_pairs={{0,2},{2,0},{4,6},{6,4},{8,10},{10,8},{12,14},{14,12},{16,18},{18,... | collective-permute-start | bytes 1572872 | tf_op jit(solution)/shard_map/ppermute | solution.py:209
  521.8 25.8 %collective-permute-start.57 = (bf16[128,2048]{1,0:T(8,128)(2,1)}, bf16[128,2048]{1,0:T(8,128)(2,1)S(1)}, u32[]{:S(2)}, u32[]{:S(2)}) collective-permute-start(bf16[128,2048]{1,0:T(8,128)(2,1)} %get-tuple-element.386), channel_id=1, source_target_pairs={{0,2},{2,0},{4,6},{6,4},{8,10},{10,8},{12,14},{14,12},{16,18},{18,... | collective-permute-start | bytes 1572872 | tf_op jit(solution)/shard_map/ppermute | solution.py:209
  523.3 24.3 %collective-permute-start.58 = (bf16[128,2048]{1,0:T(8,128)(2,1)S(1)}, bf16[128,2048]{1,0:T(8,128)(2,1)S(1)}, u32[]{:S(2)}, u32[]{:S(2)}) collective-permute-start(bf16[128,2048]{1,0:T(8,128)(2,1)S(1)} %get-tuple-element.387), channel_id=1, source_target_pairs={{0,4},{2,6},{4,0},{6,2},{8,12},{10,14},{12,8},{14,10},{16,20},{18,... | collective-permute-start | bytes 1572872 | tf_op jit(solution)/shard_map/ppermute | solution.py:209
  529.2 6.6 %collective-permute-start.63 = (f32[2,2048]{1,0:T(2,128)S(1)}, f32[2,2048]{1,0:T(2,128)S(1)}, u32[]{:S(2)}, u32[]{:S(2)}) collective-permute-start(f32[2,2048]{1,0:T(2,128)S(1)} %add.263), channel_id=1, source_target_pairs={{0,8},{2,10},{4,12},{6,14},{8,0},{10,2},{12,4},{14,6},{16,24},{18,... | collective-permute-start | bytes 49160 | tf_op jit(solution)/shard_map/ppermute | solution.py:209
  535.7 5.7 collective-permute-start.61
  541.4 6.2 %collective-permute-start.64 = (f32[2,2048]{1,0:T(2,128)S(1)}, f32[2,2048]{1,0:T(2,128)S(1)}, u32[]{:S(2)}, u32[]{:S(2)}) collective-permute-start(f32[2,2048]{1,0:T(2,128)S(1)} %add.264), channel_id=1, source_target_pairs={{0,16},{2,18},{4,20},{6,22},{8,24},{10,26},{12,28},{14,30},{16,0},... | collective-permute-start | bytes 49160 | tf_op jit(solution)/shard_map/ppermute | solution.py:209
  (87 other events, 728.6 us)
Sparse Core Ops, SparseCore 0:
  10.2 83.5 all-gather.4
  95.4 57.6 all-gather.6
  163.4 57.4 all-gather.8
  227.8 56.0 all-gather.10
  290.8 53.9 reduce-scatter.4
  348.2 54.8 reduce-scatter.6
  423.3 54.8 reduce-scatter.8
  482.4 77.4 reduce-scatter.10

commit v3 on v2

--- a/solution.py
+++ b/solution.py
@@ -32,56 +32,133 @@
     return value.astype(jnp.float32)
 
 
-def kernel_call(body, grid, in_specs, out_specs, out_shape, flops, moved):
+def whole(shape):
+    return pl.BlockSpec(shape, lambda i: (0, 0), pipeline_mode=pl.Buffered(1))
+
+
+def sum_of_products(lefts, rights, tile=256):
+    rows, width = lefts[0].shape[0], rights[0].shape[1]
+    count = len(lefts)
+    tile = min(tile, rows)
+    depths = [left.shape[1] for left in lefts]
+    starts, depth = [], 0
+    for size in depths:
+        starts.append(depth)
+        depth += -(-size // 256) * 256
+    limit = 2 * depth * (width + 3 * tile) + 8 * tile * width + 4 * 1024 * 1024
+
+    def body(*refs):
+        left_refs, right_refs, out_ref = refs[:count], refs[count : 2 * count], refs[2 * count]
+        side, stacked, sems = refs[2 * count + 1 :]
+        copies = [
+            pltpu.make_async_copy(right, stacked.at[pl.ds(start, size)], sems.at[k])
+            for k, (right, start, size) in enumerate(zip(right_refs, starts, depths))
+        ]
+
+        @pl.when(pl.program_id(0) == 0)
+        def _():
+            for copy in copies:
+                copy.start()
+            for start, end, size in zip(starts, starts[1:] + [depth], depths):
+                if start + size < end:
+                    side[:, start + size : end] = jnp.zeros(
+                        (tile, end - start - size), jnp.bfloat16
+                    )
+                    stacked[start + size : end, :] = jnp.zeros(
+                        (end - start - size, width), jnp.bfloat16
+                    )
+            for copy in copies:
+                copy.wait()
+
+        for left, start, size in zip(left_refs, starts, depths):
+            side[:, start : start + size] = left[...]
+        out_ref[...] = low(matmul(side[...], stacked[...]))
+
     return pl.pallas_call(
         body,
-        grid=grid,
-        in_specs=in_specs,
-        out_specs=out_specs,
-        out_shape=out_shape,
+        grid=(rows // tile,),
+        in_specs=[pl.BlockSpec((tile, size), lambda i: (i, 0)) for size in depths]
+        + [pl.BlockSpec(memory_space=pl.ANY)] * count,
+        out_specs=pl.BlockSpec((tile, width), lambda i: (i, 0)),
+        out_shape=jax.ShapeDtypeStruct((rows, width), jnp.bfloat16),
+        scratch_shapes=[
+            pltpu.VMEM((tile, depth), jnp.bfloat16),
+            pltpu.VMEM((depth, width), jnp.bfloat16),
+            pltpu.SemaphoreType.DMA((count,)),
+        ],
         compiler_params=pltpu.CompilerParams(
-            dimension_semantics=("arbitrary",), vmem_limit_bytes=48 * 1024 * 1024
+            dimension_semantics=("arbitrary",), vmem_limit_bytes=limit
         ),
         cost_estimate=pl.CostEstimate(flops=1, bytes_accessed=1, transcendentals=0),
-    )
-
-
-def size_of(*arrays):
-    return sum(array.size * array.dtype.itemsize for array in arrays)
-
-
-def whole(shape):
-    return pl.BlockSpec(shape, lambda i: (0, 0), pipeline_mode=pl.Buffered(1))
-
-
-def sum_of_products(lefts, rights, tile=512):
-    rows, width = lefts[0].shape[0], rights[0].shape[1]
-    count = len(lefts)
-
-    def body(*refs):
-        total = matmul(refs[0][...], refs[count][...])
-        for k in range(1, count):
-            total = total + matmul(refs[k][...], refs[count + k][...])
+    )(*lefts, *rights)
+
+
+def rows_product(left, right, tile=256):
+    rows, width = left.shape
+    count = right.shape[0]
+    tile = min(tile, rows)
+
+    def body(left_ref, right_ref, out_ref):
+        out_ref[...] = low(times_trans(left_ref[...], right_ref[...]))
+
+    return pl.pallas_call(
+        body,
+        grid=(rows // tile,),
+        in_specs=[pl.BlockSpec((tile, width), lambda i: (i, 0)), whole(right.shape)],
+        out_specs=pl.BlockSpec((tile, count), lambda i: (i, 0)),
+        out_shape=jax.ShapeDtypeStruct((rows, count), jnp.bfloat16),
+        compiler_params=pltpu.CompilerParams(
+            dimension_semantics=("arbitrary",), vmem_limit_bytes=12 * 1024 * 1024
+        ),
+        cost_estimate=pl.CostEstimate(flops=1, bytes_accessed=1, transcendentals=0),
+    )(left, right)
+
+
+def columns_product(left, right, more=(), flops=1, far=False, tile=512):
+    rows, count = left.shape
+    width = right.shape[1]
+
+    def body(left_ref, right_ref, *refs):
+        total = trans_times(left_ref[...], right_ref[...])
+        for ref in refs[:-1]:
+            total = total + high(ref[...])
         refs[-1][...] = low(total)
 
-    depth = sum(left.shape[1] for left in lefts)
-    return kernel_call(
+    spec = pl.BlockSpec((count, tile), lambda i: (0, i))
+    return pl.pallas_call(
         body,
-        (width // tile,),
-        [whole(left.shape) for left in lefts]
-        + [pl.BlockSpec((right.shape[0], tile), lambda i: (0, i)) for right in rights],
-        pl.BlockSpec((rows, tile), lambda i: (0, i)),
-        jax.ShapeDtypeStruct((rows, width), jnp.bfloat16),
-        2 * rows * depth * width,
-        size_of(*lefts, *rights) + 2 * rows * width,
-    )(*lefts, *rights)
-
-
-def ffn_ahead(normed, gate, up, tile=256):
-    rows, width = normed.shape
-    units = gate.shape[0]
+        grid=(width // tile,),
+        in_specs=[whole(left.shape), pl.BlockSpec((rows, tile), lambda i: (0, i))]
+        + [spec] * len(more),
+        out_specs=spec,
+        out_shape=(pltpu.HBM if far else jax.ShapeDtypeStruct)((count, width), jnp.bfloat16),
+        compiler_params=pltpu.CompilerParams(
+            dimension_semantics=("arbitrary",), vmem_limit_bytes=14 * 1024 * 1024
+        ),
+        cost_estimate=pl.CostEstimate(flops=flops, bytes_accessed=1, transcendentals=0),
+    )(left, right, *more)
+
+
+def ffn_call(body, lefts, rights, slopes, count, tile=256):
+    rows, units = lefts[0].shape[0], rights[0].shape[0]
     tile = min(tile, rows)
-
+    spec = pl.BlockSpec((tile, units), lambda i: (i, 0))
+    return pl.pallas_call(
+        body,
+        grid=(rows // tile,),
+        in_specs=[pl.BlockSpec((tile, left.shape[1]), lambda i: (i, 0)) for left in lefts]
+        + [whole(right.shape) for right in rights]
+        + [spec] * len(slopes),
+        out_specs=[spec] * count,
+        out_shape=[jax.ShapeDtypeStruct((rows, units), jnp.bfloat16)] * count,
+        compiler_params=pltpu.CompilerParams(
+            dimension_semantics=("arbitrary",), vmem_limit_bytes=20 * 1024 * 1024
+        ),
+        cost_estimate=pl.CostEstimate(flops=1, bytes_accessed=1, transcendentals=0),
+    )(*lefts, *rights, *slopes)
+
+
+def ffn_ahead(normed, gate, up):
     def body(normed_ref, gate_ref, up_ref, hidden_ref, gate_slope_ref, up_slope_ref):
         pre = times_trans(normed_ref[...], gate_ref[...])
         value = times_trans(normed_ref[...], up_ref[...])
@@ -91,93 +168,16 @@
         gate_slope_ref[...] = low(value * sigma * (1.0 + pre * (1.0 - sigma)))
         up_slope_ref[...] = low(activated)
 
-    out = jax.ShapeDtypeStruct((rows, units), jnp.bfloat16)
-    spec = pl.BlockSpec((tile, units), lambda i: (i, 0))
-    return kernel_call(
-        body,
-        (rows // tile,),
-        [pl.BlockSpec((tile, width), lambda i: (i, 0)), whole(gate.shape), whole(up.shape)],
-        [spec] * 3,
-        [out] * 3,
-        4 * rows * width * units,
-        size_of(normed, gate, up) + 6 * rows * units,
-    )(normed, gate, up)
-
-
-def ffn_back(grad, down, gate, up, gate_slope, up_slope, tile=256):
-    rows, width = grad.shape
-    units = down[0].shape[0]
-    tile = min(tile, rows)
-    count = len(down)
-    mats = [mat for group in zip(down, gate, up) for mat in group]
-    slopes = [slope for group in zip(gate_slope, up_slope) for slope in group]
-
-    wide = -(-units // 256) * 256
-
-    def body(grad_ref, *refs):
-        mat_refs, slope_refs = refs[: 3 * count], refs[3 * count : 5 * count]
-        out_refs, total_ref = refs[5 * count : 7 * count], refs[7 * count]
-        downs, others, pieces, sems = refs[7 * count + 1 :]
-        first = pl.program_id(0) == 0
-        copies = []
-        for j in range(count):
-            targets = [downs.at[j]]
-            targets += [others.at[pl.ds((2 * j + k) * wide, units)] for k in range(2)]
-            for k, target in enumerate(targets):
-                at = 3 * j + k
-                copies.append(pltpu.make_async_copy(mat_refs[at], target, sems.at[at]))
-
-        @pl.when(first)
-        def _():
-            for copy in copies[::3] + copies[1::3] + copies[2::3]:
-                copy.start()
-            if wide > units:
-                pieces[...] = jnp.zeros_like(pieces)
-                for at in range(2 * count):
-                    others[at * wide + units : (at + 1) * wide, :] = jnp.zeros(
-                        (wide - units, width), jnp.bfloat16
-                    )
-            for copy in copies[::3]:
-                copy.wait()
-
-        for j in range(count):
-            grad_hidden = times_trans(grad_ref[...], downs[j])
-            for k in range(2):
-                at = 2 * j + k
-                piece = low(grad_hidden * high(slope_refs[at][...]))
-                out_refs[at][...] = piece
-                pieces[:, at * wide : at * wide + units] = piece
-
-        @pl.when(first)
-        def _():
-            for copy in copies[1::3] + copies[2::3]:
-                copy.wait()
-
-        total_ref[...] = low(matmul(pieces[...], others[...]))
-
-    out = jax.ShapeDtypeStruct((rows, units), jnp.bfloat16)
-    spec = pl.BlockSpec((tile, units), lambda i: (i, 0))
-    row_spec = pl.BlockSpec((tile, width), lambda i: (i, 0))
-    found = pl.pallas_call(
-        body,
-        grid=(rows // tile,),
-        in_specs=[row_spec]
-        + [pl.BlockSpec(memory_space=pl.ANY)] * (3 * count)
-        + [spec] * (2 * count),
-        out_specs=[spec] * (2 * count) + [row_spec],
-        out_shape=[out] * (2 * count) + [jax.ShapeDtypeStruct((rows, width), jnp.bfloat16)],
-        scratch_shapes=[
-            pltpu.VMEM((count, units, width), jnp.bfloat16),
-            pltpu.VMEM((2 * count * wide, width), jnp.bfloat16),
-            pltpu.VMEM((tile, 2 * count * wide), jnp.bfloat16),
-            pltpu.SemaphoreType.DMA((3 * count,)),
-        ],
-        compiler_params=pltpu.CompilerParams(
-            dimension_semantics=("arbitrary",), vmem_limit_bytes=48 * 1024 * 1024
-        ),
-        cost_estimate=pl.CostEstimate(flops=1, bytes_accessed=1, transcendentals=0),
-    )(grad, *mats, *slopes)
-    return [found[2 * j] for j in range(count)], [found[2 * j + 1] for j in range(count)], found[-1]
+    return ffn_call(body, [normed], [gate, up], [], 3)
+
+
+def ffn_back(grad, down, gate_slope, up_slope):
+    def body(grad_ref, down_ref, gate_slope_ref, up_slope_ref, gate_ref, up_ref):
+        grad_hidden = times_trans(grad_ref[...], down_ref[...])
+        gate_ref[...] = low(grad_hidden * high(gate_slope_ref[...]))
+        up_ref[...] = low(grad_hidden * high(up_slope_ref[...]))
+
+    return ffn_call(body, [grad], [down], [gate_slope, up_slope], 2)
 
 
 class Order:
@@ -224,12 +224,6 @@
 
     def sum_cores(self, sent):
         return [self.across(self.order(value), -j) for j, value in enumerate(sent, 1)]
-
-    def sum_cores_of(self, value):
-        total = value
-        for j in range(1, self.tp):
-            total = total + self.across(value, j)
-        return total
 
     def sum_bits(self, value, bits):
         for bit in bits:
@@ -373,10 +367,9 @@
         [in_weight.transpose(1, 2, 0).reshape(3 * share, width), out_weight], 0
     )
     mixer_all = groups.gather_ordered(mixer_own)
-    gate_own, up_own = gate_weight.T, up_weight.T
-    gate_all = groups.gather_ordered(after(gate_own, mixer_own))
-    up_all = groups.gather_ordered(after(up_own, gate_own))
-    down_all = groups.gather_ordered(after(down_weight, up_own))
+    pair_own = jnp.concatenate([gate_weight.T, up_weight.T], 0)
+    pair_all = groups.gather_ordered(after(pair_own, mixer_own))
+    down_all = groups.gather_ordered(after(down_weight, pair_own))
 
     plane = chip // 4
     same = []
@@ -388,7 +381,7 @@
     cot_own = cotangent.reshape(rows, width)
     token_rows = Rows(groups, tokens_own)
     gains = groups.stack(jnp.stack([norm1_gain, norm2_gain]), column_bits)
-    order.wait(gains, gate_own, up_own)
+    order.wait(gains, pair_own)
     taps = groups.stack(conv_weight, column_bits)
     order.wait(taps)
     gains = groups.stack(gains, plane_bits[:1])
@@ -451,7 +444,6 @@
     mixer_sums = Sums(groups, mixer_out)
     mixer_sums.middle()
     mixer_sum = mixer_sums.end()
-    order.wait(gate_all)
     mixer_sum, tokens_now = order(mixer_sum, tokens_own)
     tokens_f = high(tokens_own)
     resid = high(tokens_now) + mixer_sum
@@ -461,71 +453,76 @@
     order.did(normed_own)
     two_rows = Rows(groups, normed_own)
     two_rows.middle()
-    gate = groups.cores(gate_all)
-    order.wait(gate)
-    order.wait(up_all)
-    up = groups.cores(up_all)
+    order.wait(pair_all)
+    pairs = groups.cores(pair_all)
+    gate, up = [], []
     normed_two = two_rows.end()
     order.did(normed_two)
-    hidden, gate_slope, up_slope = [], [], []
+    hidden, gate_slope, up_slope, grad_gate, grad_up = [], [], [], [], []
     for j in range(tp):
-        if j:
-            order.wait(up[j])
+        order.wait(pairs[j])
+        pair = order(pairs[j]).reshape(deep, 2, hidden_share, width)
+        gate.append(pair[:, 0].reshape(deep * hidden_share, width))
+        up.append(pair[:, 1].reshape(deep * hidden_share, width))
+        order.did(gate[j], up[j])
         found = ffn_ahead(*order(normed_two, gate[j], up[j]))
         order.did(*found)
         for kept, value in zip((hidden, gate_slope, up_slope), found):
             kept.append(value)
-    def core_terms(left, right):
+
+    def core_terms(left, right, flops=1):
         left, right = order(left, right)
-        sent = [low(trans_times(value, right)) for value in left[1:]]
+        sent = [columns_product(value, right, (), flops) for value in left[1:]]
         order.did(sent)
         return groups.sum_cores(sent)
 
-    def own_term(left, right, got):
+    def own_term(left, right, got, flops=1, far=True):
         order.wait(got)
         left, right, got = order(left, right, got)
-        total = trans_times(left, right)
-        for value in got:
-            total = total + high(value)
-        total = low(total)
+        total = columns_product(left, right, got, flops, far)
         order.did(total)
         return total
 
     got = core_terms(hidden, cot_all)
     down_total = own_term(hidden[0], cot_all, got)
     order.wait(down_all)
+    down_mats = groups.cores(down_all)
     down_grad = groups.reduce_ordered(order(down_total))
-    down_mats = groups.cores(down_all)
-    order.wait(down_mats)
-    grad_gate, grad_up, back_two = ffn_back(
-        *order(cot_all, down_mats, gate, up, gate_slope, up_slope)
-    )
-    order.did(grad_gate, grad_up, back_two)
+    for j in range(tp):
+        if j:
+            order.wait(down_mats[j])
+        found = ffn_back(*order(cot_all, down_mats[j], gate_slope[j], up_slope[j]))
+        order.did(*found)
+        grad_gate.append(found[0])
+        grad_up.append(found[1])
+    back_two = sum_of_products(*order(grad_gate + grad_up, gate + up))
+    order.did(back_two)
     two_sums = Sums(groups, back_two)
     gate_got = core_terms(grad_gate, normed_two)
     gate_total = own_term(grad_gate[0], normed_two, gate_got)
     two_sums.middle()
+    up_got = core_terms(grad_up, normed_two)
+    gate_grad = groups.reduce_ordered(order(gate_total))
+    up_total = own_term(grad_up[0], normed_two, up_got)
+    grad_normed_two = two_sums.end()
     order.wait(down_grad)
-    gate_grad = groups.reduce_ordered(order(gate_total))
-    up_got = core_terms(grad_up, normed_two)
-    grad_normed_two = two_sums.end()
+    up_grad = groups.reduce_ordered(order(up_total))
+    grad_normed_two = order(grad_normed_two)
     resid_back = norm_back(resid, scale_two, gain_two, grad_normed_two)
     grad_resid = high(cot_own) + resid_back
     grad_low = low(grad_resid)
     order.did(grad_low)
     mixer_rows = Rows(groups, grad_low)
-    up_total = own_term(grad_up[0], normed_two, up_got)
-    mixer_rows.middle()
     norm_two_term = jnp.sum(grad_normed_two * resid * scale_two, 0)
-    order.wait(gate_grad)
-    up_grad = groups.reduce_ordered(order(up_total))
     hidden_now, down_now = order(hidden, down_mats)
     ffn_out = sum_of_products(hidden_now, down_now)
     order.did(ffn_out, norm_two_term)
+    mixer_rows.middle()
     ffn_sums = Sums(groups, ffn_out, True)
     grad_mixer = mixer_rows.end()
     order.did(grad_mixer)
 
+    many = 4 * rows * width * width
     grad_now, mats_now = order(grad_mixer, out_mats)
     grad_mixed = [
         times_trans(grad_now, mat).reshape(segments, own_rows, -1) for mat in mats_now
@@ -542,8 +539,8 @@
     order.did(grad_b, grad_conv, edges)
     starts = groups.last_core(order(edges))
     ffn_sums.middle()
-    b_got = core_terms(grad_b, normed)
-    out_got = core_terms(mixed, grad_mixer)
+    b_got = core_terms(grad_b, normed, many)
+    out_got = core_terms(mixed, grad_mixer, many)
     order.wait(starts)
     grad_conv_now, masked_one, masked_two, starts = order(
         grad_conv, masked_one, masked_two, starts
@@ -562,10 +559,12 @@
         for gg, part in zip(grad_gated, parts)
     ]
     order.did(grad_cx)
-    cx_got = core_terms(grad_cx, normed)
-    b_total = own_term(grad_b[0], normed, b_got)
-    out_total = own_term(mixed[0], grad_mixer, out_got)
-    cx_total = own_term(grad_cx[0], normed, cx_got)
+    cx_got = core_terms(grad_cx, normed, many)
+    order.wait(gate_grad)
+    b_total = own_term(grad_b[0], normed, b_got, many, False)
+    out_total = own_term(mixed[0], grad_mixer, out_got, many, False)
+    order.wait(ffn_sums.summed)
+    cx_total = own_term(grad_cx[0], normed, cx_got, many, False)
     mixer_total = (
         jnp.concatenate([b_total, cx_total, out_total], 0)
         .reshape(4, deep, share, width)
@@ -574,9 +573,9 @@
     )
     order.did(mixer_total)
     order.wait(up_grad)
+    mixer_grad = groups.reduce_ordered(order(mixer_total))
     block_output = low(resid + ffn_sums.end())
     order.did(block_output)
-    mixer_grad = groups.reduce_ordered(order(mixer_total))
     b_mats = [mat[:wide_share] for mat in in_mats]
     cx_mats = [mat[wide_share:] for mat in in_mats]
     back_one = sum_of_products(*order(grad_b + grad_cx, b_mats + cx_mats))
@@ -588,35 +587,50 @@
         jnp.stack([jnp.sum(gc * value, (0, 1)) for value in (gi, one, two)])
         for gc, gi, one, two in zip(grad_conv, gated_in, one_back, two_back)
     ]
-    order.did(norm_one_term, conv_terms)
+    small = [
+        jnp.stack(
+            [
+                norm_one_term,
+                norm_two_term,
+                jnp.pad(term.reshape(-1), (0, width - 3 * wide_share)),
+            ]
+        )
+        for term in conv_terms
+    ]
+    order.did(small)
     one_rows.middle()
-    conv_sum = conv_terms[0]
+    small = order(small)
+    total = small[0]
     for j in range(1, tp):
-        conv_sum = conv_sum + groups.across(order(conv_terms[j]), -j)
-    gain_sums = groups.sum_cores_of(order(jnp.stack([norm_one_term, norm_two_term])))
-    conv_sum = groups.sum_bits(conv_sum, column_bits)
-    gain_sums = groups.sum_bits(gain_sums, column_bits)
-    conv_total = lax.dynamic_slice_in_dim(conv_sum, plane * share, share, 1)
-    order.wait(conv_total, gain_sums)
+        total = total + groups.across(small[j], -j)
+    total = groups.sum_bits(total, column_bits)
+    order.wait(total)
     grad_normed = one_rows.end()
     input_back = norm_back(tokens_f, rms_scale(tokens_f), gain_one, grad_normed)
     input_grad = low(grad_resid + input_back)
     order.did(input_grad)
-    gain_sums = groups.sum_bits(order(gain_sums), plane_bits)
+    total = order(total)
+    conv_total = lax.dynamic_slice_in_dim(
+        total[2, : 3 * wide_share].reshape(3, wide_share), plane * share, share, 1
+    )
+    gain_sums = groups.sum_bits(total[:2], plane_bits)
     gate_grad, up_grad = order(gate_grad, up_grad)
     gate_grad, up_grad = high(gate_grad).T, high(up_grad).T
     order.did(gate_grad, up_grad)
+    order.wait(gain_sums)
     order.wait(mixer_grad)
-    mixer_grad = high(mixer_grad).reshape(4, share, width)
+    mixer_grad = order(mixer_grad)
+    in_grad = high(mixer_grad[: 3 * share]).reshape(3, share, width)
+    out_grad = high(mixer_grad[3 * share :])
     gain_share = norm1_gain.shape[0]
     gain_grads = lax.dynamic_slice_in_dim(gain_sums, chip * gain_share, gain_share, 1)
     return (
         block_output.reshape(tokens.shape),
         input_grad.reshape(tokens.shape),
         gain_grads[0],
-        mixer_grad[:3].transpose(2, 0, 1),
+        in_grad.transpose(2, 0, 1),
         conv_total,
-        mixer_grad[3],
+        out_grad,
         gain_grads[1],
         gate_grad,
         up_grad,

time: 582 us -> 562 us (0.966)
  matrix products: 52.3 us -> 9.47 us
  Pallas kernels: 74.1 us -> 112 us
  waiting for transfers between devices: 236 us -> 219 us
    dot_general x12 -> x0, matrix products: 42.8 us -> none  [trans_times(): lax.dot_general(left, right, (((0,), (0,)), ((), ())), preferred_element_...]
    pallas_call x6 -> x20, Pallas kernels: 74.1 us -> 112 us  [the longest x12 51.2 us: columns_product(): pl.pallas_call(body, grid=(width // tile,), in_specs=[whole(left.shape),...]
    ppermute x52 -> x50, waiting for transfers between devices: 198 us -> 165 us  [swap(): return lax.ppermute(value, 'fsdp', [(i, i ^ bit) for i in range(self.fsdp)])]
    all_gather x4 -> x3, waiting for transfers between devices: 20 us -> 33.5 us  [gather_ordered(): lax.all_gather(value, 'fsdp', axis=0, tiled=True, axis_index_groups=self....]
    unnamed x168 -> x222, local copies, waits for them, and re-layouts: 33 us -> 40.4 us
    ppermute x13 -> x11, waiting for transfers between devices: 16.7 us -> 13.9 us  [across(): return lax.ppermute(value, 'tp', pairs)]
    ppermute x52 -> x50, starting transfers between devices: 55.6 us -> 56.3 us  [swap(): return lax.ppermute(value, 'fsdp', [(i, i ^ bit) for i in range(self.fsdp)])]
  transfers between devices with their start and end apart: 75 -> 70, of which waited for: 43 -> 43; matrix products, arithmetic and copies ran while one was open for 26% -> 18% of each run, Pallas kernels for 13% -> 20%
where the time goes in v3:
time: 562 us; the launch traced here: 557 us
  waiting for transfers between devices  219 us (39%)
  Pallas kernels  112 us (20%)
  local copies, waits for them, and re-layouts  82.6 us (15%)
  starting transfers between devices  64.3 us (11%)
  other arithmetic  53.2 us (9%)
  between operations  16.2 us (3%)
  matrix products  9.47 us (2%)
    ppermute x50, waiting for transfers between devices, swap(): return lax.ppermute(value, 'fsdp', [(i, i ^ bit) for i in range(self.fsdp)])  165 us
    ppermute x50, starting transfers between devices, swap(): return lax.ppermute(value, 'fsdp', [(i, i ^ bit) for i in range(self.fsdp)])  56.3 us
    pallas_call x12, Pallas kernels, columns_product(): pl.pallas_call(body, grid=(width // tile,), in_specs=[whole(left.shape),...  51.2 us
    unnamed x222, local copies, waits for them, and re-layouts  40.4 us
    pallas_call x4, Pallas kernels, sum_of_products(): pl.pallas_call(body, grid=(rows // tile,), in_specs=[pl.BlockSpec((tile,...  34.9 us
    all_gather x3, waiting for transfers between devices, gather_ordered(): lax.all_gather(value, 'fsdp', axis=0, tiled=True, axis_index_groups=self....  33.5 us
    pallas_call x4, Pallas kernels, ffn_call(): pl.pallas_call(body, grid=(rows // tile,), in_specs=[pl.BlockSpec((tile,...  26.3 us
    convert_element_type x15, other arithmetic, low(): return value.astype(jnp.bfloat16)  21.1 us
  transfers between devices with their start and end apart: 70, of which 43 were waited for; matrix products, arithmetic and copies ran while one was open for 18% of the time, Pallas kernels for 20%

profile of v3, /device:TPU:0, one launch (start us, length us, event | category | flops | bytes accessed | tf_op | source)
XLA Modules:
  0.0 557.2 jit_solution(3722241952935829901)
XLA Ops:
  7.3 2.4 pad_maximum_fusion.5
  9.7 3.0 collective-permute-start.1
  16.1 2.6 pad_maximum_fusion.4
  18.7 2.7 collective-permute-start.3
  24.0 2.8 collective-permute-done.4
  26.8 2.7 collective-permute-start.5
  34.2 3.3 collective-permute-done.8
  43.2 10.1 %collective-permute-done.10 = bf16[1,2,4,2,128]{4,3,2,1,0:T(2,128)(2,1)S(1)} collective-permute-done((bf16[1,2,4,2,128]{4,3,2,1,0:T(2,128)(2,1)S(1)}, bf16[1,2,4,2,128]{4,3,2,1,0:T(2,128)(2,1)S(1)}, u32[]{:S(2)}, u32[]{:S(2)}) %collective-permute-start.10) | collective-permute-done | bytes 4128 | tf_op jit(solution)/shard_map/ppermute | solution.py:209
  59.8 3.1 fusion.2.right_ref
  62.9 20.0 %collective-permute-done.14 = bf16[256,2048]{1,0:T(8,128)(2,1)S(1)} collective-permute-done((bf16[256,2048]{1,0:T(8,128)(2,1)S(1)}, bf16[256,2048]{1,0:T(8,128)(2,1)S(1)}, u32[]{:S(2)}, u32[]{:S(2)}) %collective-permute-start.14) | collective-permute-done | bytes 1048608 | tf_op jit(solution)/shard_map/ppermute | solution.py:209
  83.2 10.6 %all-gather.4.cloned.1.call-done = bf16[1024,2048]{1,0:T(8,128)(2,1)} async-done(((bf16[256,2048]{1,0:T(8,128)(2,1)}), bf16[1024,2048]{1,0:T(8,128)(2,1)}) %all-gather.4.cloned.1.call-update) | async-done | bytes 4194320 | tf_op jit(solution)/shard_map/all_gather | solution.py:234
  94.1 2.3 slice.492
  101.6 3.4 fusion.32
  107.0 3.5 fusion.24
  110.5 2.7 slice.497
  113.6 3.4 fusion.33
  118.9 2.7 collective-permute-start.16
  127.8 3.1 shard_map.186
  130.9 4.0 collective-permute-done.17
  142.8 10.8 %collective-permute-done.22 = bf16[128,2048]{1,0:T(8,128)(2,1)S(1)} collective-permute-done((bf16[128,2048]{1,0:T(8,128)(2,1)S(1)}, bf16[128,2048]{1,0:T(8,128)(2,1)S(1)}, u32[]{:S(2)}, u32[]{:S(2)}) %collective-permute-start.22) | collective-permute-done | bytes 524320 | tf_op jit(solution)/shard_map/ppermute | solution.py:209
  156.6 8.2 %collective-permute-done.20 = bf16[128,2048]{1,0:T(8,128)(2,1)S(1)} collective-permute-done((bf16[128,2048]{1,0:T(8,128)(2,1)S(1)}, bf16[128,2048]{1,0:T(8,128)(2,1)S(1)}, u32[]{:S(2)}, u32[]{:S(2)}) %collective-permute-start.20) | collective-permute-done | bytes 524320 | tf_op jit(solution)/shard_map/ppermute | solution.py:209
  166.2 8.2 %collective-permute-done.23 = bf16[128,2048]{1,0:T(8,128)(2,1)S(1)} collective-permute-done((bf16[128,2048]{1,0:T(8,128)(2,1)S(1)}, bf16[128,2048]{1,0:T(8,128)(2,1)S(1)}, u32[]{:S(2)}, u32[]{:S(2)}) %collective-permute-start.23) | collective-permute-done | bytes 524320 | tf_op jit(solution)/shard_map/ppermute | solution.py:209
  178.3 22.9 %all-gather.6.cloned.1.call-done = bf16[1408,2048]{1,0:T(8,128)(2,1)} async-done(((bf16[352,2048]{1,0:T(8,128)(2,1)}), bf16[1408,2048]{1,0:T(8,128)(2,1)}) %all-gather.6.cloned.1.call-update) | async-done | bytes 5767184 | tf_op jit(solution)/shard_map/all_gather | solution.py:234
  207.0 11.5 %collective-permute-done.27 = bf16[128,2048]{1,0:T(8,128)(2,1)S(1)} collective-permute-done((bf16[128,2048]{1,0:T(8,128)(2,1)}, bf16[128,2048]{1,0:T(8,128)(2,1)S(1)}, u32[]{:S(2)}, u32[]{:S(2)}) %collective-permute-start.27) | collective-permute-done | bytes 524320 | tf_op jit(solution)/shard_map/ppermute | solution.py:209
  223.8 7.8 %shard_map.187 = (bf16[1024,704]{1,0:T(8,128)(2,1)S(1)}, bf16[1024,704]{1,0:T(8,128)(2,1)S(1)}, bf16[1024,704]{1,0:T(8,128)(2,1)S(1)}) custom-call(bf16[1024,2048]{1,0:T(8,128)(2,1)S(1)} %constant_dynamic-update-slice_fusion.10.normed_ref.right_ref, bf16[704,2048]{1,0:T(8,128)(2,1)S(1)} %bitcast.159, bf16[704,2048]{1,0:T(8,128)(2,1)S(1)} %bitcast.157), custom_call_target="tpu_custom_call" | custom-call | flops 1 | bytes 1 | tf_op jit(solution)/shard_map/pallas_call | solution.py:146
  232.7 4.8 fusion.21
  237.6 7.8 %shard_map.188 = (bf16[1024,704]{1,0:T(8,128)(2,1)S(1)}, bf16[1024,704]{1,0:T(8,128)(2,1)S(1)}, bf16[1024,704]{1,0:T(8,128)(2,1)S(1)}) custom-call(bf16[1024,2048]{1,0:T(8,128)(2,1)S(1)} %constant_dynamic-update-slice_fusion.10.normed_ref.right_ref, bf16[704,2048]{1,0:T(8,128)(2,1)S(1)} %bitcast.163, bf16[704,2048]{1,0:T(8,128)(2,1)S(1)} %bitcast.161), custom_call_target="tpu_custom_call" | custom-call | flops 1 | bytes 1 | tf_op jit(solution)/shard_map/pallas_call | solution.py:146
  247.7 4.3 shard_map.189
  252.1 5.3 collective-permute-done.30.refs_0_
  257.4 5.3 shard_map.190
  270.5 4.2 shard_map.191
  274.7 6.6 %shard_map.192 = (bf16[1024,704]{1,0:T(8,128)(2,1)S(1)}, bf16[1024,704]{1,0:T(8,128)(2,1)S(1)}) custom-call(bf16[1024,2048]{1,0:T(8,128)(2,1)S(1)} %copy-done.6, bf16[704,2048]{1,0:T(8,128)(2,1)} %collective-permute-done.31.down_ref.refs_3_, bf16[1024,704]{1,0:T(8,128)(2,1)S(1)} %copy-done.50, bf16[1024,704]{1,0:T(8,128)(2,1)S(1)} %copy-done.52), custom_call_target="tpu_custom_call" | custom-call | flops 1 | bytes 1 | tf_op jit(solution)/shard_map/pallas_call | solution.py:146
  281.4 14.6 %shard_map.193 = bf16[1024,2048]{1,0:T(8,128)(2,1)S(1)} custom-call(bf16[1024,704]{1,0:T(8,128)(2,1)S(1)} %get-tuple-element.314.refs_0_.left_ref, bf16[1024,704]{1,0:T(8,128)(2,1)S(1)} %get-tuple-element.311.refs_1_.left_ref, bf16[1024,704]{1,0:T(8,128)(2,1)S(1)} %get-tuple-element.324.refs_2_.left_ref, ...), custom_call_target="tpu_custom_call" | custom-call | flops 1 | bytes 1 | tf_op jit(solution)/shard_map/pallas_call | solution.py:77
  296.1 4.3 shard_map.194
  305.8 5.3 shard_map.195
  311.1 5.3 collective-permute-done.35
  317.5 2.6 add_convert_fusion.6
  320.0 2.2 copy-done.2
  322.2 5.0 shard_map.196
  332.9 2.2 copy-done.3
  335.1 6.5 %shard_map.197 = bf16[704,2048]{1,0:T(8,128)(2,1)} custom-call(bf16[1024,704]{1,0:T(8,128)(2,1)S(1)} %copy-done.24, bf16[1024,2048]{1,0:T(8,128)(2,1)S(1)} %copy-done.3, bf16[704,2048]{1,0:T(8,128)(2,1)} %collective-permute-done.39.refs_0_), custom_call_target="tpu_custom_call" | custom-call | flops 1 | bytes 1 | tf_op jit(solution)/shard_map/pallas_call | solution.py:128
  343.2 10.6 %collective-permute-done.37 = bf16[128,2048]{1,0:T(8,128)(2,1)} collective-permute-done((bf16[128,2048]{1,0:T(8,128)(2,1)}, bf16[128,2048]{1,0:T(8,128)(2,1)}, u32[]{:S(2)}, u32[]{:S(2)}) %collective-permute-start.37) | collective-permute-done | bytes 524320 | tf_op jit(solution)/shard_map/ppermute | solution.py:209
  358.2 2.4 multiply_reduce_fusion
  365.6 9.2 %shard_map.198 = bf16[1024,2048]{1,0:T(8,128)(2,1)S(1)} custom-call(bf16[1024,704]{1,0:T(8,128)(2,1)S(1)} %copy-done.20, bf16[1024,704]{1,0:T(8,128)(2,1)S(1)} %copy-done.22, bf16[704,2048]{1,0:T(8,128)(2,1)S(1)} %copy-done.17, bf16[704,2048]{1,0:T(8,128)(2,1)} %collective-permute-done.31.down_ref.refs_3_), custom_call_target="tpu_custom_call" | custom-call | flops 1 | bytes 1 | tf_op jit(solution)/shard_map/pallas_call | solution.py:77
  376.9 10.3 %collective-permute-done.41 = bf16[256,2048]{1,0:T(8,128)(2,1)S(1)} collective-permute-done((bf16[256,2048]{1,0:T(8,128)(2,1)S(1)}, bf16[256,2048]{1,0:T(8,128)(2,1)S(1)}, u32[]{:S(2)}, u32[]{:S(2)}) %collective-permute-start.41) | collective-permute-done | bytes 1048608 | tf_op jit(solution)/shard_map/ppermute | solution.py:209
  395.5 9.2 %collective-permute-done.44 = bf16[128,2048]{1,0:T(8,128)(2,1)} collective-permute-done((bf16[128,2048]{1,0:T(8,128)(2,1)}, bf16[128,2048]{1,0:T(8,128)(2,1)}, u32[]{:S(2)}, u32[]{:S(2)}) %collective-permute-start.44) | collective-permute-done | bytes 524320 | tf_op jit(solution)/shard_map/ppermute | solution.py:209
  421.4 2.3 shard_map.199
  423.7 3.2 shard_map.200
  430.5 4.2 shard_map.201
  438.1 4.5 collective-permute-done.48.refs_0_
  443.5 2.2 copy-done.29
  446.9 2.4 shard_map.202
  449.4 3.8 shard_map.203
  453.2 8.6 %collective-permute-done.46 = bf16[256,2048]{1,0:T(8,128)(2,1)} collective-permute-done((bf16[256,2048]{1,0:T(8,128)(2,1)}, bf16[256,2048]{1,0:T(8,128)(2,1)}, u32[]{:S(2)}, u32[]{:S(2)}) %collective-permute-start.46) | collective-permute-done | bytes 1048608 | tf_op jit(solution)/shard_map/ppermute | solution.py:209
  462.0 4.7 shard_map.204
  467.1 2.4 copy.44
  474.8 4.3 add_convert_fusion.1
  479.3 7.9 %shard_map.205 = bf16[1024,2048]{1,0:T(8,128)(2,1)S(1)} custom-call(bf16[1024,256]{1,0:T(8,128)(2,1)S(1)} %bitcast.180, bf16[1024,256]{1,0:T(8,128)(2,1)S(1)} %bitcast.178, bf16[1024,512]{1,0:T(8,128)(2,1)S(1)} %pad_maximum_fusion.8.left_ref.refs_2_, bf16[1024,512]{1,0:T(8,128)(2,1)S(1)} %copy-done.36, bf16[256,2048]{1,0:T(8,128)(2,1)S(1)} %bitcast.171, ...), custom_call_target="tpu_custom_call" | custom-call | flops 1 | bytes 1 | tf_op jit(solution)/shard_map/pallas_call | solution.py:77
  493.9 9.4 %collective-permute-done.55 = bf16[128,2048]{1,0:T(8,128)(2,1)S(1)} collective-permute-done((bf16[128,2048]{1,0:T(8,128)(2,1)S(1)}, bf16[128,2048]{1,0:T(8,128)(2,1)S(1)}, u32[]{:S(2)}, u32[]{:S(2)}) %collective-permute-start.55) | collective-permute-done | bytes 524320 | tf_op jit(solution)/shard_map/ppermute | solution.py:209
  509.4 6.5 %collective-permute-done.59 = f32[3,2048]{1,0:T(4,128)S(1)} collective-permute-done((f32[3,2048]{1,0:T(4,128)S(1)}, f32[3,2048]{1,0:T(4,128)S(1)}, u32[]{:S(2)}, u32[]{:S(2)}) %collective-permute-start.59) | collective-permute-done | bytes 24608 | tf_op jit(solution)/shard_map/ppermute | solution.py:209
  517.2 5.7 %collective-permute-done.60 = f32[3,2048]{1,0:T(4,128)S(1)} collective-permute-done((f32[3,2048]{1,0:T(4,128)S(1)}, f32[3,2048]{1,0:T(4,128)S(1)}, u32[]{:S(2)}, u32[]{:S(2)}) %collective-permute-start.60) | collective-permute-done | bytes 24608 | tf_op jit(solution)/shard_map/ppermute | solution.py:209
  522.9 2.4 collective-permute-done.56
  536.1 2.3 collective-permute-done.62
  539.0 6.8 %reduce-scatter.11.cloned.1.call-done = bf16[256,2048]{1,0:T(8,128)(2,1)} async-done(((bf16[1024,2048]{1,0:T(8,128)(2,1)}), bf16[256,2048]{1,0:T(8,128)(2,1)}) %reduce-scatter.11.cloned.1.call-update) | async-done | bytes 1048592 | tf_op jit(solution)/shard_map/reduce_scatter | solution.py:239
  (473 shorter events, 172.0 us)
Async XLA Ops:
  7.2 86.6 %all-gather.4.cloned.1.call-start = ((), (), s32[]{:S(2)}) async-start(), calls=%async_computation.4 | async-start | bytes 5242880 | tf_op jit(solution)/shard_map/all_gather | solution.py:234
  9.7 191.5 %all-gather.6.cloned.1.call-start = ((), (), s32[]{:S(2)}) async-start(), calls=%async_computation.5 | async-start | bytes 7208960 | tf_op jit(solution)/shard_map/all_gather | solution.py:234
  9.7 27.7 %collective-permute-start.1 = (bf16[256,2048]{1,0:T(8,128)(2,1)S(1)}, bf16[256,2048]{1,0:T(8,128)(2,1)S(1)}, u32[]{:S(2)}, u32[]{:S(2)}) collective-permute-start(bf16[256,2048]{1,0:T(8,128)(2,1)S(1)} %bitcast.191), channel_id=1, source_target_pairs={{0,4},{2,6},{4,0},{6,2},{8,12},{10,14},{12,8},{14,10},{16,20},{18,... | collective-permute-start | bytes 3145736 | tf_op jit(solution)/shard_map/ppermute | solution.py:209
  12.8 25.5 %collective-permute-start = (bf16[256,2048]{1,0:T(8,128)(2,1)S(1)}, bf16[256,2048]{1,0:T(8,128)(2,1)S(1)}, u32[]{:S(2)}, u32[]{:S(2)}) collective-permute-start(bf16[256,2048]{1,0:T(8,128)(2,1)S(1)} %bitcast.192), channel_id=1, source_target_pairs={{0,2},{2,0},{4,6},{6,4},{8,10},{10,8},{12,14},{14,12},{16,18},{18,... | collective-permute-start | bytes 3145736 | tf_op jit(solution)/shard_map/ppermute | solution.py:209
  18.7 4.5 collective-permute-start.3
  26.8 4.6 collective-permute-start.5
  31.4 6.0 %collective-permute-start.8 = (bf16[1,4,2,128]{3,2,1,0:T(2,128)(2,1)S(1)}, bf16[1,4,2,128]{3,2,1,0:T(2,128)(2,1)S(1)}, u32[]{:S(2)}, u32[]{:S(2)}) collective-permute-start(bf16[1,4,2,128]{3,2,1,0:T(2,128)(2,1)S(1)} %fusion.45), channel_id=1, source_target_pairs={{0,2},{2,0},{4,6},{6,4},{8,10},{10,8},{12,14},{14,12},{16,18},{18,... | collective-permute-start | bytes 6152 | tf_op jit(solution)/shard_map/ppermute | solution.py:209
  32.9 8.3 %collective-permute-start.9 = (f32[1,2,2,128]{3,2,1,0:T(2,128)S(1)}, f32[1,2,2,128]{3,2,1,0:T(2,128)S(1)}, u32[]{:S(2)}, u32[]{:S(2)}) collective-permute-start(f32[1,2,2,128]{3,2,1,0:T(2,128)S(1)} %maximum_bitcast_fusion.2), channel_id=1, source_target_pairs={{0,2},{2,0},{4,6},{6,4},{8,10},{10,8},{12,14},{14,12},{16,18},{18,... | collective-permute-start | bytes 6152 | tf_op jit(solution)/shard_map/ppermute | solution.py:209
  39.1 14.8 %collective-permute-start.6 = (bf16[128,2048]{1,0:T(8,128)(2,1)}, bf16[128,2048]{1,0:T(8,128)(2,1)}, u32[]{:S(2)}, u32[]{:S(2)}) collective-permute-start(bf16[128,2048]{1,0:T(8,128)(2,1)} %slice.489), channel_id=1, source_target_pairs={{0,2},{2,0},{4,6},{6,4},{8,10},{10,8},{12,14},{14,12},{16,18},{18,... | collective-permute-start | bytes 1572872 | tf_op jit(solution)/shard_map/ppermute | solution.py:209
  40.6 13.4 %collective-permute-start.7 = (bf16[128,2048]{1,0:T(8,128)(2,1)}, bf16[128,2048]{1,0:T(8,128)(2,1)}, u32[]{:S(2)}, u32[]{:S(2)}) collective-permute-start(bf16[128,2048]{1,0:T(8,128)(2,1)} %slice.490), channel_id=1, source_target_pairs={{0,4},{2,6},{4,0},{6,2},{8,12},{10,14},{12,8},{14,10},{16,20},{18,... | collective-permute-start | bytes 1572872 | tf_op jit(solution)/shard_map/ppermute | solution.py:209
  41.1 12.2 %collective-permute-start.10 = (bf16[1,2,4,2,128]{4,3,2,1,0:T(2,128)(2,1)S(1)}, bf16[1,2,4,2,128]{4,3,2,1,0:T(2,128)(2,1)S(1)}, u32[]{:S(2)}, u32[]{:S(2)}) collective-permute-start(bf16[1,2,4,2,128]{4,3,2,1,0:T(2,128)(2,1)S(1)} %fusion.44), channel_id=1, source_target_pairs={{0,4},{2,6},{4,0},{6,2},{8,12},{10,14},{12,8},{14,10},{16,20},{18,... | collective-permute-start | bytes 12296 | tf_op jit(solution)/shard_map/ppermute | solution.py:209
  42.7 11.2 %collective-permute-start.11 = (f32[1,2,2,2,128]{4,3,2,1,0:T(2,128)S(1)}, f32[1,2,2,2,128]{4,3,2,1,0:T(2,128)S(1)}, u32[]{:S(2)}, u32[]{:S(2)}) collective-permute-start(f32[1,2,2,2,128]{4,3,2,1,0:T(2,128)S(1)} %fusion.17), channel_id=1, source_target_pairs={{0,4},{2,6},{4,0},{6,2},{8,12},{10,14},{12,8},{14,10},{16,20},{18,... | collective-permute-start | bytes 12296 | tf_op jit(solution)/shard_map/ppermute | solution.py:209
  57.7 25.2 %collective-permute-start.14 = (bf16[256,2048]{1,0:T(8,128)(2,1)S(1)}, bf16[256,2048]{1,0:T(8,128)(2,1)S(1)}, u32[]{:S(2)}, u32[]{:S(2)}) collective-permute-start(bf16[256,2048]{1,0:T(8,128)(2,1)S(1)} %bitcast.200), channel_id=1, source_target_pairs={{0,4},{2,6},{4,0},{6,2},{8,12},{10,14},{12,8},{14,10},{16,20},{18,... | collective-permute-start | bytes 3145736 | tf_op jit(solution)/shard_map/ppermute | solution.py:209
  58.3 25.0 %collective-permute-start.13 = (bf16[256,2048]{1,0:T(8,128)(2,1)S(1)}, bf16[256,2048]{1,0:T(8,128)(2,1)S(1)}, u32[]{:S(2)}, u32[]{:S(2)}) collective-permute-start(bf16[256,2048]{1,0:T(8,128)(2,1)S(1)} %bitcast.201), channel_id=1, source_target_pairs={{0,2},{2,0},{4,6},{6,4},{8,10},{10,8},{12,14},{14,12},{16,18},{18,... | collective-permute-start | bytes 3145736 | tf_op jit(solution)/shard_map/ppermute | solution.py:209
  93.8 13.1 %collective-permute-start.15 = (bf16[1024,2048]{1,0:T(8,128)(2,1)}, bf16[1024,2048]{1,0:T(8,128)(2,1)}, u32[]{:S(2)}, u32[]{:S(2)}) collective-permute-start(bf16[1024,2048]{1,0:T(8,128)(2,1)} %all-gather.4.cloned.1.call-done), channel_id=1, source_target_pairs={{0,1},{1,0},{2,3},{3,2},{4,5},{5,4},{6,7},{7,6},{8,9},{9,8},{10,11... | collective-permute-start | bytes 12582920 | tf_op jit(solution)/shard_map/ppermute | solution.py:213
  93.8 168.9 %all-gather.8.cloned.1.call-start = ((), (), s32[]{:S(2)}) async-start(), calls=%async_computation.6 | async-start | bytes 3604480 | tf_op jit(solution)/shard_map/all_gather | solution.py:234
  118.9 5.8 %collective-permute-start.16 = (f32[2,8,2,256]{3,2,1,0:T(2,128)S(1)}, f32[2,8,2,256]{3,2,1,0:T(2,128)S(1)}, u32[]{:S(2)}, u32[]{:S(2)}) collective-permute-start(f32[2,8,2,256]{3,2,1,0:T(2,128)S(1)} %pad_maximum_fusion.11), channel_id=1, source_target_pairs={{0,1},{2,3},{4,5},{6,7},{8,9},{10,11},{12,13},{14,15},{16,17},{18,... | collective-permute-start | bytes 98312 | tf_op jit(solution)/shard_map/ppermute | solution.py:216
  121.7 13.3 %collective-permute-start.17 = (bf16[128,2048]{1,0:T(8,128)(2,1)S(1)}, bf16[128,2048]{1,0:T(8,128)(2,1)S(1)}, u32[]{:S(2)}, u32[]{:S(2)}) collective-permute-start(bf16[128,2048]{1,0:T(8,128)(2,1)S(1)} %slice.514), channel_id=1, source_target_pairs={{0,2},{2,0},{4,6},{6,4},{8,10},{10,8},{12,14},{14,12},{16,18},{18,... | collective-permute-start | bytes 1572872 | tf_op jit(solution)/shard_map/ppermute | solution.py:209
  123.2 12.9 %collective-permute-start.18 = (bf16[128,2048]{1,0:T(8,128)(2,1)S(1)}, bf16[128,2048]{1,0:T(8,128)(2,1)S(1)}, u32[]{:S(2)}, u32[]{:S(2)}) collective-permute-start(bf16[128,2048]{1,0:T(8,128)(2,1)S(1)} %slice.515), channel_id=1, source_target_pairs={{0,4},{2,6},{4,0},{6,2},{8,12},{10,14},{12,8},{14,10},{16,20},{18,... | collective-permute-start | bytes 1572872 | tf_op jit(solution)/shard_map/ppermute | solution.py:209
  138.6 14.9 %collective-permute-start.22 = (bf16[128,2048]{1,0:T(8,128)(2,1)S(1)}, bf16[128,2048]{1,0:T(8,128)(2,1)S(1)}, u32[]{:S(2)}, u32[]{:S(2)}) collective-permute-start(bf16[128,2048]{1,0:T(8,128)(2,1)S(1)} %get-tuple-element.468), channel_id=1, source_target_pairs={{0,4},{2,6},{4,0},{6,2},{8,12},{10,14},{12,8},{14,10},{16,20},{18,... | collective-permute-start | bytes 1572872 | tf_op jit(solution)/shard_map/ppermute | solution.py:209
  140.1 14.9 %collective-permute-start.21 = (bf16[128,2048]{1,0:T(8,128)(2,1)S(1)}, bf16[128,2048]{1,0:T(8,128)(2,1)S(1)}, u32[]{:S(2)}, u32[]{:S(2)}) collective-permute-start(bf16[128,2048]{1,0:T(8,128)(2,1)S(1)} %get-tuple-element.469), channel_id=1, source_target_pairs={{0,2},{2,0},{4,6},{6,4},{8,10},{10,8},{12,14},{14,12},{16,18},{18,... | collective-permute-start | bytes 1572872 | tf_op jit(solution)/shard_map/ppermute | solution.py:209
  140.7 24.1 %collective-permute-start.20 = (bf16[128,2048]{1,0:T(8,128)(2,1)S(1)}, bf16[128,2048]{1,0:T(8,128)(2,1)S(1)}, u32[]{:S(2)}, u32[]{:S(2)}) collective-permute-start(bf16[128,2048]{1,0:T(8,128)(2,1)S(1)} %get-tuple-element.470), channel_id=1, source_target_pairs={{0,4},{2,6},{4,0},{6,2},{8,12},{10,14},{12,8},{14,10},{16,20},{18,... | collective-permute-start | bytes 1572872 | tf_op jit(solution)/shard_map/ppermute | solution.py:209
  141.3 24.9 %collective-permute-start.19 = (bf16[128,2048]{1,0:T(8,128)(2,1)S(1)}, bf16[128,2048]{1,0:T(8,128)(2,1)S(1)}, u32[]{:S(2)}, u32[]{:S(2)}) collective-permute-start(bf16[128,2048]{1,0:T(8,128)(2,1)S(1)} %get-tuple-element.471), channel_id=1, source_target_pairs={{0,2},{2,0},{4,6},{6,4},{8,10},{10,8},{12,14},{14,12},{16,18},{18,... | collective-permute-start | bytes 1572872 | tf_op jit(solution)/shard_map/ppermute | solution.py:209
  155.3 19.1 %collective-permute-start.23 = (bf16[128,2048]{1,0:T(8,128)(2,1)S(1)}, bf16[128,2048]{1,0:T(8,128)(2,1)S(1)}, u32[]{:S(2)}, u32[]{:S(2)}) collective-permute-start(bf16[128,2048]{1,0:T(8,128)(2,1)S(1)} %get-tuple-element.250), channel_id=1, source_target_pairs={{0,2},{2,0},{4,6},{6,4},{8,10},{10,8},{12,14},{14,12},{16,18},{18,... | collective-permute-start | bytes 1572872 | tf_op jit(solution)/shard_map/ppermute | solution.py:209
  156.0 18.4 %collective-permute-start.24 = (bf16[128,2048]{1,0:T(8,128)(2,1)S(1)}, bf16[128,2048]{1,0:T(8,128)(2,1)S(1)}, u32[]{:S(2)}, u32[]{:S(2)}) collective-permute-start(bf16[128,2048]{1,0:T(8,128)(2,1)S(1)} %get-tuple-element.251), channel_id=1, source_target_pairs={{0,4},{2,6},{4,0},{6,2},{8,12},{10,14},{12,8},{14,10},{16,20},{18,... | collective-permute-start | bytes 1572872 | tf_op jit(solution)/shard_map/ppermute | solution.py:209
  177.1 24.1 %collective-permute-start.26 = (bf16[256,2048]{1,0:T(8,128)(2,1)S(1)}, bf16[256,2048]{1,0:T(8,128)(2,1)S(1)}, u32[]{:S(2)}, u32[]{:S(2)}) collective-permute-start(bf16[256,2048]{1,0:T(8,128)(2,1)S(1)} %multiply_convert_fusion), channel_id=1, source_target_pairs={{0,4},{2,6},{4,0},{6,2},{8,12},{10,14},{12,8},{14,10},{16,20},{18,... | collective-permute-start | bytes 3145736 | tf_op jit(solution)/shard_map/ppermute | solution.py:209
  177.8 23.4 %collective-permute-start.25 = (bf16[256,2048]{1,0:T(8,128)(2,1)S(1)}, bf16[256,2048]{1,0:T(8,128)(2,1)}, u32[]{:S(2)}, u32[]{:S(2)}) collective-permute-start(bf16[256,2048]{1,0:T(8,128)(2,1)S(1)} %multiply_convert_fusion), channel_id=1, source_target_pairs={{0,2},{2,0},{4,6},{6,4},{8,10},{10,8},{12,14},{14,12},{16,18},{18,... | collective-permute-start | bytes 3145736 | tf_op jit(solution)/shard_map/ppermute | solution.py:209
  201.2 31.5 %collective-permute-start.29 = (bf16[1408,2048]{1,0:T(8,128)(2,1)}, bf16[1408,2048]{1,0:T(8,128)(2,1)}, u32[]{:S(2)}, u32[]{:S(2)}) collective-permute-start(bf16[1408,2048]{1,0:T(8,128)(2,1)} %all-gather.6.cloned.1.call-done), channel_id=1, source_target_pairs={{0,1},{1,0},{2,3},{3,2},{4,5},{5,4},{6,7},{7,6},{8,9},{9,8},{10,11... | collective-permute-start | bytes 17301512 | tf_op jit(solution)/shard_map/ppermute | solution.py:213
  204.0 14.5 %collective-permute-start.27 = (bf16[128,2048]{1,0:T(8,128)(2,1)}, bf16[128,2048]{1,0:T(8,128)(2,1)S(1)}, u32[]{:S(2)}, u32[]{:S(2)}) collective-permute-start(bf16[128,2048]{1,0:T(8,128)(2,1)} %slice.517), channel_id=1, source_target_pairs={{0,2},{2,0},{4,6},{6,4},{8,10},{10,8},{12,14},{14,12},{16,18},{18,... | collective-permute-start | bytes 1572872 | tf_op jit(solution)/shard_map/ppermute | solution.py:209
  205.4 14.3 %collective-permute-start.28 = (bf16[128,2048]{1,0:T(8,128)(2,1)}, bf16[128,2048]{1,0:T(8,128)(2,1)}, u32[]{:S(2)}, u32[]{:S(2)}) collective-permute-start(bf16[128,2048]{1,0:T(8,128)(2,1)} %slice.518), channel_id=1, source_target_pairs={{0,4},{2,6},{4,0},{6,2},{8,12},{10,14},{12,8},{14,10},{16,20},{18,... | collective-permute-start | bytes 1572872 | tf_op jit(solution)/shard_map/ppermute | solution.py:209
  206.9 150.5 %reduce-scatter.5.cloned.1.call-start = ((), (), s32[]{:S(2)}) async-start(), calls=%async_computation.7 | async-start | bytes 3604480 | tf_op jit(solution)/shard_map/reduce_scatter | solution.py:239
  252.0 5.3 collective-permute-start.30
  262.7 12.0 %collective-permute-start.31 = (bf16[704,2048]{1,0:T(8,128)(2,1)}, bf16[704,2048]{1,0:T(8,128)(2,1)}, u32[]{:S(2)}, u32[]{:S(2)}) collective-permute-start(bf16[704,2048]{1,0:T(8,128)(2,1)} %all-gather.8.cloned.1.call-done.down_ref.refs_2_), channel_id=1, source_target_pairs={{0,1},{1,0},{2,3},{3,2},{4,5},{5,4},{6,7},{7,6},{8,9},{9,8},{10,11... | collective-permute-start | bytes 8650760 | tf_op jit(solution)/shard_map/ppermute | solution.py:213
  262.8 180.7 %reduce-scatter.7.cloned.1.call-start = ((), (), s32[]{:S(2)}) async-start(), calls=%async_computation.8 | async-start | bytes 3604480 | tf_op jit(solution)/shard_map/reduce_scatter | solution.py:239
  300.4 5.4 collective-permute-start.36
  302.3 14.1 %collective-permute-start.35 = (bf16[128,2048]{1,0:T(8,128)(2,1)}, bf16[128,2048]{1,0:T(8,128)(2,1)S(1)}, u32[]{:S(2)}, u32[]{:S(2)}) collective-permute-start(bf16[128,2048]{1,0:T(8,128)(2,1)} %get-tuple-element.460), channel_id=1, source_target_pairs={{0,4},{2,6},{4,0},{6,2},{8,12},{10,14},{12,8},{14,10},{16,20},{18,... | collective-permute-start | bytes 1572872 | tf_op jit(solution)/shard_map/ppermute | solution.py:209
  303.7 13.8 %collective-permute-start.34 = (bf16[128,2048]{1,0:T(8,128)(2,1)}, bf16[128,2048]{1,0:T(8,128)(2,1)S(1)}, u32[]{:S(2)}, u32[]{:S(2)}) collective-permute-start(bf16[128,2048]{1,0:T(8,128)(2,1)} %get-tuple-element.461), channel_id=1, source_target_pairs={{0,2},{2,0},{4,6},{6,4},{8,10},{10,8},{12,14},{14,12},{16,18},{18,... | collective-permute-start | bytes 1572872 | tf_op jit(solution)/shard_map/ppermute | solution.py:209
  327.3 5.6 %collective-permute-start.39 = (bf16[704,2048]{1,0:T(8,128)(2,1)}, bf16[704,2048]{1,0:T(8,128)(2,1)}, u32[]{:S(2)}, u32[]{:S(2)}) collective-permute-start(bf16[704,2048]{1,0:T(8,128)(2,1)} %shard_map.196), channel_id=1, source_target_pairs={{0,1},{1,0},{2,3},{3,2},{4,5},{5,4},{6,7},{7,6},{8,9},{9,8},{10,11... | collective-permute-start | bytes 8650760 | tf_op jit(solution)/shard_map/ppermute | solution.py:213
  327.3 142.2 %reduce-scatter.9.cloned.1.call-start = ((), (), s32[]{:S(2)}) async-start(), calls=%async_computation.9 | async-start | bytes 3604480 | tf_op jit(solution)/shard_map/reduce_scatter | solution.py:239
  327.5 15.0 %collective-permute-start.33 = (bf16[128,2048]{1,0:T(8,128)(2,1)}, bf16[128,2048]{1,0:T(8,128)(2,1)S(1)}, u32[]{:S(2)}, u32[]{:S(2)}) collective-permute-start(bf16[128,2048]{1,0:T(8,128)(2,1)} %get-tuple-element.462), channel_id=1, source_target_pairs={{0,4},{2,6},{4,0},{6,2},{8,12},{10,14},{12,8},{14,10},{16,20},{18,... | collective-permute-start | bytes 1572872 | tf_op jit(solution)/shard_map/ppermute | solution.py:209
  328.2 15.0 %collective-permute-start.32 = (bf16[128,2048]{1,0:T(8,128)(2,1)}, bf16[128,2048]{1,0:T(8,128)(2,1)S(1)}, u32[]{:S(2)}, u32[]{:S(2)}) collective-permute-start(bf16[128,2048]{1,0:T(8,128)(2,1)} %get-tuple-element.463), channel_id=1, source_target_pairs={{0,2},{2,0},{4,6},{6,4},{8,10},{10,8},{12,14},{14,12},{16,18},{18,... | collective-permute-start | bytes 1572872 | tf_op jit(solution)/shard_map/ppermute | solution.py:209
  329.6 24.2 %collective-permute-start.37 = (bf16[128,2048]{1,0:T(8,128)(2,1)}, bf16[128,2048]{1,0:T(8,128)(2,1)}, u32[]{:S(2)}, u32[]{:S(2)}) collective-permute-start(bf16[128,2048]{1,0:T(8,128)(2,1)} %get-tuple-element.319), channel_id=1, source_target_pairs={{0,2},{2,0},{4,6},{6,4},{8,10},{10,8},{12,14},{14,12},{16,18},{18,... | collective-permute-start | bytes 1572872 | tf_op jit(solution)/shard_map/ppermute | solution.py:209
  330.3 23.6 %collective-permute-start.38 = (bf16[128,2048]{1,0:T(8,128)(2,1)}, bf16[128,2048]{1,0:T(8,128)(2,1)}, u32[]{:S(2)}, u32[]{:S(2)}) collective-permute-start(bf16[128,2048]{1,0:T(8,128)(2,1)} %get-tuple-element.320), channel_id=1, source_target_pairs={{0,4},{2,6},{4,0},{6,2},{8,12},{10,14},{12,8},{14,10},{16,20},{18,... | collective-permute-start | bytes 1572872 | tf_op jit(solution)/shard_map/ppermute | solution.py:209
  362.8 24.5 %collective-permute-start.41 = (bf16[256,2048]{1,0:T(8,128)(2,1)S(1)}, bf16[256,2048]{1,0:T(8,128)(2,1)S(1)}, u32[]{:S(2)}, u32[]{:S(2)}) collective-permute-start(bf16[256,2048]{1,0:T(8,128)(2,1)S(1)} %get-tuple-element.341), channel_id=1, source_target_pairs={{0,4},{2,6},{4,0},{6,2},{8,12},{10,14},{12,8},{14,10},{16,20},{18,... | collective-permute-start | bytes 3145736 | tf_op jit(solution)/shard_map/ppermute | solution.py:209
  364.2 24.2 %collective-permute-start.40 = (bf16[256,2048]{1,0:T(8,128)(2,1)S(1)}, bf16[256,2048]{1,0:T(8,128)(2,1)S(1)}, u32[]{:S(2)}, u32[]{:S(2)}) collective-permute-start(bf16[256,2048]{1,0:T(8,128)(2,1)S(1)} %get-tuple-element.341), channel_id=1, source_target_pairs={{0,2},{2,0},{4,6},{6,4},{8,10},{10,8},{12,14},{14,12},{16,18},{18,... | collective-permute-start | bytes 3145736 | tf_op jit(solution)/shard_map/ppermute | solution.py:209
  389.5 15.2 %collective-permute-start.44 = (bf16[128,2048]{1,0:T(8,128)(2,1)}, bf16[128,2048]{1,0:T(8,128)(2,1)}, u32[]{:S(2)}, u32[]{:S(2)}) collective-permute-start(bf16[128,2048]{1,0:T(8,128)(2,1)} %slice.523), channel_id=1, source_target_pairs={{0,2},{2,0},{4,6},{6,4},{8,10},{10,8},{12,14},{14,12},{16,18},{18,... | collective-permute-start | bytes 1572872 | tf_op jit(solution)/shard_map/ppermute | solution.py:209
  391.0 15.2 %collective-permute-start.45 = (bf16[128,2048]{1,0:T(8,128)(2,1)}, bf16[128,2048]{1,0:T(8,128)(2,1)}, u32[]{:S(2)}, u32[]{:S(2)}) collective-permute-start(bf16[128,2048]{1,0:T(8,128)(2,1)} %slice.524), channel_id=1, source_target_pairs={{0,4},{2,6},{4,0},{6,2},{8,12},{10,14},{12,8},{14,10},{16,20},{18,... | collective-permute-start | bytes 1572872 | tf_op jit(solution)/shard_map/ppermute | solution.py:209
  392.1 153.7 %reduce-scatter.11.cloned.1.call-start = ((), (), s32[]{:S(2)}) async-start(), calls=%async_computation.10 | async-start | bytes 5242880 | tf_op jit(solution)/shard_map/reduce_scatter | solution.py:239
  393.9 22.0 %collective-permute-start.43 = (bf16[128,2048]{1,0:T(8,128)(2,1)S(1)}, bf16[128,2048]{1,0:T(8,128)(2,1)S(1)}, u32[]{:S(2)}, u32[]{:S(2)}) collective-permute-start(bf16[128,2048]{1,0:T(8,128)(2,1)S(1)} %get-tuple-element.452), channel_id=1, source_target_pairs={{0,4},{2,6},{4,0},{6,2},{8,12},{10,14},{12,8},{14,10},{16,20},{18,... | collective-permute-start | bytes 1572872 | tf_op jit(solution)/shard_map/ppermute | solution.py:209
  394.9 21.0 %collective-permute-start.42 = (bf16[128,2048]{1,0:T(8,128)(2,1)S(1)}, bf16[128,2048]{1,0:T(8,128)(2,1)S(1)}, u32[]{:S(2)}, u32[]{:S(2)}) collective-permute-start(bf16[128,2048]{1,0:T(8,128)(2,1)S(1)} %get-tuple-element.453), channel_id=1, source_target_pairs={{0,2},{2,0},{4,6},{6,4},{8,10},{10,8},{12,14},{14,12},{16,18},{18,... | collective-permute-start | bytes 1572872 | tf_op jit(solution)/shard_map/ppermute | solution.py:209
  415.9 10.9 %collective-permute-start.49 = (f32[2,16,2,256]{3,2,1,0:T(2,128)S(1)}, f32[2,16,2,256]{3,2,1,0:T(2,128)S(1)}, u32[]{:S(2)}, u32[]{:S(2)}) collective-permute-start(f32[2,16,2,256]{3,2,1,0:T(2,128)S(1)} %pad_maximum_fusion.10), channel_id=1, source_target_pairs={{1,0},{3,2},{5,4},{7,6},{9,8},{11,10},{13,12},{15,14},{17,16},{19,... | collective-permute-start | bytes 196616 | tf_op jit(solution)/shard_map/ppermute | solution.py:219
  434.7 27.3 %collective-permute-start.50 = (bf16[512,2048]{1,0:T(8,128)(2,1)}, bf16[512,2048]{1,0:T(8,128)(2,1)}, u32[]{:S(2)}, u32[]{:S(2)}) collective-permute-start(bf16[512,2048]{1,0:T(8,128)(2,1)} %shard_map.201), channel_id=1, source_target_pairs={{0,1},{1,0},{2,3},{3,2},{4,5},{5,4},{6,7},{7,6},{8,9},{9,8},{10,11... | collective-permute-start | bytes 6291464 | tf_op jit(solution)/shard_map/ppermute | solution.py:213
  435.9 6.7 %collective-permute-start.48 = (bf16[256,2048]{1,0:T(8,128)(2,1)S(1)}, bf16[256,2048]{1,0:T(8,128)(2,1)S(1)}, u32[]{:S(2)}, u32[]{:S(2)}) collective-permute-start(bf16[256,2048]{1,0:T(8,128)(2,1)S(1)} %shard_map.199), channel_id=1, source_target_pairs={{0,1},{1,0},{2,3},{3,2},{4,5},{5,4},{6,7},{7,6},{8,9},{9,8},{10,11... | collective-permute-start | bytes 3145736 | tf_op jit(solution)/shard_map/ppermute | solution.py:213
  435.9 13.5 %collective-permute-start.51 = (bf16[256,2048]{1,0:T(8,128)(2,1)}, bf16[256,2048]{1,0:T(8,128)(2,1)}, u32[]{:S(2)}, u32[]{:S(2)}) collective-permute-start(bf16[256,2048]{1,0:T(8,128)(2,1)} %shard_map.200), channel_id=1, source_target_pairs={{0,1},{1,0},{2,3},{3,2},{4,5},{5,4},{6,7},{7,6},{8,9},{9,8},{10,11... | collective-permute-start | bytes 3145736 | tf_op jit(solution)/shard_map/ppermute | solution.py:213
  436.4 25.4 %collective-permute-start.46 = (bf16[256,2048]{1,0:T(8,128)(2,1)}, bf16[256,2048]{1,0:T(8,128)(2,1)}, u32[]{:S(2)}, u32[]{:S(2)}) collective-permute-start(bf16[256,2048]{1,0:T(8,128)(2,1)} %pad_maximum_fusion.7), channel_id=1, source_target_pairs={{0,2},{2,0},{4,6},{6,4},{8,10},{10,8},{12,14},{14,12},{16,18},{18,... | collective-permute-start | bytes 3145736 | tf_op jit(solution)/shard_map/ppermute | solution.py:209
  436.9 25.1 %collective-permute-start.47 = (bf16[256,2048]{1,0:T(8,128)(2,1)}, bf16[256,2048]{1,0:T(8,128)(2,1)}, u32[]{:S(2)}, u32[]{:S(2)}) collective-permute-start(bf16[256,2048]{1,0:T(8,128)(2,1)} %pad_maximum_fusion.6), channel_id=1, source_target_pairs={{0,4},{2,6},{4,0},{6,2},{8,12},{10,14},{12,8},{14,10},{16,20},{18,... | collective-permute-start | bytes 3145736 | tf_op jit(solution)/shard_map/ppermute | solution.py:209
  488.4 14.9 %collective-permute-start.55 = (bf16[128,2048]{1,0:T(8,128)(2,1)S(1)}, bf16[128,2048]{1,0:T(8,128)(2,1)S(1)}, u32[]{:S(2)}, u32[]{:S(2)}) collective-permute-start(bf16[128,2048]{1,0:T(8,128)(2,1)S(1)} %get-tuple-element.442), channel_id=1, source_target_pairs={{0,4},{2,6},{4,0},{6,2},{8,12},{10,14},{12,8},{14,10},{16,20},{18,... | collective-permute-start | bytes 1572872 | tf_op jit(solution)/shard_map/ppermute | solution.py:209
  489.8 14.9 %collective-permute-start.54 = (bf16[128,2048]{1,0:T(8,128)(2,1)S(1)}, bf16[128,2048]{1,0:T(8,128)(2,1)S(1)}, u32[]{:S(2)}, u32[]{:S(2)}) collective-permute-start(bf16[128,2048]{1,0:T(8,128)(2,1)S(1)} %get-tuple-element.443), channel_id=1, source_target_pairs={{0,2},{2,0},{4,6},{6,4},{8,10},{10,8},{12,14},{14,12},{16,18},{18,... | collective-permute-start | bytes 1572872 | tf_op jit(solution)/shard_map/ppermute | solution.py:209
  491.3 31.7 %collective-permute-start.53 = (bf16[128,2048]{1,0:T(8,128)(2,1)}, bf16[128,2048]{1,0:T(8,128)(2,1)S(1)}, u32[]{:S(2)}, u32[]{:S(2)}) collective-permute-start(bf16[128,2048]{1,0:T(8,128)(2,1)} %get-tuple-element.444), channel_id=1, source_target_pairs={{0,4},{2,6},{4,0},{6,2},{8,12},{10,14},{12,8},{14,10},{16,20},{18,... | collective-permute-start | bytes 1572872 | tf_op jit(solution)/shard_map/ppermute | solution.py:209
  492.0 30.9 %collective-permute-start.52 = (bf16[128,2048]{1,0:T(8,128)(2,1)}, bf16[128,2048]{1,0:T(8,128)(2,1)S(1)}, u32[]{:S(2)}, u32[]{:S(2)}) collective-permute-start(bf16[128,2048]{1,0:T(8,128)(2,1)} %get-tuple-element.445), channel_id=1, source_target_pairs={{0,2},{2,0},{4,6},{6,4},{8,10},{10,8},{12,14},{14,12},{16,18},{18,... | collective-permute-start | bytes 1572872 | tf_op jit(solution)/shard_map/ppermute | solution.py:209
  505.8 19.5 %collective-permute-start.56 = (bf16[128,2048]{1,0:T(8,128)(2,1)}, bf16[128,2048]{1,0:T(8,128)(2,1)S(1)}, u32[]{:S(2)}, u32[]{:S(2)}) collective-permute-start(bf16[128,2048]{1,0:T(8,128)(2,1)} %get-tuple-element.397), channel_id=1, source_target_pairs={{0,2},{2,0},{4,6},{6,4},{8,10},{10,8},{12,14},{14,12},{16,18},{18,... | collective-permute-start | bytes 1572872 | tf_op jit(solution)/shard_map/ppermute | solution.py:209
  507.3 18.1 %collective-permute-start.57 = (bf16[128,2048]{1,0:T(8,128)(2,1)S(1)}, bf16[128,2048]{1,0:T(8,128)(2,1)S(1)}, u32[]{:S(2)}, u32[]{:S(2)}) collective-permute-start(bf16[128,2048]{1,0:T(8,128)(2,1)S(1)} %get-tuple-element.398), channel_id=1, source_target_pairs={{0,4},{2,6},{4,0},{6,2},{8,12},{10,14},{12,8},{14,10},{16,20},{18,... | collective-permute-start | bytes 1572872 | tf_op jit(solution)/shard_map/ppermute | solution.py:209
  509.3 6.6 %collective-permute-start.59 = (f32[3,2048]{1,0:T(4,128)S(1)}, f32[3,2048]{1,0:T(4,128)S(1)}, u32[]{:S(2)}, u32[]{:S(2)}) collective-permute-start(f32[3,2048]{1,0:T(4,128)S(1)} %add.230), channel_id=1, source_target_pairs={{0,8},{2,10},{4,12},{6,14},{8,0},{10,2},{12,4},{14,6},{16,24},{18,... | collective-permute-start | bytes 73736 | tf_op jit(solution)/shard_map/ppermute | solution.py:209
  515.9 7.0 %collective-permute-start.60 = (f32[3,2048]{1,0:T(4,128)S(1)}, f32[3,2048]{1,0:T(4,128)S(1)}, u32[]{:S(2)}, u32[]{:S(2)}) collective-permute-start(f32[3,2048]{1,0:T(4,128)S(1)} %add.231), channel_id=1, source_target_pairs={{0,16},{2,18},{4,20},{6,22},{8,24},{10,26},{12,28},{14,30},{16,0},... | collective-permute-start | bytes 73736 | tf_op jit(solution)/shard_map/ppermute | solution.py:209
  (109 other events, 716.1 us)
Sparse Core Ops, SparseCore 0:
  10.2 83.5 all-gather.3
  95.9 105.2 all-gather.5
  207.1 55.6 all-gather.7
  264.9 54.8 reduce-scatter.4
  327.4 53.7 reduce-scatter.6
  392.2 53.0 reduce-scatter.8
  469.6 76.0 reduce-scatter.10

commit v4 on v3

--- a/solution.py
+++ b/solution.py
@@ -37,6 +37,9 @@
 
 
 def sum_of_products(lefts, rights, tile=256):
+    rights = [right if isinstance(right, tuple) else (right, 0) for right in rights]
+    offsets = [right[1] for right in rights]
+    rights = [right[0] for right in rights]
     rows, width = lefts[0].shape[0], rights[0].shape[1]
     count = len(lefts)
     tile = min(tile, rows)
@@ -51,8 +54,12 @@
         left_refs, right_refs, out_ref = refs[:count], refs[count : 2 * count], refs[2 * count]
         side, stacked, sems = refs[2 * count + 1 :]
         copies = [
-            pltpu.make_async_copy(right, stacked.at[pl.ds(start, size)], sems.at[k])
-            for k, (right, start, size) in enumerate(zip(right_refs, starts, depths))
+            pltpu.make_async_copy(
+                right.at[pl.ds(offset, size)], stacked.at[pl.ds(start, size)], sems.at[k]
+            )
+            for k, (right, offset, start, size) in enumerate(
+                zip(right_refs, offsets, starts, depths)
+            )
         ]
 
         @pl.when(pl.program_id(0) == 0)
@@ -522,7 +529,7 @@
     grad_mixer = mixer_rows.end()
     order.did(grad_mixer)
 
-    many = 4 * rows * width * width
+    many = 10**11
     grad_now, mats_now = order(grad_mixer, out_mats)
     grad_mixed = [
         times_trans(grad_now, mat).reshape(segments, own_rows, -1) for mat in mats_now
@@ -560,10 +567,9 @@
     ]
     order.did(grad_cx)
     cx_got = core_terms(grad_cx, normed, many)
-    order.wait(gate_grad)
     b_total = own_term(grad_b[0], normed, b_got, many, False)
     out_total = own_term(mixed[0], grad_mixer, out_got, many, False)
-    order.wait(ffn_sums.summed)
+    order.wait(gate_grad)
     cx_total = own_term(grad_cx[0], normed, cx_got, many, False)
     mixer_total = (
         jnp.concatenate([b_total, cx_total, out_total], 0)
@@ -572,15 +578,14 @@
         .reshape(4 * wide_share, width)
     )
     order.did(mixer_total)
+    order.wait(ffn_sums.summed)
     order.wait(up_grad)
     mixer_grad = groups.reduce_ordered(order(mixer_total))
-    block_output = low(resid + ffn_sums.end())
-    order.did(block_output)
-    b_mats = [mat[:wide_share] for mat in in_mats]
-    cx_mats = [mat[wide_share:] for mat in in_mats]
-    back_one = sum_of_products(*order(grad_b + grad_cx, b_mats + cx_mats))
+    grads_now, mats_now = order(grad_b + grad_cx, in_mats)
+    cuts = [(mat, start) for start in (0, wide_share) for mat in mats_now]
+    back_one = sum_of_products(grads_now, cuts)
     order.did(back_one)
-    one_rows = Sums(groups, back_one)
+    one_rows = Sums(groups, back_one, True)
     back_now = order(back_one)
     norm_one_term = jnp.sum(high(back_now) * wide * scale_all, 0)
     conv_terms = [
@@ -599,6 +604,8 @@
     ]
     order.did(small)
     one_rows.middle()
+    block_output = low(resid + ffn_sums.end())
+    order.did(block_output)
     small = order(small)
     total = small[0]
     for j in range(1, tp):

time: 562 us -> 553 us (0.984)
  waiting for transfers between devices: 219 us -> 200 us
  other arithmetic: 53.2 us -> 58.9 us
    unnamed x222 -> x270, local copies, waits for them, and re-layouts: 40.4 us -> 48.8 us
    ppermute x50 -> x48, waiting for transfers between devices: 165 us -> 156 us  [swap(): return lax.ppermute(value, 'fsdp', [(i, i ^ bit) for i in range(self.fsdp)])]
    slice x6 -> x2, local copies, waits for them, and re-layouts: 9.91 us -> 3.4 us  [on_device(): out_mats.append(mat[3].reshape(wide_share, width))]
    ppermute x50 -> x48, starting transfers between devices: 56.3 us -> 55.1 us  [swap(): return lax.ppermute(value, 'fsdp', [(i, i ^ bit) for i in range(self.fsdp)])]
  transfers between devices with their start and end apart: 70 -> 68, of which waited for: 43 -> 42; matrix products, arithmetic and copies ran while one was open for 18% -> 19% of each run, Pallas kernels for 20% -> 21%
where the time goes in v4:
time: 553 us; the launch traced here: 543 us
  waiting for transfers between devices  200 us (36%)
  Pallas kernels  112 us (20%)
  local copies, waits for them, and re-layouts  83.2 us (15%)
  starting transfers between devices  62.8 us (11%)
  other arithmetic  58.9 us (11%)
  between operations  16.4 us (3%)
  matrix products  9.46 us (2%)
    ppermute x48, waiting for transfers between devices, swap(): return lax.ppermute(value, 'fsdp', [(i, i ^ bit) for i in range(self.fsdp)])  156 us
    ppermute x48, starting transfers between devices, swap(): return lax.ppermute(value, 'fsdp', [(i, i ^ bit) for i in range(self.fsdp)])  55.1 us
    pallas_call x12, Pallas kernels, columns_product(): pl.pallas_call(body, grid=(width // tile,), in_specs=[whole(left.shape),...  51 us
    unnamed x270, local copies, waits for them, and re-layouts  48.8 us
    pallas_call x4, Pallas kernels, sum_of_products(): pl.pallas_call(body, grid=(rows // tile,), in_specs=[pl.BlockSpec((tile,...  34.9 us
    all_gather x3, waiting for transfers between devices, gather_ordered(): lax.all_gather(value, 'fsdp', axis=0, tiled=True, axis_index_groups=self....  31.2 us
    pallas_call x4, Pallas kernels, ffn_call(): pl.pallas_call(body, grid=(rows // tile,), in_specs=[pl.BlockSpec((tile,...  26.3 us
    convert_element_type x15, other arithmetic, low(): return value.astype(jnp.bfloat16)  21.2 us
  transfers between devices with their start and end apart: 68, of which 42 were waited for; matrix products, arithmetic and copies ran while one was open for 19% of the time, Pallas kernels for 21%

profile of v4, /device:TPU:0, one launch (start us, length us, event | category | flops | bytes accessed | tf_op | source)
XLA Modules:
  0.0 542.7 jit_solution(12185476740376029173)
XLA Ops:
  7.3 2.4 pad_maximum_fusion.4
  9.7 3.0 collective-permute-start.1
  16.1 2.6 pad_maximum_fusion.3
  18.7 2.7 collective-permute-start.3
  24.0 2.8 collective-permute-done.4
  26.8 2.7 collective-permute-start.5
  34.2 3.3 collective-permute-done.8
  43.3 10.1 %collective-permute-done.10 = bf16[1,2,4,2,128]{4,3,2,1,0:T(2,128)(2,1)S(1)} collective-permute-done((bf16[1,2,4,2,128]{4,3,2,1,0:T(2,128)(2,1)S(1)}, bf16[1,2,4,2,128]{4,3,2,1,0:T(2,128)(2,1)S(1)}, u32[]{:S(2)}, u32[]{:S(2)}) %collective-permute-start.10) | collective-permute-done | bytes 4128 | tf_op jit(solution)/shard_map/ppermute | solution.py:216
  61.2 3.1 fusion.2.right_ref
  64.3 20.0 %collective-permute-done.14 = bf16[256,2048]{1,0:T(8,128)(2,1)S(1)} collective-permute-done((bf16[256,2048]{1,0:T(8,128)(2,1)S(1)}, bf16[256,2048]{1,0:T(8,128)(2,1)S(1)}, u32[]{:S(2)}, u32[]{:S(2)}) %collective-permute-start.14) | collective-permute-done | bytes 1048608 | tf_op jit(solution)/shard_map/ppermute | solution.py:216
  84.7 9.1 %all-gather.4.cloned.1.call-done = bf16[1024,2048]{1,0:T(8,128)(2,1)} async-done(((bf16[256,2048]{1,0:T(8,128)(2,1)}), bf16[1024,2048]{1,0:T(8,128)(2,1)}) %all-gather.4.cloned.1.call-update) | async-done | bytes 4194320 | tf_op jit(solution)/shard_map/all_gather | solution.py:241
  95.3 2.7 slice.451
  98.4 3.0 copy-done.38
  101.4 3.4 fusion.33
  108.9 2.7 slice.456
  112.0 3.4 fusion.34
  117.3 2.6 collective-permute-start.16
  127.3 3.1 shard_map.186
  130.5 4.0 collective-permute-done.17
  143.6 10.8 %collective-permute-done.22 = bf16[128,2048]{1,0:T(8,128)(2,1)S(1)} collective-permute-done((bf16[128,2048]{1,0:T(8,128)(2,1)S(1)}, bf16[128,2048]{1,0:T(8,128)(2,1)S(1)}, u32[]{:S(2)}, u32[]{:S(2)}) %collective-permute-start.22) | collective-permute-done | bytes 524320 | tf_op jit(solution)/shard_map/ppermute | solution.py:216
  157.5 8.2 %collective-permute-done.20 = bf16[128,2048]{1,0:T(8,128)(2,1)S(1)} collective-permute-done((bf16[128,2048]{1,0:T(8,128)(2,1)S(1)}, bf16[128,2048]{1,0:T(8,128)(2,1)S(1)}, u32[]{:S(2)}, u32[]{:S(2)}) %collective-permute-start.20) | collective-permute-done | bytes 524320 | tf_op jit(solution)/shard_map/ppermute | solution.py:216
  167.1 8.2 %collective-permute-done.23 = bf16[128,2048]{1,0:T(8,128)(2,1)S(1)} collective-permute-done((bf16[128,2048]{1,0:T(8,128)(2,1)S(1)}, bf16[128,2048]{1,0:T(8,128)(2,1)S(1)}, u32[]{:S(2)}, u32[]{:S(2)}) %collective-permute-start.23) | collective-permute-done | bytes 524320 | tf_op jit(solution)/shard_map/ppermute | solution.py:216
  179.3 21.9 %all-gather.6.cloned.1.call-done = bf16[1408,2048]{1,0:T(8,128)(2,1)} async-done(((bf16[352,2048]{1,0:T(8,128)(2,1)}), bf16[1408,2048]{1,0:T(8,128)(2,1)}) %all-gather.6.cloned.1.call-update) | async-done | bytes 5767184 | tf_op jit(solution)/shard_map/all_gather | solution.py:241
  205.9 11.6 %collective-permute-done.27 = bf16[128,2048]{1,0:T(8,128)(2,1)} collective-permute-done((bf16[128,2048]{1,0:T(8,128)(2,1)}, bf16[128,2048]{1,0:T(8,128)(2,1)}, u32[]{:S(2)}, u32[]{:S(2)}) %collective-permute-start.27) | collective-permute-done | bytes 524320 | tf_op jit(solution)/shard_map/ppermute | solution.py:216
  222.5 7.8 %shard_map.187 = (bf16[1024,704]{1,0:T(8,128)(2,1)S(1)}, bf16[1024,704]{1,0:T(8,128)(2,1)S(1)}, bf16[1024,704]{1,0:T(8,128)(2,1)S(1)}) custom-call(bf16[1024,2048]{1,0:T(8,128)(2,1)S(1)} %constant_dynamic-update-slice_fusion.10.normed_ref.right_ref, bf16[704,2048]{1,0:T(8,128)(2,1)S(1)} %bitcast.159, bf16[704,2048]{1,0:T(8,128)(2,1)S(1)} %bitcast.157), custom_call_target="tpu_custom_call" | custom-call | flops 1 | bytes 1 | tf_op jit(solution)/shard_map/pallas_call | solution.py:153
  231.5 4.8 fusion.24
  236.4 7.8 %shard_map.188 = (bf16[1024,704]{1,0:T(8,128)(2,1)S(1)}, bf16[1024,704]{1,0:T(8,128)(2,1)S(1)}, bf16[1024,704]{1,0:T(8,128)(2,1)S(1)}) custom-call(bf16[1024,2048]{1,0:T(8,128)(2,1)S(1)} %constant_dynamic-update-slice_fusion.10.normed_ref.right_ref, bf16[704,2048]{1,0:T(8,128)(2,1)S(1)} %bitcast.163, bf16[704,2048]{1,0:T(8,128)(2,1)S(1)} %bitcast.161), custom_call_target="tpu_custom_call" | custom-call | flops 1 | bytes 1 | tf_op jit(solution)/shard_map/pallas_call | solution.py:153
  246.6 4.3 shard_map.189
  250.9 5.3 collective-permute-done.30.refs_0_
  256.2 5.3 shard_map.190
  261.9 2.2 copy-done.6
  269.0 4.2 shard_map.191
  273.3 6.6 %shard_map.192 = (bf16[1024,704]{1,0:T(8,128)(2,1)S(1)}, bf16[1024,704]{1,0:T(8,128)(2,1)S(1)}) custom-call(bf16[1024,2048]{1,0:T(8,128)(2,1)S(1)} %copy-done.6, bf16[704,2048]{1,0:T(8,128)(2,1)} %collective-permute-done.31.down_ref.refs_3_, bf16[1024,704]{1,0:T(8,128)(2,1)S(1)} %copy-done.54, bf16[1024,704]{1,0:T(8,128)(2,1)S(1)} %copy-done.56), custom_call_target="tpu_custom_call" | custom-call | flops 1 | bytes 1 | tf_op jit(solution)/shard_map/pallas_call | solution.py:153
  279.9 14.6 %shard_map.193 = bf16[1024,2048]{1,0:T(8,128)(2,1)S(1)} custom-call(bf16[1024,704]{1,0:T(8,128)(2,1)S(1)} %get-tuple-element.310.refs_0_.left_ref, bf16[1024,704]{1,0:T(8,128)(2,1)S(1)} %get-tuple-element.307.refs_1_.left_ref, bf16[1024,704]{1,0:T(8,128)(2,1)S(1)} %get-tuple-element.320.refs_2_.left_ref, ...), custom_call_target="tpu_custom_call" | custom-call | flops 1 | bytes 1 | tf_op jit(solution)/shard_map/pallas_call | solution.py:84
  294.6 4.3 shard_map.194
  304.5 5.3 shard_map.195
  309.8 5.1 collective-permute-done.35
  315.7 2.6 add_convert_fusion.5
  318.3 2.2 copy-done.2
  320.5 5.0 shard_map.196
  331.2 2.2 copy-done.3
  333.4 6.5 %shard_map.197 = bf16[704,2048]{1,0:T(8,128)(2,1)} custom-call(bf16[1024,704]{1,0:T(8,128)(2,1)S(1)} %copy-done.27, bf16[1024,2048]{1,0:T(8,128)(2,1)S(1)} %copy-done.3, bf16[704,2048]{1,0:T(8,128)(2,1)} %collective-permute-done.39.refs_0_), custom_call_target="tpu_custom_call" | custom-call | flops 1 | bytes 1 | tf_op jit(solution)/shard_map/pallas_call | solution.py:135
  341.8 10.5 %collective-permute-done.37 = bf16[128,2048]{1,0:T(8,128)(2,1)S(1)} collective-permute-done((bf16[128,2048]{1,0:T(8,128)(2,1)}, bf16[128,2048]{1,0:T(8,128)(2,1)S(1)}, u32[]{:S(2)}, u32[]{:S(2)}) %collective-permute-start.37) | collective-permute-done | bytes 524320 | tf_op jit(solution)/shard_map/ppermute | solution.py:216
  356.6 2.9 multiply_reduce_fusion.1
  364.4 9.2 %shard_map.198 = bf16[1024,2048]{1,0:T(8,128)(2,1)S(1)} custom-call(bf16[1024,704]{1,0:T(8,128)(2,1)S(1)} %copy-done.23, bf16[1024,704]{1,0:T(8,128)(2,1)S(1)} %copy-done.25, bf16[704,2048]{1,0:T(8,128)(2,1)S(1)} %copy-done.21, bf16[704,2048]{1,0:T(8,128)(2,1)} %collective-permute-done.31.down_ref.refs_3_), custom_call_target="tpu_custom_call" | custom-call | flops 1 | bytes 1 | tf_op jit(solution)/shard_map/pallas_call | solution.py:84
  375.6 10.6 %collective-permute-done.41 = bf16[256,2048]{1,0:T(8,128)(2,1)S(1)} collective-permute-done((bf16[256,2048]{1,0:T(8,128)(2,1)S(1)}, bf16[256,2048]{1,0:T(8,128)(2,1)S(1)}, u32[]{:S(2)}, u32[]{:S(2)}) %collective-permute-start.41) | collective-permute-done | bytes 1048608 | tf_op jit(solution)/shard_map/ppermute | solution.py:216
  393.9 9.3 %collective-permute-done.44 = bf16[128,2048]{1,0:T(8,128)(2,1)} collective-permute-done((bf16[128,2048]{1,0:T(8,128)(2,1)}, bf16[128,2048]{1,0:T(8,128)(2,1)}, u32[]{:S(2)}, u32[]{:S(2)}) %collective-permute-start.44) | collective-permute-done | bytes 524320 | tf_op jit(solution)/shard_map/ppermute | solution.py:216
  420.8 2.3 shard_map.199
  423.1 3.1 shard_map.200
  435.9 4.2 shard_map.201
  440.1 2.4 shard_map.202
  442.5 3.6 shard_map.203
  446.2 2.2 copy-done.40
  448.4 4.7 shard_map.204
  453.5 2.4 copy.44
  464.6 7.9 %shard_map.205 = bf16[1024,2048]{1,0:T(8,128)(2,1)S(1)} custom-call(bf16[1024,256]{1,0:T(8,128)(2,1)S(1)} %bitcast.176, bf16[1024,256]{1,0:T(8,128)(2,1)S(1)} %bitcast.174, bf16[1024,512]{1,0:T(8,128)(2,1)S(1)} %copy-done.35, bf16[1024,512]{1,0:T(8,128)(2,1)S(1)} %copy-done.37, bf16[768,2048]{1,0:T(8,128)(2,1)S(1)} %bitcast.152, ...), custom_call_target="tpu_custom_call" | custom-call | flops 1 | bytes 1 | tf_op jit(solution)/shard_map/pallas_call | solution.py:84
  477.6 9.4 %collective-permute-done.53 = bf16[128,2048]{1,0:T(8,128)(2,1)S(1)} collective-permute-done((bf16[128,2048]{1,0:T(8,128)(2,1)S(1)}, bf16[128,2048]{1,0:T(8,128)(2,1)S(1)}, u32[]{:S(2)}, u32[]{:S(2)}) %collective-permute-start.53) | collective-permute-done | bytes 524320 | tf_op jit(solution)/shard_map/ppermute | solution.py:216
  493.0 3.5 add_convert_fusion
  497.8 4.9 collective-permute-done.57
  503.5 2.5 convert_element_type.291
  506.0 3.6 collective-permute-done.58
  509.6 5.5 %collective-permute-done.54 = bf16[256,2048]{1,0:T(8,128)(2,1)S(1)} collective-permute-done((bf16[256,2048]{1,0:T(8,128)(2,1)}, bf16[256,2048]{1,0:T(8,128)(2,1)S(1)}, u32[]{:S(2)}, u32[]{:S(2)}) %collective-permute-start.54) | collective-permute-done | bytes 1048608 | tf_op jit(solution)/shard_map/ppermute | solution.py:216
  518.3 3.2 fusion.8
  529.6 2.8 reduce-scatter.11.cloned.1.call-done
  (515 shorter events, 172.2 us)
Async XLA Ops:
  7.2 86.6 %all-gather.4.cloned.1.call-start = ((), (), s32[]{:S(2)}) async-start(), calls=%async_computation.4 | async-start | bytes 5242880 | tf_op jit(solution)/shard_map/all_gather | solution.py:241
  9.7 191.5 %all-gather.6.cloned.1.call-start = ((), (), s32[]{:S(2)}) async-start(), calls=%async_computation.5 | async-start | bytes 7208960 | tf_op jit(solution)/shard_map/all_gather | solution.py:241
  9.7 27.7 %collective-permute-start.1 = (bf16[256,2048]{1,0:T(8,128)(2,1)S(1)}, bf16[256,2048]{1,0:T(8,128)(2,1)S(1)}, u32[]{:S(2)}, u32[]{:S(2)}) collective-permute-start(bf16[256,2048]{1,0:T(8,128)(2,1)S(1)} %bitcast.185), channel_id=1, source_target_pairs={{0,4},{2,6},{4,0},{6,2},{8,12},{10,14},{12,8},{14,10},{16,20},{18,... | collective-permute-start | bytes 3145736 | tf_op jit(solution)/shard_map/ppermute | solution.py:216
  12.8 25.5 %collective-permute-start = (bf16[256,2048]{1,0:T(8,128)(2,1)S(1)}, bf16[256,2048]{1,0:T(8,128)(2,1)S(1)}, u32[]{:S(2)}, u32[]{:S(2)}) collective-permute-start(bf16[256,2048]{1,0:T(8,128)(2,1)S(1)} %bitcast.186), channel_id=1, source_target_pairs={{0,2},{2,0},{4,6},{6,4},{8,10},{10,8},{12,14},{14,12},{16,18},{18,... | collective-permute-start | bytes 3145736 | tf_op jit(solution)/shard_map/ppermute | solution.py:216
  14.3 4.4 collective-permute-start.2
  18.7 4.5 collective-permute-start.3
  26.8 4.6 collective-permute-start.5
  31.4 6.0 %collective-permute-start.8 = (bf16[1,4,2,128]{3,2,1,0:T(2,128)(2,1)S(1)}, bf16[1,4,2,128]{3,2,1,0:T(2,128)(2,1)S(1)}, u32[]{:S(2)}, u32[]{:S(2)}) collective-permute-start(bf16[1,4,2,128]{3,2,1,0:T(2,128)(2,1)S(1)} %fusion.46), channel_id=1, source_target_pairs={{0,2},{2,0},{4,6},{6,4},{8,10},{10,8},{12,14},{14,12},{16,18},{18,... | collective-permute-start | bytes 6152 | tf_op jit(solution)/shard_map/ppermute | solution.py:216
  32.9 8.3 %collective-permute-start.9 = (f32[1,2,2,128]{3,2,1,0:T(2,128)S(1)}, f32[1,2,2,128]{3,2,1,0:T(2,128)S(1)}, u32[]{:S(2)}, u32[]{:S(2)}) collective-permute-start(f32[1,2,2,128]{3,2,1,0:T(2,128)S(1)} %maximum_bitcast_fusion.2), channel_id=1, source_target_pairs={{0,2},{2,0},{4,6},{6,4},{8,10},{10,8},{12,14},{14,12},{16,18},{18,... | collective-permute-start | bytes 6152 | tf_op jit(solution)/shard_map/ppermute | solution.py:216
  39.2 14.8 %collective-permute-start.6 = (bf16[128,2048]{1,0:T(8,128)(2,1)}, bf16[128,2048]{1,0:T(8,128)(2,1)}, u32[]{:S(2)}, u32[]{:S(2)}) collective-permute-start(bf16[128,2048]{1,0:T(8,128)(2,1)} %slice.448), channel_id=1, source_target_pairs={{0,2},{2,0},{4,6},{6,4},{8,10},{10,8},{12,14},{14,12},{16,18},{18,... | collective-permute-start | bytes 1572872 | tf_op jit(solution)/shard_map/ppermute | solution.py:216
  40.7 13.4 %collective-permute-start.7 = (bf16[128,2048]{1,0:T(8,128)(2,1)}, bf16[128,2048]{1,0:T(8,128)(2,1)}, u32[]{:S(2)}, u32[]{:S(2)}) collective-permute-start(bf16[128,2048]{1,0:T(8,128)(2,1)} %slice.449), channel_id=1, source_target_pairs={{0,4},{2,6},{4,0},{6,2},{8,12},{10,14},{12,8},{14,10},{16,20},{18,... | collective-permute-start | bytes 1572872 | tf_op jit(solution)/shard_map/ppermute | solution.py:216
  41.2 12.2 %collective-permute-start.10 = (bf16[1,2,4,2,128]{4,3,2,1,0:T(2,128)(2,1)S(1)}, bf16[1,2,4,2,128]{4,3,2,1,0:T(2,128)(2,1)S(1)}, u32[]{:S(2)}, u32[]{:S(2)}) collective-permute-start(bf16[1,2,4,2,128]{4,3,2,1,0:T(2,128)(2,1)S(1)} %fusion.45), channel_id=1, source_target_pairs={{0,4},{2,6},{4,0},{6,2},{8,12},{10,14},{12,8},{14,10},{16,20},{18,... | collective-permute-start | bytes 12296 | tf_op jit(solution)/shard_map/ppermute | solution.py:216
  42.8 11.2 %collective-permute-start.11 = (f32[1,2,2,2,128]{4,3,2,1,0:T(2,128)S(1)}, f32[1,2,2,2,128]{4,3,2,1,0:T(2,128)S(1)}, u32[]{:S(2)}, u32[]{:S(2)}) collective-permute-start(f32[1,2,2,2,128]{4,3,2,1,0:T(2,128)S(1)} %fusion.20), channel_id=1, source_target_pairs={{0,4},{2,6},{4,0},{6,2},{8,12},{10,14},{12,8},{14,10},{16,20},{18,... | collective-permute-start | bytes 12296 | tf_op jit(solution)/shard_map/ppermute | solution.py:216
  59.0 25.2 %collective-permute-start.14 = (bf16[256,2048]{1,0:T(8,128)(2,1)S(1)}, bf16[256,2048]{1,0:T(8,128)(2,1)S(1)}, u32[]{:S(2)}, u32[]{:S(2)}) collective-permute-start(bf16[256,2048]{1,0:T(8,128)(2,1)S(1)} %bitcast.194), channel_id=1, source_target_pairs={{0,4},{2,6},{4,0},{6,2},{8,12},{10,14},{12,8},{14,10},{16,20},{18,... | collective-permute-start | bytes 3145736 | tf_op jit(solution)/shard_map/ppermute | solution.py:216
  59.6 25.1 %collective-permute-start.13 = (bf16[256,2048]{1,0:T(8,128)(2,1)S(1)}, bf16[256,2048]{1,0:T(8,128)(2,1)}, u32[]{:S(2)}, u32[]{:S(2)}) collective-permute-start(bf16[256,2048]{1,0:T(8,128)(2,1)S(1)} %bitcast.195), channel_id=1, source_target_pairs={{0,2},{2,0},{4,6},{6,4},{8,10},{10,8},{12,14},{14,12},{16,18},{18,... | collective-permute-start | bytes 3145736 | tf_op jit(solution)/shard_map/ppermute | solution.py:216
  93.8 13.0 %collective-permute-start.15 = (bf16[1024,2048]{1,0:T(8,128)(2,1)}, bf16[1024,2048]{1,0:T(8,128)(2,1)}, u32[]{:S(2)}, u32[]{:S(2)}) collective-permute-start(bf16[1024,2048]{1,0:T(8,128)(2,1)} %all-gather.4.cloned.1.call-done), channel_id=1, source_target_pairs={{0,1},{1,0},{2,3},{3,2},{4,5},{5,4},{6,7},{7,6},{8,9},{9,8},{10,11... | collective-permute-start | bytes 12582920 | tf_op jit(solution)/shard_map/ppermute | solution.py:220
  93.8 167.8 %all-gather.8.cloned.1.call-start = ((), (), s32[]{:S(2)}) async-start(), calls=%async_computation.6 | async-start | bytes 3604480 | tf_op jit(solution)/shard_map/all_gather | solution.py:241
  117.3 6.8 %collective-permute-start.16 = (f32[2,8,2,256]{3,2,1,0:T(2,128)S(1)}, f32[2,8,2,256]{3,2,1,0:T(2,128)S(1)}, u32[]{:S(2)}, u32[]{:S(2)}) collective-permute-start(f32[2,8,2,256]{3,2,1,0:T(2,128)S(1)} %pad_maximum_fusion.12), channel_id=1, source_target_pairs={{0,1},{2,3},{4,5},{6,7},{8,9},{10,11},{12,13},{14,15},{16,17},{18,... | collective-permute-start | bytes 98312 | tf_op jit(solution)/shard_map/ppermute | solution.py:223
  121.1 13.3 %collective-permute-start.17 = (bf16[128,2048]{1,0:T(8,128)(2,1)S(1)}, bf16[128,2048]{1,0:T(8,128)(2,1)S(1)}, u32[]{:S(2)}, u32[]{:S(2)}) collective-permute-start(bf16[128,2048]{1,0:T(8,128)(2,1)S(1)} %slice.473), channel_id=1, source_target_pairs={{0,2},{2,0},{4,6},{6,4},{8,10},{10,8},{12,14},{14,12},{16,18},{18,... | collective-permute-start | bytes 1572872 | tf_op jit(solution)/shard_map/ppermute | solution.py:216
  122.7 12.9 %collective-permute-start.18 = (bf16[128,2048]{1,0:T(8,128)(2,1)S(1)}, bf16[128,2048]{1,0:T(8,128)(2,1)S(1)}, u32[]{:S(2)}, u32[]{:S(2)}) collective-permute-start(bf16[128,2048]{1,0:T(8,128)(2,1)S(1)} %slice.474), channel_id=1, source_target_pairs={{0,4},{2,6},{4,0},{6,2},{8,12},{10,14},{12,8},{14,10},{16,20},{18,... | collective-permute-start | bytes 1572872 | tf_op jit(solution)/shard_map/ppermute | solution.py:216
  139.5 14.9 %collective-permute-start.22 = (bf16[128,2048]{1,0:T(8,128)(2,1)S(1)}, bf16[128,2048]{1,0:T(8,128)(2,1)S(1)}, u32[]{:S(2)}, u32[]{:S(2)}) collective-permute-start(bf16[128,2048]{1,0:T(8,128)(2,1)S(1)} %get-tuple-element.452), channel_id=1, source_target_pairs={{0,4},{2,6},{4,0},{6,2},{8,12},{10,14},{12,8},{14,10},{16,20},{18,... | collective-permute-start | bytes 1572872 | tf_op jit(solution)/shard_map/ppermute | solution.py:216
  141.0 14.9 %collective-permute-start.21 = (bf16[128,2048]{1,0:T(8,128)(2,1)S(1)}, bf16[128,2048]{1,0:T(8,128)(2,1)S(1)}, u32[]{:S(2)}, u32[]{:S(2)}) collective-permute-start(bf16[128,2048]{1,0:T(8,128)(2,1)S(1)} %get-tuple-element.453), channel_id=1, source_target_pairs={{0,2},{2,0},{4,6},{6,4},{8,10},{10,8},{12,14},{14,12},{16,18},{18,... | collective-permute-start | bytes 1572872 | tf_op jit(solution)/shard_map/ppermute | solution.py:216
  141.6 24.0 %collective-permute-start.20 = (bf16[128,2048]{1,0:T(8,128)(2,1)S(1)}, bf16[128,2048]{1,0:T(8,128)(2,1)S(1)}, u32[]{:S(2)}, u32[]{:S(2)}) collective-permute-start(bf16[128,2048]{1,0:T(8,128)(2,1)S(1)} %get-tuple-element.454), channel_id=1, source_target_pairs={{0,4},{2,6},{4,0},{6,2},{8,12},{10,14},{12,8},{14,10},{16,20},{18,... | collective-permute-start | bytes 1572872 | tf_op jit(solution)/shard_map/ppermute | solution.py:216
  142.1 24.9 %collective-permute-start.19 = (bf16[128,2048]{1,0:T(8,128)(2,1)S(1)}, bf16[128,2048]{1,0:T(8,128)(2,1)S(1)}, u32[]{:S(2)}, u32[]{:S(2)}) collective-permute-start(bf16[128,2048]{1,0:T(8,128)(2,1)S(1)} %get-tuple-element.455), channel_id=1, source_target_pairs={{0,2},{2,0},{4,6},{6,4},{8,10},{10,8},{12,14},{14,12},{16,18},{18,... | collective-permute-start | bytes 1572872 | tf_op jit(solution)/shard_map/ppermute | solution.py:216
  156.2 19.1 %collective-permute-start.23 = (bf16[128,2048]{1,0:T(8,128)(2,1)S(1)}, bf16[128,2048]{1,0:T(8,128)(2,1)S(1)}, u32[]{:S(2)}, u32[]{:S(2)}) collective-permute-start(bf16[128,2048]{1,0:T(8,128)(2,1)S(1)} %get-tuple-element.246), channel_id=1, source_target_pairs={{0,2},{2,0},{4,6},{6,4},{8,10},{10,8},{12,14},{14,12},{16,18},{18,... | collective-permute-start | bytes 1572872 | tf_op jit(solution)/shard_map/ppermute | solution.py:216
  156.9 18.4 %collective-permute-start.24 = (bf16[128,2048]{1,0:T(8,128)(2,1)S(1)}, bf16[128,2048]{1,0:T(8,128)(2,1)S(1)}, u32[]{:S(2)}, u32[]{:S(2)}) collective-permute-start(bf16[128,2048]{1,0:T(8,128)(2,1)S(1)} %get-tuple-element.247), channel_id=1, source_target_pairs={{0,4},{2,6},{4,0},{6,2},{8,12},{10,14},{12,8},{14,10},{16,20},{18,... | collective-permute-start | bytes 1572872 | tf_op jit(solution)/shard_map/ppermute | solution.py:216
  178.1 23.1 %collective-permute-start.26 = (bf16[256,2048]{1,0:T(8,128)(2,1)S(1)}, bf16[256,2048]{1,0:T(8,128)(2,1)S(1)}, u32[]{:S(2)}, u32[]{:S(2)}) collective-permute-start(bf16[256,2048]{1,0:T(8,128)(2,1)S(1)} %multiply_convert_fusion), channel_id=1, source_target_pairs={{0,4},{2,6},{4,0},{6,2},{8,12},{10,14},{12,8},{14,10},{16,20},{18,... | collective-permute-start | bytes 3145736 | tf_op jit(solution)/shard_map/ppermute | solution.py:216
  178.7 22.5 %collective-permute-start.25 = (bf16[256,2048]{1,0:T(8,128)(2,1)S(1)}, bf16[256,2048]{1,0:T(8,128)(2,1)S(1)}, u32[]{:S(2)}, u32[]{:S(2)}) collective-permute-start(bf16[256,2048]{1,0:T(8,128)(2,1)S(1)} %multiply_convert_fusion), channel_id=1, source_target_pairs={{0,2},{2,0},{4,6},{6,4},{8,10},{10,8},{12,14},{14,12},{16,18},{18,... | collective-permute-start | bytes 3145736 | tf_op jit(solution)/shard_map/ppermute | solution.py:216
  201.2 30.3 %collective-permute-start.29 = (bf16[1408,2048]{1,0:T(8,128)(2,1)}, bf16[1408,2048]{1,0:T(8,128)(2,1)}, u32[]{:S(2)}, u32[]{:S(2)}) collective-permute-start(bf16[1408,2048]{1,0:T(8,128)(2,1)} %all-gather.6.cloned.1.call-done), channel_id=1, source_target_pairs={{0,1},{1,0},{2,3},{3,2},{4,5},{5,4},{6,7},{7,6},{8,9},{9,8},{10,11... | collective-permute-start | bytes 17301512 | tf_op jit(solution)/shard_map/ppermute | solution.py:220
  202.9 14.6 %collective-permute-start.27 = (bf16[128,2048]{1,0:T(8,128)(2,1)}, bf16[128,2048]{1,0:T(8,128)(2,1)}, u32[]{:S(2)}, u32[]{:S(2)}) collective-permute-start(bf16[128,2048]{1,0:T(8,128)(2,1)} %slice.476), channel_id=1, source_target_pairs={{0,2},{2,0},{4,6},{6,4},{8,10},{10,8},{12,14},{14,12},{16,18},{18,... | collective-permute-start | bytes 1572872 | tf_op jit(solution)/shard_map/ppermute | solution.py:216
  204.4 14.3 %collective-permute-start.28 = (bf16[128,2048]{1,0:T(8,128)(2,1)}, bf16[128,2048]{1,0:T(8,128)(2,1)}, u32[]{:S(2)}, u32[]{:S(2)}) collective-permute-start(bf16[128,2048]{1,0:T(8,128)(2,1)} %slice.477), channel_id=1, source_target_pairs={{0,4},{2,6},{4,0},{6,2},{8,12},{10,14},{12,8},{14,10},{16,20},{18,... | collective-permute-start | bytes 1572872 | tf_op jit(solution)/shard_map/ppermute | solution.py:216
  205.9 149.9 %reduce-scatter.5.cloned.1.call-start = ((), (), s32[]{:S(2)}) async-start(), calls=%async_computation.7 | async-start | bytes 3604480 | tf_op jit(solution)/shard_map/reduce_scatter | solution.py:246
  250.9 5.3 collective-permute-start.30
  261.6 11.6 %collective-permute-start.31 = (bf16[704,2048]{1,0:T(8,128)(2,1)}, bf16[704,2048]{1,0:T(8,128)(2,1)}, u32[]{:S(2)}, u32[]{:S(2)}) collective-permute-start(bf16[704,2048]{1,0:T(8,128)(2,1)} %all-gather.8.cloned.1.call-done.down_ref.refs_2_), channel_id=1, source_target_pairs={{0,1},{1,0},{2,3},{3,2},{4,5},{5,4},{6,7},{7,6},{8,9},{9,8},{10,11... | collective-permute-start | bytes 8650760 | tf_op jit(solution)/shard_map/ppermute | solution.py:220
  261.7 184.5 %reduce-scatter.7.cloned.1.call-start = ((), (), s32[]{:S(2)}) async-start(), calls=%async_computation.8 | async-start | bytes 3604480 | tf_op jit(solution)/shard_map/reduce_scatter | solution.py:246
  298.9 5.6 %collective-permute-start.36 = (bf16[704,2048]{1,0:T(8,128)(2,1)S(1)}, bf16[704,2048]{1,0:T(8,128)(2,1)S(1)}, u32[]{:S(2)}, u32[]{:S(2)}) collective-permute-start(bf16[704,2048]{1,0:T(8,128)(2,1)S(1)} %shard_map.194), channel_id=1, source_target_pairs={{0,1},{1,0},{2,3},{3,2},{4,5},{5,4},{6,7},{7,6},{8,9},{9,8},{10,11... | collective-permute-start | bytes 8650760 | tf_op jit(solution)/shard_map/ppermute | solution.py:220
  300.8 14.1 %collective-permute-start.35 = (bf16[128,2048]{1,0:T(8,128)(2,1)}, bf16[128,2048]{1,0:T(8,128)(2,1)S(1)}, u32[]{:S(2)}, u32[]{:S(2)}) collective-permute-start(bf16[128,2048]{1,0:T(8,128)(2,1)} %get-tuple-element.444), channel_id=1, source_target_pairs={{0,4},{2,6},{4,0},{6,2},{8,12},{10,14},{12,8},{14,10},{16,20},{18,... | collective-permute-start | bytes 1572872 | tf_op jit(solution)/shard_map/ppermute | solution.py:216
  302.1 13.6 %collective-permute-start.34 = (bf16[128,2048]{1,0:T(8,128)(2,1)S(1)}, bf16[128,2048]{1,0:T(8,128)(2,1)S(1)}, u32[]{:S(2)}, u32[]{:S(2)}) collective-permute-start(bf16[128,2048]{1,0:T(8,128)(2,1)S(1)} %get-tuple-element.445), channel_id=1, source_target_pairs={{0,2},{2,0},{4,6},{6,4},{8,10},{10,8},{12,14},{14,12},{16,18},{18,... | collective-permute-start | bytes 1572872 | tf_op jit(solution)/shard_map/ppermute | solution.py:216
  325.6 5.6 %collective-permute-start.39 = (bf16[704,2048]{1,0:T(8,128)(2,1)}, bf16[704,2048]{1,0:T(8,128)(2,1)}, u32[]{:S(2)}, u32[]{:S(2)}) collective-permute-start(bf16[704,2048]{1,0:T(8,128)(2,1)} %shard_map.196), channel_id=1, source_target_pairs={{0,1},{1,0},{2,3},{3,2},{4,5},{5,4},{6,7},{7,6},{8,9},{9,8},{10,11... | collective-permute-start | bytes 8650760 | tf_op jit(solution)/shard_map/ppermute | solution.py:220
  325.6 130.4 %reduce-scatter.9.cloned.1.call-start = ((), (), s32[]{:S(2)}) async-start(), calls=%async_computation.9 | async-start | bytes 3604480 | tf_op jit(solution)/shard_map/reduce_scatter | solution.py:246
  326.0 15.0 %collective-permute-start.33 = (bf16[128,2048]{1,0:T(8,128)(2,1)}, bf16[128,2048]{1,0:T(8,128)(2,1)S(1)}, u32[]{:S(2)}, u32[]{:S(2)}) collective-permute-start(bf16[128,2048]{1,0:T(8,128)(2,1)} %get-tuple-element.446), channel_id=1, source_target_pairs={{0,4},{2,6},{4,0},{6,2},{8,12},{10,14},{12,8},{14,10},{16,20},{18,... | collective-permute-start | bytes 1572872 | tf_op jit(solution)/shard_map/ppermute | solution.py:216
  326.9 15.0 %collective-permute-start.32 = (bf16[128,2048]{1,0:T(8,128)(2,1)}, bf16[128,2048]{1,0:T(8,128)(2,1)S(1)}, u32[]{:S(2)}, u32[]{:S(2)}) collective-permute-start(bf16[128,2048]{1,0:T(8,128)(2,1)} %get-tuple-element.447), channel_id=1, source_target_pairs={{0,2},{2,0},{4,6},{6,4},{8,10},{10,8},{12,14},{14,12},{16,18},{18,... | collective-permute-start | bytes 1572872 | tf_op jit(solution)/shard_map/ppermute | solution.py:216
  328.2 24.2 %collective-permute-start.37 = (bf16[128,2048]{1,0:T(8,128)(2,1)}, bf16[128,2048]{1,0:T(8,128)(2,1)S(1)}, u32[]{:S(2)}, u32[]{:S(2)}) collective-permute-start(bf16[128,2048]{1,0:T(8,128)(2,1)} %get-tuple-element.315), channel_id=1, source_target_pairs={{0,2},{2,0},{4,6},{6,4},{8,10},{10,8},{12,14},{14,12},{16,18},{18,... | collective-permute-start | bytes 1572872 | tf_op jit(solution)/shard_map/ppermute | solution.py:216
  328.9 23.5 %collective-permute-start.38 = (bf16[128,2048]{1,0:T(8,128)(2,1)}, bf16[128,2048]{1,0:T(8,128)(2,1)}, u32[]{:S(2)}, u32[]{:S(2)}) collective-permute-start(bf16[128,2048]{1,0:T(8,128)(2,1)} %get-tuple-element.316), channel_id=1, source_target_pairs={{0,4},{2,6},{4,0},{6,2},{8,12},{10,14},{12,8},{14,10},{16,20},{18,... | collective-permute-start | bytes 1572872 | tf_op jit(solution)/shard_map/ppermute | solution.py:216
  361.7 24.5 %collective-permute-start.41 = (bf16[256,2048]{1,0:T(8,128)(2,1)S(1)}, bf16[256,2048]{1,0:T(8,128)(2,1)S(1)}, u32[]{:S(2)}, u32[]{:S(2)}) collective-permute-start(bf16[256,2048]{1,0:T(8,128)(2,1)S(1)} %get-tuple-element.337), channel_id=1, source_target_pairs={{0,4},{2,6},{4,0},{6,2},{8,12},{10,14},{12,8},{14,10},{16,20},{18,... | collective-permute-start | bytes 3145736 | tf_op jit(solution)/shard_map/ppermute | solution.py:216
  362.9 24.3 %collective-permute-start.40 = (bf16[256,2048]{1,0:T(8,128)(2,1)S(1)}, bf16[256,2048]{1,0:T(8,128)(2,1)S(1)}, u32[]{:S(2)}, u32[]{:S(2)}) collective-permute-start(bf16[256,2048]{1,0:T(8,128)(2,1)S(1)} %get-tuple-element.337), channel_id=1, source_target_pairs={{0,2},{2,0},{4,6},{6,4},{8,10},{10,8},{12,14},{14,12},{16,18},{18,... | collective-permute-start | bytes 3145736 | tf_op jit(solution)/shard_map/ppermute | solution.py:216
  388.0 15.2 %collective-permute-start.44 = (bf16[128,2048]{1,0:T(8,128)(2,1)}, bf16[128,2048]{1,0:T(8,128)(2,1)}, u32[]{:S(2)}, u32[]{:S(2)}) collective-permute-start(bf16[128,2048]{1,0:T(8,128)(2,1)} %slice.482), channel_id=1, source_target_pairs={{0,2},{2,0},{4,6},{6,4},{8,10},{10,8},{12,14},{14,12},{16,18},{18,... | collective-permute-start | bytes 1572872 | tf_op jit(solution)/shard_map/ppermute | solution.py:216
  389.5 15.2 %collective-permute-start.45 = (bf16[128,2048]{1,0:T(8,128)(2,1)}, bf16[128,2048]{1,0:T(8,128)(2,1)}, u32[]{:S(2)}, u32[]{:S(2)}) collective-permute-start(bf16[128,2048]{1,0:T(8,128)(2,1)} %slice.483), channel_id=1, source_target_pairs={{0,4},{2,6},{4,0},{6,2},{8,12},{10,14},{12,8},{14,10},{16,20},{18,... | collective-permute-start | bytes 1572872 | tf_op jit(solution)/shard_map/ppermute | solution.py:216
  390.6 141.8 %reduce-scatter.11.cloned.1.call-start = ((), (), s32[]{:S(2)}) async-start(), calls=%async_computation.10 | async-start | bytes 5242880 | tf_op jit(solution)/shard_map/reduce_scatter | solution.py:246
  392.3 22.4 %collective-permute-start.43 = (bf16[128,2048]{1,0:T(8,128)(2,1)S(1)}, bf16[128,2048]{1,0:T(8,128)(2,1)S(1)}, u32[]{:S(2)}, u32[]{:S(2)}) collective-permute-start(bf16[128,2048]{1,0:T(8,128)(2,1)S(1)} %get-tuple-element.436), channel_id=1, source_target_pairs={{0,4},{2,6},{4,0},{6,2},{8,12},{10,14},{12,8},{14,10},{16,20},{18,... | collective-permute-start | bytes 1572872 | tf_op jit(solution)/shard_map/ppermute | solution.py:216
  393.3 21.5 %collective-permute-start.42 = (bf16[128,2048]{1,0:T(8,128)(2,1)S(1)}, bf16[128,2048]{1,0:T(8,128)(2,1)S(1)}, u32[]{:S(2)}, u32[]{:S(2)}) collective-permute-start(bf16[128,2048]{1,0:T(8,128)(2,1)S(1)} %get-tuple-element.437), channel_id=1, source_target_pairs={{0,2},{2,0},{4,6},{6,4},{8,10},{10,8},{12,14},{14,12},{16,18},{18,... | collective-permute-start | bytes 1572872 | tf_op jit(solution)/shard_map/ppermute | solution.py:216
  414.8 14.9 %collective-permute-start.48 = (f32[2,16,2,256]{3,2,1,0:T(2,128)}, f32[2,16,2,256]{3,2,1,0:T(2,128)}, u32[]{:S(2)}, u32[]{:S(2)}) collective-permute-start(f32[2,16,2,256]{3,2,1,0:T(2,128)} %pad_maximum_fusion.11), channel_id=1, source_target_pairs={{1,0},{3,2},{5,4},{7,6},{9,8},{11,10},{13,12},{15,14},{17,16},{19,... | collective-permute-start | bytes 196616 | tf_op jit(solution)/shard_map/ppermute | solution.py:226
  426.2 16.3 %collective-permute-start.51 = (bf16[256,2048]{1,0:T(8,128)(2,1)}, bf16[256,2048]{1,0:T(8,128)(2,1)}, u32[]{:S(2)}, u32[]{:S(2)}) collective-permute-start(bf16[256,2048]{1,0:T(8,128)(2,1)} %shard_map.200), channel_id=1, source_target_pairs={{0,1},{1,0},{2,3},{3,2},{4,5},{5,4},{6,7},{7,6},{8,9},{9,8},{10,11... | collective-permute-start | bytes 3145736 | tf_op jit(solution)/shard_map/ppermute | solution.py:220
  428.0 12.1 %collective-permute-start.49 = (bf16[256,2048]{1,0:T(8,128)(2,1)S(1)}, bf16[256,2048]{1,0:T(8,128)(2,1)S(1)}, u32[]{:S(2)}, u32[]{:S(2)}) collective-permute-start(bf16[256,2048]{1,0:T(8,128)(2,1)S(1)} %shard_map.199), channel_id=1, source_target_pairs={{0,1},{1,0},{2,3},{3,2},{4,5},{5,4},{6,7},{7,6},{8,9},{9,8},{10,11... | collective-permute-start | bytes 3145736 | tf_op jit(solution)/shard_map/ppermute | solution.py:220
  428.1 27.9 %collective-permute-start.46 = (bf16[256,2048]{1,0:T(8,128)(2,1)}, bf16[256,2048]{1,0:T(8,128)(2,1)}, u32[]{:S(2)}, u32[]{:S(2)}) collective-permute-start(bf16[256,2048]{1,0:T(8,128)(2,1)} %pad_maximum_fusion.6), channel_id=1, source_target_pairs={{0,2},{2,0},{4,6},{6,4},{8,10},{10,8},{12,14},{14,12},{16,18},{18,... | collective-permute-start | bytes 3145736 | tf_op jit(solution)/shard_map/ppermute | solution.py:216
  428.5 27.4 %collective-permute-start.47 = (bf16[256,2048]{1,0:T(8,128)(2,1)}, bf16[256,2048]{1,0:T(8,128)(2,1)}, u32[]{:S(2)}, u32[]{:S(2)}) collective-permute-start(bf16[256,2048]{1,0:T(8,128)(2,1)} %pad_maximum_fusion.5), channel_id=1, source_target_pairs={{0,4},{2,6},{4,0},{6,2},{8,12},{10,14},{12,8},{14,10},{16,20},{18,... | collective-permute-start | bytes 3145736 | tf_op jit(solution)/shard_map/ppermute | solution.py:216
  440.1 6.1 %collective-permute-start.50 = (bf16[512,2048]{1,0:T(8,128)(2,1)}, bf16[512,2048]{1,0:T(8,128)(2,1)}, u32[]{:S(2)}, u32[]{:S(2)}) collective-permute-start(bf16[512,2048]{1,0:T(8,128)(2,1)} %shard_map.201), channel_id=1, source_target_pairs={{0,1},{1,0},{2,3},{3,2},{4,5},{5,4},{6,7},{7,6},{8,9},{9,8},{10,11... | collective-permute-start | bytes 6291464 | tf_op jit(solution)/shard_map/ppermute | solution.py:220
  472.7 14.4 %collective-permute-start.53 = (bf16[128,2048]{1,0:T(8,128)(2,1)S(1)}, bf16[128,2048]{1,0:T(8,128)(2,1)S(1)}, u32[]{:S(2)}, u32[]{:S(2)}) collective-permute-start(bf16[128,2048]{1,0:T(8,128)(2,1)S(1)} %get-tuple-element.430), channel_id=1, source_target_pairs={{0,4},{2,6},{4,0},{6,2},{8,12},{10,14},{12,8},{14,10},{16,20},{18,... | collective-permute-start | bytes 1572872 | tf_op jit(solution)/shard_map/ppermute | solution.py:216
  473.7 14.1 %collective-permute-start.52 = (bf16[128,2048]{1,0:T(8,128)(2,1)S(1)}, bf16[128,2048]{1,0:T(8,128)(2,1)S(1)}, u32[]{:S(2)}, u32[]{:S(2)}) collective-permute-start(bf16[128,2048]{1,0:T(8,128)(2,1)S(1)} %get-tuple-element.431), channel_id=1, source_target_pairs={{0,2},{2,0},{4,6},{6,4},{8,10},{10,8},{12,14},{14,12},{16,18},{18,... | collective-permute-start | bytes 1572872 | tf_op jit(solution)/shard_map/ppermute | solution.py:216
  490.3 24.8 %collective-permute-start.54 = (bf16[256,2048]{1,0:T(8,128)(2,1)}, bf16[256,2048]{1,0:T(8,128)(2,1)S(1)}, u32[]{:S(2)}, u32[]{:S(2)}) collective-permute-start(bf16[256,2048]{1,0:T(8,128)(2,1)} %pad_maximum_fusion.10), channel_id=1, source_target_pairs={{0,2},{2,0},{4,6},{6,4},{8,10},{10,8},{12,14},{14,12},{16,18},{18,... | collective-permute-start | bytes 3145736 | tf_op jit(solution)/shard_map/ppermute | solution.py:216
  491.8 24.5 %collective-permute-start.55 = (bf16[256,2048]{1,0:T(8,128)(2,1)}, bf16[256,2048]{1,0:T(8,128)(2,1)S(1)}, u32[]{:S(2)}, u32[]{:S(2)}) collective-permute-start(bf16[256,2048]{1,0:T(8,128)(2,1)} %pad_maximum_fusion.9), channel_id=1, source_target_pairs={{0,4},{2,6},{4,0},{6,2},{8,12},{10,14},{12,8},{14,10},{16,20},{18,... | collective-permute-start | bytes 3145736 | tf_op jit(solution)/shard_map/ppermute | solution.py:216
  497.7 5.0 collective-permute-start.57
  502.7 6.9 %collective-permute-start.58 = (f32[3,2048]{1,0:T(4,128)S(1)}, f32[3,2048]{1,0:T(4,128)S(1)}, u32[]{:S(2)}, u32[]{:S(2)}) collective-permute-start(f32[3,2048]{1,0:T(4,128)S(1)} %add.225), channel_id=1, source_target_pairs={{0,16},{2,18},{4,20},{6,22},{8,24},{10,26},{12,28},{14,30},{16,0},... | collective-permute-start | bytes 73736 | tf_op jit(solution)/shard_map/ppermute | solution.py:216
  525.2 3.8 collective-permute-start.60
  (132 other events, 797.1 us)
Sparse Core Ops, SparseCore 0:
  10.2 83.5 all-gather.3
  95.9 105.2 all-gather.5
  206.0 55.6 all-gather.7
  263.8 54.8 reduce-scatter.4
  325.7 53.9 reduce-scatter.6
  390.7 53.1 reduce-scatter.8
  456.1 76.2 reduce-scatter.10

commit v5 on v4

--- a/solution.py
+++ b/solution.py
@@ -144,6 +144,41 @@
         ),
         cost_estimate=pl.CostEstimate(flops=flops, bytes_accessed=1, transcendentals=0),
     )(left, right, *more)
+
+
+def mixer_product(left, right, more, first, last, deep, flops, tile=512):
+    rows, count = left.shape
+    width = right.shape[1]
+    wide = first.shape[0]
+    share, parts = wide // deep, count // wide
+
+    def body(left_ref, right_ref, first_ref, last_ref, *refs):
+        total = trans_times(left_ref[...], right_ref[...])
+        for ref in refs[:-1]:
+            total = total + high(ref[...])
+        total = low(total)
+        for plane in range(deep):
+            own = slice(plane * share, (plane + 1) * share)
+            refs[-1][plane, 0] = first_ref[own, :]
+            for k in range(parts):
+                refs[-1][plane, 1 + k] = total[k * wide + own.start : k * wide + own.stop]
+            refs[-1][plane, 1 + parts] = last_ref[own, :]
+
+    def columns(size):
+        return pl.BlockSpec((size, tile), lambda i: (0, i))
+
+    return pl.pallas_call(
+        body,
+        grid=(width // tile,),
+        in_specs=[whole(left.shape), columns(rows), columns(wide), columns(wide)]
+        + [columns(count)] * len(more),
+        out_specs=pl.BlockSpec((deep, 2 + parts, share, tile), lambda i: (0, 0, 0, i)),
+        out_shape=pltpu.HBM((deep, 2 + parts, share, width), jnp.bfloat16),
+        compiler_params=pltpu.CompilerParams(
+            dimension_semantics=("arbitrary",), vmem_limit_bytes=16 * 1024 * 1024
+        ),
+        cost_estimate=pl.CostEstimate(flops=flops, bytes_accessed=1, transcendentals=0),
+    )(left, right, first, last, *more)
 
 
 def ffn_call(body, lefts, rights, slopes, count, tile=256):
@@ -448,7 +483,7 @@
     order.did(mixer_out)
     cot_all = cot_rows.end()
     order.wait(cot_all)
-    mixer_sums = Sums(groups, mixer_out)
+    mixer_sums = Sums(groups, mixer_out, True)
     mixer_sums.middle()
     mixer_sum = mixer_sums.end()
     mixer_sum, tokens_now = order(mixer_sum, tokens_own)
@@ -504,7 +539,7 @@
         grad_up.append(found[1])
     back_two = sum_of_products(*order(grad_gate + grad_up, gate + up))
     order.did(back_two)
-    two_sums = Sums(groups, back_two)
+    two_sums = Sums(groups, back_two, True)
     gate_got = core_terms(grad_gate, normed_two)
     gate_total = own_term(grad_gate[0], normed_two, gate_got)
     two_sums.middle()
@@ -570,13 +605,10 @@
     b_total = own_term(grad_b[0], normed, b_got, many, False)
     out_total = own_term(mixed[0], grad_mixer, out_got, many, False)
     order.wait(gate_grad)
-    cx_total = own_term(grad_cx[0], normed, cx_got, many, False)
-    mixer_total = (
-        jnp.concatenate([b_total, cx_total, out_total], 0)
-        .reshape(4, deep, share, width)
-        .transpose(1, 0, 2, 3)
-        .reshape(4 * wide_share, width)
-    )
+    order.wait(cx_got)
+    mixer_total = mixer_product(
+        *order(grad_cx[0], normed, cx_got, b_total, out_total), deep, many
+    ).reshape(4 * wide_share, width)
     order.did(mixer_total)
     order.wait(ffn_sums.summed)
     order.wait(up_grad)

time: 553 us -> 550 us (level)
    pallas_call x12 -> x11, Pallas kernels: 51 us -> 44.4 us  [columns_product(): pl.pallas_call(body, grid=(width // tile,), in_specs=[whole(left.shape),...]
    pallas_call x0 -> x1, Pallas kernels: none -> 6 us  [mixer_product(): pl.pallas_call(body, grid=(width // tile,), in_specs=[whole(left.shape),...]
    ppermute x48 -> x44, starting transfers between devices: 55.1 us -> 50.2 us  [swap(): return lax.ppermute(value, 'fsdp', [(i, i ^ bit) for i in range(self.fsdp)])]
    ppermute x48 -> x44, waiting for transfers between devices: 156 us -> 159 us  [swap(): return lax.ppermute(value, 'fsdp', [(i, i ^ bit) for i in range(self.fsdp)])]
    unnamed x270 -> x272, local copies, waits for them, and re-layouts: 48.8 us -> 49.5 us
  transfers between devices with their start and end apart: 68 -> 64, of which waited for: 42 -> 38; matrix products, arithmetic and copies ran while one was open for 19% -> 19% of each run, Pallas kernels for 21% -> 21%
where the time goes in v5:
time: 550 us; the launch traced here: 540 us
  waiting for transfers between devices  204 us (37%)
  Pallas kernels  112 us (20%)
  local copies, waits for them, and re-layouts  80.4 us (15%)
  other arithmetic  59.7 us (11%)
  starting transfers between devices  58.1 us (11%)
  between operations  16.7 us (3%)
  matrix products  9.46 us (2%)
    ppermute x44, waiting for transfers between devices, swap(): return lax.ppermute(value, 'fsdp', [(i, i ^ bit) for i in range(self.fsdp)])  159 us
    ppermute x44, starting transfers between devices, swap(): return lax.ppermute(value, 'fsdp', [(i, i ^ bit) for i in range(self.fsdp)])  50.2 us
    unnamed x272, local copies, waits for them, and re-layouts  49.5 us
    pallas_call x11, Pallas kernels, columns_product(): pl.pallas_call(body, grid=(width // tile,), in_specs=[whole(left.shape),...  44.4 us
    pallas_call x4, Pallas kernels, sum_of_products(): pl.pallas_call(body, grid=(rows // tile,), in_specs=[pl.BlockSpec((tile,...  34.9 us
    all_gather x3, waiting for transfers between devices, gather_ordered(): lax.all_gather(value, 'fsdp', axis=0, tiled=True, axis_index_groups=self....  29.4 us
    pallas_call x4, Pallas kernels, ffn_call(): pl.pallas_call(body, grid=(rows // tile,), in_specs=[pl.BlockSpec((tile,...  26.3 us
    convert_element_type x15, other arithmetic, low(): return value.astype(jnp.bfloat16)  20.3 us
  transfers between devices with their start and end apart: 64, of which 38 were waited for; matrix products, arithmetic and copies ran while one was open for 19% of the time, Pallas kernels for 21%

profile of v5, /device:TPU:0, one launch (start us, length us, event | category | flops | bytes accessed | tf_op | source)
XLA Modules:
  0.0 539.9 jit_solution(13663620968625476662)
XLA Ops:
  7.3 2.4 pad_maximum_fusion.1
  9.7 3.0 collective-permute-start.1
  16.1 2.6 pad_maximum_fusion
  18.7 2.7 collective-permute-start.3
  24.0 2.8 collective-permute-done.4
  26.8 2.7 collective-permute-start.5
  34.2 3.3 collective-permute-done.8
  43.3 10.1 %collective-permute-done.10 = bf16[1,2,4,2,128]{4,3,2,1,0:T(2,128)(2,1)S(1)} collective-permute-done((bf16[1,2,4,2,128]{4,3,2,1,0:T(2,128)(2,1)S(1)}, bf16[1,2,4,2,128]{4,3,2,1,0:T(2,128)(2,1)S(1)}, u32[]{:S(2)}, u32[]{:S(2)}) %collective-permute-start.10) | collective-permute-done | bytes 4128 | tf_op jit(solution)/shard_map/ppermute | solution.py:251
  61.2 3.0 fusion.2.right_ref
  64.2 20.1 %collective-permute-done.14 = bf16[256,2048]{1,0:T(8,128)(2,1)S(1)} collective-permute-done((bf16[256,2048]{1,0:T(8,128)(2,1)S(1)}, bf16[256,2048]{1,0:T(8,128)(2,1)S(1)}, u32[]{:S(2)}, u32[]{:S(2)}) %collective-permute-start.14) | collective-permute-done | bytes 1048608 | tf_op jit(solution)/shard_map/ppermute | solution.py:251
  84.7 9.1 %all-gather.4.cloned.1.call-done = bf16[1024,2048]{1,0:T(8,128)(2,1)} async-done(((bf16[256,2048]{1,0:T(8,128)(2,1)}), bf16[1024,2048]{1,0:T(8,128)(2,1)}) %all-gather.4.cloned.1.call-update) | async-done | bytes 4194320 | tf_op jit(solution)/shard_map/all_gather | solution.py:276
  95.3 2.7 slice.441
  98.4 3.0 copy-done.38
  101.4 3.4 fusion.33
  106.8 2.1 slice.447
  108.9 2.7 slice.446
  112.0 3.4 fusion.34
  117.3 2.9 collective-permute-start.16
  127.6 3.1 shard_map.186
  130.8 3.9 collective-permute-done.17
  137.6 2.1 copy-done.4
  141.9 10.1 %collective-permute-done.20 = bf16[128,2048]{1,0:T(8,128)(2,1)S(1)} collective-permute-done((bf16[128,2048]{1,0:T(8,128)(2,1)S(1)}, bf16[128,2048]{1,0:T(8,128)(2,1)S(1)}, u32[]{:S(2)}, u32[]{:S(2)}) %collective-permute-start.20) | collective-permute-done | bytes 524320 | tf_op jit(solution)/shard_map/ppermute | solution.py:251
  155.0 21.1 %collective-permute-done.21 = bf16[256,2048]{1,0:T(8,128)(2,1)S(1)} collective-permute-done((bf16[256,2048]{1,0:T(8,128)(2,1)S(1)}, bf16[256,2048]{1,0:T(8,128)(2,1)S(1)}, u32[]{:S(2)}, u32[]{:S(2)}) %collective-permute-start.21) | collective-permute-done | bytes 1048608 | tf_op jit(solution)/shard_map/ppermute | solution.py:251
  181.0 20.1 %all-gather.6.cloned.1.call-done = bf16[1408,2048]{1,0:T(8,128)(2,1)} async-done(((bf16[352,2048]{1,0:T(8,128)(2,1)}), bf16[1408,2048]{1,0:T(8,128)(2,1)}) %all-gather.6.cloned.1.call-update) | async-done | bytes 5767184 | tf_op jit(solution)/shard_map/all_gather | solution.py:276
  205.9 11.6 %collective-permute-done.25 = bf16[128,2048]{1,0:T(8,128)(2,1)} collective-permute-done((bf16[128,2048]{1,0:T(8,128)(2,1)}, bf16[128,2048]{1,0:T(8,128)(2,1)}, u32[]{:S(2)}, u32[]{:S(2)}) %collective-permute-start.25) | collective-permute-done | bytes 524320 | tf_op jit(solution)/shard_map/ppermute | solution.py:251
  222.5 7.8 %shard_map.187 = (bf16[1024,704]{1,0:T(8,128)(2,1)S(1)}, bf16[1024,704]{1,0:T(8,128)(2,1)S(1)}, bf16[1024,704]{1,0:T(8,128)(2,1)S(1)}) custom-call(bf16[1024,2048]{1,0:T(8,128)(2,1)S(1)} %constant_dynamic-update-slice_fusion.10.normed_ref.right_ref, bf16[704,2048]{1,0:T(8,128)(2,1)S(1)} %bitcast.156, bf16[704,2048]{1,0:T(8,128)(2,1)S(1)} %bitcast.154), custom_call_target="tpu_custom_call" | custom-call | flops 1 | bytes 1 | tf_op jit(solution)/shard_map/pallas_call | solution.py:188
  231.5 4.8 fusion.24
  236.4 7.8 %shard_map.188 = (bf16[1024,704]{1,0:T(8,128)(2,1)S(1)}, bf16[1024,704]{1,0:T(8,128)(2,1)S(1)}, bf16[1024,704]{1,0:T(8,128)(2,1)S(1)}) custom-call(bf16[1024,2048]{1,0:T(8,128)(2,1)S(1)} %constant_dynamic-update-slice_fusion.10.normed_ref.right_ref, bf16[704,2048]{1,0:T(8,128)(2,1)S(1)} %bitcast.160, bf16[704,2048]{1,0:T(8,128)(2,1)S(1)} %bitcast.158), custom_call_target="tpu_custom_call" | custom-call | flops 1 | bytes 1 | tf_op jit(solution)/shard_map/pallas_call | solution.py:188
  246.5 4.3 shard_map.189
  250.9 5.3 collective-permute-done.28.refs_0_
  256.2 5.3 shard_map.190
  261.9 2.2 copy-done.6
  268.9 4.2 shard_map.191
  273.2 6.6 %shard_map.192 = (bf16[1024,704]{1,0:T(8,128)(2,1)S(1)}, bf16[1024,704]{1,0:T(8,128)(2,1)S(1)}) custom-call(bf16[1024,2048]{1,0:T(8,128)(2,1)S(1)} %copy-done.6, bf16[704,2048]{1,0:T(8,128)(2,1)} %collective-permute-done.29.down_ref.refs_3_, bf16[1024,704]{1,0:T(8,128)(2,1)S(1)} %copy-done.55, bf16[1024,704]{1,0:T(8,128)(2,1)S(1)} %copy-done.57), custom_call_target="tpu_custom_call" | custom-call | flops 1 | bytes 1 | tf_op jit(solution)/shard_map/pallas_call | solution.py:188
  279.8 14.6 %shard_map.193 = bf16[1024,2048]{1,0:T(8,128)(2,1)S(1)} custom-call(bf16[1024,704]{1,0:T(8,128)(2,1)S(1)} %get-tuple-element.306.refs_0_.left_ref, bf16[1024,704]{1,0:T(8,128)(2,1)S(1)} %get-tuple-element.303.refs_1_.left_ref, bf16[1024,704]{1,0:T(8,128)(2,1)S(1)} %get-tuple-element.316.refs_2_.left_ref, ...), custom_call_target="tpu_custom_call" | custom-call | flops 1 | bytes 1 | tf_op jit(solution)/shard_map/pallas_call | solution.py:84
  294.5 4.3 shard_map.194
  304.5 5.2 shard_map.195
  309.7 3.9 collective-permute-done.31
  319.3 4.3 shard_map.196
  327.7 3.4 collective-permute-done.35.refs_0_
  331.1 2.2 copy-done.3
  333.3 5.3 shard_map.197
  338.5 12.8 %collective-permute-done.33 = bf16[256,2048]{1,0:T(8,128)(2,1)S(1)} collective-permute-done((bf16[256,2048]{1,0:T(8,128)(2,1)}, bf16[256,2048]{1,0:T(8,128)(2,1)S(1)}, u32[]{:S(2)}, u32[]{:S(2)}) %collective-permute-start.33) | collective-permute-done | bytes 1048608 | tf_op jit(solution)/shard_map/ppermute | solution.py:251
  352.7 3.4 convert_add_fusion
  356.1 2.9 multiply_reduce_fusion.1
  362.9 9.2 %shard_map.198 = bf16[1024,2048]{1,0:T(8,128)(2,1)S(1)} custom-call(bf16[1024,704]{1,0:T(8,128)(2,1)S(1)} %copy-done.23, bf16[1024,704]{1,0:T(8,128)(2,1)S(1)} %copy-done.25, bf16[704,2048]{1,0:T(8,128)(2,1)S(1)} %copy-done.21, bf16[704,2048]{1,0:T(8,128)(2,1)} %collective-permute-done.29.down_ref.refs_3_), custom_call_target="tpu_custom_call" | custom-call | flops 1 | bytes 1 | tf_op jit(solution)/shard_map/pallas_call | solution.py:84
  374.2 11.3 %collective-permute-done.37 = bf16[256,2048]{1,0:T(8,128)(2,1)S(1)} collective-permute-done((bf16[256,2048]{1,0:T(8,128)(2,1)S(1)}, bf16[256,2048]{1,0:T(8,128)(2,1)S(1)}, u32[]{:S(2)}, u32[]{:S(2)}) %collective-permute-start.37) | collective-permute-done | bytes 1048608 | tf_op jit(solution)/shard_map/ppermute | solution.py:251
  393.0 9.3 %collective-permute-done.40 = bf16[128,2048]{1,0:T(8,128)(2,1)} collective-permute-done((bf16[128,2048]{1,0:T(8,128)(2,1)}, bf16[128,2048]{1,0:T(8,128)(2,1)}, u32[]{:S(2)}, u32[]{:S(2)}) %collective-permute-start.40) | collective-permute-done | bytes 524320 | tf_op jit(solution)/shard_map/ppermute | solution.py:251
  419.1 2.3 shard_map.199
  421.4 3.1 shard_map.200
  434.9 4.3 shard_map.201
  439.2 2.4 shard_map.202.first_ref
  441.6 3.6 shard_map.203.last_ref
  445.3 2.2 copy-done.40
  447.5 6.0 %shard_map.204 = bf16[4,4,64,2048]{3,2,1,0:T(8,128)(2,1)} custom-call(bf16[1024,512]{1,0:T(8,128)(2,1)S(1)} %pad_maximum_fusion.8.left_ref.refs_2_, bf16[1024,2048]{1,0:T(8,128)(2,1)S(1)} %copy-done.40, bf16[256,2048]{1,0:T(8,128)(2,1)S(1)} %shard_map.202.first_ref, bf16[256,2048]{1,0:T(8,128)(2,1)S(1)} %shard_map.203.last_ref, ...), custom_call_target="tpu_custom_call" | custom-call | flops 99999997952 | bytes 1 | tf_op jit(solution)/shard_map/pallas_call | solution.py:170
  462.2 7.9 %shard_map.205 = bf16[1024,2048]{1,0:T(8,128)(2,1)S(1)} custom-call(bf16[1024,256]{1,0:T(8,128)(2,1)S(1)} %bitcast.173, bf16[1024,256]{1,0:T(8,128)(2,1)S(1)} %bitcast.171, bf16[1024,512]{1,0:T(8,128)(2,1)S(1)} %copy-done.35, bf16[1024,512]{1,0:T(8,128)(2,1)S(1)} %copy-done.37, bf16[768,2048]{1,0:T(8,128)(2,1)S(1)} %bitcast.149, ...), custom_call_target="tpu_custom_call" | custom-call | flops 1 | bytes 1 | tf_op jit(solution)/shard_map/pallas_call | solution.py:84
  475.3 9.6 %collective-permute-done.49 = bf16[128,2048]{1,0:T(8,128)(2,1)S(1)} collective-permute-done((bf16[128,2048]{1,0:T(8,128)(2,1)S(1)}, bf16[128,2048]{1,0:T(8,128)(2,1)S(1)}, u32[]{:S(2)}, u32[]{:S(2)}) %collective-permute-start.49) | collective-permute-done | bytes 524320 | tf_op jit(solution)/shard_map/ppermute | solution.py:251
  489.7 3.5 add_convert_fusion
  494.5 5.0 collective-permute-done.53
  500.4 2.5 convert_element_type.267
  503.0 3.6 collective-permute-done.54
  506.6 6.3 %collective-permute-done.50 = bf16[256,2048]{1,0:T(8,128)(2,1)S(1)} collective-permute-done((bf16[256,2048]{1,0:T(8,128)(2,1)}, bf16[256,2048]{1,0:T(8,128)(2,1)S(1)}, u32[]{:S(2)}, u32[]{:S(2)}) %collective-permute-start.50) | collective-permute-done | bytes 1048608 | tf_op jit(solution)/shard_map/ppermute | solution.py:251
  515.3 3.2 fusion.8
  526.7 2.7 reduce-scatter.11.cloned.1.call-done
  (509 shorter events, 160.8 us)
Async XLA Ops:
  7.2 86.6 %all-gather.4.cloned.1.call-start = ((), (), s32[]{:S(2)}) async-start(), calls=%async_computation.4 | async-start | bytes 5242880 | tf_op jit(solution)/shard_map/all_gather | solution.py:276
  9.7 191.5 %all-gather.6.cloned.1.call-start = ((), (), s32[]{:S(2)}) async-start(), calls=%async_computation.5 | async-start | bytes 7208960 | tf_op jit(solution)/shard_map/all_gather | solution.py:276
  9.7 27.7 %collective-permute-start.1 = (bf16[256,2048]{1,0:T(8,128)(2,1)S(1)}, bf16[256,2048]{1,0:T(8,128)(2,1)S(1)}, u32[]{:S(2)}, u32[]{:S(2)}) collective-permute-start(bf16[256,2048]{1,0:T(8,128)(2,1)S(1)} %bitcast.182), channel_id=1, source_target_pairs={{0,4},{2,6},{4,0},{6,2},{8,12},{10,14},{12,8},{14,10},{16,20},{18,... | collective-permute-start | bytes 3145736 | tf_op jit(solution)/shard_map/ppermute | solution.py:251
  12.8 25.5 %collective-permute-start = (bf16[256,2048]{1,0:T(8,128)(2,1)S(1)}, bf16[256,2048]{1,0:T(8,128)(2,1)S(1)}, u32[]{:S(2)}, u32[]{:S(2)}) collective-permute-start(bf16[256,2048]{1,0:T(8,128)(2,1)S(1)} %bitcast.183), channel_id=1, source_target_pairs={{0,2},{2,0},{4,6},{6,4},{8,10},{10,8},{12,14},{14,12},{16,18},{18,... | collective-permute-start | bytes 3145736 | tf_op jit(solution)/shard_map/ppermute | solution.py:251
  14.3 4.4 collective-permute-start.2
  18.7 4.5 collective-permute-start.3
  23.2 3.6 collective-permute-start.4
  26.8 4.6 collective-permute-start.5
  31.4 6.0 %collective-permute-start.8 = (bf16[1,4,2,128]{3,2,1,0:T(2,128)(2,1)S(1)}, bf16[1,4,2,128]{3,2,1,0:T(2,128)(2,1)S(1)}, u32[]{:S(2)}, u32[]{:S(2)}) collective-permute-start(bf16[1,4,2,128]{3,2,1,0:T(2,128)(2,1)S(1)} %fusion.46), channel_id=1, source_target_pairs={{0,2},{2,0},{4,6},{6,4},{8,10},{10,8},{12,14},{14,12},{16,18},{18,... | collective-permute-start | bytes 6152 | tf_op jit(solution)/shard_map/ppermute | solution.py:251
  32.9 8.3 %collective-permute-start.9 = (f32[1,2,2,128]{3,2,1,0:T(2,128)S(1)}, f32[1,2,2,128]{3,2,1,0:T(2,128)S(1)}, u32[]{:S(2)}, u32[]{:S(2)}) collective-permute-start(f32[1,2,2,128]{3,2,1,0:T(2,128)S(1)} %maximum_bitcast_fusion.2), channel_id=1, source_target_pairs={{0,2},{2,0},{4,6},{6,4},{8,10},{10,8},{12,14},{14,12},{16,18},{18,... | collective-permute-start | bytes 6152 | tf_op jit(solution)/shard_map/ppermute | solution.py:251
  39.2 14.8 %collective-permute-start.6 = (bf16[128,2048]{1,0:T(8,128)(2,1)}, bf16[128,2048]{1,0:T(8,128)(2,1)}, u32[]{:S(2)}, u32[]{:S(2)}) collective-permute-start(bf16[128,2048]{1,0:T(8,128)(2,1)} %slice.438), channel_id=1, source_target_pairs={{0,2},{2,0},{4,6},{6,4},{8,10},{10,8},{12,14},{14,12},{16,18},{18,... | collective-permute-start | bytes 1572872 | tf_op jit(solution)/shard_map/ppermute | solution.py:251
  40.7 13.4 %collective-permute-start.7 = (bf16[128,2048]{1,0:T(8,128)(2,1)}, bf16[128,2048]{1,0:T(8,128)(2,1)}, u32[]{:S(2)}, u32[]{:S(2)}) collective-permute-start(bf16[128,2048]{1,0:T(8,128)(2,1)} %slice.439), channel_id=1, source_target_pairs={{0,4},{2,6},{4,0},{6,2},{8,12},{10,14},{12,8},{14,10},{16,20},{18,... | collective-permute-start | bytes 1572872 | tf_op jit(solution)/shard_map/ppermute | solution.py:251
  41.2 12.2 %collective-permute-start.10 = (bf16[1,2,4,2,128]{4,3,2,1,0:T(2,128)(2,1)S(1)}, bf16[1,2,4,2,128]{4,3,2,1,0:T(2,128)(2,1)S(1)}, u32[]{:S(2)}, u32[]{:S(2)}) collective-permute-start(bf16[1,2,4,2,128]{4,3,2,1,0:T(2,128)(2,1)S(1)} %fusion.45), channel_id=1, source_target_pairs={{0,4},{2,6},{4,0},{6,2},{8,12},{10,14},{12,8},{14,10},{16,20},{18,... | collective-permute-start | bytes 12296 | tf_op jit(solution)/shard_map/ppermute | solution.py:251
  42.8 11.2 %collective-permute-start.11 = (f32[1,2,2,2,128]{4,3,2,1,0:T(2,128)S(1)}, f32[1,2,2,2,128]{4,3,2,1,0:T(2,128)S(1)}, u32[]{:S(2)}, u32[]{:S(2)}) collective-permute-start(f32[1,2,2,2,128]{4,3,2,1,0:T(2,128)S(1)} %fusion.20), channel_id=1, source_target_pairs={{0,4},{2,6},{4,0},{6,2},{8,12},{10,14},{12,8},{14,10},{16,20},{18,... | collective-permute-start | bytes 12296 | tf_op jit(solution)/shard_map/ppermute | solution.py:251
  57.8 1.2 collective-permute-start.12
  59.0 25.2 %collective-permute-start.14 = (bf16[256,2048]{1,0:T(8,128)(2,1)S(1)}, bf16[256,2048]{1,0:T(8,128)(2,1)S(1)}, u32[]{:S(2)}, u32[]{:S(2)}) collective-permute-start(bf16[256,2048]{1,0:T(8,128)(2,1)S(1)} %bitcast.190), channel_id=1, source_target_pairs={{0,4},{2,6},{4,0},{6,2},{8,12},{10,14},{12,8},{14,10},{16,20},{18,... | collective-permute-start | bytes 3145736 | tf_op jit(solution)/shard_map/ppermute | solution.py:251
  59.6 25.1 %collective-permute-start.13 = (bf16[256,2048]{1,0:T(8,128)(2,1)S(1)}, bf16[256,2048]{1,0:T(8,128)(2,1)}, u32[]{:S(2)}, u32[]{:S(2)}) collective-permute-start(bf16[256,2048]{1,0:T(8,128)(2,1)S(1)} %bitcast.191), channel_id=1, source_target_pairs={{0,2},{2,0},{4,6},{6,4},{8,10},{10,8},{12,14},{14,12},{16,18},{18,... | collective-permute-start | bytes 3145736 | tf_op jit(solution)/shard_map/ppermute | solution.py:251
  93.8 13.0 %collective-permute-start.15 = (bf16[1024,2048]{1,0:T(8,128)(2,1)}, bf16[1024,2048]{1,0:T(8,128)(2,1)}, u32[]{:S(2)}, u32[]{:S(2)}) collective-permute-start(bf16[1024,2048]{1,0:T(8,128)(2,1)} %all-gather.4.cloned.1.call-done), channel_id=1, source_target_pairs={{0,1},{1,0},{2,3},{3,2},{4,5},{5,4},{6,7},{7,6},{8,9},{9,8},{10,11... | collective-permute-start | bytes 12582920 | tf_op jit(solution)/shard_map/ppermute | solution.py:255
  93.8 167.8 %all-gather.8.cloned.1.call-start = ((), (), s32[]{:S(2)}) async-start(), calls=%async_computation.6 | async-start | bytes 3604480 | tf_op jit(solution)/shard_map/all_gather | solution.py:276
  117.3 7.1 %collective-permute-start.16 = (f32[2,8,2,256]{3,2,1,0:T(2,128)S(1)}, f32[2,8,2,256]{3,2,1,0:T(2,128)S(1)}, u32[]{:S(2)}, u32[]{:S(2)}) collective-permute-start(f32[2,8,2,256]{3,2,1,0:T(2,128)S(1)} %pad_maximum_fusion.13), channel_id=1, source_target_pairs={{0,1},{2,3},{4,5},{6,7},{8,9},{10,11},{12,13},{14,15},{16,17},{18,... | collective-permute-start | bytes 98312 | tf_op jit(solution)/shard_map/ppermute | solution.py:258
  121.4 13.3 %collective-permute-start.17 = (bf16[128,2048]{1,0:T(8,128)(2,1)S(1)}, bf16[128,2048]{1,0:T(8,128)(2,1)S(1)}, u32[]{:S(2)}, u32[]{:S(2)}) collective-permute-start(bf16[128,2048]{1,0:T(8,128)(2,1)S(1)} %slice.463), channel_id=1, source_target_pairs={{0,2},{2,0},{4,6},{6,4},{8,10},{10,8},{12,14},{14,12},{16,18},{18,... | collective-permute-start | bytes 1572872 | tf_op jit(solution)/shard_map/ppermute | solution.py:251
  123.0 12.9 %collective-permute-start.18 = (bf16[128,2048]{1,0:T(8,128)(2,1)S(1)}, bf16[128,2048]{1,0:T(8,128)(2,1)S(1)}, u32[]{:S(2)}, u32[]{:S(2)}) collective-permute-start(bf16[128,2048]{1,0:T(8,128)(2,1)S(1)} %slice.464), channel_id=1, source_target_pairs={{0,4},{2,6},{4,0},{6,2},{8,12},{10,14},{12,8},{14,10},{16,20},{18,... | collective-permute-start | bytes 1572872 | tf_op jit(solution)/shard_map/ppermute | solution.py:251
  139.8 12.2 %collective-permute-start.20 = (bf16[128,2048]{1,0:T(8,128)(2,1)S(1)}, bf16[128,2048]{1,0:T(8,128)(2,1)S(1)}, u32[]{:S(2)}, u32[]{:S(2)}) collective-permute-start(bf16[128,2048]{1,0:T(8,128)(2,1)S(1)} %get-tuple-element.444), channel_id=1, source_target_pairs={{0,4},{2,6},{4,0},{6,2},{8,12},{10,14},{12,8},{14,10},{16,20},{18,... | collective-permute-start | bytes 1572872 | tf_op jit(solution)/shard_map/ppermute | solution.py:251
  141.3 11.9 %collective-permute-start.19 = (bf16[128,2048]{1,0:T(8,128)(2,1)S(1)}, bf16[128,2048]{1,0:T(8,128)(2,1)S(1)}, u32[]{:S(2)}, u32[]{:S(2)}) collective-permute-start(bf16[128,2048]{1,0:T(8,128)(2,1)S(1)} %get-tuple-element.445), channel_id=1, source_target_pairs={{0,2},{2,0},{4,6},{6,4},{8,10},{10,8},{12,14},{14,12},{16,18},{18,... | collective-permute-start | bytes 1572872 | tf_op jit(solution)/shard_map/ppermute | solution.py:251
  153.8 22.3 %collective-permute-start.21 = (bf16[256,2048]{1,0:T(8,128)(2,1)S(1)}, bf16[256,2048]{1,0:T(8,128)(2,1)S(1)}, u32[]{:S(2)}, u32[]{:S(2)}) collective-permute-start(bf16[256,2048]{1,0:T(8,128)(2,1)S(1)} %pad_maximum_fusion.3), channel_id=1, source_target_pairs={{0,2},{2,0},{4,6},{6,4},{8,10},{10,8},{12,14},{14,12},{16,18},{18,... | collective-permute-start | bytes 3145736 | tf_op jit(solution)/shard_map/ppermute | solution.py:251
  154.4 22.0 %collective-permute-start.22 = (bf16[256,2048]{1,0:T(8,128)(2,1)S(1)}, bf16[256,2048]{1,0:T(8,128)(2,1)S(1)}, u32[]{:S(2)}, u32[]{:S(2)}) collective-permute-start(bf16[256,2048]{1,0:T(8,128)(2,1)S(1)} %pad_maximum_fusion.2), channel_id=1, source_target_pairs={{0,4},{2,6},{4,0},{6,2},{8,12},{10,14},{12,8},{14,10},{16,20},{18,... | collective-permute-start | bytes 3145736 | tf_op jit(solution)/shard_map/ppermute | solution.py:251
  178.9 22.3 %collective-permute-start.24 = (bf16[256,2048]{1,0:T(8,128)(2,1)S(1)}, bf16[256,2048]{1,0:T(8,128)(2,1)S(1)}, u32[]{:S(2)}, u32[]{:S(2)}) collective-permute-start(bf16[256,2048]{1,0:T(8,128)(2,1)S(1)} %multiply_convert_fusion), channel_id=1, source_target_pairs={{0,4},{2,6},{4,0},{6,2},{8,12},{10,14},{12,8},{14,10},{16,20},{18,... | collective-permute-start | bytes 3145736 | tf_op jit(solution)/shard_map/ppermute | solution.py:251
  179.6 21.6 %collective-permute-start.23 = (bf16[256,2048]{1,0:T(8,128)(2,1)S(1)}, bf16[256,2048]{1,0:T(8,128)(2,1)S(1)}, u32[]{:S(2)}, u32[]{:S(2)}) collective-permute-start(bf16[256,2048]{1,0:T(8,128)(2,1)S(1)} %multiply_convert_fusion), channel_id=1, source_target_pairs={{0,2},{2,0},{4,6},{6,4},{8,10},{10,8},{12,14},{14,12},{16,18},{18,... | collective-permute-start | bytes 3145736 | tf_op jit(solution)/shard_map/ppermute | solution.py:251
  201.2 30.3 %collective-permute-start.27 = (bf16[1408,2048]{1,0:T(8,128)(2,1)}, bf16[1408,2048]{1,0:T(8,128)(2,1)}, u32[]{:S(2)}, u32[]{:S(2)}) collective-permute-start(bf16[1408,2048]{1,0:T(8,128)(2,1)} %all-gather.6.cloned.1.call-done), channel_id=1, source_target_pairs={{0,1},{1,0},{2,3},{3,2},{4,5},{5,4},{6,7},{7,6},{8,9},{9,8},{10,11... | collective-permute-start | bytes 17301512 | tf_op jit(solution)/shard_map/ppermute | solution.py:255
  202.9 14.6 %collective-permute-start.25 = (bf16[128,2048]{1,0:T(8,128)(2,1)}, bf16[128,2048]{1,0:T(8,128)(2,1)}, u32[]{:S(2)}, u32[]{:S(2)}) collective-permute-start(bf16[128,2048]{1,0:T(8,128)(2,1)} %slice.466), channel_id=1, source_target_pairs={{0,2},{2,0},{4,6},{6,4},{8,10},{10,8},{12,14},{14,12},{16,18},{18,... | collective-permute-start | bytes 1572872 | tf_op jit(solution)/shard_map/ppermute | solution.py:251
  204.4 14.3 %collective-permute-start.26 = (bf16[128,2048]{1,0:T(8,128)(2,1)}, bf16[128,2048]{1,0:T(8,128)(2,1)}, u32[]{:S(2)}, u32[]{:S(2)}) collective-permute-start(bf16[128,2048]{1,0:T(8,128)(2,1)} %slice.467), channel_id=1, source_target_pairs={{0,4},{2,6},{4,0},{6,2},{8,12},{10,14},{12,8},{14,10},{16,20},{18,... | collective-permute-start | bytes 1572872 | tf_op jit(solution)/shard_map/ppermute | solution.py:251
  205.9 150.2 %reduce-scatter.5.cloned.1.call-start = ((), (), s32[]{:S(2)}) async-start(), calls=%async_computation.7 | async-start | bytes 3604480 | tf_op jit(solution)/shard_map/reduce_scatter | solution.py:281
  250.8 5.3 collective-permute-start.28
  261.6 11.5 %collective-permute-start.29 = (bf16[704,2048]{1,0:T(8,128)(2,1)}, bf16[704,2048]{1,0:T(8,128)(2,1)}, u32[]{:S(2)}, u32[]{:S(2)}) collective-permute-start(bf16[704,2048]{1,0:T(8,128)(2,1)} %all-gather.8.cloned.1.call-done.down_ref.refs_2_), channel_id=1, source_target_pairs={{0,1},{1,0},{2,3},{3,2},{4,5},{5,4},{6,7},{7,6},{8,9},{9,8},{10,11... | collective-permute-start | bytes 8650760 | tf_op jit(solution)/shard_map/ppermute | solution.py:255
  261.7 183.6 %reduce-scatter.7.cloned.1.call-start = ((), (), s32[]{:S(2)}) async-start(), calls=%async_computation.8 | async-start | bytes 3604480 | tf_op jit(solution)/shard_map/reduce_scatter | solution.py:281
  298.8 5.6 %collective-permute-start.32 = (bf16[704,2048]{1,0:T(8,128)(2,1)S(1)}, bf16[704,2048]{1,0:T(8,128)(2,1)S(1)}, u32[]{:S(2)}, u32[]{:S(2)}) collective-permute-start(bf16[704,2048]{1,0:T(8,128)(2,1)S(1)} %shard_map.194), channel_id=1, source_target_pairs={{0,1},{1,0},{2,3},{3,2},{4,5},{5,4},{6,7},{7,6},{8,9},{9,8},{10,11... | collective-permute-start | bytes 8650760 | tf_op jit(solution)/shard_map/ppermute | solution.py:255
  299.7 13.9 %collective-permute-start.31 = (bf16[128,2048]{1,0:T(8,128)(2,1)S(1)}, bf16[128,2048]{1,0:T(8,128)(2,1)S(1)}, u32[]{:S(2)}, u32[]{:S(2)}) collective-permute-start(bf16[128,2048]{1,0:T(8,128)(2,1)S(1)} %get-tuple-element.438), channel_id=1, source_target_pairs={{0,4},{2,6},{4,0},{6,2},{8,12},{10,14},{12,8},{14,10},{16,20},{18,... | collective-permute-start | bytes 1572872 | tf_op jit(solution)/shard_map/ppermute | solution.py:251
  301.1 13.6 %collective-permute-start.30 = (bf16[128,2048]{1,0:T(8,128)(2,1)S(1)}, bf16[128,2048]{1,0:T(8,128)(2,1)S(1)}, u32[]{:S(2)}, u32[]{:S(2)}) collective-permute-start(bf16[128,2048]{1,0:T(8,128)(2,1)S(1)} %get-tuple-element.439), channel_id=1, source_target_pairs={{0,2},{2,0},{4,6},{6,4},{8,10},{10,8},{12,14},{14,12},{16,18},{18,... | collective-permute-start | bytes 1572872 | tf_op jit(solution)/shard_map/ppermute | solution.py:251
  325.3 128.3 %reduce-scatter.9.cloned.1.call-start = ((), (), s32[]{:S(2)}) async-start(), calls=%async_computation.9 | async-start | bytes 3604480 | tf_op jit(solution)/shard_map/reduce_scatter | solution.py:281
  325.5 5.6 %collective-permute-start.35 = (bf16[704,2048]{1,0:T(8,128)(2,1)}, bf16[704,2048]{1,0:T(8,128)(2,1)S(1)}, u32[]{:S(2)}, u32[]{:S(2)}) collective-permute-start(bf16[704,2048]{1,0:T(8,128)(2,1)} %copy-done.41), channel_id=1, source_target_pairs={{0,1},{1,0},{2,3},{3,2},{4,5},{5,4},{6,7},{7,6},{8,9},{9,8},{10,11... | collective-permute-start | bytes 8650760 | tf_op jit(solution)/shard_map/ppermute | solution.py:255
  325.6 25.8 %collective-permute-start.33 = (bf16[256,2048]{1,0:T(8,128)(2,1)}, bf16[256,2048]{1,0:T(8,128)(2,1)S(1)}, u32[]{:S(2)}, u32[]{:S(2)}) collective-permute-start(bf16[256,2048]{1,0:T(8,128)(2,1)} %pad_maximum_fusion.5), channel_id=1, source_target_pairs={{0,2},{2,0},{4,6},{6,4},{8,10},{10,8},{12,14},{14,12},{16,18},{18,... | collective-permute-start | bytes 3145736 | tf_op jit(solution)/shard_map/ppermute | solution.py:251
  327.1 25.5 %collective-permute-start.34 = (bf16[256,2048]{1,0:T(8,128)(2,1)}, bf16[256,2048]{1,0:T(8,128)(2,1)}, u32[]{:S(2)}, u32[]{:S(2)}) collective-permute-start(bf16[256,2048]{1,0:T(8,128)(2,1)} %pad_maximum_fusion.4), channel_id=1, source_target_pairs={{0,4},{2,6},{4,0},{6,2},{8,12},{10,14},{12,8},{14,10},{16,20},{18,... | collective-permute-start | bytes 3145736 | tf_op jit(solution)/shard_map/ppermute | solution.py:251
  361.1 24.4 %collective-permute-start.37 = (bf16[256,2048]{1,0:T(8,128)(2,1)S(1)}, bf16[256,2048]{1,0:T(8,128)(2,1)S(1)}, u32[]{:S(2)}, u32[]{:S(2)}) collective-permute-start(bf16[256,2048]{1,0:T(8,128)(2,1)S(1)} %get-tuple-element.331), channel_id=1, source_target_pairs={{0,4},{2,6},{4,0},{6,2},{8,12},{10,14},{12,8},{14,10},{16,20},{18,... | collective-permute-start | bytes 3145736 | tf_op jit(solution)/shard_map/ppermute | solution.py:251
  361.6 24.7 %collective-permute-start.36 = (bf16[256,2048]{1,0:T(8,128)(2,1)S(1)}, bf16[256,2048]{1,0:T(8,128)(2,1)S(1)}, u32[]{:S(2)}, u32[]{:S(2)}) collective-permute-start(bf16[256,2048]{1,0:T(8,128)(2,1)S(1)} %get-tuple-element.331), channel_id=1, source_target_pairs={{0,2},{2,0},{4,6},{6,4},{8,10},{10,8},{12,14},{14,12},{16,18},{18,... | collective-permute-start | bytes 3145736 | tf_op jit(solution)/shard_map/ppermute | solution.py:251
  387.1 15.2 %collective-permute-start.40 = (bf16[128,2048]{1,0:T(8,128)(2,1)}, bf16[128,2048]{1,0:T(8,128)(2,1)}, u32[]{:S(2)}, u32[]{:S(2)}) collective-permute-start(bf16[128,2048]{1,0:T(8,128)(2,1)} %slice.472), channel_id=1, source_target_pairs={{0,2},{2,0},{4,6},{6,4},{8,10},{10,8},{12,14},{14,12},{16,18},{18,... | collective-permute-start | bytes 1572872 | tf_op jit(solution)/shard_map/ppermute | solution.py:251
  387.7 15.2 %collective-permute-start.41 = (bf16[128,2048]{1,0:T(8,128)(2,1)}, bf16[128,2048]{1,0:T(8,128)(2,1)}, u32[]{:S(2)}, u32[]{:S(2)}) collective-permute-start(bf16[128,2048]{1,0:T(8,128)(2,1)} %slice.473), channel_id=1, source_target_pairs={{0,4},{2,6},{4,0},{6,2},{8,12},{10,14},{12,8},{14,10},{16,20},{18,... | collective-permute-start | bytes 1572872 | tf_op jit(solution)/shard_map/ppermute | solution.py:251
  388.6 140.8 %reduce-scatter.11.cloned.1.call-start = ((), (), s32[]{:S(2)}) async-start(), calls=%async_computation.10 | async-start | bytes 5242880 | tf_op jit(solution)/shard_map/reduce_scatter | solution.py:281
  390.3 22.6 %collective-permute-start.39 = (bf16[128,2048]{1,0:T(8,128)(2,1)S(1)}, bf16[128,2048]{1,0:T(8,128)(2,1)S(1)}, u32[]{:S(2)}, u32[]{:S(2)}) collective-permute-start(bf16[128,2048]{1,0:T(8,128)(2,1)S(1)} %get-tuple-element.432), channel_id=1, source_target_pairs={{0,4},{2,6},{4,0},{6,2},{8,12},{10,14},{12,8},{14,10},{16,20},{18,... | collective-permute-start | bytes 1572872 | tf_op jit(solution)/shard_map/ppermute | solution.py:251
  391.5 21.4 %collective-permute-start.38 = (bf16[128,2048]{1,0:T(8,128)(2,1)S(1)}, bf16[128,2048]{1,0:T(8,128)(2,1)S(1)}, u32[]{:S(2)}, u32[]{:S(2)}) collective-permute-start(bf16[128,2048]{1,0:T(8,128)(2,1)S(1)} %get-tuple-element.433), channel_id=1, source_target_pairs={{0,2},{2,0},{4,6},{6,4},{8,10},{10,8},{12,14},{14,12},{16,18},{18,... | collective-permute-start | bytes 1572872 | tf_op jit(solution)/shard_map/ppermute | solution.py:251
  412.9 15.7 %collective-permute-start.44 = (f32[2,16,2,256]{3,2,1,0:T(2,128)}, f32[2,16,2,256]{3,2,1,0:T(2,128)}, u32[]{:S(2)}, u32[]{:S(2)}) collective-permute-start(f32[2,16,2,256]{3,2,1,0:T(2,128)} %pad_maximum_fusion.12), channel_id=1, source_target_pairs={{1,0},{3,2},{5,4},{7,6},{9,8},{11,10},{13,12},{15,14},{17,16},{19,... | collective-permute-start | bytes 196616 | tf_op jit(solution)/shard_map/ppermute | solution.py:261
  424.5 17.1 %collective-permute-start.47 = (bf16[256,2048]{1,0:T(8,128)(2,1)}, bf16[256,2048]{1,0:T(8,128)(2,1)}, u32[]{:S(2)}, u32[]{:S(2)}) collective-permute-start(bf16[256,2048]{1,0:T(8,128)(2,1)} %shard_map.200), channel_id=1, source_target_pairs={{0,1},{1,0},{2,3},{3,2},{4,5},{5,4},{6,7},{7,6},{8,9},{9,8},{10,11... | collective-permute-start | bytes 3145736 | tf_op jit(solution)/shard_map/ppermute | solution.py:255
  426.3 12.9 %collective-permute-start.46 = (bf16[256,2048]{1,0:T(8,128)(2,1)S(1)}, bf16[256,2048]{1,0:T(8,128)(2,1)S(1)}, u32[]{:S(2)}, u32[]{:S(2)}) collective-permute-start(bf16[256,2048]{1,0:T(8,128)(2,1)S(1)} %shard_map.199), channel_id=1, source_target_pairs={{0,1},{1,0},{2,3},{3,2},{4,5},{5,4},{6,7},{7,6},{8,9},{9,8},{10,11... | collective-permute-start | bytes 3145736 | tf_op jit(solution)/shard_map/ppermute | solution.py:255
  426.3 27.2 %collective-permute-start.42 = (bf16[256,2048]{1,0:T(8,128)(2,1)}, bf16[256,2048]{1,0:T(8,128)(2,1)}, u32[]{:S(2)}, u32[]{:S(2)}) collective-permute-start(bf16[256,2048]{1,0:T(8,128)(2,1)} %pad_maximum_fusion.7), channel_id=1, source_target_pairs={{0,2},{2,0},{4,6},{6,4},{8,10},{10,8},{12,14},{14,12},{16,18},{18,... | collective-permute-start | bytes 3145736 | tf_op jit(solution)/shard_map/ppermute | solution.py:251
  427.8 25.8 %collective-permute-start.43 = (bf16[256,2048]{1,0:T(8,128)(2,1)}, bf16[256,2048]{1,0:T(8,128)(2,1)}, u32[]{:S(2)}, u32[]{:S(2)}) collective-permute-start(bf16[256,2048]{1,0:T(8,128)(2,1)} %pad_maximum_fusion.6), channel_id=1, source_target_pairs={{0,4},{2,6},{4,0},{6,2},{8,12},{10,14},{12,8},{14,10},{16,20},{18,... | collective-permute-start | bytes 3145736 | tf_op jit(solution)/shard_map/ppermute | solution.py:251
  439.2 6.1 %collective-permute-start.45 = (bf16[512,2048]{1,0:T(8,128)(2,1)}, bf16[512,2048]{1,0:T(8,128)(2,1)}, u32[]{:S(2)}, u32[]{:S(2)}) collective-permute-start(bf16[512,2048]{1,0:T(8,128)(2,1)} %shard_map.201), channel_id=1, source_target_pairs={{0,1},{1,0},{2,3},{3,2},{4,5},{5,4},{6,7},{7,6},{8,9},{9,8},{10,11... | collective-permute-start | bytes 6291464 | tf_op jit(solution)/shard_map/ppermute | solution.py:255
  470.4 14.5 %collective-permute-start.49 = (bf16[128,2048]{1,0:T(8,128)(2,1)S(1)}, bf16[128,2048]{1,0:T(8,128)(2,1)S(1)}, u32[]{:S(2)}, u32[]{:S(2)}) collective-permute-start(bf16[128,2048]{1,0:T(8,128)(2,1)S(1)} %get-tuple-element.426), channel_id=1, source_target_pairs={{0,4},{2,6},{4,0},{6,2},{8,12},{10,14},{12,8},{14,10},{16,20},{18,... | collective-permute-start | bytes 1572872 | tf_op jit(solution)/shard_map/ppermute | solution.py:251
  471.6 14.0 %collective-permute-start.48 = (bf16[128,2048]{1,0:T(8,128)(2,1)S(1)}, bf16[128,2048]{1,0:T(8,128)(2,1)S(1)}, u32[]{:S(2)}, u32[]{:S(2)}) collective-permute-start(bf16[128,2048]{1,0:T(8,128)(2,1)S(1)} %get-tuple-element.427), channel_id=1, source_target_pairs={{0,2},{2,0},{4,6},{6,4},{8,10},{10,8},{12,14},{14,12},{16,18},{18,... | collective-permute-start | bytes 1572872 | tf_op jit(solution)/shard_map/ppermute | solution.py:251
  488.2 24.7 %collective-permute-start.50 = (bf16[256,2048]{1,0:T(8,128)(2,1)}, bf16[256,2048]{1,0:T(8,128)(2,1)S(1)}, u32[]{:S(2)}, u32[]{:S(2)}) collective-permute-start(bf16[256,2048]{1,0:T(8,128)(2,1)} %pad_maximum_fusion.11), channel_id=1, source_target_pairs={{0,2},{2,0},{4,6},{6,4},{8,10},{10,8},{12,14},{14,12},{16,18},{18,... | collective-permute-start | bytes 3145736 | tf_op jit(solution)/shard_map/ppermute | solution.py:251
  488.8 24.5 %collective-permute-start.51 = (bf16[256,2048]{1,0:T(8,128)(2,1)}, bf16[256,2048]{1,0:T(8,128)(2,1)S(1)}, u32[]{:S(2)}, u32[]{:S(2)}) collective-permute-start(bf16[256,2048]{1,0:T(8,128)(2,1)} %pad_maximum_fusion.10), channel_id=1, source_target_pairs={{0,4},{2,6},{4,0},{6,2},{8,12},{10,14},{12,8},{14,10},{16,20},{18,... | collective-permute-start | bytes 3145736 | tf_op jit(solution)/shard_map/ppermute | solution.py:251
  493.2 1.2 collective-permute-start.52
  494.4 5.1 collective-permute-start.53
  499.6 7.0 %collective-permute-start.54 = (f32[3,2048]{1,0:T(4,128)S(1)}, f32[3,2048]{1,0:T(4,128)S(1)}, u32[]{:S(2)}, u32[]{:S(2)}) collective-permute-start(f32[3,2048]{1,0:T(4,128)S(1)} %add.209), channel_id=1, source_target_pairs={{0,16},{2,18},{4,20},{6,22},{8,24},{10,26},{12,28},{14,30},{16,0},... | collective-permute-start | bytes 73736 | tf_op jit(solution)/shard_map/ppermute | solution.py:251
  518.5 3.8 collective-permute-start.55
  522.3 3.8 collective-permute-start.56
  (129 other events, 799.0 us)
Sparse Core Ops, SparseCore 0:
  10.2 83.5 all-gather.3
  95.9 105.2 all-gather.5
  206.0 55.6 all-gather.7
  263.8 54.8 reduce-scatter.4
  325.4 53.7 reduce-scatter.6
  388.7 54.1 reduce-scatter.8
  453.7 75.6 reduce-scatter.10

commit v6 on v5

--- a/solution.py
+++ b/solution.py
@@ -556,10 +556,10 @@
     order.did(grad_low)
     mixer_rows = Rows(groups, grad_low)
     norm_two_term = jnp.sum(grad_normed_two * resid * scale_two, 0)
+    mixer_rows.middle()
     hidden_now, down_now = order(hidden, down_mats)
     ffn_out = sum_of_products(hidden_now, down_now)
     order.did(ffn_out, norm_two_term)
-    mixer_rows.middle()
     ffn_sums = Sums(groups, ffn_out, True)
     grad_mixer = mixer_rows.end()
     order.did(grad_mixer)

time: 550 us -> 550 us (level)
    unnamed x272 -> x280, local copies, waits for them, and re-layouts: 49.5 us -> 48.4 us
  transfers between devices with their start and end apart: 64 -> 64, of which waited for: 38 -> 38; matrix products, arithmetic and copies ran while one was open for 19% -> 18% of each run, Pallas kernels for 21% -> 21%
where the time goes in v6:
time: 550 us; the launch traced here: 540 us
  waiting for transfers between devices  209 us (38%)
  Pallas kernels  112 us (20%)
  local copies, waits for them, and re-layouts  77.5 us (14%)
  other arithmetic  58.4 us (11%)
  starting transfers between devices  56.9 us (10%)
  between operations  16.7 us (3%)
  matrix products  9.46 us (2%)
    ppermute x44, waiting for transfers between devices, swap(): return lax.ppermute(value, 'fsdp', [(i, i ^ bit) for i in range(self.fsdp)])  162 us
    ppermute x44, starting transfers between devices, swap(): return lax.ppermute(value, 'fsdp', [(i, i ^ bit) for i in range(self.fsdp)])  49 us
    unnamed x280, local copies, waits for them, and re-layouts  48.4 us
    pallas_call x11, Pallas kernels, columns_product(): pl.pallas_call(body, grid=(width // tile,), in_specs=[whole(left.shape),...  44.4 us
    pallas_call x4, Pallas kernels, sum_of_products(): pl.pallas_call(body, grid=(rows // tile,), in_specs=[pl.BlockSpec((tile,...  35.4 us
    all_gather x3, waiting for transfers between devices, gather_ordered(): lax.all_gather(value, 'fsdp', axis=0, tiled=True, axis_index_groups=self....  31.3 us
    pallas_call x4, Pallas kernels, ffn_call(): pl.pallas_call(body, grid=(rows // tile,), in_specs=[pl.BlockSpec((tile,...  26.3 us
    convert_element_type x15, other arithmetic, low(): return value.astype(jnp.bfloat16)  19.2 us
  transfers between devices with their start and end apart: 64, of which 38 were waited for; matrix products, arithmetic and copies ran while one was open for 18% of the time, Pallas kernels for 21%

profile of v6, /device:TPU:0, one launch (start us, length us, event | category | flops | bytes accessed | tf_op | source)
XLA Modules:
  0.0 540.0 jit_solution(6451708120512542220)
XLA Ops:
  7.3 2.4 pad_maximum_fusion.1
  9.7 3.0 collective-permute-start.1
  16.1 2.6 pad_maximum_fusion
  18.7 2.7 collective-permute-start.3
  24.0 2.8 collective-permute-done.4
  26.8 2.7 collective-permute-start.5
  34.2 3.3 collective-permute-done.8
  43.3 10.1 %collective-permute-done.10 = bf16[1,2,4,2,128]{4,3,2,1,0:T(2,128)(2,1)S(1)} collective-permute-done((bf16[1,2,4,2,128]{4,3,2,1,0:T(2,128)(2,1)S(1)}, bf16[1,2,4,2,128]{4,3,2,1,0:T(2,128)(2,1)S(1)}, u32[]{:S(2)}, u32[]{:S(2)}) %collective-permute-start.10) | collective-permute-done | bytes 4128 | tf_op jit(solution)/shard_map/ppermute | solution.py:251
  61.2 3.0 fusion.2.right_ref
  64.2 20.1 %collective-permute-done.14 = bf16[256,2048]{1,0:T(8,128)(2,1)S(1)} collective-permute-done((bf16[256,2048]{1,0:T(8,128)(2,1)S(1)}, bf16[256,2048]{1,0:T(8,128)(2,1)S(1)}, u32[]{:S(2)}, u32[]{:S(2)}) %collective-permute-start.14) | collective-permute-done | bytes 1048608 | tf_op jit(solution)/shard_map/ppermute | solution.py:251
  84.7 9.1 %all-gather.4.cloned.1.call-done = bf16[1024,2048]{1,0:T(8,128)(2,1)} async-done(((bf16[256,2048]{1,0:T(8,128)(2,1)}), bf16[1024,2048]{1,0:T(8,128)(2,1)}) %all-gather.4.cloned.1.call-update) | async-done | bytes 4194320 | tf_op jit(solution)/shard_map/all_gather | solution.py:276
  95.3 2.7 slice.441
  98.4 3.0 copy-done.38
  101.4 3.4 fusion.33
  106.8 2.1 slice.447
  108.9 2.7 slice.446
  112.0 3.4 fusion.34
  117.2 2.9 collective-permute-start.16
  127.5 3.1 shard_map.186
  130.7 3.9 collective-permute-done.17
  137.4 2.1 copy-done.4
  141.8 10.1 %collective-permute-done.20 = bf16[128,2048]{1,0:T(8,128)(2,1)S(1)} collective-permute-done((bf16[128,2048]{1,0:T(8,128)(2,1)S(1)}, bf16[128,2048]{1,0:T(8,128)(2,1)S(1)}, u32[]{:S(2)}, u32[]{:S(2)}) %collective-permute-start.20) | collective-permute-done | bytes 524320 | tf_op jit(solution)/shard_map/ppermute | solution.py:251
  154.8 21.1 %collective-permute-done.21 = bf16[256,2048]{1,0:T(8,128)(2,1)S(1)} collective-permute-done((bf16[256,2048]{1,0:T(8,128)(2,1)S(1)}, bf16[256,2048]{1,0:T(8,128)(2,1)S(1)}, u32[]{:S(2)}, u32[]{:S(2)}) %collective-permute-start.21) | collective-permute-done | bytes 1048608 | tf_op jit(solution)/shard_map/ppermute | solution.py:251
  180.9 20.3 %all-gather.6.cloned.1.call-done = bf16[1408,2048]{1,0:T(8,128)(2,1)} async-done(((bf16[352,2048]{1,0:T(8,128)(2,1)}), bf16[1408,2048]{1,0:T(8,128)(2,1)}) %all-gather.6.cloned.1.call-update) | async-done | bytes 5767184 | tf_op jit(solution)/shard_map/all_gather | solution.py:276
  205.9 11.6 %collective-permute-done.25 = bf16[128,2048]{1,0:T(8,128)(2,1)} collective-permute-done((bf16[128,2048]{1,0:T(8,128)(2,1)}, bf16[128,2048]{1,0:T(8,128)(2,1)}, u32[]{:S(2)}, u32[]{:S(2)}) %collective-permute-start.25) | collective-permute-done | bytes 524320 | tf_op jit(solution)/shard_map/ppermute | solution.py:251
  222.5 7.8 %shard_map.187 = (bf16[1024,704]{1,0:T(8,128)(2,1)S(1)}, bf16[1024,704]{1,0:T(8,128)(2,1)S(1)}, bf16[1024,704]{1,0:T(8,128)(2,1)S(1)}) custom-call(bf16[1024,2048]{1,0:T(8,128)(2,1)S(1)} %constant_dynamic-update-slice_fusion.10.normed_ref.right_ref, bf16[704,2048]{1,0:T(8,128)(2,1)S(1)} %bitcast.156, bf16[704,2048]{1,0:T(8,128)(2,1)S(1)} %bitcast.154), custom_call_target="tpu_custom_call" | custom-call | flops 1 | bytes 1 | tf_op jit(solution)/shard_map/pallas_call | solution.py:188
  232.7 4.2 fusion.24
  237.0 7.8 %shard_map.188 = (bf16[1024,704]{1,0:T(8,128)(2,1)S(1)}, bf16[1024,704]{1,0:T(8,128)(2,1)S(1)}, bf16[1024,704]{1,0:T(8,128)(2,1)S(1)}) custom-call(bf16[1024,2048]{1,0:T(8,128)(2,1)S(1)} %constant_dynamic-update-slice_fusion.10.normed_ref.right_ref, bf16[704,2048]{1,0:T(8,128)(2,1)S(1)} %bitcast.160, bf16[704,2048]{1,0:T(8,128)(2,1)S(1)} %bitcast.158), custom_call_target="tpu_custom_call" | custom-call | flops 1 | bytes 1 | tf_op jit(solution)/shard_map/pallas_call | solution.py:188
  244.8 4.3 shard_map.189
  249.2 5.3 collective-permute-done.28.refs_0_
  254.5 5.3 shard_map.190
  261.9 2.2 copy-done.6
  268.9 4.2 shard_map.191
  273.2 6.6 %shard_map.192 = (bf16[1024,704]{1,0:T(8,128)(2,1)S(1)}, bf16[1024,704]{1,0:T(8,128)(2,1)S(1)}) custom-call(bf16[1024,2048]{1,0:T(8,128)(2,1)S(1)} %copy-done.6, bf16[704,2048]{1,0:T(8,128)(2,1)} %collective-permute-done.29.down_ref.refs_3_, bf16[1024,704]{1,0:T(8,128)(2,1)S(1)} %copy-done.55, bf16[1024,704]{1,0:T(8,128)(2,1)S(1)} %copy-done.57), custom_call_target="tpu_custom_call" | custom-call | flops 1 | bytes 1 | tf_op jit(solution)/shard_map/pallas_call | solution.py:188
  279.8 14.6 %shard_map.193 = bf16[1024,2048]{1,0:T(8,128)(2,1)S(1)} custom-call(bf16[1024,704]{1,0:T(8,128)(2,1)S(1)} %get-tuple-element.306.refs_0_.left_ref, bf16[1024,704]{1,0:T(8,128)(2,1)S(1)} %get-tuple-element.303.refs_1_.left_ref, bf16[1024,704]{1,0:T(8,128)(2,1)S(1)} %get-tuple-element.316.refs_2_.left_ref, ...), custom_call_target="tpu_custom_call" | custom-call | flops 1 | bytes 1 | tf_op jit(solution)/shard_map/pallas_call | solution.py:84
  294.5 4.3 shard_map.194
  304.5 5.3 shard_map.195
  309.7 3.9 collective-permute-done.31
  319.3 4.3 shard_map.196
  327.5 3.4 collective-permute-done.35.refs_0_
  330.9 2.2 copy-done.3
  333.1 5.2 shard_map.197
  338.3 12.9 %collective-permute-done.33 = bf16[256,2048]{1,0:T(8,128)(2,1)S(1)} collective-permute-done((bf16[256,2048]{1,0:T(8,128)(2,1)}, bf16[256,2048]{1,0:T(8,128)(2,1)S(1)}, u32[]{:S(2)}, u32[]{:S(2)}) %collective-permute-start.33) | collective-permute-done | bytes 1048608 | tf_op jit(solution)/shard_map/ppermute | solution.py:251
  352.5 3.4 convert_add_fusion
  355.9 2.9 multiply_reduce_fusion.1
  362.3 22.9 %collective-permute-done.37 = bf16[256,2048]{1,0:T(8,128)(2,1)S(1)} collective-permute-done((bf16[256,2048]{1,0:T(8,128)(2,1)S(1)}, bf16[256,2048]{1,0:T(8,128)(2,1)S(1)}, u32[]{:S(2)}, u32[]{:S(2)}) %collective-permute-start.37) | collective-permute-done | bytes 1048608 | tf_op jit(solution)/shard_map/ppermute | solution.py:251
  391.9 9.7 %shard_map.198 = bf16[1024,2048]{1,0:T(8,128)(2,1)S(1)} custom-call(bf16[1024,704]{1,0:T(8,128)(2,1)S(1)} %copy-done.23, bf16[1024,704]{1,0:T(8,128)(2,1)S(1)} %copy-done.25, bf16[704,2048]{1,0:T(8,128)(2,1)S(1)} %copy-done.21, bf16[704,2048]{1,0:T(8,128)(2,1)} %collective-permute-done.29.down_ref.refs_3_), custom_call_target="tpu_custom_call" | custom-call | flops 1 | bytes 1 | tf_op jit(solution)/shard_map/pallas_call | solution.py:84
  419.2 2.3 shard_map.199
  421.5 3.2 shard_map.200
  434.7 4.3 shard_map.201
  439.0 2.4 shard_map.202.first_ref
  441.4 3.6 shard_map.203.last_ref
  445.1 2.2 copy-done.40
  447.3 6.0 %shard_map.204 = bf16[4,4,64,2048]{3,2,1,0:T(8,128)(2,1)} custom-call(bf16[1024,512]{1,0:T(8,128)(2,1)S(1)} %pad_maximum_fusion.8.left_ref.refs_2_, bf16[1024,2048]{1,0:T(8,128)(2,1)S(1)} %copy-done.40, bf16[256,2048]{1,0:T(8,128)(2,1)S(1)} %shard_map.202.first_ref, bf16[256,2048]{1,0:T(8,128)(2,1)S(1)} %shard_map.203.last_ref, ...), custom_call_target="tpu_custom_call" | custom-call | flops 99999997952 | bytes 1 | tf_op jit(solution)/shard_map/pallas_call | solution.py:170
  461.9 7.9 %shard_map.205 = bf16[1024,2048]{1,0:T(8,128)(2,1)S(1)} custom-call(bf16[1024,256]{1,0:T(8,128)(2,1)S(1)} %bitcast.173, bf16[1024,256]{1,0:T(8,128)(2,1)S(1)} %bitcast.171, bf16[1024,512]{1,0:T(8,128)(2,1)S(1)} %copy-done.35, bf16[1024,512]{1,0:T(8,128)(2,1)S(1)} %copy-done.37, bf16[768,2048]{1,0:T(8,128)(2,1)S(1)} %bitcast.149, ...), custom_call_target="tpu_custom_call" | custom-call | flops 1 | bytes 1 | tf_op jit(solution)/shard_map/pallas_call | solution.py:84
  475.0 9.5 %collective-permute-done.49 = bf16[128,2048]{1,0:T(8,128)(2,1)S(1)} collective-permute-done((bf16[128,2048]{1,0:T(8,128)(2,1)S(1)}, bf16[128,2048]{1,0:T(8,128)(2,1)S(1)}, u32[]{:S(2)}, u32[]{:S(2)}) %collective-permute-start.49) | collective-permute-done | bytes 524320 | tf_op jit(solution)/shard_map/ppermute | solution.py:251
  489.6 3.5 add_convert_fusion
  494.4 5.2 collective-permute-done.53
  500.4 2.5 convert_element_type.267
  503.0 3.7 collective-permute-done.54
  506.6 6.2 %collective-permute-done.50 = bf16[256,2048]{1,0:T(8,128)(2,1)S(1)} collective-permute-done((bf16[256,2048]{1,0:T(8,128)(2,1)}, bf16[256,2048]{1,0:T(8,128)(2,1)S(1)}, u32[]{:S(2)}, u32[]{:S(2)}) %collective-permute-start.50) | collective-permute-done | bytes 1048608 | tf_op jit(solution)/shard_map/ppermute | solution.py:251
  515.4 3.2 fusion.8
  523.8 2.4 collective-permute-done.56
  526.7 2.8 reduce-scatter.11.cloned.1.call-done
  (517 shorter events, 155.9 us)
Async XLA Ops:
  7.2 86.6 %all-gather.4.cloned.1.call-start = ((), (), s32[]{:S(2)}) async-start(), calls=%async_computation.4 | async-start | bytes 5242880 | tf_op jit(solution)/shard_map/all_gather | solution.py:276
  9.7 191.5 %all-gather.6.cloned.1.call-start = ((), (), s32[]{:S(2)}) async-start(), calls=%async_computation.5 | async-start | bytes 7208960 | tf_op jit(solution)/shard_map/all_gather | solution.py:276
  9.7 27.7 %collective-permute-start.1 = (bf16[256,2048]{1,0:T(8,128)(2,1)S(1)}, bf16[256,2048]{1,0:T(8,128)(2,1)S(1)}, u32[]{:S(2)}, u32[]{:S(2)}) collective-permute-start(bf16[256,2048]{1,0:T(8,128)(2,1)S(1)} %bitcast.182), channel_id=1, source_target_pairs={{0,4},{2,6},{4,0},{6,2},{8,12},{10,14},{12,8},{14,10},{16,20},{18,... | collective-permute-start | bytes 3145736 | tf_op jit(solution)/shard_map/ppermute | solution.py:251
  12.8 25.5 %collective-permute-start = (bf16[256,2048]{1,0:T(8,128)(2,1)S(1)}, bf16[256,2048]{1,0:T(8,128)(2,1)S(1)}, u32[]{:S(2)}, u32[]{:S(2)}) collective-permute-start(bf16[256,2048]{1,0:T(8,128)(2,1)S(1)} %bitcast.183), channel_id=1, source_target_pairs={{0,2},{2,0},{4,6},{6,4},{8,10},{10,8},{12,14},{14,12},{16,18},{18,... | collective-permute-start | bytes 3145736 | tf_op jit(solution)/shard_map/ppermute | solution.py:251
  14.3 4.4 collective-permute-start.2
  18.7 4.5 collective-permute-start.3
  23.2 3.6 collective-permute-start.4
  26.8 4.6 collective-permute-start.5
  31.4 6.0 %collective-permute-start.8 = (bf16[1,4,2,128]{3,2,1,0:T(2,128)(2,1)S(1)}, bf16[1,4,2,128]{3,2,1,0:T(2,128)(2,1)S(1)}, u32[]{:S(2)}, u32[]{:S(2)}) collective-permute-start(bf16[1,4,2,128]{3,2,1,0:T(2,128)(2,1)S(1)} %fusion.46), channel_id=1, source_target_pairs={{0,2},{2,0},{4,6},{6,4},{8,10},{10,8},{12,14},{14,12},{16,18},{18,... | collective-permute-start | bytes 6152 | tf_op jit(solution)/shard_map/ppermute | solution.py:251
  32.9 8.3 %collective-permute-start.9 = (f32[1,2,2,128]{3,2,1,0:T(2,128)S(1)}, f32[1,2,2,128]{3,2,1,0:T(2,128)S(1)}, u32[]{:S(2)}, u32[]{:S(2)}) collective-permute-start(f32[1,2,2,128]{3,2,1,0:T(2,128)S(1)} %maximum_bitcast_fusion.2), channel_id=1, source_target_pairs={{0,2},{2,0},{4,6},{6,4},{8,10},{10,8},{12,14},{14,12},{16,18},{18,... | collective-permute-start | bytes 6152 | tf_op jit(solution)/shard_map/ppermute | solution.py:251
  39.2 14.8 %collective-permute-start.6 = (bf16[128,2048]{1,0:T(8,128)(2,1)}, bf16[128,2048]{1,0:T(8,128)(2,1)}, u32[]{:S(2)}, u32[]{:S(2)}) collective-permute-start(bf16[128,2048]{1,0:T(8,128)(2,1)} %slice.438), channel_id=1, source_target_pairs={{0,2},{2,0},{4,6},{6,4},{8,10},{10,8},{12,14},{14,12},{16,18},{18,... | collective-permute-start | bytes 1572872 | tf_op jit(solution)/shard_map/ppermute | solution.py:251
  40.7 13.4 %collective-permute-start.7 = (bf16[128,2048]{1,0:T(8,128)(2,1)}, bf16[128,2048]{1,0:T(8,128)(2,1)}, u32[]{:S(2)}, u32[]{:S(2)}) collective-permute-start(bf16[128,2048]{1,0:T(8,128)(2,1)} %slice.439), channel_id=1, source_target_pairs={{0,4},{2,6},{4,0},{6,2},{8,12},{10,14},{12,8},{14,10},{16,20},{18,... | collective-permute-start | bytes 1572872 | tf_op jit(solution)/shard_map/ppermute | solution.py:251
  41.2 12.2 %collective-permute-start.10 = (bf16[1,2,4,2,128]{4,3,2,1,0:T(2,128)(2,1)S(1)}, bf16[1,2,4,2,128]{4,3,2,1,0:T(2,128)(2,1)S(1)}, u32[]{:S(2)}, u32[]{:S(2)}) collective-permute-start(bf16[1,2,4,2,128]{4,3,2,1,0:T(2,128)(2,1)S(1)} %fusion.45), channel_id=1, source_target_pairs={{0,4},{2,6},{4,0},{6,2},{8,12},{10,14},{12,8},{14,10},{16,20},{18,... | collective-permute-start | bytes 12296 | tf_op jit(solution)/shard_map/ppermute | solution.py:251
  42.8 11.2 %collective-permute-start.11 = (f32[1,2,2,2,128]{4,3,2,1,0:T(2,128)S(1)}, f32[1,2,2,2,128]{4,3,2,1,0:T(2,128)S(1)}, u32[]{:S(2)}, u32[]{:S(2)}) collective-permute-start(f32[1,2,2,2,128]{4,3,2,1,0:T(2,128)S(1)} %fusion.20), channel_id=1, source_target_pairs={{0,4},{2,6},{4,0},{6,2},{8,12},{10,14},{12,8},{14,10},{16,20},{18,... | collective-permute-start | bytes 12296 | tf_op jit(solution)/shard_map/ppermute | solution.py:251
  57.8 1.2 collective-permute-start.12
  59.0 25.2 %collective-permute-start.14 = (bf16[256,2048]{1,0:T(8,128)(2,1)S(1)}, bf16[256,2048]{1,0:T(8,128)(2,1)S(1)}, u32[]{:S(2)}, u32[]{:S(2)}) collective-permute-start(bf16[256,2048]{1,0:T(8,128)(2,1)S(1)} %bitcast.190), channel_id=1, source_target_pairs={{0,4},{2,6},{4,0},{6,2},{8,12},{10,14},{12,8},{14,10},{16,20},{18,... | collective-permute-start | bytes 3145736 | tf_op jit(solution)/shard_map/ppermute | solution.py:251
  59.6 25.1 %collective-permute-start.13 = (bf16[256,2048]{1,0:T(8,128)(2,1)S(1)}, bf16[256,2048]{1,0:T(8,128)(2,1)}, u32[]{:S(2)}, u32[]{:S(2)}) collective-permute-start(bf16[256,2048]{1,0:T(8,128)(2,1)S(1)} %bitcast.191), channel_id=1, source_target_pairs={{0,2},{2,0},{4,6},{6,4},{8,10},{10,8},{12,14},{14,12},{16,18},{18,... | collective-permute-start | bytes 3145736 | tf_op jit(solution)/shard_map/ppermute | solution.py:251
  93.8 13.0 %collective-permute-start.15 = (bf16[1024,2048]{1,0:T(8,128)(2,1)}, bf16[1024,2048]{1,0:T(8,128)(2,1)}, u32[]{:S(2)}, u32[]{:S(2)}) collective-permute-start(bf16[1024,2048]{1,0:T(8,128)(2,1)} %all-gather.4.cloned.1.call-done), channel_id=1, source_target_pairs={{0,1},{1,0},{2,3},{3,2},{4,5},{5,4},{6,7},{7,6},{8,9},{9,8},{10,11... | collective-permute-start | bytes 12582920 | tf_op jit(solution)/shard_map/ppermute | solution.py:255
  93.8 167.8 %all-gather.8.cloned.1.call-start = ((), (), s32[]{:S(2)}) async-start(), calls=%async_computation.6 | async-start | bytes 3604480 | tf_op jit(solution)/shard_map/all_gather | solution.py:276
  117.2 7.1 %collective-permute-start.16 = (f32[2,8,2,256]{3,2,1,0:T(2,128)S(1)}, f32[2,8,2,256]{3,2,1,0:T(2,128)S(1)}, u32[]{:S(2)}, u32[]{:S(2)}) collective-permute-start(f32[2,8,2,256]{3,2,1,0:T(2,128)S(1)} %pad_maximum_fusion.13), channel_id=1, source_target_pairs={{0,1},{2,3},{4,5},{6,7},{8,9},{10,11},{12,13},{14,15},{16,17},{18,... | collective-permute-start | bytes 98312 | tf_op jit(solution)/shard_map/ppermute | solution.py:258
  121.3 13.3 %collective-permute-start.17 = (bf16[128,2048]{1,0:T(8,128)(2,1)S(1)}, bf16[128,2048]{1,0:T(8,128)(2,1)S(1)}, u32[]{:S(2)}, u32[]{:S(2)}) collective-permute-start(bf16[128,2048]{1,0:T(8,128)(2,1)S(1)} %slice.463), channel_id=1, source_target_pairs={{0,2},{2,0},{4,6},{6,4},{8,10},{10,8},{12,14},{14,12},{16,18},{18,... | collective-permute-start | bytes 1572872 | tf_op jit(solution)/shard_map/ppermute | solution.py:251
  122.9 12.9 %collective-permute-start.18 = (bf16[128,2048]{1,0:T(8,128)(2,1)S(1)}, bf16[128,2048]{1,0:T(8,128)(2,1)S(1)}, u32[]{:S(2)}, u32[]{:S(2)}) collective-permute-start(bf16[128,2048]{1,0:T(8,128)(2,1)S(1)} %slice.464), channel_id=1, source_target_pairs={{0,4},{2,6},{4,0},{6,2},{8,12},{10,14},{12,8},{14,10},{16,20},{18,... | collective-permute-start | bytes 1572872 | tf_op jit(solution)/shard_map/ppermute | solution.py:251
  139.7 12.2 %collective-permute-start.20 = (bf16[128,2048]{1,0:T(8,128)(2,1)S(1)}, bf16[128,2048]{1,0:T(8,128)(2,1)S(1)}, u32[]{:S(2)}, u32[]{:S(2)}) collective-permute-start(bf16[128,2048]{1,0:T(8,128)(2,1)S(1)} %get-tuple-element.444), channel_id=1, source_target_pairs={{0,4},{2,6},{4,0},{6,2},{8,12},{10,14},{12,8},{14,10},{16,20},{18,... | collective-permute-start | bytes 1572872 | tf_op jit(solution)/shard_map/ppermute | solution.py:251
  141.1 11.8 %collective-permute-start.19 = (bf16[128,2048]{1,0:T(8,128)(2,1)S(1)}, bf16[128,2048]{1,0:T(8,128)(2,1)S(1)}, u32[]{:S(2)}, u32[]{:S(2)}) collective-permute-start(bf16[128,2048]{1,0:T(8,128)(2,1)S(1)} %get-tuple-element.445), channel_id=1, source_target_pairs={{0,2},{2,0},{4,6},{6,4},{8,10},{10,8},{12,14},{14,12},{16,18},{18,... | collective-permute-start | bytes 1572872 | tf_op jit(solution)/shard_map/ppermute | solution.py:251
  153.6 22.3 %collective-permute-start.21 = (bf16[256,2048]{1,0:T(8,128)(2,1)S(1)}, bf16[256,2048]{1,0:T(8,128)(2,1)S(1)}, u32[]{:S(2)}, u32[]{:S(2)}) collective-permute-start(bf16[256,2048]{1,0:T(8,128)(2,1)S(1)} %pad_maximum_fusion.3), channel_id=1, source_target_pairs={{0,2},{2,0},{4,6},{6,4},{8,10},{10,8},{12,14},{14,12},{16,18},{18,... | collective-permute-start | bytes 3145736 | tf_op jit(solution)/shard_map/ppermute | solution.py:251
  154.3 22.0 %collective-permute-start.22 = (bf16[256,2048]{1,0:T(8,128)(2,1)S(1)}, bf16[256,2048]{1,0:T(8,128)(2,1)S(1)}, u32[]{:S(2)}, u32[]{:S(2)}) collective-permute-start(bf16[256,2048]{1,0:T(8,128)(2,1)S(1)} %pad_maximum_fusion.2), channel_id=1, source_target_pairs={{0,4},{2,6},{4,0},{6,2},{8,12},{10,14},{12,8},{14,10},{16,20},{18,... | collective-permute-start | bytes 3145736 | tf_op jit(solution)/shard_map/ppermute | solution.py:251
  178.8 22.4 %collective-permute-start.24 = (bf16[256,2048]{1,0:T(8,128)(2,1)S(1)}, bf16[256,2048]{1,0:T(8,128)(2,1)S(1)}, u32[]{:S(2)}, u32[]{:S(2)}) collective-permute-start(bf16[256,2048]{1,0:T(8,128)(2,1)S(1)} %multiply_convert_fusion), channel_id=1, source_target_pairs={{0,4},{2,6},{4,0},{6,2},{8,12},{10,14},{12,8},{14,10},{16,20},{18,... | collective-permute-start | bytes 3145736 | tf_op jit(solution)/shard_map/ppermute | solution.py:251
  179.5 21.7 %collective-permute-start.23 = (bf16[256,2048]{1,0:T(8,128)(2,1)S(1)}, bf16[256,2048]{1,0:T(8,128)(2,1)S(1)}, u32[]{:S(2)}, u32[]{:S(2)}) collective-permute-start(bf16[256,2048]{1,0:T(8,128)(2,1)S(1)} %multiply_convert_fusion), channel_id=1, source_target_pairs={{0,2},{2,0},{4,6},{6,4},{8,10},{10,8},{12,14},{14,12},{16,18},{18,... | collective-permute-start | bytes 3145736 | tf_op jit(solution)/shard_map/ppermute | solution.py:251
  201.2 31.5 %collective-permute-start.27 = (bf16[1408,2048]{1,0:T(8,128)(2,1)}, bf16[1408,2048]{1,0:T(8,128)(2,1)}, u32[]{:S(2)}, u32[]{:S(2)}) collective-permute-start(bf16[1408,2048]{1,0:T(8,128)(2,1)} %all-gather.6.cloned.1.call-done), channel_id=1, source_target_pairs={{0,1},{1,0},{2,3},{3,2},{4,5},{5,4},{6,7},{7,6},{8,9},{9,8},{10,11... | collective-permute-start | bytes 17301512 | tf_op jit(solution)/shard_map/ppermute | solution.py:255
  202.9 14.6 %collective-permute-start.25 = (bf16[128,2048]{1,0:T(8,128)(2,1)}, bf16[128,2048]{1,0:T(8,128)(2,1)}, u32[]{:S(2)}, u32[]{:S(2)}) collective-permute-start(bf16[128,2048]{1,0:T(8,128)(2,1)} %slice.466), channel_id=1, source_target_pairs={{0,2},{2,0},{4,6},{6,4},{8,10},{10,8},{12,14},{14,12},{16,18},{18,... | collective-permute-start | bytes 1572872 | tf_op jit(solution)/shard_map/ppermute | solution.py:251
  204.4 14.3 %collective-permute-start.26 = (bf16[128,2048]{1,0:T(8,128)(2,1)}, bf16[128,2048]{1,0:T(8,128)(2,1)}, u32[]{:S(2)}, u32[]{:S(2)}) collective-permute-start(bf16[128,2048]{1,0:T(8,128)(2,1)} %slice.467), channel_id=1, source_target_pairs={{0,4},{2,6},{4,0},{6,2},{8,12},{10,14},{12,8},{14,10},{16,20},{18,... | collective-permute-start | bytes 1572872 | tf_op jit(solution)/shard_map/ppermute | solution.py:251
  205.9 150.0 %reduce-scatter.5.cloned.1.call-start = ((), (), s32[]{:S(2)}) async-start(), calls=%async_computation.7 | async-start | bytes 3604480 | tf_op jit(solution)/shard_map/reduce_scatter | solution.py:281
  249.1 5.3 collective-permute-start.28
  261.6 11.5 %collective-permute-start.29 = (bf16[704,2048]{1,0:T(8,128)(2,1)}, bf16[704,2048]{1,0:T(8,128)(2,1)}, u32[]{:S(2)}, u32[]{:S(2)}) collective-permute-start(bf16[704,2048]{1,0:T(8,128)(2,1)} %all-gather.8.cloned.1.call-done.down_ref.refs_2_), channel_id=1, source_target_pairs={{0,1},{1,0},{2,3},{3,2},{4,5},{5,4},{6,7},{7,6},{8,9},{9,8},{10,11... | collective-permute-start | bytes 8650760 | tf_op jit(solution)/shard_map/ppermute | solution.py:255
  261.7 183.4 %reduce-scatter.7.cloned.1.call-start = ((), (), s32[]{:S(2)}) async-start(), calls=%async_computation.8 | async-start | bytes 3604480 | tf_op jit(solution)/shard_map/reduce_scatter | solution.py:281
  298.8 5.6 %collective-permute-start.32 = (bf16[704,2048]{1,0:T(8,128)(2,1)S(1)}, bf16[704,2048]{1,0:T(8,128)(2,1)S(1)}, u32[]{:S(2)}, u32[]{:S(2)}) collective-permute-start(bf16[704,2048]{1,0:T(8,128)(2,1)S(1)} %shard_map.194), channel_id=1, source_target_pairs={{0,1},{1,0},{2,3},{3,2},{4,5},{5,4},{6,7},{7,6},{8,9},{9,8},{10,11... | collective-permute-start | bytes 8650760 | tf_op jit(solution)/shard_map/ppermute | solution.py:255
  299.7 13.9 %collective-permute-start.31 = (bf16[128,2048]{1,0:T(8,128)(2,1)S(1)}, bf16[128,2048]{1,0:T(8,128)(2,1)S(1)}, u32[]{:S(2)}, u32[]{:S(2)}) collective-permute-start(bf16[128,2048]{1,0:T(8,128)(2,1)S(1)} %get-tuple-element.438), channel_id=1, source_target_pairs={{0,4},{2,6},{4,0},{6,2},{8,12},{10,14},{12,8},{14,10},{16,20},{18,... | collective-permute-start | bytes 1572872 | tf_op jit(solution)/shard_map/ppermute | solution.py:251
  301.1 13.6 %collective-permute-start.30 = (bf16[128,2048]{1,0:T(8,128)(2,1)S(1)}, bf16[128,2048]{1,0:T(8,128)(2,1)S(1)}, u32[]{:S(2)}, u32[]{:S(2)}) collective-permute-start(bf16[128,2048]{1,0:T(8,128)(2,1)S(1)} %get-tuple-element.439), channel_id=1, source_target_pairs={{0,2},{2,0},{4,6},{6,4},{8,10},{10,8},{12,14},{14,12},{16,18},{18,... | collective-permute-start | bytes 1572872 | tf_op jit(solution)/shard_map/ppermute | solution.py:251
  325.3 128.1 %reduce-scatter.9.cloned.1.call-start = ((), (), s32[]{:S(2)}) async-start(), calls=%async_computation.9 | async-start | bytes 3604480 | tf_op jit(solution)/shard_map/reduce_scatter | solution.py:281
  325.3 5.6 %collective-permute-start.35 = (bf16[704,2048]{1,0:T(8,128)(2,1)}, bf16[704,2048]{1,0:T(8,128)(2,1)S(1)}, u32[]{:S(2)}, u32[]{:S(2)}) collective-permute-start(bf16[704,2048]{1,0:T(8,128)(2,1)} %copy-done.41), channel_id=1, source_target_pairs={{0,1},{1,0},{2,3},{3,2},{4,5},{5,4},{6,7},{7,6},{8,9},{9,8},{10,11... | collective-permute-start | bytes 8650760 | tf_op jit(solution)/shard_map/ppermute | solution.py:255
  325.4 25.8 %collective-permute-start.33 = (bf16[256,2048]{1,0:T(8,128)(2,1)}, bf16[256,2048]{1,0:T(8,128)(2,1)S(1)}, u32[]{:S(2)}, u32[]{:S(2)}) collective-permute-start(bf16[256,2048]{1,0:T(8,128)(2,1)} %pad_maximum_fusion.5), channel_id=1, source_target_pairs={{0,2},{2,0},{4,6},{6,4},{8,10},{10,8},{12,14},{14,12},{16,18},{18,... | collective-permute-start | bytes 3145736 | tf_op jit(solution)/shard_map/ppermute | solution.py:251
  326.9 25.5 %collective-permute-start.34 = (bf16[256,2048]{1,0:T(8,128)(2,1)}, bf16[256,2048]{1,0:T(8,128)(2,1)}, u32[]{:S(2)}, u32[]{:S(2)}) collective-permute-start(bf16[256,2048]{1,0:T(8,128)(2,1)} %pad_maximum_fusion.4), channel_id=1, source_target_pairs={{0,4},{2,6},{4,0},{6,2},{8,12},{10,14},{12,8},{14,10},{16,20},{18,... | collective-permute-start | bytes 3145736 | tf_op jit(solution)/shard_map/ppermute | solution.py:251
  360.8 24.3 %collective-permute-start.37 = (bf16[256,2048]{1,0:T(8,128)(2,1)S(1)}, bf16[256,2048]{1,0:T(8,128)(2,1)S(1)}, u32[]{:S(2)}, u32[]{:S(2)}) collective-permute-start(bf16[256,2048]{1,0:T(8,128)(2,1)S(1)} %get-tuple-element.331), channel_id=1, source_target_pairs={{0,4},{2,6},{4,0},{6,2},{8,12},{10,14},{12,8},{14,10},{16,20},{18,... | collective-permute-start | bytes 3145736 | tf_op jit(solution)/shard_map/ppermute | solution.py:251
  361.8 24.3 %collective-permute-start.36 = (bf16[256,2048]{1,0:T(8,128)(2,1)S(1)}, bf16[256,2048]{1,0:T(8,128)(2,1)S(1)}, u32[]{:S(2)}, u32[]{:S(2)}) collective-permute-start(bf16[256,2048]{1,0:T(8,128)(2,1)S(1)} %get-tuple-element.331), channel_id=1, source_target_pairs={{0,2},{2,0},{4,6},{6,4},{8,10},{10,8},{12,14},{14,12},{16,18},{18,... | collective-permute-start | bytes 3145736 | tf_op jit(solution)/shard_map/ppermute | solution.py:251
  387.5 16.9 %collective-permute-start.40 = (bf16[128,2048]{1,0:T(8,128)(2,1)}, bf16[128,2048]{1,0:T(8,128)(2,1)S(1)}, u32[]{:S(2)}, u32[]{:S(2)}) collective-permute-start(bf16[128,2048]{1,0:T(8,128)(2,1)} %slice.472), channel_id=1, source_target_pairs={{0,2},{2,0},{4,6},{6,4},{8,10},{10,8},{12,14},{14,12},{16,18},{18,... | collective-permute-start | bytes 1572872 | tf_op jit(solution)/shard_map/ppermute | solution.py:251
  388.1 16.3 %collective-permute-start.41 = (bf16[128,2048]{1,0:T(8,128)(2,1)}, bf16[128,2048]{1,0:T(8,128)(2,1)}, u32[]{:S(2)}, u32[]{:S(2)}) collective-permute-start(bf16[128,2048]{1,0:T(8,128)(2,1)} %slice.473), channel_id=1, source_target_pairs={{0,4},{2,6},{4,0},{6,2},{8,12},{10,14},{12,8},{14,10},{16,20},{18,... | collective-permute-start | bytes 1572872 | tf_op jit(solution)/shard_map/ppermute | solution.py:251
  388.8 140.7 %reduce-scatter.11.cloned.1.call-start = ((), (), s32[]{:S(2)}) async-start(), calls=%async_computation.10 | async-start | bytes 5242880 | tf_op jit(solution)/shard_map/reduce_scatter | solution.py:281
  401.9 11.9 %collective-permute-start.39 = (bf16[128,2048]{1,0:T(8,128)(2,1)S(1)}, bf16[128,2048]{1,0:T(8,128)(2,1)S(1)}, u32[]{:S(2)}, u32[]{:S(2)}) collective-permute-start(bf16[128,2048]{1,0:T(8,128)(2,1)S(1)} %get-tuple-element.432), channel_id=1, source_target_pairs={{0,4},{2,6},{4,0},{6,2},{8,12},{10,14},{12,8},{14,10},{16,20},{18,... | collective-permute-start | bytes 1572872 | tf_op jit(solution)/shard_map/ppermute | solution.py:251
  403.0 11.2 %collective-permute-start.38 = (bf16[128,2048]{1,0:T(8,128)(2,1)S(1)}, bf16[128,2048]{1,0:T(8,128)(2,1)S(1)}, u32[]{:S(2)}, u32[]{:S(2)}) collective-permute-start(bf16[128,2048]{1,0:T(8,128)(2,1)S(1)} %get-tuple-element.433), channel_id=1, source_target_pairs={{0,2},{2,0},{4,6},{6,4},{8,10},{10,8},{12,14},{14,12},{16,18},{18,... | collective-permute-start | bytes 1572872 | tf_op jit(solution)/shard_map/ppermute | solution.py:251
  414.3 14.1 %collective-permute-start.44 = (f32[2,16,2,256]{3,2,1,0:T(2,128)}, f32[2,16,2,256]{3,2,1,0:T(2,128)}, u32[]{:S(2)}, u32[]{:S(2)}) collective-permute-start(f32[2,16,2,256]{3,2,1,0:T(2,128)} %pad_maximum_fusion.12), channel_id=1, source_target_pairs={{1,0},{3,2},{5,4},{7,6},{9,8},{11,10},{13,12},{15,14},{17,16},{19,... | collective-permute-start | bytes 196616 | tf_op jit(solution)/shard_map/ppermute | solution.py:261
  424.7 16.7 %collective-permute-start.47 = (bf16[256,2048]{1,0:T(8,128)(2,1)}, bf16[256,2048]{1,0:T(8,128)(2,1)}, u32[]{:S(2)}, u32[]{:S(2)}) collective-permute-start(bf16[256,2048]{1,0:T(8,128)(2,1)} %shard_map.200), channel_id=1, source_target_pairs={{0,1},{1,0},{2,3},{3,2},{4,5},{5,4},{6,7},{7,6},{8,9},{9,8},{10,11... | collective-permute-start | bytes 3145736 | tf_op jit(solution)/shard_map/ppermute | solution.py:255
  426.4 12.6 %collective-permute-start.46 = (bf16[256,2048]{1,0:T(8,128)(2,1)S(1)}, bf16[256,2048]{1,0:T(8,128)(2,1)S(1)}, u32[]{:S(2)}, u32[]{:S(2)}) collective-permute-start(bf16[256,2048]{1,0:T(8,128)(2,1)S(1)} %shard_map.199), channel_id=1, source_target_pairs={{0,1},{1,0},{2,3},{3,2},{4,5},{5,4},{6,7},{7,6},{8,9},{9,8},{10,11... | collective-permute-start | bytes 3145736 | tf_op jit(solution)/shard_map/ppermute | solution.py:255
  426.4 26.9 %collective-permute-start.42 = (bf16[256,2048]{1,0:T(8,128)(2,1)}, bf16[256,2048]{1,0:T(8,128)(2,1)}, u32[]{:S(2)}, u32[]{:S(2)}) collective-permute-start(bf16[256,2048]{1,0:T(8,128)(2,1)} %pad_maximum_fusion.7), channel_id=1, source_target_pairs={{0,2},{2,0},{4,6},{6,4},{8,10},{10,8},{12,14},{14,12},{16,18},{18,... | collective-permute-start | bytes 3145736 | tf_op jit(solution)/shard_map/ppermute | solution.py:251
  427.8 25.6 %collective-permute-start.43 = (bf16[256,2048]{1,0:T(8,128)(2,1)}, bf16[256,2048]{1,0:T(8,128)(2,1)}, u32[]{:S(2)}, u32[]{:S(2)}) collective-permute-start(bf16[256,2048]{1,0:T(8,128)(2,1)} %pad_maximum_fusion.6), channel_id=1, source_target_pairs={{0,4},{2,6},{4,0},{6,2},{8,12},{10,14},{12,8},{14,10},{16,20},{18,... | collective-permute-start | bytes 3145736 | tf_op jit(solution)/shard_map/ppermute | solution.py:251
  438.9 6.1 %collective-permute-start.45 = (bf16[512,2048]{1,0:T(8,128)(2,1)}, bf16[512,2048]{1,0:T(8,128)(2,1)}, u32[]{:S(2)}, u32[]{:S(2)}) collective-permute-start(bf16[512,2048]{1,0:T(8,128)(2,1)} %shard_map.201), channel_id=1, source_target_pairs={{0,1},{1,0},{2,3},{3,2},{4,5},{5,4},{6,7},{7,6},{8,9},{9,8},{10,11... | collective-permute-start | bytes 6291464 | tf_op jit(solution)/shard_map/ppermute | solution.py:255
  470.1 14.4 %collective-permute-start.49 = (bf16[128,2048]{1,0:T(8,128)(2,1)S(1)}, bf16[128,2048]{1,0:T(8,128)(2,1)S(1)}, u32[]{:S(2)}, u32[]{:S(2)}) collective-permute-start(bf16[128,2048]{1,0:T(8,128)(2,1)S(1)} %get-tuple-element.426), channel_id=1, source_target_pairs={{0,4},{2,6},{4,0},{6,2},{8,12},{10,14},{12,8},{14,10},{16,20},{18,... | collective-permute-start | bytes 1572872 | tf_op jit(solution)/shard_map/ppermute | solution.py:251
  471.6 14.0 %collective-permute-start.48 = (bf16[128,2048]{1,0:T(8,128)(2,1)S(1)}, bf16[128,2048]{1,0:T(8,128)(2,1)S(1)}, u32[]{:S(2)}, u32[]{:S(2)}) collective-permute-start(bf16[128,2048]{1,0:T(8,128)(2,1)S(1)} %get-tuple-element.427), channel_id=1, source_target_pairs={{0,2},{2,0},{4,6},{6,4},{8,10},{10,8},{12,14},{14,12},{16,18},{18,... | collective-permute-start | bytes 1572872 | tf_op jit(solution)/shard_map/ppermute | solution.py:251
  488.2 24.7 %collective-permute-start.50 = (bf16[256,2048]{1,0:T(8,128)(2,1)}, bf16[256,2048]{1,0:T(8,128)(2,1)S(1)}, u32[]{:S(2)}, u32[]{:S(2)}) collective-permute-start(bf16[256,2048]{1,0:T(8,128)(2,1)} %pad_maximum_fusion.11), channel_id=1, source_target_pairs={{0,2},{2,0},{4,6},{6,4},{8,10},{10,8},{12,14},{14,12},{16,18},{18,... | collective-permute-start | bytes 3145736 | tf_op jit(solution)/shard_map/ppermute | solution.py:251
  488.9 24.5 %collective-permute-start.51 = (bf16[256,2048]{1,0:T(8,128)(2,1)}, bf16[256,2048]{1,0:T(8,128)(2,1)S(1)}, u32[]{:S(2)}, u32[]{:S(2)}) collective-permute-start(bf16[256,2048]{1,0:T(8,128)(2,1)} %pad_maximum_fusion.10), channel_id=1, source_target_pairs={{0,4},{2,6},{4,0},{6,2},{8,12},{10,14},{12,8},{14,10},{16,20},{18,... | collective-permute-start | bytes 3145736 | tf_op jit(solution)/shard_map/ppermute | solution.py:251
  493.1 1.2 collective-permute-start.52
  494.4 5.3 collective-permute-start.53
  499.6 7.0 %collective-permute-start.54 = (f32[3,2048]{1,0:T(4,128)S(1)}, f32[3,2048]{1,0:T(4,128)S(1)}, u32[]{:S(2)}, u32[]{:S(2)}) collective-permute-start(f32[3,2048]{1,0:T(4,128)S(1)} %add.209), channel_id=1, source_target_pairs={{0,16},{2,18},{4,20},{6,22},{8,24},{10,26},{12,28},{14,30},{16,0},... | collective-permute-start | bytes 73736 | tf_op jit(solution)/shard_map/ppermute | solution.py:251
  518.6 3.7 collective-permute-start.55
  522.3 3.8 collective-permute-start.56
  (133 other events, 806.7 us)
Sparse Core Ops, SparseCore 0:
  10.2 83.5 all-gather.3
  95.9 105.2 all-gather.5
  206.0 55.6 all-gather.7
  263.8 54.8 reduce-scatter.4
  325.4 53.7 reduce-scatter.6
  388.9 54.4 reduce-scatter.8
  453.5 75.9 reduce-scatter.10
